TPU v7x, 128 devices: a whole 4x4x4 slice. The times are simulated.
128 devices in a mesh: seq: 16 (over y, z), tp: 8 (over x, core).
Axes of the slice: x: 4, y: 4, z: 4, core: 2. Of those that a mesh axis runs over, the one named last changes fastest.
Arguments:
- encoded: bfloat16 [32768, 1280], P(('seq', 'tp')), may hold values from -6 to 6
- starts: int32 [128, 32], replicated, may hold values from 0 to 256, as said below
- w_up: bfloat16 [1280, 4096], P(None, 'tp'), may hold values from -0.15625 to 0.15625
- norm_gain: float32 [4096], replicated, may hold values from 0.25 to 1.75
- w_query: bfloat16 [4096, 4096], P(None, 'tp'), may hold values from -8 to 8
- w_key: bfloat16 [4096, 4096], P(None, 'tp'), may hold values from -8 to 8
- w_value: bfloat16 [4096, 4096], P(None, 'tp'), may hold values from -0.09375 to 0.09375
- w_out: bfloat16 [4096, 4096], P('tp'), may hold values from -0.09375 to 0.09375
- cotangent: bfloat16 [4096, 4096], P('seq', 'tp'), may hold values from -6 to 6
Outputs:
- latent_out: bfloat16 [4096, 4096], P('seq', 'tp')
- latent_grad: float32 [4096, 4096], P('seq', 'tp')
Inputs may be any that keep to these rules, and one draw needn't show every extreme that they name: `starts`: row i lists in increasing order the distinct offsets at which patches begin in byte shard i, followed by 256 in unused slots; every shard has at least one patch and at least 8, some shard exactly 32; shard 0 begins a patch at offset 0.
All inputs are finite; a program needn't handle non-finite values.
Results may differ from a plain program's by a relative error of at most 0.014.
Values may be sent and summed in bfloat16 or wider, within the bound.
No kernel may reach another device: no remote copies, remote signals or barrier semaphores. Data moves between devices by JAX's collectives and lax.ppermute only.
A program may use at most 128 MiB of HBM per device.

v0:
```python
import functools

import jax
import jax.numpy as jnp
from jax import lax
from jax.experimental import pallas as pl
from jax.experimental.pallas import tpu as pltpu
from jax.sharding import Mesh
from jax.sharding import PartitionSpec as P

HEAD = 128
SEQ = ("y", "z")
TP = ("x", "c")
ALL = ("y", "z", "x", "c")
EPS = 1e-05
NEG = -1e30
SCALE = HEAD ** (-0.5)
LOG2E = 1.4426950408889634
EXP2_SCALE = SCALE * LOG2E
F32 = jnp.float32
BF16 = jnp.bfloat16
NT = (((1,), (1,)), ((), ()))
TN = (((0,), (0,)), ((), ()))
VMEM = pl.BlockSpec(memory_space=pltpu.VMEM)
XC = ("x", "c")


def shape(*dims, dtype=BF16):
    return jax.ShapeDtypeStruct(dims, dtype)


def call(kernel, ins, outs, scratch=(), name=None, megabytes=8, micros=1.0, stay=0):
    return pl.pallas_call(
        kernel,
        in_specs=[VMEM] * (len(ins) - stay) + [pl.BlockSpec(memory_space=pl.ANY)] * stay,
        out_specs=[VMEM] * len(outs),
        out_shape=list(outs),
        scratch_shapes=list(scratch),
        compiler_params=pltpu.CompilerParams(vmem_limit_bytes=megabytes * 1024 * 1024),
        cost_estimate=pl.CostEstimate(
            flops=int(micros * 1e9), transcendentals=0, bytes_accessed=int(micros * 3e6)
        ),
        name=name,
    )(*ins)


def place(axis):
    return lax.axis_index(axis)


def other_core(block):
    return lax.ppermute(block, "c", [(0, 1), (1, 0)])


def along_x(block):
    route = []
    for x in range(4):
        for c in range(2):
            route.append((x * 2 + c, ((x + 1 - 2 * c) % 4) * 2 + c))
    return lax.ppermute(block, XC, route)


def bounds(starts_ref, shard, byte_rows):
    row = starts_ref[pl.ds(shard, 1), :]
    end = jnp.full((1, 1), byte_rows, jnp.int32)
    return row, jnp.concatenate([row[:, 1:], end], axis=1)


def pool_kernel(starts_ref, enc_ref, sums_ref, lead_ref):
    byte_rows = enc_ref.shape[0]
    cap = starts_ref.shape[1]
    row, following = bounds(starts_ref, place(ALL), byte_rows)
    places = lax.broadcasted_iota(jnp.int32, (byte_rows, cap), 0)
    inside = ((places >= row) & (places < following)).astype(F32).astype(BF16)
    enc = enc_ref[...]
    sums_ref[...] = lax.dot_general(inside, enc, TN, preferred_element_type=F32)
    leading = (places < row[:, :1]).astype(F32).astype(BF16)
    lead = lax.dot_general(leading, enc, TN, preferred_element_type=F32)
    lead_ref[...] = lead[:1]


def as_column(row, eye):
    return jnp.sum(jnp.where(eye, row, 0.0), axis=1, keepdims=True)


def as_row(column, eye):
    return jnp.sum(jnp.where(eye, column, 0.0), axis=0, keepdims=True)


def eye_of(n):
    return lax.broadcasted_iota(jnp.int32, (n, n), 0) == lax.broadcasted_iota(jnp.int32, (n, n), 1)


def patch_kernel(byte_rows, starts_ref, sums_ref, next_ref, out_ref):
    shards, cap = starts_ref.shape
    shard = place(ALL)
    row, following = bounds(starts_ref, shard, byte_rows)
    count = jnp.sum((row < byte_rows).astype(F32), axis=1, keepdims=True)
    slot = lax.broadcasted_iota(jnp.int32, (1, cap), 1).astype(F32)
    last = (slot == count - 1.0).astype(F32)
    after = starts_ref[pl.ds(jnp.minimum(shard + 1, shards - 1), 1), :][:, :1].astype(F32)
    after = jnp.where(shard + 1 < shards, after, 0.0)
    sizes = (following - row).astype(F32) + last * after
    eye = eye_of(cap)
    total = sums_ref[...] + as_column(last, eye) * next_ref[...]
    out_ref[...] = (total / as_column(jnp.maximum(sizes, 1.0), eye)).astype(BF16)


def latent_kernel(own_ref, other_ref, w_ref, out_ref, group):
    x, c = place("x"), place("c")
    count, rows, width = own_ref.shape
    for k in range(count):
        at = lax.rem(x + count - k, count) * 2
        group[at + c] = own_ref[k]
        group[at + 1 - c] = other_ref[k]
    whole = group[...].reshape(2 * count * rows, width)
    out_ref[...] = jnp.dot(whole, w_ref[...], preferred_element_type=F32).astype(BF16)


def tp_places():
    x, c = place("x"), place("c")
    back = lax.rem(x + 3 + 2 * c, 4) * 2
    ahead = lax.rem(x + 1 + 2 * c, 4) * 2
    far = lax.rem(x + 2, 4) * 2
    o = 1 - c
    return [2 * x + c, 2 * x + o, back + c, back + o, ahead + o, ahead + c, far + c, far + o]


def piece_rows(ref, at, size):
    return ref[pl.ds(pl.multiple_of(at * size, size), size), :]


def project_kernel(*refs):
    pieces, (do_ref, gain_ref), weights = refs[:8], refs[8:10], refs[10:13]
    outs, (held, sems, lats, accs, heads) = refs[13:19], refs[19:24]
    keep_ref, send_ref, qkv_refs, rinv_ref = outs[0], outs[1], outs[2:5], outs[5]
    rows, size = pieces[0].shape
    width = gain_ref.shape[1]
    c = place("c")
    places = tp_places()
    copies = []
    for t in range(8):
        for kind in range(3):
            part = weights[kind].at[t * size : (t + 1) * size, :]
            copies.append(pltpu.make_async_copy(part, held.at[t, kind], sems.at[t, kind]))
    for copy in copies:
        copy.start()
    for piece, at in zip(pieces, places):
        lats[at] = piece[...]
    for h in range(4):
        heads[12 + h] = do_ref[:, h * HEAD : (h + 1) * HEAD]
    square = jnp.zeros((rows, 128), F32)
    for t in range(8):
        wide = lats[t].astype(F32)
        squares = wide * wide
        for part in range(0, size, 128):
            square = square + squares[:, part : part + 128]
        scaled = (wide * gain_ref[:, t * size : (t + 1) * size]).astype(BF16)
        for kind in range(3):
            copies[3 * t + kind].wait()
            made = jnp.dot(scaled, held[t, kind], preferred_element_type=F32)
            accs[kind] = made if t == 0 else accs[kind] + made
    total = jnp.sum(square, axis=1, keepdims=True)
    rinv = lax.rsqrt(total / width + EPS)
    rinv_ref[...] = rinv
    for kind in range(3):
        rounded = (rinv * accs[kind]).astype(BF16)
        qkv_refs[kind][...] = rounded
        for h in range(4):
            heads[kind * 4 + h] = rounded[:, h * HEAD : (h + 1) * HEAD]
    half = rows // 2
    for out, which in ((keep_ref, c), (send_ref, 1 - c)):
        span = pl.ds(pl.multiple_of(which * half, half), half)
        for h in range(4):
            out[h, :half, :HEAD] = heads[4 + h, span, :]
            out[h, :half, HEAD:] = heads[8 + h, span, :]
            out[h, half:, :HEAD] = heads[h, span, :]
            out[h, half:, HEAD:] = heads[12 + h, span, :]


def project(pieces, d_attn, gain, weights):
    rows, size = pieces[0].shape
    both = shape(4, rows, 2 * HEAD)
    return call(
        project_kernel,
        (*pieces, d_attn, gain, *weights),
        [both, both] + [shape(rows, size)] * 3 + [shape(rows, 1, dtype=F32)],
        [
            pltpu.VMEM((8, 3, size, size), BF16),
            pltpu.SemaphoreType.DMA((8, 3)),
            pltpu.VMEM((8, rows, size), BF16),
            pltpu.VMEM((3, rows, size), F32),
            pltpu.VMEM((16, rows, HEAD), BF16),
        ],
        name="project",
        megabytes=28,
        micros=5.0,
        stay=3,
    )


def d_attn_kernel(*refs):
    grads, valid_ref, w_ref, out_ref, held, sems = refs[:8], *refs[8:]
    size = grads[0].shape[1]
    copies = []
    for h in range(4):
        span = slice(h * HEAD, (h + 1) * HEAD)
        copies.append(pltpu.make_async_copy(w_ref.at[span, :], held.at[span, :], sems.at[h]))
    for copy in copies:
        copy.start()
    valid = valid_ref[...] > 0.0
    places = tp_places()
    for h in range(4):
        copies[h].wait()
        span = slice(h * HEAD, (h + 1) * HEAD)
        acc = 0.0
        for piece, at in zip(grads, places):
            w = held[span, pl.ds(pl.multiple_of(at * size, size), size)]
            acc = acc + lax.dot_general(piece[...], w, NT, preferred_element_type=F32)
        out_ref[:, span] = jnp.where(valid, acc, 0.0).astype(BF16)


def d_attn_of(grads, valid, w_out):
    return call(
        d_attn_kernel,
        (*grads, valid, w_out),
        [shape(*grads[0].shape)],
        [pltpu.VMEM(w_out.shape, BF16), pltpu.SemaphoreType.DMA((4,))],
        name="d_attn",
        megabytes=12,
        micros=2.0,
        stay=1,
    )[0]


def pack_kernel(keep_ref, got_ref, out_ref):
    c = place("c")
    half = keep_ref.shape[1] // 2
    strip = half // 2
    for ref, core in ((keep_ref, c), (got_ref, 1 - c)):
        for h in range(4):
            for e in range(2):
                s = (core * 4 + h) * 2 + e
                out_ref[s, :half, :] = ref[h, :half, :]
                out_ref[s, half:, :] = ref[h, half + e * strip : half + (e + 1) * strip, :]


def attention_kernel(bias_ref, mine_ref, theirs_ref, keep_ref, send_ref, strip_ref, *scratch):
    scores, dks, dvs, biases = scratch
    c, e = place("c"), lax.rem(place("z"), 2)
    blocks = mine_ref.shape[0]
    half, strip, span, rows = 128, 64, 512, 256
    sources = (mine_ref, theirs_ref)

    def kv_of(side, u):
        ref = sources[side]
        keys = ref[4 * u : 4 * u + 4, :half, :HEAD].reshape(span, HEAD)
        return keys, ref[4 * u : 4 * u + 4, :half, HEAD:].reshape(span, HEAD)

    biases[0], biases[1] = bias_ref[c], bias_ref[1 - c]
    dks[...] = jnp.zeros_like(dks)
    dvs[...] = jnp.zeros_like(dvs)
    lane = lax.broadcasted_iota(jnp.int32, (1, rows), 1)
    place_q = (lane // strip) * 256 + lax.rem(lane, strip) + c * half + e * strip
    line = lax.broadcasted_iota(jnp.int32, (span, 1), 0)
    place_k = (line // half) * 256 + lax.rem(line, half)
    allowed = [place_k + which * half <= place_q for which in (c, 1 - c)]
    for t in range(4):
        q = mine_ref[4 * t : 4 * t + 4, half:, :HEAD].reshape(rows, HEAD)
        do = mine_ref[4 * t : 4 * t + 4, half:, HEAD:].reshape(rows, HEAD)
        peak = jnp.full((1, rows), NEG, F32)
        for side in range(2):
            for u in range(t + 1):
                keys, _ = kv_of(side, u)
                s = lax.dot_general(keys, q, NT, preferred_element_type=F32)
                bias = biases[side, u * span : (u + 1) * span, :]
                s = s + jnp.concatenate([bias, bias], axis=1)
                if u == t:
                    s = jnp.where(allowed[side], s, NEG)
                scores[side * 4 + u] = s
                peak = jnp.maximum(peak, jnp.max(s, axis=0, keepdims=True))
        total = jnp.zeros((1, rows), F32)
        mixed = jnp.zeros((HEAD, rows), F32)
        for side in range(2):
            for u in range(t + 1):
                _, values = kv_of(side, u)
                p = jnp.exp2((scores[side * 4 + u] - peak) * EXP2_SCALE)
                total = total + jnp.sum(p, axis=0, keepdims=True)
                scores[side * 4 + u] = p
                mixed = mixed + lax.dot_general(
                    values, p.astype(BF16), TN, preferred_element_type=F32
                )
        inverse = 1.0 / total
        attn = jnp.transpose(mixed * inverse).astype(BF16)
        products = do.astype(F32) * attn.astype(F32)
        delta = jnp.sum(jnp.transpose(products), axis=0, keepdims=True)
        dq = jnp.zeros((HEAD, rows), F32)
        for side in range(2):
            for u in range(t + 1):
                keys, values = kv_of(side, u)
                p = scores[side * 4 + u] * inverse
                dp = lax.dot_general(values, do, NT, preferred_element_type=F32)
                ds = (p * (dp - delta)).astype(BF16)
                at = slice(u * span, (u + 1) * span)
                dvs[side, at, :] += jnp.dot(p.astype(BF16), do, preferred_element_type=F32)
                dks[side, at, :] += jnp.dot(ds, q, preferred_element_type=F32)
                dq = dq + lax.dot_general(keys, ds, TN, preferred_element_type=F32)
        dq = jnp.transpose(dq * SCALE).astype(BF16)
        strip_ref[4 * t : 4 * t + 4, :, :HEAD] = dq.reshape(4, strip, HEAD)
        strip_ref[4 * t : 4 * t + 4, :, HEAD:] = attn.reshape(4, strip, HEAD)
    for side, ref in ((0, keep_ref), (1, send_ref)):
        ref[:, :, :HEAD] = (dks[side] * SCALE).astype(BF16).reshape(blocks, half, HEAD)
        ref[:, :, HEAD:] = dvs[side].astype(BF16).reshape(blocks, half, HEAD)


def attention(bias, mine, theirs):
    blocks, _, both = mine.shape
    grads = shape(blocks, 128, both)
    return call(
        attention_kernel,
        (bias, mine, theirs),
        [grads, grads, shape(blocks, 64, both)],
        [pltpu.VMEM((8, 512, 256), F32)] + [pltpu.VMEM((2, blocks * 128, HEAD), F32)] * 3,
        name="attention",
        megabytes=28,
        micros=12.0,
    )


def return_kernel(keep_ref, got_ref, strip_ref, out_ref):
    half = keep_ref.shape[1]
    out_ref[:, :half, :] = (keep_ref[...].astype(F32) + got_ref[...].astype(F32)).astype(BF16)
    out_ref[:, half:, :] = strip_ref[...]


def regroup_kernel(in_ref, keep_ref, send_ref):
    c = place("c")
    half, strip = 128, 64
    for out, core in ((keep_ref, c), (send_ref, 1 - c)):
        for h in range(4):
            s = (core * 4 + h) * 2
            total = in_ref[s, :half, :].astype(F32) + in_ref[s + 1, :half, :].astype(F32)
            out[h, :half, :] = total.astype(BF16)
            out[h, half : half + strip, :] = in_ref[s, half:, :]
            out[h, half + strip :, :] = in_ref[s + 1, half:, :]


def output_kernel(which, keep_ref, got_ref, *refs):
    qkv, rinv_ref, lats, gain_ref = refs[:3], refs[3], refs[4:8], refs[8]
    weights, w_out_ref, out_ref, wide = refs[9:12], refs[12], refs[13], refs[14]
    rows, size = qkv[0].shape
    width = gain_ref.shape[1]
    half = rows // 2
    c = place("c")
    for ref, core in ((keep_ref, c), (got_ref, 1 - c)):
        span = pl.ds(pl.multiple_of(core * half, half), half)
        for h in range(4):
            at = slice(h * HEAD, (h + 1) * HEAD)
            wide[0, span, at] = ref[h, half:, :HEAD]
            wide[1, span, at] = ref[h, :half, :HEAD]
            wide[2, span, at] = ref[h, :half, HEAD:]
            wide[3, span, at] = ref[h, half:, HEAD:]
    both = sum(wide[n].astype(F32) * qkv[n][...].astype(F32) for n in range(3))
    factor = jnp.sum(both, axis=1, keepdims=True) * rinv_ref[...] / width
    places = tp_places()
    for n, kind in enumerate(which):
        at = places[kind]
        acc = sum(
            lax.dot_general(
                wide[i], piece_rows(weights[i], at, size), NT, preferred_element_type=F32
            )
            for i in range(3)
        )
        columns = pl.ds(pl.multiple_of(at * size, size), size)
        grad = gain_ref[:, columns] * acc - lats[n][...].astype(F32) * factor
        out_ref[n, :rows, :] = grad.astype(BF16)
        mixed = jnp.dot(wide[3], w_out_ref[:, columns], preferred_element_type=F32)
        out_ref[n, rows:, :] = mixed.astype(BF16)


def outputs_for(which, pieces, keep, got, qkv, rinv, gain, weights, w_out):
    rows, size = pieces[0].shape
    lats = [pieces[kind] for kind in which]
    return call(
        functools.partial(output_kernel, which),
        (keep, got, *qkv, rinv, *lats, gain, *weights, w_out),
        [shape(4, 2 * rows, size)],
        [pltpu.VMEM((4, rows, size), BF16)],
        name="outputs",
        megabytes=28,
        micros=3.0,
    )[0]


def add_kernel(own_ref, other_ref, far_ref, side_ref, near_ref, kept_ref):
    for n, ref in enumerate((far_ref, near_ref, side_ref, kept_ref)):
        total = own_ref[n].astype(F32) + other_ref[n].astype(F32)
        ref[...] = total.astype(ref.dtype)


def pass_kernel(near_ref, far_ref, out_ref):
    out_ref[...] = (near_ref[...] + far_ref[...].astype(F32)).astype(BF16)


def final_kernel(valid_ref, rinv_ref, cot_ref, lat_ref, kept_ref, ahead_ref, side_ref, *outs):
    out_ref, grad_ref = outs
    rows = cot_ref.shape[0]
    total = kept_ref[...] + ahead_ref[...].astype(F32) + side_ref[...].astype(F32)
    valid = valid_ref[...] > 0.0
    grad_out = jnp.where(valid, cot_ref[...].astype(F32), 0.0)
    grad_ref[...] = grad_out + rinv_ref[...] * total[:rows]
    result = lat_ref[...].astype(F32) + total[rows:]
    out_ref[...] = jnp.where(valid, result, 0.0).astype(BF16)


def tp_pieces(block):
    piece_a = along_x(block)
    sibling = other_core(block)
    piece_b = along_x(sibling)
    piece_f = along_x(piece_a)
    pieces = [block, sibling, piece_a, piece_b]
    return pieces + [other_core(piece_a), other_core(piece_b), piece_f, other_core(piece_f)]


def per_device(encoded, starts, w_up, norm_gain, w_query, w_key, w_value, w_out, cotangent):
    byte_rows, byte_width = encoded.shape
    shards, patch_cap = starts.shape
    columns = w_up.shape[1]
    rows = cotangent.shape[0]
    gain = norm_gain.reshape(1, -1)
    weights = (w_query, w_key, w_value)
    is_valid = (starts < byte_rows).reshape(-1, rows)
    by_half = jnp.moveaxis(is_valid.reshape(-1, 2, rows // 2), 1, 0).reshape(2, -1, 1)
    bias = jnp.broadcast_to(jnp.where(by_half, 0.0, NEG), (*by_half.shape[:2], 128))
    row_valid = lax.dynamic_slice_in_dim(is_valid, lax.axis_index(SEQ), 1, 0)
    valid = row_valid.reshape(rows, 1).astype(F32)

    cots = tp_pieces(cotangent)
    sums, lead = call(
        pool_kernel,
        (starts, encoded),
        [shape(patch_cap, byte_width, dtype=F32), shape(1, byte_width, dtype=F32)],
        name="pool",
        megabytes=4,
    )
    next_lead = lax.ppermute(lead, ALL, [(i, i - 1) for i in range(1, shards)])
    patches = call(
        functools.partial(patch_kernel, byte_rows),
        (starts, sums, next_lead),
        [shape(patch_cap, byte_width)],
        name="patch",
        megabytes=4,
    )[0]
    shifted = [lax.ppermute(patches, "x", [(i, (i + k) % 4) for i in range(4)]) for k in (1, 2, 3)]
    own_blocks = jnp.stack([patches, *shifted])
    other_blocks = other_core(own_blocks)
    other_blocks, cots = lax.optimization_barrier((other_blocks, cots))
    latent = call(
        latent_kernel,
        (own_blocks, other_blocks, w_up),
        [shape(rows, columns)],
        [pltpu.VMEM((8, patch_cap, byte_width), BF16)],
        name="latent",
        megabytes=8,
    )[0]

    d_attn = d_attn_of(cots, valid, w_out)
    pieces = tp_pieces(latent)
    keep, send, *qkv, rinv = project(pieces, d_attn, gain, weights)
    half = rows // 2
    packed = shape(shards // 8, half + half // 2, 2 * HEAD)
    sent = call(pack_kernel, (keep, other_core(send)), [packed], name="pack")[0]
    mine = lax.all_to_all(sent, SEQ, 0, 0, tiled=True)
    keep, send, strips = attention(bias, mine, other_core(mine))
    back = call(return_kernel, (keep, other_core(send), strips), [packed], name="return")[0]
    back = lax.all_to_all(back, SEQ, 0, 0, tiled=True)
    both = shape(4, rows, 2 * HEAD)
    keep, send = call(regroup_kernel, (back,), [both, both], name="regroup")
    rest = (pieces, keep, other_core(send), qkv, rinv, gain, weights, w_out)

    from_other = other_core(outputs_for((7, 3, 2, 1), *rest))
    for_own = outputs_for((6, 5, 4, 0), *rest)
    block = (2 * rows, columns)
    far, side, near, kept = call(
        add_kernel,
        (for_own, from_other),
        [shape(*block), shape(*block), shape(*block, dtype=F32), shape(*block, dtype=F32)],
        name="add",
        megabytes=16,
    )
    far_in = along_x(far)
    side_in = other_core(along_x(side))
    ahead = call(pass_kernel, (near, far_in), [shape(*block)], name="pass")[0]
    return tuple(
        call(
            final_kernel,
            (valid, rinv, cotangent, latent, kept, along_x(ahead), side_in),
            [shape(rows, columns), shape(rows, columns, dtype=F32)],
            name="final",
        )
    )


def solution(mesh):
    split = Mesh(mesh.devices.reshape(4, 4, 4, 2), ALL)
    in_specs = (
        P(ALL, None),
        P(),
        P(None, TP),
        P(),
        P(None, TP),
        P(None, TP),
        P(None, TP),
        P(TP, None),
        P(SEQ, TP),
    )
    out_specs = (P(SEQ, TP), P(SEQ, TP))
    return jax.shard_map(
        per_device, mesh=split, in_specs=in_specs, out_specs=out_specs, check_vma=False
    )
```

profile of v0, /device:TPU:0, one launch (start us, length us, event | category | flops | bytes accessed | tf_op | source)
XLA Modules:
  0.0 181.9 jit_solution(2883648879111852156)
XLA Ops:
  0.6 1.6 collective-permute-start.6
  2.3 0.8 collective-permute-start.5
  3.1 0.8 copy.15.starts_ref
  3.9 1.1 copy-done.22
  5.0 0.4 pool.1
  5.4 1.3 collective-permute-start
  6.7 1.8 collective-permute-done.next_ref
  8.7 2.8 %collective-permute-start.3 = (bf16[32,1280]{1,0:T(8,128)(2,1)S(1)}, bf16[32,1280]{1,0:T(8,128)(2,1)S(1)}, u32[]{:S(2)}, u32[]{:S(2)}) collective-permute-start(bf16[32,1280]{1,0:T(8,128)(2,1)S(1)} %patch.1), channel_id=1, source_target_pairs={{0,6},{2,0},{4,2},{6,4},{1,7},{3,1},{5,3},{7,5},{8,14},{10,8},{12,... | collective-permute-start | bytes 245768 | tf_op jit(solution)/shard_map/ppermute | solution.py:454
  11.5 1.1 collective-permute-start.2
  12.6 0.6 collective-permute-start.1
  13.2 1.8 collective-permute-start.10
  15.1 2.4 %collective-permute-done.2 = bf16[32,1280]{1,0:T(8,128)(2,1)S(1)} collective-permute-done((bf16[32,1280]{1,0:T(8,128)(2,1)S(1)}, bf16[32,1280]{1,0:T(8,128)(2,1)S(1)}, u32[]{:S(2)}, u32[]{:S(2)}) %collective-permute-start.2) | collective-permute-done | bytes 81952 | tf_op jit(solution)/shard_map/ppermute | solution.py:454
  17.5 2.5 %collective-permute-done.1 = bf16[32,1280]{1,0:T(8,128)(2,1)S(1)} collective-permute-done((bf16[32,1280]{1,0:T(8,128)(2,1)S(1)}, bf16[32,1280]{1,0:T(8,128)(2,1)S(1)}, u32[]{:S(2)}, u32[]{:S(2)}) %collective-permute-start.1) | collective-permute-done | bytes 81952 | tf_op jit(solution)/shard_map/ppermute | solution.py:454
  20.0 0.5 collective-permute-start.4
  20.6 2.3 %collective-permute-done.10.refs_6_ = bf16[256,512]{1,0:T(8,128)(2,1)S(1)} collective-permute-done((bf16[256,512]{1,0:T(8,128)(2,1)S(1)}, bf16[256,512]{1,0:T(8,128)(2,1)S(1)}, u32[]{:S(2)}, u32[]{:S(2)}) %collective-permute-start.10) | collective-permute-done | bytes 262176 | tf_op jit(solution)/shard_map/ppermute | solution.py:60
  22.9 2.8 %collective-permute-done.7.refs_3_ = bf16[256,512]{1,0:T(8,128)(2,1)S(1)} collective-permute-done((bf16[256,512]{1,0:T(8,128)(2,1)S(1)}, bf16[256,512]{1,0:T(8,128)(2,1)S(1)}, u32[]{:S(2)}, u32[]{:S(2)}) %collective-permute-start.7) | collective-permute-done | bytes 262176 | tf_op jit(solution)/shard_map/ppermute | solution.py:60
  25.8 1.5 collective-permute-done.9.refs_5_
  27.3 0.5 latent.1.refs_0_.refs_7_.lat_ref
  27.9 0.4 collective-permute-start.12
  28.3 7.2 %collective-permute-done.13.refs_2_.refs_6_ = bf16[256,512]{1,0:T(8,128)(2,1)S(1)} collective-permute-done((bf16[256,512]{1,0:T(8,128)(2,1)S(1)}, bf16[256,512]{1,0:T(8,128)(2,1)S(1)}, u32[]{:S(2)}, u32[]{:S(2)}) %collective-permute-start.13) | collective-permute-done | bytes 262176 | tf_op jit(solution)/shard_map/ppermute | solution.py:60
  35.9 7.1 %collective-permute-done.17.refs_6_.refs_4_ = bf16[256,512]{1,0:T(8,128)(2,1)S(1)} collective-permute-done((bf16[256,512]{1,0:T(8,128)(2,1)S(1)}, bf16[256,512]{1,0:T(8,128)(2,1)S(1)}, u32[]{:S(2)}, u32[]{:S(2)}) %collective-permute-start.17) | collective-permute-done | bytes 262176 | tf_op jit(solution)/shard_map/ppermute | solution.py:60
  43.0 2.8 %collective-permute-done.14.refs_3_.refs_5_ = bf16[256,512]{1,0:T(8,128)(2,1)S(1)} collective-permute-done((bf16[256,512]{1,0:T(8,128)(2,1)S(1)}, bf16[256,512]{1,0:T(8,128)(2,1)S(1)}, u32[]{:S(2)}, u32[]{:S(2)}) %collective-permute-start.14) | collective-permute-done | bytes 262176 | tf_op jit(solution)/shard_map/ppermute | solution.py:60
  46.0 2.2 %copy-done = bf16[512,4096]{1,0:T(8,128)(2,1)S(1)} copy-done((bf16[512,4096]{1,0:T(8,128)(2,1)S(1)}, bf16[512,4096]{1,0:T(8,128)(2,1)}, u32[]{:S(2)}) %copy-start) | copy-done | bytes 4194328
  48.2 0.9 copy-done.26
  49.2 0.9 copy-done.28
  50.1 0.9 copy-done.30
  51.1 0.9 copy-done.32
  52.0 5.2 %d_attn.1.refs_8_ = bf16[256,512]{1,0:T(8,128)(2,1)S(1)} custom-call(bf16[256,512]{1,0:T(8,128)(2,1)S(1)} %copy-done.23, bf16[256,512]{1,0:T(8,128)(2,1)S(1)} %collective-permute-done.5.refs_1_, bf16[256,512]{1,0:T(8,128)(2,1)S(1)} %collective-permute-done.6.refs_2_, bf16[256,512]{1,0:T(8,128)(2,1)S(1)} %copy-done.26, bf16[256,512]{1,0:T(8,128)(2,1)S(1)} %copy-done.28, ...), custom_call_target="tpu_custom_call" | custom-call | flops 2000000000 | bytes 6000000 | tf_op jit(solution)/shard_map/d_attn/pallas_call | solution.py:33
  57.4 2.4 %copy-done.4 = bf16[4096,512]{1,0:T(8,128)(2,1)S(1)} copy-done((bf16[4096,512]{1,0:T(8,128)(2,1)S(1)}, bf16[4096,512]{1,0:T(8,128)(2,1)}, u32[]{:S(2)}) %copy-start.4) | copy-done | bytes 4194328
  59.8 2.2 %copy-done.6 = bf16[4096,512]{1,0:T(8,128)(2,1)S(1)} copy-done((bf16[4096,512]{1,0:T(8,128)(2,1)S(1)}, bf16[4096,512]{1,0:T(8,128)(2,1)}, u32[]{:S(2)}) %copy-start.6) | copy-done | bytes 4194328
  62.0 7.0 %project.1 = (bf16[4,256,256]{2,1,0:T(8,128)(2,1)S(1)}, bf16[4,256,256]{2,1,0:T(8,128)(2,1)S(1)}, bf16[256,512]{1,0:T(8,128)(2,1)S(1)}, bf16[256,512]{1,0:T(8,12...) custom-call(bf16[256,512]{1,0:T(8,128)(2,1)S(1)} %latent.1.refs_0_.refs_7_.lat_ref, ...), custom_call_target="tpu_custom_call" | custom-call | flops 5000000000 | bytes 15000000 | tf_op jit(solution)/shard_map/project/pallas_call | solution.py:33
  69.0 0.6 collective-permute-start.19
  69.6 1.5 collective-permute-done.19.got_ref
  71.2 31.1 %all_to_all.10.mine_ref = bf16[16,192,256]{2,1,0:T(8,128)(2,1)S(1)} all-to-all(bf16[16,192,256]{2,1,0:T(8,128)(2,1)S(1)} %pack.1), channel_id=1, replica_groups=mesh['y'=4,'z'=4,'x'=4,'c'=2] {'y','z'}, dimensions={0} | all-to-all | bytes 3145728 | tf_op jit(solution)/shard_map/all_to_all | solution.py:473
  102.5 3.3 %collective-permute-done.20.theirs_ref = bf16[16,192,256]{2,1,0:T(8,128)(2,1)} collective-permute-done((bf16[16,192,256]{2,1,0:T(8,128)(2,1)S(1)}, bf16[16,192,256]{2,1,0:T(8,128)(2,1)}, u32[]{:S(2)}, u32[]{:S(2)}) %collective-permute-start.20) | collective-permute-done | bytes 1572896 | tf_op jit(solution)/shard_map/ppermute | solution.py:52
  105.9 0.6 broadcast_in_dim.15.bias_ref
  106.5 13.1 %attention.1 = (bf16[16,128,256]{2,1,0:T(8,128)(2,1)S(1)}, bf16[16,128,256]{2,1,0:T(8,128)(2,1)S(1)}, bf16[16,64,256]{2,1,0:T(8,128)(2,1)S(1)}) custom-call(f32[2,2048,128]{2,1,0:T(8,128)S(1)} %broadcast_in_dim.15.bias_ref, bf16[16,192,256]{2,1,0:T(8,128)(2,1)S(1)} %all_to_all.10.mine_ref, bf16[16,192,256]{2,1,0:T(8,128)(2,1)} %collective-permute-done.20.theirs_ref), custom_call_target="tpu_custom_call" | custom-call | flops 12000000000 | bytes 36000000 | tf_op jit(solution)/shard_map/attention/pallas_call | solution.py:33
  119.9 2.5 %collective-permute-done.21.got_ref = bf16[16,128,256]{2,1,0:T(8,128)(2,1)S(1)} collective-permute-done((bf16[16,128,256]{2,1,0:T(8,128)(2,1)S(1)}, bf16[16,128,256]{2,1,0:T(8,128)(2,1)S(1)}, u32[]{:S(2)}, u32[]{:S(2)}) %collective-permute-start.21) | collective-permute-done | bytes 1048608 | tf_op jit(solution)/shard_map/ppermute | solution.py:52
  122.7 26.8 %all_to_all.11.in_ref = bf16[16,192,256]{2,1,0:T(8,128)(2,1)S(1)} all-to-all(bf16[16,192,256]{2,1,0:T(8,128)(2,1)S(1)} %return.1), channel_id=1, replica_groups=mesh['y'=4,'z'=4,'x'=4,'c'=2] {'y','z'}, dimensions={0} | all-to-all | bytes 3145728 | tf_op jit(solution)/shard_map/all_to_all | solution.py:476
  149.7 1.9 %collective-permute-done.22.got_ref = bf16[4,256,256]{2,1,0:T(8,128)(2,1)S(1)} collective-permute-done((bf16[4,256,256]{2,1,0:T(8,128)(2,1)S(1)}, bf16[4,256,256]{2,1,0:T(8,128)(2,1)S(1)}, u32[]{:S(2)}, u32[]{:S(2)}) %collective-permute-start.22) | collective-permute-done | bytes 524320 | tf_op jit(solution)/shard_map/ppermute | solution.py:52
  151.7 2.7 %outputs.3 = bf16[4,512,512]{2,1,0:T(8,128)(2,1)S(1)} custom-call(bf16[4,256,256]{2,1,0:T(8,128)(2,1)S(1)} %get-tuple-element.45.keep_ref, bf16[4,256,256]{2,1,0:T(8,128)(2,1)S(1)} %collective-permute-done.22.got_ref, bf16[256,512]{1,0:T(8,128)(2,1)S(1)} %get-tuple-element.47.refs_0_, bf16[256,512]{1,0:T(8,128)(2,1)S(1)} %get-tuple-element.48.refs_1_, ...), custom_call_target="tpu_custom_call" | custom-call | flops 3000000000 | bytes 9000000 | tf_op jit(solution)/shard_map/outputs/pallas_call | solution.py:33
  154.6 2.7 %outputs.2.own_ref = bf16[4,512,512]{2,1,0:T(8,128)(2,1)S(1)} custom-call(bf16[4,256,256]{2,1,0:T(8,128)(2,1)S(1)} %get-tuple-element.45.keep_ref, bf16[4,256,256]{2,1,0:T(8,128)(2,1)S(1)} %collective-permute-done.22.got_ref, bf16[256,512]{1,0:T(8,128)(2,1)S(1)} %get-tuple-element.47.refs_0_, bf16[256,512]{1,0:T(8,128)(2,1)S(1)} %get-tuple-element.48.refs_1_, ...), custom_call_target="tpu_custom_call" | custom-call | flops 3000000000 | bytes 9000000 | tf_op jit(solution)/shard_map/outputs/pallas_call | solution.py:33
  157.3 1.3 collective-permute-done.23.other_ref
  158.6 0.4 add.9
  159.2 10.3 %collective-permute-done.24.far_ref = bf16[512,512]{1,0:T(8,128)(2,1)S(1)} collective-permute-done((bf16[512,512]{1,0:T(8,128)(2,1)S(1)}, bf16[512,512]{1,0:T(8,128)(2,1)S(1)}, u32[]{:S(2)}, u32[]{:S(2)}) %collective-permute-start.24) | collective-permute-done | bytes 524320 | tf_op jit(solution)/shard_map/ppermute | solution.py:60
  169.7 5.4 %collective-permute-done.26 = bf16[512,512]{1,0:T(8,128)(2,1)S(1)} collective-permute-done((bf16[512,512]{1,0:T(8,128)(2,1)S(1)}, bf16[512,512]{1,0:T(8,128)(2,1)S(1)}, u32[]{:S(2)}, u32[]{:S(2)}) %collective-permute-start.26) | collective-permute-done | bytes 524320 | tf_op jit(solution)/shard_map/ppermute | solution.py:60
  175.2 5.6 %collective-permute-done.25.ahead_ref = bf16[512,512]{1,0:T(8,128)(2,1)S(1)} collective-permute-done((bf16[512,512]{1,0:T(8,128)(2,1)S(1)}, bf16[512,512]{1,0:T(8,128)(2,1)S(1)}, u32[]{:S(2)}, u32[]{:S(2)}) %collective-permute-start.25) | collective-permute-done | bytes 524320 | tf_op jit(solution)/shard_map/ppermute | solution.py:60
  180.8 1.1 final.1
  (102 shorter events, 2.7 us)
Async XLA Ops:
  0.6 12.6 %collective-permute-start.6 = (bf16[256,512]{1,0:T(8,128)(2,1)}, bf16[256,512]{1,0:T(8,128)(2,1)S(1)}, u32[]{:S(2)}, u32[]{:S(2)}) collective-permute-start(bf16[256,512]{1,0:T(8,128)(2,1)} %cot_ref.1), channel_id=1, source_target_pairs={{0,2},{1,7},{2,4},{3,1},{4,6},{5,3},{6,0},{7,5},{8,10},{9,15},{10,... | collective-permute-start | bytes 786440 | tf_op jit(solution)/shard_map/ppermute | solution.py:60
  2.3 12.8 %collective-permute-start.5 = (bf16[256,512]{1,0:T(8,128)(2,1)}, bf16[256,512]{1,0:T(8,128)(2,1)S(1)}, u32[]{:S(2)}, u32[]{:S(2)}) collective-permute-start(bf16[256,512]{1,0:T(8,128)(2,1)} %cot_ref.1), channel_id=1, source_target_pairs={{0,1},{1,0},{2,3},{3,2},{4,5},{5,4},{6,7},{7,6},{8,9},{9,8},{10,11... | collective-permute-start | bytes 786440 | tf_op jit(solution)/shard_map/ppermute | solution.py:52
  5.4 3.1 %collective-permute-start = (f32[1,1280]{1,0:T(1,128)S(1)}, f32[1,1280]{1,0:T(1,128)S(1)}, u32[]{:S(2)}, u32[]{:S(2)}) collective-permute-start(f32[1,1280]{1,0:T(1,128)S(1)} %get-tuple-element.29), channel_id=1, source_target_pairs={{1,0},{2,1},{3,2},{4,3},{5,4},{6,5},{7,6},{8,7},{9,8},{10,9},{11,1... | collective-permute-start | bytes 15368 | tf_op jit(solution)/shard_map/ppermute | solution.py:446
  8.5 18.8 %copy-start.21 = (bf16[1280,512]{1,0:T(8,128)(2,1)S(1)}, bf16[1280,512]{1,0:T(8,128)(2,1)}, u32[]{:S(2)}) copy-start(bf16[1280,512]{1,0:T(8,128)(2,1)} %w_ref.1) | copy-start | bytes 3932164
  8.7 6.4 %collective-permute-start.3 = (bf16[32,1280]{1,0:T(8,128)(2,1)S(1)}, bf16[32,1280]{1,0:T(8,128)(2,1)S(1)}, u32[]{:S(2)}, u32[]{:S(2)}) collective-permute-start(bf16[32,1280]{1,0:T(8,128)(2,1)S(1)} %patch.1), channel_id=1, source_target_pairs={{0,6},{2,0},{4,2},{6,4},{1,7},{3,1},{5,3},{7,5},{8,14},{10,8},{12,... | collective-permute-start | bytes 245768 | tf_op jit(solution)/shard_map/ppermute | solution.py:454
  11.5 5.9 %collective-permute-start.2 = (bf16[32,1280]{1,0:T(8,128)(2,1)S(1)}, bf16[32,1280]{1,0:T(8,128)(2,1)S(1)}, u32[]{:S(2)}, u32[]{:S(2)}) collective-permute-start(bf16[32,1280]{1,0:T(8,128)(2,1)S(1)} %patch.1), channel_id=1, source_target_pairs={{0,4},{2,6},{4,0},{6,2},{1,5},{3,7},{5,1},{7,3},{8,12},{10,14},{12... | collective-permute-start | bytes 245768 | tf_op jit(solution)/shard_map/ppermute | solution.py:454
  12.6 7.3 %collective-permute-start.1 = (bf16[32,1280]{1,0:T(8,128)(2,1)S(1)}, bf16[32,1280]{1,0:T(8,128)(2,1)S(1)}, u32[]{:S(2)}, u32[]{:S(2)}) collective-permute-start(bf16[32,1280]{1,0:T(8,128)(2,1)S(1)} %patch.1), channel_id=1, source_target_pairs={{0,2},{2,4},{4,6},{6,0},{1,3},{3,5},{5,7},{7,1},{8,10},{10,12},{12... | collective-permute-start | bytes 245768 | tf_op jit(solution)/shard_map/ppermute | solution.py:454
  13.2 9.7 %collective-permute-start.10 = (bf16[256,512]{1,0:T(8,128)(2,1)S(1)}, bf16[256,512]{1,0:T(8,128)(2,1)S(1)}, u32[]{:S(2)}, u32[]{:S(2)}) collective-permute-start(bf16[256,512]{1,0:T(8,128)(2,1)S(1)} %collective-permute-done.6.refs_2_), channel_id=1, source_target_pairs={{0,2},{1,7},{2,4},{3,1},{4,6},{5,3},{6,0},{7,5},{8,10},{9,15},{10,... | collective-permute-start | bytes 786440 | tf_op jit(solution)/shard_map/ppermute | solution.py:60
  15.0 10.7 %collective-permute-start.7 = (bf16[256,512]{1,0:T(8,128)(2,1)S(1)}, bf16[256,512]{1,0:T(8,128)(2,1)S(1)}, u32[]{:S(2)}, u32[]{:S(2)}) collective-permute-start(bf16[256,512]{1,0:T(8,128)(2,1)S(1)} %collective-permute-done.5.refs_1_), channel_id=1, source_target_pairs={{0,2},{1,7},{2,4},{3,1},{4,6},{5,3},{6,0},{7,5},{8,10},{9,15},{10,... | collective-permute-start | bytes 786440 | tf_op jit(solution)/shard_map/ppermute | solution.py:60
  19.9 15.7 %copy-start.33 = (s32[128,32]{0,1:T(8,128)S(1)}, s32[128,32]{0,1:T(8,128)}, u32[]{:S(2)}) copy-start(s32[128,32]{0,1:T(8,128)} %param.10) | copy-start | bytes 49156
  20.0 26.0 %copy-start.23 = (bf16[256,512]{1,0:T(8,128)(2,1)S(1)}, bf16[256,512]{1,0:T(8,128)(2,1)}, u32[]{:S(2)}) copy-start(bf16[256,512]{1,0:T(8,128)(2,1)} %cot_ref.1) | copy-start | bytes 786436
  20.0 5.7 %collective-permute-start.4 = (bf16[4,32,1280]{2,1,0:T(8,128)(2,1)S(1)}, bf16[4,32,1280]{2,1,0:T(8,128)(2,1)S(1)}, u32[]{:S(2)}, u32[]{:S(2)}) collective-permute-start(bf16[4,32,1280]{2,1,0:T(8,128)(2,1)S(1)} %pad_maximum_fusion.own_ref), channel_id=1, source_target_pairs={{0,1},{1,0},{2,3},{3,2},{4,5},{5,4},{6,7},{7,6},{8,9},{9,8},{10,11... | collective-permute-start | bytes 983048 | tf_op jit(solution)/shard_map/ppermute | solution.py:52
  20.5 5.2 %collective-permute-start.8 = (bf16[256,512]{1,0:T(8,128)(2,1)S(1)}, bf16[256,512]{1,0:T(8,128)(2,1)S(1)}, u32[]{:S(2)}, u32[]{:S(2)}) collective-permute-start(bf16[256,512]{1,0:T(8,128)(2,1)S(1)} %collective-permute-done.6.refs_2_), channel_id=1, source_target_pairs={{0,1},{1,0},{2,3},{3,2},{4,5},{5,4},{6,7},{7,6},{8,9},{9,8},{10,11... | collective-permute-start | bytes 786440 | tf_op jit(solution)/shard_map/ppermute | solution.py:52
  22.9 2.8 %collective-permute-start.11 = (bf16[256,512]{1,0:T(8,128)(2,1)S(1)}, bf16[256,512]{1,0:T(8,128)(2,1)S(1)}, u32[]{:S(2)}, u32[]{:S(2)}) collective-permute-start(bf16[256,512]{1,0:T(8,128)(2,1)S(1)} %collective-permute-done.10.refs_6_), channel_id=1, source_target_pairs={{0,1},{1,0},{2,3},{3,2},{4,5},{5,4},{6,7},{7,6},{8,9},{9,8},{10,11... | collective-permute-start | bytes 786440 | tf_op jit(solution)/shard_map/ppermute | solution.py:52
  25.7 9.7 %copy-start.25 = (bf16[256,512]{1,0:T(8,128)(2,1)}, bf16[256,512]{1,0:T(8,128)(2,1)S(1)}, u32[]{:S(2)}) copy-start(bf16[256,512]{1,0:T(8,128)(2,1)S(1)} %collective-permute-done.7.refs_3_) | copy-start | bytes 786436
  25.7 1.5 collective-permute-start.9
  25.7 9.8 %copy-start.27 = (bf16[256,512]{1,0:T(8,128)(2,1)}, bf16[256,512]{1,0:T(8,128)(2,1)S(1)}, u32[]{:S(2)}) copy-start(bf16[256,512]{1,0:T(8,128)(2,1)S(1)} %collective-permute-done.8.refs_4_) | copy-start | bytes 786436
  25.8 9.8 %copy-start.29 = (bf16[256,512]{1,0:T(8,128)(2,1)}, bf16[256,512]{1,0:T(8,128)(2,1)S(1)}, u32[]{:S(2)}) copy-start(bf16[256,512]{1,0:T(8,128)(2,1)S(1)} %collective-permute-done.11.refs_7_) | copy-start | bytes 786436
  27.3 8.3 %copy-start.31 = (bf16[256,512]{1,0:T(8,128)(2,1)}, bf16[256,512]{1,0:T(8,128)(2,1)S(1)}, u32[]{:S(2)}) copy-start(bf16[256,512]{1,0:T(8,128)(2,1)S(1)} %collective-permute-done.9.refs_5_) | copy-start | bytes 786436
  27.8 7.7 %collective-permute-start.13 = (bf16[256,512]{1,0:T(8,128)(2,1)S(1)}, bf16[256,512]{1,0:T(8,128)(2,1)S(1)}, u32[]{:S(2)}, u32[]{:S(2)}) collective-permute-start(bf16[256,512]{1,0:T(8,128)(2,1)S(1)} %latent.1.refs_0_.refs_7_.lat_ref), channel_id=1, source_target_pairs={{0,2},{1,7},{2,4},{3,1},{4,6},{5,3},{6,0},{7,5},{8,10},{9,15},{10,... | collective-permute-start | bytes 786440 | tf_op jit(solution)/shard_map/ppermute | solution.py:60
  27.9 7.6 %collective-permute-start.12 = (bf16[256,512]{1,0:T(8,128)(2,1)S(1)}, bf16[256,512]{1,0:T(8,128)(2,1)S(1)}, u32[]{:S(2)}, u32[]{:S(2)}) collective-permute-start(bf16[256,512]{1,0:T(8,128)(2,1)S(1)} %latent.1.refs_0_.refs_7_.lat_ref), channel_id=1, source_target_pairs={{0,1},{1,0},{2,3},{3,2},{4,5},{5,4},{6,7},{7,6},{8,9},{9,8},{10,11... | collective-permute-start | bytes 786440 | tf_op jit(solution)/shard_map/ppermute | solution.py:52
  35.5 7.6 %collective-permute-start.17 = (bf16[256,512]{1,0:T(8,128)(2,1)S(1)}, bf16[256,512]{1,0:T(8,128)(2,1)S(1)}, u32[]{:S(2)}, u32[]{:S(2)}) collective-permute-start(bf16[256,512]{1,0:T(8,128)(2,1)S(1)} %collective-permute-done.13.refs_2_.refs_6_), channel_id=1, source_target_pairs={{0,2},{1,7},{2,4},{3,1},{4,6},{5,3},{6,0},{7,5},{8,10},{9,15},{10,... | collective-permute-start | bytes 786440 | tf_op jit(solution)/shard_map/ppermute | solution.py:60
  35.5 21.9 %copy-start.10 = (bf16[256,512]{1,0:T(8,128)(2,1)}, bf16[256,512]{1,0:T(8,128)(2,1)S(1)}, u32[]{:S(2)}) copy-start(bf16[256,512]{1,0:T(8,128)(2,1)S(1)} %collective-permute-done.12.refs_1_.refs_7_) | copy-start | bytes 786436
  35.5 10.4 %collective-permute-start.14 = (bf16[256,512]{1,0:T(8,128)(2,1)S(1)}, bf16[256,512]{1,0:T(8,128)(2,1)S(1)}, u32[]{:S(2)}, u32[]{:S(2)}) collective-permute-start(bf16[256,512]{1,0:T(8,128)(2,1)S(1)} %collective-permute-done.12.refs_1_.refs_7_), channel_id=1, source_target_pairs={{0,2},{1,7},{2,4},{3,1},{4,6},{5,3},{6,0},{7,5},{8,10},{9,15},{10,... | collective-permute-start | bytes 786440 | tf_op jit(solution)/shard_map/ppermute | solution.py:60
  35.9 21.4 %collective-permute-start.15 = (bf16[256,512]{1,0:T(8,128)(2,1)S(1)}, bf16[256,512]{1,0:T(8,128)(2,1)S(1)}, u32[]{:S(2)}, u32[]{:S(2)}) collective-permute-start(bf16[256,512]{1,0:T(8,128)(2,1)S(1)} %collective-permute-done.13.refs_2_.refs_6_), channel_id=1, source_target_pairs={{0,1},{1,0},{2,3},{3,2},{4,5},{5,4},{6,7},{7,6},{8,9},{9,8},{10,11... | collective-permute-start | bytes 786440 | tf_op jit(solution)/shard_map/ppermute | solution.py:52
  43.0 14.3 %copy-start.8 = (bf16[256,512]{1,0:T(8,128)(2,1)}, bf16[256,512]{1,0:T(8,128)(2,1)S(1)}, u32[]{:S(2)}) copy-start(bf16[256,512]{1,0:T(8,128)(2,1)S(1)} %collective-permute-done.17.refs_6_.refs_4_) | copy-start | bytes 786436
  43.0 14.3 %collective-permute-start.18 = (bf16[256,512]{1,0:T(8,128)(2,1)S(1)}, bf16[256,512]{1,0:T(8,128)(2,1)S(1)}, u32[]{:S(2)}, u32[]{:S(2)}) collective-permute-start(bf16[256,512]{1,0:T(8,128)(2,1)S(1)} %collective-permute-done.17.refs_6_.refs_4_), channel_id=1, source_target_pairs={{0,1},{1,0},{2,3},{3,2},{4,5},{5,4},{6,7},{7,6},{8,9},{9,8},{10,11... | collective-permute-start | bytes 786440 | tf_op jit(solution)/shard_map/ppermute | solution.py:52
  45.8 11.5 %copy-start.12 = (bf16[256,512]{1,0:T(8,128)(2,1)}, bf16[256,512]{1,0:T(8,128)(2,1)S(1)}, u32[]{:S(2)}) copy-start(bf16[256,512]{1,0:T(8,128)(2,1)S(1)} %collective-permute-done.14.refs_3_.refs_5_) | copy-start | bytes 786436
  45.9 11.5 %collective-permute-start.16 = (bf16[256,512]{1,0:T(8,128)(2,1)S(1)}, bf16[256,512]{1,0:T(8,128)(2,1)S(1)}, u32[]{:S(2)}, u32[]{:S(2)}) collective-permute-start(bf16[256,512]{1,0:T(8,128)(2,1)S(1)} %collective-permute-done.14.refs_3_.refs_5_), channel_id=1, source_target_pairs={{0,1},{1,0},{2,3},{3,2},{4,5},{5,4},{6,7},{7,6},{8,9},{9,8},{10,11... | collective-permute-start | bytes 786440 | tf_op jit(solution)/shard_map/ppermute | solution.py:52
  52.0 5.4 %copy-start.2 = (bf16[4096,512]{1,0:T(8,128)(2,1)S(1)}, bf16[4096,512]{1,0:T(8,128)(2,1)}, u32[]{:S(2)}) copy-start(bf16[4096,512]{1,0:T(8,128)(2,1)} %refs_9_.5) | copy-start | bytes 12582916
  52.0 5.4 %copy-start.20 = (f32[4096]{0:T(1024)S(1)}, f32[4096]{0:T(1024)}, u32[]{:S(2)}) copy-start(f32[4096]{0:T(1024)} %param.12) | copy-start | bytes 49156
  57.3 11.7 %copy-start.14 = (bf16[256,512]{1,0:T(8,128)(2,1)}, bf16[256,512]{1,0:T(8,128)(2,1)S(1)}, u32[]{:S(2)}) copy-start(bf16[256,512]{1,0:T(8,128)(2,1)S(1)} %collective-permute-done.15.refs_4_.refs_6_) | copy-start | bytes 786436
  57.3 11.7 %copy-start.18 = (bf16[256,512]{1,0:T(8,128)(2,1)}, bf16[256,512]{1,0:T(8,128)(2,1)S(1)}, u32[]{:S(2)}) copy-start(bf16[256,512]{1,0:T(8,128)(2,1)S(1)} %collective-permute-done.18.refs_7_.refs_4_) | copy-start | bytes 786436
  57.3 11.7 %copy-start.16 = (bf16[256,512]{1,0:T(8,128)(2,1)}, bf16[256,512]{1,0:T(8,128)(2,1)S(1)}, u32[]{:S(2)}) copy-start(bf16[256,512]{1,0:T(8,128)(2,1)S(1)} %collective-permute-done.16.refs_5_) | copy-start | bytes 786436
  69.0 2.1 %collective-permute-start.19 = (bf16[4,256,256]{2,1,0:T(8,128)(2,1)S(1)}, bf16[4,256,256]{2,1,0:T(8,128)(2,1)S(1)}, u32[]{:S(2)}, u32[]{:S(2)}) collective-permute-start(bf16[4,256,256]{2,1,0:T(8,128)(2,1)S(1)} %get-tuple-element.41), channel_id=1, source_target_pairs={{0,1},{1,0},{2,3},{3,2},{4,5},{5,4},{6,7},{7,6},{8,9},{9,8},{10,11... | collective-permute-start | bytes 1572872 | tf_op jit(solution)/shard_map/ppermute | solution.py:52
  102.4 3.5 %collective-permute-start.20 = (bf16[16,192,256]{2,1,0:T(8,128)(2,1)S(1)}, bf16[16,192,256]{2,1,0:T(8,128)(2,1)}, u32[]{:S(2)}, u32[]{:S(2)}) collective-permute-start(bf16[16,192,256]{2,1,0:T(8,128)(2,1)S(1)} %all_to_all.10.mine_ref), channel_id=1, source_target_pairs={{0,1},{1,0},{2,3},{3,2},{4,5},{5,4},{6,7},{7,6},{8,9},{9,8},{10,11... | collective-permute-start | bytes 4718600 | tf_op jit(solution)/shard_map/ppermute | solution.py:52
  106.5 45.1 %copy-start.5 = (bf16[4096,512]{1,0:T(8,128)(2,1)S(1)}, bf16[4096,512]{1,0:T(8,128)(2,1)}, u32[]{:S(2)}) copy-start(bf16[4096,512]{1,0:T(8,128)(2,1)} %refs_10_.5) | copy-start | bytes 12582916
  106.5 45.1 %copy-start.7 = (bf16[4096,512]{1,0:T(8,128)(2,1)S(1)}, bf16[4096,512]{1,0:T(8,128)(2,1)}, u32[]{:S(2)}) copy-start(bf16[4096,512]{1,0:T(8,128)(2,1)} %refs_11_.5) | copy-start | bytes 12582916
  119.6 2.7 %collective-permute-start.21 = (bf16[16,128,256]{2,1,0:T(8,128)(2,1)S(1)}, bf16[16,128,256]{2,1,0:T(8,128)(2,1)S(1)}, u32[]{:S(2)}, u32[]{:S(2)}) collective-permute-start(bf16[16,128,256]{2,1,0:T(8,128)(2,1)S(1)} %get-tuple-element.43), channel_id=1, source_target_pairs={{0,1},{1,0},{2,3},{3,2},{4,5},{5,4},{6,7},{7,6},{8,9},{9,8},{10,11... | collective-permute-start | bytes 3145736 | tf_op jit(solution)/shard_map/ppermute | solution.py:52
  122.4 29.2 %copy-start.3 = (bf16[4096,512]{1,0:T(8,128)(2,1)S(1)}, bf16[4096,512]{1,0:T(8,128)(2,1)}, u32[]{:S(2)}) copy-start(bf16[4096,512]{1,0:T(8,128)(2,1)} %refs_9_.5) | copy-start | bytes 12582916
  122.6 29.0 %copy-start.1 = (bf16[512,4096]{1,0:T(8,128)(2,1)S(1)}, bf16[512,4096]{1,0:T(8,128)(2,1)}, u32[]{:S(2)}) copy-start(bf16[512,4096]{1,0:T(8,128)(2,1)} %refs_12_.5) | copy-start | bytes 12582916
  149.6 2.0 %collective-permute-start.22 = (bf16[4,256,256]{2,1,0:T(8,128)(2,1)S(1)}, bf16[4,256,256]{2,1,0:T(8,128)(2,1)S(1)}, u32[]{:S(2)}, u32[]{:S(2)}) collective-permute-start(bf16[4,256,256]{2,1,0:T(8,128)(2,1)S(1)} %get-tuple-element.46), channel_id=1, source_target_pairs={{0,1},{1,0},{2,3},{3,2},{4,5},{5,4},{6,7},{7,6},{8,9},{9,8},{10,11... | collective-permute-start | bytes 1572872 | tf_op jit(solution)/shard_map/ppermute | solution.py:52
  154.4 4.2 %collective-permute-start.23 = (bf16[4,512,512]{2,1,0:T(8,128)(2,1)S(1)}, bf16[4,512,512]{2,1,0:T(8,128)(2,1)S(1)}, u32[]{:S(2)}, u32[]{:S(2)}) collective-permute-start(bf16[4,512,512]{2,1,0:T(8,128)(2,1)S(1)} %outputs.3), channel_id=1, source_target_pairs={{0,1},{1,0},{2,3},{3,2},{4,5},{5,4},{6,7},{7,6},{8,9},{9,8},{10,11... | collective-permute-start | bytes 6291464 | tf_op jit(solution)/shard_map/ppermute | solution.py:52
  159.1 21.7 %copy-start.24 = (bf16[256,512]{1,0:T(8,128)(2,1)S(1)}, bf16[256,512]{1,0:T(8,128)(2,1)}, u32[]{:S(2)}) copy-start(bf16[256,512]{1,0:T(8,128)(2,1)} %cot_ref.1) | copy-start | bytes 786436
  159.1 10.5 %collective-permute-start.24 = (bf16[512,512]{1,0:T(8,128)(2,1)S(1)}, bf16[512,512]{1,0:T(8,128)(2,1)S(1)}, u32[]{:S(2)}, u32[]{:S(2)}) collective-permute-start(bf16[512,512]{1,0:T(8,128)(2,1)S(1)} %get-tuple-element.52), channel_id=1, source_target_pairs={{0,2},{1,7},{2,4},{3,1},{4,6},{5,3},{6,0},{7,5},{8,10},{9,15},{10,... | collective-permute-start | bytes 1572872 | tf_op jit(solution)/shard_map/ppermute | solution.py:60
  159.2 16.0 %collective-permute-start.26 = (bf16[512,512]{1,0:T(8,128)(2,1)S(1)}, bf16[512,512]{1,0:T(8,128)(2,1)S(1)}, u32[]{:S(2)}, u32[]{:S(2)}) collective-permute-start(bf16[512,512]{1,0:T(8,128)(2,1)S(1)} %get-tuple-element.53), channel_id=1, source_target_pairs={{0,2},{1,7},{2,4},{3,1},{4,6},{5,3},{6,0},{7,5},{8,10},{9,15},{10,... | collective-permute-start | bytes 1572872 | tf_op jit(solution)/shard_map/ppermute | solution.py:60
  169.6 11.1 %collective-permute-start.25 = (bf16[512,512]{1,0:T(8,128)(2,1)S(1)}, bf16[512,512]{1,0:T(8,128)(2,1)S(1)}, u32[]{:S(2)}, u32[]{:S(2)}) collective-permute-start(bf16[512,512]{1,0:T(8,128)(2,1)S(1)} %pass.1), channel_id=1, source_target_pairs={{0,2},{1,7},{2,4},{3,1},{4,6},{5,3},{6,0},{7,5},{8,10},{9,15},{10,... | collective-permute-start | bytes 1572872 | tf_op jit(solution)/shard_map/ppermute | solution.py:60
  175.2 5.6 %collective-permute-start.27 = (bf16[512,512]{1,0:T(8,128)(2,1)S(1)}, bf16[512,512]{1,0:T(8,128)(2,1)S(1)}, u32[]{:S(2)}, u32[]{:S(2)}) collective-permute-start(bf16[512,512]{1,0:T(8,128)(2,1)S(1)} %collective-permute-done.26), channel_id=1, source_target_pairs={{0,1},{1,0},{2,3},{3,2},{4,5},{5,4},{6,7},{7,6},{8,9},{9,8},{10,11... | collective-permute-start | bytes 1572872 | tf_op jit(solution)/shard_map/ppermute | solution.py:52
  (14 other events, 26.9 us)
where the time goes:
time: 182 us
  waiting for transfers between devices  62.3 us (34%)
  blocking collectives  57.9 us (32%)
  Pallas kernels  34 us (19%)
  local copies, waits for them, and re-layouts  13.7 us (8%)
  starting transfers between devices  12.7 us (7%)
    ppermute x9, waiting for transfers between devices, along_x(): return lax.ppermute(block, XC, route)  43.5 us
    pallas_call x14, Pallas kernels, call(): pl.pallas_call(kernel, in_specs=[VMEM] * (len(ins) - stay) + [pl.BlockSpe...  34 us
    all_to_all x1, blocking collectives, per_device(): mine = lax.all_to_all(sent, SEQ, 0, 0, tiled=True)  31.1 us
    all_to_all x1, blocking collectives, per_device(): back = lax.all_to_all(back, SEQ, 0, 0, tiled=True)  26.8 us
    unnamed x69, local copies, waits for them, and re-layouts  12.6 us
    ppermute x15, waiting for transfers between devices, other_core(): return lax.ppermute(block, 'c', [(0, 1), (1, 0)])  12.1 us
    ppermute x3, waiting for transfers between devices, per_device(): lax.ppermute(patches, 'x', [(i, (i + k) % 4) for i in range(4)])  4.84 us
    ppermute x3, starting transfers between devices, per_device(): lax.ppermute(patches, 'x', [(i, (i + k) % 4) for i in range(4)])  4.51 us
  transfers between devices with their start and end apart: 28, of which 17 were waited for; matrix products, arithmetic and copies ran while one was open for 1% of the time, Pallas kernels for 5%

commit v1 on v0

--- a/solution.py
+++ b/solution.py
@@ -30,9 +30,11 @@
 
 
 def call(kernel, ins, outs, scratch=(), name=None, megabytes=8, micros=1.0, stay=0):
+    here = len(ins) - stay
+    ins = [*ins[:here], *(pltpu.with_memory_space_constraint(a, pltpu.HBM) for a in ins[here:])]
     return pl.pallas_call(
         kernel,
-        in_specs=[VMEM] * (len(ins) - stay) + [pl.BlockSpec(memory_space=pl.ANY)] * stay,
+        in_specs=[VMEM] * (len(ins) - stay) + [pl.BlockSpec(memory_space=pltpu.HBM)] * stay,
         out_specs=[VMEM] * len(outs),
         out_shape=list(outs),
         scratch_shapes=list(scratch),
@@ -199,37 +201,48 @@
     )
 
 
-def d_attn_kernel(*refs):
-    grads, valid_ref, w_ref, out_ref, held, sems = refs[:8], *refs[8:]
-    size = grads[0].shape[1]
-    copies = []
+def d_attn_kernel(valid_ref, *refs):
+    grads, w_ref, out_ref, pieces, held, grad_sems, sems = refs[:8], *refs[8:]
+    rows, size = grads[0].shape
+    copies = [
+        pltpu.make_async_copy(grad, pieces.at[n], grad_sems.at[n]) for n, grad in enumerate(grads)
+    ]
     for h in range(4):
         span = slice(h * HEAD, (h + 1) * HEAD)
         copies.append(pltpu.make_async_copy(w_ref.at[span, :], held.at[span, :], sems.at[h]))
     for copy in copies:
         copy.start()
+    for copy in copies[:8]:
+        copy.wait()
     valid = valid_ref[...] > 0.0
     places = tp_places()
-    for h in range(4):
-        copies[h].wait()
-        span = slice(h * HEAD, (h + 1) * HEAD)
+    for h in range(0, 4, 2):
+        copies[8 + h].wait()
+        copies[9 + h].wait()
+        span = slice(h * HEAD, (h + 2) * HEAD)
         acc = 0.0
-        for piece, at in zip(grads, places):
+        for n, at in enumerate(places):
             w = held[span, pl.ds(pl.multiple_of(at * size, size), size)]
-            acc = acc + lax.dot_general(piece[...], w, NT, preferred_element_type=F32)
+            acc = acc + lax.dot_general(pieces[n], w, NT, preferred_element_type=F32)
         out_ref[:, span] = jnp.where(valid, acc, 0.0).astype(BF16)
 
 
 def d_attn_of(grads, valid, w_out):
+    rows, size = grads[0].shape
     return call(
         d_attn_kernel,
-        (*grads, valid, w_out),
-        [shape(*grads[0].shape)],
-        [pltpu.VMEM(w_out.shape, BF16), pltpu.SemaphoreType.DMA((4,))],
+        (valid, *grads, w_out),
+        [shape(rows, size)],
+        [
+            pltpu.VMEM((8, rows, size), BF16),
+            pltpu.VMEM(w_out.shape, BF16),
+            pltpu.SemaphoreType.DMA((8,)),
+            pltpu.SemaphoreType.DMA((4,)),
+        ],
         name="d_attn",
         megabytes=12,
         micros=2.0,
-        stay=1,
+        stay=9,
     )[0]
 
 
@@ -413,13 +426,16 @@
     out_ref[...] = jnp.where(valid, result, 0.0).astype(BF16)
 
 
-def tp_pieces(block):
+def tp_pieces(block, beside=None):
     piece_a = along_x(block)
     sibling = other_core(block)
+    if beside is not None:
+        piece_a, beside = lax.optimization_barrier((piece_a, beside))
     piece_b = along_x(sibling)
     piece_f = along_x(piece_a)
     pieces = [block, sibling, piece_a, piece_b]
-    return pieces + [other_core(piece_a), other_core(piece_b), piece_f, other_core(piece_f)]
+    pieces += [other_core(piece_a), other_core(piece_b), piece_f, other_core(piece_f)]
+    return pieces if beside is None else (pieces, beside)
 
 
 def per_device(encoded, starts, w_up, norm_gain, w_query, w_key, w_value, w_out, cotangent):
@@ -465,7 +481,7 @@
     )[0]
 
     d_attn = d_attn_of(cots, valid, w_out)
-    pieces = tp_pieces(latent)
+    pieces, d_attn = tp_pieces(latent, d_attn)
     keep, send, *qkv, rinv = project(pieces, d_attn, gain, weights)
     half = rows // 2
     packed = shape(shards // 8, half + half // 2, 2 * HEAD)
@@ -489,6 +505,7 @@
         megabytes=16,
     )
     far_in = along_x(far)
+    far_in, side = lax.optimization_barrier((far_in, side))
     side_in = other_core(along_x(side))
     ahead = call(pass_kernel, (near, far_in), [shape(*block)], name="pass")[0]
     return tuple(

time: 182 us -> 172 us (0.945)
  local copies, waits for them, and re-layouts: 13.7 us -> 3.83 us
    unnamed x69 -> x53, local copies, waits for them, and re-layouts: 12.6 us -> 2.69 us
  transfers between devices with their start and end apart: 28 -> 28, of which waited for: 17 -> 18; matrix products, arithmetic and copies ran while one was open for 1% -> 1% of each run, Pallas kernels for 5% -> 5%
where the time goes in v1:
time: 172 us
  waiting for transfers between devices  61.9 us (36%)
  blocking collectives  57.6 us (33%)
  Pallas kernels  33.8 us (20%)
  starting transfers between devices  13.7 us (8%)
  local copies, waits for them, and re-layouts  3.83 us (2%)
    ppermute x9, waiting for transfers between devices, along_x(): return lax.ppermute(block, XC, route)  42.2 us
    pallas_call x14, Pallas kernels, call(): pl.pallas_call(kernel, in_specs=[VMEM] * (len(ins) - stay) + [pl.BlockSpe...  33.8 us
    all_to_all x1, blocking collectives, per_device(): mine = lax.all_to_all(sent, SEQ, 0, 0, tiled=True)  30.9 us
    all_to_all x1, blocking collectives, per_device(): back = lax.all_to_all(back, SEQ, 0, 0, tiled=True)  26.8 us
    ppermute x15, waiting for transfers between devices, other_core(): return lax.ppermute(block, 'c', [(0, 1), (1, 0)])  13.1 us
    ppermute x3, waiting for transfers between devices, per_device(): lax.ppermute(patches, 'x', [(i, (i + k) % 4) for i in range(4)])  4.82 us
    ppermute x3, starting transfers between devices, per_device(): lax.ppermute(patches, 'x', [(i, (i + k) % 4) for i in range(4)])  4.51 us
    ppermute x15, starting transfers between devices, other_core(): return lax.ppermute(block, 'c', [(0, 1), (1, 0)])  4.01 us
  transfers between devices with their start and end apart: 28, of which 18 were waited for; matrix products, arithmetic and copies ran while one was open for 1% of the time, Pallas kernels for 5%

profile of v1, /device:TPU:0, one launch (start us, length us, event | category | flops | bytes accessed | tf_op | source)
XLA Modules:
  0.0 172.0 jit_solution(16696339083983399879)
XLA Ops:
  0.6 1.6 collective-permute-start.6
  2.3 0.8 collective-permute-start.5
  3.1 0.8 copy.15.starts_ref
  3.9 1.1 copy-done.18
  5.0 0.4 pool.1
  5.4 1.3 collective-permute-start
  6.7 1.8 %collective-permute-done.next_ref = f32[1,1280]{1,0:T(1,128)S(1)} collective-permute-done((f32[1,1280]{1,0:T(1,128)S(1)}, f32[1,1280]{1,0:T(1,128)S(1)}, u32[]{:S(2)}, u32[]{:S(2)}) %collective-permute-start) | collective-permute-done | bytes 5152 | tf_op jit(solution)/shard_map/ppermute | solution.py:462
  8.7 2.8 %collective-permute-start.3 = (bf16[32,1280]{1,0:T(8,128)(2,1)S(1)}, bf16[32,1280]{1,0:T(8,128)(2,1)S(1)}, u32[]{:S(2)}, u32[]{:S(2)}) collective-permute-start(bf16[32,1280]{1,0:T(8,128)(2,1)S(1)} %patch.1), channel_id=1, source_target_pairs={{0,6},{2,0},{4,2},{6,4},{1,7},{3,1},{5,3},{7,5},{8,14},{10,8},{12,... | collective-permute-start | bytes 245768 | tf_op jit(solution)/shard_map/ppermute | solution.py:470
  11.5 1.1 collective-permute-start.2
  12.6 0.6 collective-permute-start.1
  13.2 1.8 %collective-permute-start.10 = (bf16[256,512]{1,0:T(8,128)(2,1)S(1)}, bf16[256,512]{1,0:T(8,128)(2,1)S(1)}, u32[]{:S(2)}, u32[]{:S(2)}) collective-permute-start(bf16[256,512]{1,0:T(8,128)(2,1)S(1)} %collective-permute-done.6.refs_2_), channel_id=1, source_target_pairs={{0,2},{1,7},{2,4},{3,1},{4,6},{5,3},{6,0},{7,5},{8,10},{9,15},{10,... | collective-permute-start | bytes 786440 | tf_op jit(solution)/shard_map/ppermute | solution.py:62
  15.1 2.3 %collective-permute-done.2 = bf16[32,1280]{1,0:T(8,128)(2,1)S(1)} collective-permute-done((bf16[32,1280]{1,0:T(8,128)(2,1)S(1)}, bf16[32,1280]{1,0:T(8,128)(2,1)S(1)}, u32[]{:S(2)}, u32[]{:S(2)}) %collective-permute-start.2) | collective-permute-done | bytes 81952 | tf_op jit(solution)/shard_map/ppermute | solution.py:470
  17.5 2.5 %collective-permute-done.1 = bf16[32,1280]{1,0:T(8,128)(2,1)S(1)} collective-permute-done((bf16[32,1280]{1,0:T(8,128)(2,1)S(1)}, bf16[32,1280]{1,0:T(8,128)(2,1)S(1)}, u32[]{:S(2)}, u32[]{:S(2)}) %collective-permute-start.1) | collective-permute-done | bytes 81952 | tf_op jit(solution)/shard_map/ppermute | solution.py:470
  20.0 0.5 collective-permute-start.4
  20.6 2.3 %collective-permute-done.10.refs_6_ = bf16[256,512]{1,0:T(8,128)(2,1)S(1)} collective-permute-done((bf16[256,512]{1,0:T(8,128)(2,1)S(1)}, bf16[256,512]{1,0:T(8,128)(2,1)S(1)}, u32[]{:S(2)}, u32[]{:S(2)}) %collective-permute-start.10) | collective-permute-done | bytes 262176 | tf_op jit(solution)/shard_map/ppermute | solution.py:62
  22.9 2.8 %collective-permute-done.7.refs_3_ = bf16[256,512]{1,0:T(8,128)(2,1)S(1)} collective-permute-done((bf16[256,512]{1,0:T(8,128)(2,1)S(1)}, bf16[256,512]{1,0:T(8,128)(2,1)S(1)}, u32[]{:S(2)}, u32[]{:S(2)}) %collective-permute-start.7) | collective-permute-done | bytes 262176 | tf_op jit(solution)/shard_map/ppermute | solution.py:62
  26.0 0.4 copy-done.24
  26.4 0.3 copy-done.25
  26.7 0.7 collective-permute-done.9.refs_5_
  27.4 0.5 latent.1.refs_0_.refs_7_.lat_ref
  28.0 0.4 collective-permute-start.12
  28.6 5.1 %d_attn.1.refs_8_ = bf16[256,512]{1,0:T(8,128)(2,1)S(1)} custom-call(f32[256,1]{1,0:T(8,128)S(1)} %copy.18.valid_ref, bf16[256,512]{1,0:T(8,128)(2,1)} %cot_ref.1, bf16[256,512]{1,0:T(8,128)(2,1)} %copy-done.22, bf16[256,512]{1,0:T(8,128)(2,1)} %copy-done.21, bf16[256,512]{1,0:T(8,128)(2,1)} %copy-done.24, bf16[256,512]{1,0:T(8,128)(2,1)} %copy-done.25, ...), custom_call_target="tpu_custom_call" | custom-call | flops 2000000000 | bytes 6000000 | tf_op jit(solution)/shard_map/d_attn/pallas_call | solution.py:35
  33.7 1.9 %collective-permute-done.13.refs_2_.refs_6_ = bf16[256,512]{1,0:T(8,128)(2,1)S(1)} collective-permute-done((bf16[256,512]{1,0:T(8,128)(2,1)S(1)}, bf16[256,512]{1,0:T(8,128)(2,1)S(1)}, u32[]{:S(2)}, u32[]{:S(2)}) %collective-permute-start.13) | collective-permute-done | bytes 262176 | tf_op jit(solution)/shard_map/ppermute | solution.py:62
  35.7 1.3 collective-permute-start.15
  37.0 6.2 %collective-permute-done.17.refs_6_.refs_4_ = bf16[256,512]{1,0:T(8,128)(2,1)S(1)} collective-permute-done((bf16[256,512]{1,0:T(8,128)(2,1)S(1)}, bf16[256,512]{1,0:T(8,128)(2,1)S(1)}, u32[]{:S(2)}, u32[]{:S(2)}) %collective-permute-start.17) | collective-permute-done | bytes 262176 | tf_op jit(solution)/shard_map/ppermute | solution.py:62
  43.2 2.8 %collective-permute-done.14.refs_3_.refs_5_ = bf16[256,512]{1,0:T(8,128)(2,1)S(1)} collective-permute-done((bf16[256,512]{1,0:T(8,128)(2,1)S(1)}, bf16[256,512]{1,0:T(8,128)(2,1)S(1)}, u32[]{:S(2)}, u32[]{:S(2)}) %collective-permute-start.14) | collective-permute-done | bytes 262176 | tf_op jit(solution)/shard_map/ppermute | solution.py:62
  46.0 1.5 collective-permute-done.16.refs_5_
  47.5 7.0 %project.1 = (bf16[4,256,256]{2,1,0:T(8,128)(2,1)S(1)}, bf16[4,256,256]{2,1,0:T(8,128)(2,1)S(1)}, bf16[256,512]{1,0:T(8,128)(2,1)S(1)}, bf16[256,512]{1,0:T(8,12...) custom-call(bf16[256,512]{1,0:T(8,128)(2,1)S(1)} %latent.1.refs_0_.refs_7_.lat_ref, ...), custom_call_target="tpu_custom_call" | custom-call | flops 5000000000 | bytes 15000000 | tf_op jit(solution)/shard_map/project/pallas_call | solution.py:35
  54.6 0.4 collective-permute-start.19
  55.0 1.8 %collective-permute-done.19.got_ref = bf16[4,256,256]{2,1,0:T(8,128)(2,1)S(1)} collective-permute-done((bf16[4,256,256]{2,1,0:T(8,128)(2,1)S(1)}, bf16[4,256,256]{2,1,0:T(8,128)(2,1)S(1)}, u32[]{:S(2)}, u32[]{:S(2)}) %collective-permute-start.19) | collective-permute-done | bytes 524320 | tf_op jit(solution)/shard_map/ppermute | solution.py:54
  56.9 30.9 %all_to_all.10.mine_ref = bf16[16,192,256]{2,1,0:T(8,128)(2,1)S(1)} all-to-all(bf16[16,192,256]{2,1,0:T(8,128)(2,1)S(1)} %pack.1), channel_id=1, replica_groups=mesh['y'=4,'z'=4,'x'=4,'c'=2] {'y','z'}, dimensions={0} | all-to-all | bytes 3145728 | tf_op jit(solution)/shard_map/all_to_all | solution.py:489
  87.9 3.3 %collective-permute-done.20.theirs_ref = bf16[16,192,256]{2,1,0:T(8,128)(2,1)} collective-permute-done((bf16[16,192,256]{2,1,0:T(8,128)(2,1)S(1)}, bf16[16,192,256]{2,1,0:T(8,128)(2,1)}, u32[]{:S(2)}, u32[]{:S(2)}) %collective-permute-start.20) | collective-permute-done | bytes 1572896 | tf_op jit(solution)/shard_map/ppermute | solution.py:54
  91.3 0.6 broadcast_in_dim.15.bias_ref
  91.9 13.1 %attention.1 = (bf16[16,128,256]{2,1,0:T(8,128)(2,1)S(1)}, bf16[16,128,256]{2,1,0:T(8,128)(2,1)S(1)}, bf16[16,64,256]{2,1,0:T(8,128)(2,1)S(1)}) custom-call(f32[2,2048,128]{2,1,0:T(8,128)S(1)} %broadcast_in_dim.15.bias_ref, bf16[16,192,256]{2,1,0:T(8,128)(2,1)S(1)} %all_to_all.10.mine_ref, bf16[16,192,256]{2,1,0:T(8,128)(2,1)} %collective-permute-done.20.theirs_ref), custom_call_target="tpu_custom_call" | custom-call | flops 12000000000 | bytes 36000000 | tf_op jit(solution)/shard_map/attention/pallas_call | solution.py:35
  105.0 0.2 collective-permute-start.21
  105.2 2.5 %collective-permute-done.21.got_ref = bf16[16,128,256]{2,1,0:T(8,128)(2,1)S(1)} collective-permute-done((bf16[16,128,256]{2,1,0:T(8,128)(2,1)S(1)}, bf16[16,128,256]{2,1,0:T(8,128)(2,1)S(1)}, u32[]{:S(2)}, u32[]{:S(2)}) %collective-permute-start.21) | collective-permute-done | bytes 1048608 | tf_op jit(solution)/shard_map/ppermute | solution.py:54
  107.8 0.3 return.1
  108.0 26.8 %all_to_all.11.in_ref = bf16[16,192,256]{2,1,0:T(8,128)(2,1)S(1)} all-to-all(bf16[16,192,256]{2,1,0:T(8,128)(2,1)S(1)} %return.1), channel_id=1, replica_groups=mesh['y'=4,'z'=4,'x'=4,'c'=2] {'y','z'}, dimensions={0} | all-to-all | bytes 3145728 | tf_op jit(solution)/shard_map/all_to_all | solution.py:492
  135.0 1.9 %collective-permute-done.22.got_ref = bf16[4,256,256]{2,1,0:T(8,128)(2,1)S(1)} collective-permute-done((bf16[4,256,256]{2,1,0:T(8,128)(2,1)S(1)}, bf16[4,256,256]{2,1,0:T(8,128)(2,1)S(1)}, u32[]{:S(2)}, u32[]{:S(2)}) %collective-permute-start.22) | collective-permute-done | bytes 524320 | tf_op jit(solution)/shard_map/ppermute | solution.py:54
  137.0 2.7 %outputs.3 = bf16[4,512,512]{2,1,0:T(8,128)(2,1)S(1)} custom-call(bf16[4,256,256]{2,1,0:T(8,128)(2,1)S(1)} %get-tuple-element.51.keep_ref, bf16[4,256,256]{2,1,0:T(8,128)(2,1)S(1)} %collective-permute-done.22.got_ref, bf16[256,512]{1,0:T(8,128)(2,1)S(1)} %get-tuple-element.53.refs_0_, bf16[256,512]{1,0:T(8,128)(2,1)S(1)} %get-tuple-element.54.refs_1_, ...), custom_call_target="tpu_custom_call" | custom-call | flops 3000000000 | bytes 9000000 | tf_op jit(solution)/shard_map/outputs/pallas_call | solution.py:35
  139.7 0.2 collective-permute-start.23
  139.9 2.7 %outputs.2.own_ref = bf16[4,512,512]{2,1,0:T(8,128)(2,1)S(1)} custom-call(bf16[4,256,256]{2,1,0:T(8,128)(2,1)S(1)} %get-tuple-element.51.keep_ref, bf16[4,256,256]{2,1,0:T(8,128)(2,1)S(1)} %collective-permute-done.22.got_ref, bf16[256,512]{1,0:T(8,128)(2,1)S(1)} %get-tuple-element.53.refs_0_, bf16[256,512]{1,0:T(8,128)(2,1)S(1)} %get-tuple-element.54.refs_1_, ...), custom_call_target="tpu_custom_call" | custom-call | flops 3000000000 | bytes 9000000 | tf_op jit(solution)/shard_map/outputs/pallas_call | solution.py:35
  142.6 1.3 collective-permute-done.23.other_ref
  143.9 0.4 add.9
  144.5 10.4 %collective-permute-done.24.far_ref = bf16[512,512]{1,0:T(8,128)(2,1)S(1)} collective-permute-done((bf16[512,512]{1,0:T(8,128)(2,1)S(1)}, bf16[512,512]{1,0:T(8,128)(2,1)S(1)}, u32[]{:S(2)}, u32[]{:S(2)}) %collective-permute-start.24) | collective-permute-done | bytes 524320 | tf_op jit(solution)/shard_map/ppermute | solution.py:62
  155.0 10.2 %collective-permute-done.26 = bf16[512,512]{1,0:T(8,128)(2,1)S(1)} collective-permute-done((bf16[512,512]{1,0:T(8,128)(2,1)S(1)}, bf16[512,512]{1,0:T(8,128)(2,1)S(1)}, u32[]{:S(2)}, u32[]{:S(2)}) %collective-permute-start.26) | collective-permute-done | bytes 524320 | tf_op jit(solution)/shard_map/ppermute | solution.py:62
  165.3 5.6 %collective-permute-done.25.ahead_ref = bf16[512,512]{1,0:T(8,128)(2,1)S(1)} collective-permute-done((bf16[512,512]{1,0:T(8,128)(2,1)S(1)}, bf16[512,512]{1,0:T(8,128)(2,1)S(1)}, u32[]{:S(2)}, u32[]{:S(2)}) %collective-permute-start.25) | collective-permute-done | bytes 524320 | tf_op jit(solution)/shard_map/ppermute | solution.py:62
  170.9 1.1 final.1
  (86 shorter events, 1.8 us)
Async XLA Ops:
  0.6 12.6 %collective-permute-start.6 = (bf16[256,512]{1,0:T(8,128)(2,1)}, bf16[256,512]{1,0:T(8,128)(2,1)S(1)}, u32[]{:S(2)}, u32[]{:S(2)}) collective-permute-start(bf16[256,512]{1,0:T(8,128)(2,1)} %cot_ref.1), channel_id=1, source_target_pairs={{0,2},{1,7},{2,4},{3,1},{4,6},{5,3},{6,0},{7,5},{8,10},{9,15},{10,... | collective-permute-start | bytes 786440 | tf_op jit(solution)/shard_map/ppermute | solution.py:62
  2.3 12.8 %collective-permute-start.5 = (bf16[256,512]{1,0:T(8,128)(2,1)}, bf16[256,512]{1,0:T(8,128)(2,1)S(1)}, u32[]{:S(2)}, u32[]{:S(2)}) collective-permute-start(bf16[256,512]{1,0:T(8,128)(2,1)} %cot_ref.1), channel_id=1, source_target_pairs={{0,1},{1,0},{2,3},{3,2},{4,5},{5,4},{6,7},{7,6},{8,9},{9,8},{10,11... | collective-permute-start | bytes 786440 | tf_op jit(solution)/shard_map/ppermute | solution.py:54
  5.4 3.1 %collective-permute-start = (f32[1,1280]{1,0:T(1,128)S(1)}, f32[1,1280]{1,0:T(1,128)S(1)}, u32[]{:S(2)}, u32[]{:S(2)}) collective-permute-start(f32[1,1280]{1,0:T(1,128)S(1)} %get-tuple-element.33), channel_id=1, source_target_pairs={{1,0},{2,1},{3,2},{4,3},{5,4},{6,5},{7,6},{8,7},{9,8},{10,9},{11,1... | collective-permute-start | bytes 15368 | tf_op jit(solution)/shard_map/ppermute | solution.py:462
  8.5 17.2 %copy-start.20 = (s32[128,32]{0,1:T(8,128)S(1)}, s32[128,32]{0,1:T(8,128)}, u32[]{:S(2)}) copy-start(s32[128,32]{0,1:T(8,128)} %param.10) | copy-start | bytes 49156
  8.5 18.9 %copy-start.17 = (bf16[1280,512]{1,0:T(8,128)(2,1)S(1)}, bf16[1280,512]{1,0:T(8,128)(2,1)}, u32[]{:S(2)}) copy-start(bf16[1280,512]{1,0:T(8,128)(2,1)} %w_ref.1) | copy-start | bytes 3932164
  8.7 6.4 %collective-permute-start.3 = (bf16[32,1280]{1,0:T(8,128)(2,1)S(1)}, bf16[32,1280]{1,0:T(8,128)(2,1)S(1)}, u32[]{:S(2)}, u32[]{:S(2)}) collective-permute-start(bf16[32,1280]{1,0:T(8,128)(2,1)S(1)} %patch.1), channel_id=1, source_target_pairs={{0,6},{2,0},{4,2},{6,4},{1,7},{3,1},{5,3},{7,5},{8,14},{10,8},{12,... | collective-permute-start | bytes 245768 | tf_op jit(solution)/shard_map/ppermute | solution.py:470
  11.5 5.9 %collective-permute-start.2 = (bf16[32,1280]{1,0:T(8,128)(2,1)S(1)}, bf16[32,1280]{1,0:T(8,128)(2,1)S(1)}, u32[]{:S(2)}, u32[]{:S(2)}) collective-permute-start(bf16[32,1280]{1,0:T(8,128)(2,1)S(1)} %patch.1), channel_id=1, source_target_pairs={{0,4},{2,6},{4,0},{6,2},{1,5},{3,7},{5,1},{7,3},{8,12},{10,14},{12... | collective-permute-start | bytes 245768 | tf_op jit(solution)/shard_map/ppermute | solution.py:470
  12.6 7.3 %collective-permute-start.1 = (bf16[32,1280]{1,0:T(8,128)(2,1)S(1)}, bf16[32,1280]{1,0:T(8,128)(2,1)S(1)}, u32[]{:S(2)}, u32[]{:S(2)}) collective-permute-start(bf16[32,1280]{1,0:T(8,128)(2,1)S(1)} %patch.1), channel_id=1, source_target_pairs={{0,2},{2,4},{4,6},{6,0},{1,3},{3,5},{5,7},{7,1},{8,10},{10,12},{12... | collective-permute-start | bytes 245768 | tf_op jit(solution)/shard_map/ppermute | solution.py:470
  13.2 14.7 %copy-start.21 = (bf16[256,512]{1,0:T(8,128)(2,1)}, bf16[256,512]{1,0:T(8,128)(2,1)S(1)}, u32[]{:S(2)}) copy-start(bf16[256,512]{1,0:T(8,128)(2,1)S(1)} %collective-permute-done.6.refs_2_) | copy-start | bytes 786436
  13.2 9.7 %collective-permute-start.10 = (bf16[256,512]{1,0:T(8,128)(2,1)S(1)}, bf16[256,512]{1,0:T(8,128)(2,1)S(1)}, u32[]{:S(2)}, u32[]{:S(2)}) collective-permute-start(bf16[256,512]{1,0:T(8,128)(2,1)S(1)} %collective-permute-done.6.refs_2_), channel_id=1, source_target_pairs={{0,2},{1,7},{2,4},{3,1},{4,6},{5,3},{6,0},{7,5},{8,10},{9,15},{10,... | collective-permute-start | bytes 786440 | tf_op jit(solution)/shard_map/ppermute | solution.py:62
  15.0 12.9 %copy-start.22 = (bf16[256,512]{1,0:T(8,128)(2,1)}, bf16[256,512]{1,0:T(8,128)(2,1)S(1)}, u32[]{:S(2)}) copy-start(bf16[256,512]{1,0:T(8,128)(2,1)S(1)} %collective-permute-done.5.refs_1_) | copy-start | bytes 786436
  15.0 10.7 %collective-permute-start.7 = (bf16[256,512]{1,0:T(8,128)(2,1)S(1)}, bf16[256,512]{1,0:T(8,128)(2,1)S(1)}, u32[]{:S(2)}, u32[]{:S(2)}) collective-permute-start(bf16[256,512]{1,0:T(8,128)(2,1)S(1)} %collective-permute-done.5.refs_1_), channel_id=1, source_target_pairs={{0,2},{1,7},{2,4},{3,1},{4,6},{5,3},{6,0},{7,5},{8,10},{9,15},{10,... | collective-permute-start | bytes 786440 | tf_op jit(solution)/shard_map/ppermute | solution.py:62
  20.0 6.0 %collective-permute-start.4 = (bf16[4,32,1280]{2,1,0:T(8,128)(2,1)S(1)}, bf16[4,32,1280]{2,1,0:T(8,128)(2,1)S(1)}, u32[]{:S(2)}, u32[]{:S(2)}) collective-permute-start(bf16[4,32,1280]{2,1,0:T(8,128)(2,1)S(1)} %pad_maximum_fusion.own_ref), channel_id=1, source_target_pairs={{0,1},{1,0},{2,3},{3,2},{4,5},{5,4},{6,7},{7,6},{8,9},{9,8},{10,11... | collective-permute-start | bytes 983048 | tf_op jit(solution)/shard_map/ppermute | solution.py:54
  20.5 5.5 %collective-permute-start.8 = (bf16[256,512]{1,0:T(8,128)(2,1)S(1)}, bf16[256,512]{1,0:T(8,128)(2,1)S(1)}, u32[]{:S(2)}, u32[]{:S(2)}) collective-permute-start(bf16[256,512]{1,0:T(8,128)(2,1)S(1)} %collective-permute-done.6.refs_2_), channel_id=1, source_target_pairs={{0,1},{1,0},{2,3},{3,2},{4,5},{5,4},{6,7},{7,6},{8,9},{9,8},{10,11... | collective-permute-start | bytes 786440 | tf_op jit(solution)/shard_map/ppermute | solution.py:54
  22.9 5.7 %copy-start.23 = (bf16[256,512]{1,0:T(8,128)(2,1)}, bf16[256,512]{1,0:T(8,128)(2,1)S(1)}, u32[]{:S(2)}) copy-start(bf16[256,512]{1,0:T(8,128)(2,1)S(1)} %collective-permute-done.10.refs_6_) | copy-start | bytes 786436
  22.9 3.1 %collective-permute-start.11 = (bf16[256,512]{1,0:T(8,128)(2,1)S(1)}, bf16[256,512]{1,0:T(8,128)(2,1)}, u32[]{:S(2)}, u32[]{:S(2)}) collective-permute-start(bf16[256,512]{1,0:T(8,128)(2,1)S(1)} %collective-permute-done.10.refs_6_), channel_id=1, source_target_pairs={{0,1},{1,0},{2,3},{3,2},{4,5},{5,4},{6,7},{7,6},{8,9},{9,8},{10,11... | collective-permute-start | bytes 786440 | tf_op jit(solution)/shard_map/ppermute | solution.py:54
  25.7 1.7 collective-permute-start.9
  28.0 7.7 %collective-permute-start.13 = (bf16[256,512]{1,0:T(8,128)(2,1)S(1)}, bf16[256,512]{1,0:T(8,128)(2,1)S(1)}, u32[]{:S(2)}, u32[]{:S(2)}) collective-permute-start(bf16[256,512]{1,0:T(8,128)(2,1)S(1)} %latent.1.refs_0_.refs_7_.lat_ref), channel_id=1, source_target_pairs={{0,2},{1,7},{2,4},{3,1},{4,6},{5,3},{6,0},{7,5},{8,10},{9,15},{10,... | collective-permute-start | bytes 786440 | tf_op jit(solution)/shard_map/ppermute | solution.py:62
  28.0 7.6 %collective-permute-start.12 = (bf16[256,512]{1,0:T(8,128)(2,1)S(1)}, bf16[256,512]{1,0:T(8,128)(2,1)S(1)}, u32[]{:S(2)}, u32[]{:S(2)}) collective-permute-start(bf16[256,512]{1,0:T(8,128)(2,1)S(1)} %latent.1.refs_0_.refs_7_.lat_ref), channel_id=1, source_target_pairs={{0,1},{1,0},{2,3},{3,2},{4,5},{5,4},{6,7},{7,6},{8,9},{9,8},{10,11... | collective-permute-start | bytes 786440 | tf_op jit(solution)/shard_map/ppermute | solution.py:54
  28.6 18.9 %copy-start.16 = (f32[4096]{0:T(1024)S(1)}, f32[4096]{0:T(1024)}, u32[]{:S(2)}) copy-start(f32[4096]{0:T(1024)} %param.12) | copy-start | bytes 49156
  35.6 7.6 %collective-permute-start.17 = (bf16[256,512]{1,0:T(8,128)(2,1)S(1)}, bf16[256,512]{1,0:T(8,128)(2,1)S(1)}, u32[]{:S(2)}, u32[]{:S(2)}) collective-permute-start(bf16[256,512]{1,0:T(8,128)(2,1)S(1)} %collective-permute-done.13.refs_2_.refs_6_), channel_id=1, source_target_pairs={{0,2},{1,7},{2,4},{3,1},{4,6},{5,3},{6,0},{7,5},{8,10},{9,15},{10,... | collective-permute-start | bytes 786440 | tf_op jit(solution)/shard_map/ppermute | solution.py:62
  35.6 18.9 %copy-start.4 = (bf16[256,512]{1,0:T(8,128)(2,1)}, bf16[256,512]{1,0:T(8,128)(2,1)S(1)}, u32[]{:S(2)}) copy-start(bf16[256,512]{1,0:T(8,128)(2,1)S(1)} %collective-permute-done.12.refs_1_.refs_7_) | copy-start | bytes 786436
  35.6 10.4 %collective-permute-start.14 = (bf16[256,512]{1,0:T(8,128)(2,1)S(1)}, bf16[256,512]{1,0:T(8,128)(2,1)S(1)}, u32[]{:S(2)}, u32[]{:S(2)}) collective-permute-start(bf16[256,512]{1,0:T(8,128)(2,1)S(1)} %collective-permute-done.12.refs_1_.refs_7_), channel_id=1, source_target_pairs={{0,2},{1,7},{2,4},{3,1},{4,6},{5,3},{6,0},{7,5},{8,10},{9,15},{10,... | collective-permute-start | bytes 786440 | tf_op jit(solution)/shard_map/ppermute | solution.py:62
  35.7 10.3 %collective-permute-start.15 = (bf16[256,512]{1,0:T(8,128)(2,1)S(1)}, bf16[256,512]{1,0:T(8,128)(2,1)S(1)}, u32[]{:S(2)}, u32[]{:S(2)}) collective-permute-start(bf16[256,512]{1,0:T(8,128)(2,1)S(1)} %collective-permute-done.13.refs_2_.refs_6_), channel_id=1, source_target_pairs={{0,1},{1,0},{2,3},{3,2},{4,5},{5,4},{6,7},{7,6},{8,9},{9,8},{10,11... | collective-permute-start | bytes 786440 | tf_op jit(solution)/shard_map/ppermute | solution.py:54
  43.2 11.3 %copy-start.6 = (bf16[256,512]{1,0:T(8,128)(2,1)}, bf16[256,512]{1,0:T(8,128)(2,1)S(1)}, u32[]{:S(2)}) copy-start(bf16[256,512]{1,0:T(8,128)(2,1)S(1)} %collective-permute-done.17.refs_6_.refs_4_) | copy-start | bytes 786436
  43.2 2.8 %collective-permute-start.18 = (bf16[256,512]{1,0:T(8,128)(2,1)S(1)}, bf16[256,512]{1,0:T(8,128)(2,1)S(1)}, u32[]{:S(2)}, u32[]{:S(2)}) collective-permute-start(bf16[256,512]{1,0:T(8,128)(2,1)S(1)} %collective-permute-done.17.refs_6_.refs_4_), channel_id=1, source_target_pairs={{0,1},{1,0},{2,3},{3,2},{4,5},{5,4},{6,7},{7,6},{8,9},{9,8},{10,11... | collective-permute-start | bytes 786440 | tf_op jit(solution)/shard_map/ppermute | solution.py:54
  46.0 8.5 %copy-start.10 = (bf16[256,512]{1,0:T(8,128)(2,1)}, bf16[256,512]{1,0:T(8,128)(2,1)S(1)}, u32[]{:S(2)}) copy-start(bf16[256,512]{1,0:T(8,128)(2,1)S(1)} %collective-permute-done.14.refs_3_.refs_5_) | copy-start | bytes 786436
  46.0 1.5 collective-permute-start.16
  46.0 8.5 %copy-start.8 = (bf16[256,512]{1,0:T(8,128)(2,1)}, bf16[256,512]{1,0:T(8,128)(2,1)S(1)}, u32[]{:S(2)}) copy-start(bf16[256,512]{1,0:T(8,128)(2,1)S(1)} %collective-permute-done.15.refs_4_.refs_6_) | copy-start | bytes 786436
  46.0 8.5 %copy-start.14 = (bf16[256,512]{1,0:T(8,128)(2,1)}, bf16[256,512]{1,0:T(8,128)(2,1)S(1)}, u32[]{:S(2)}) copy-start(bf16[256,512]{1,0:T(8,128)(2,1)S(1)} %collective-permute-done.18.refs_7_.refs_4_) | copy-start | bytes 786436
  47.5 7.0 %copy-start.12 = (bf16[256,512]{1,0:T(8,128)(2,1)}, bf16[256,512]{1,0:T(8,128)(2,1)S(1)}, u32[]{:S(2)}) copy-start(bf16[256,512]{1,0:T(8,128)(2,1)S(1)} %collective-permute-done.16.refs_5_) | copy-start | bytes 786436
  54.6 2.2 %collective-permute-start.19 = (bf16[4,256,256]{2,1,0:T(8,128)(2,1)S(1)}, bf16[4,256,256]{2,1,0:T(8,128)(2,1)S(1)}, u32[]{:S(2)}, u32[]{:S(2)}) collective-permute-start(bf16[4,256,256]{2,1,0:T(8,128)(2,1)S(1)} %get-tuple-element.47), channel_id=1, source_target_pairs={{0,1},{1,0},{2,3},{3,2},{4,5},{5,4},{6,7},{7,6},{8,9},{9,8},{10,11... | collective-permute-start | bytes 1572872 | tf_op jit(solution)/shard_map/ppermute | solution.py:54
  87.7 3.5 %collective-permute-start.20 = (bf16[16,192,256]{2,1,0:T(8,128)(2,1)S(1)}, bf16[16,192,256]{2,1,0:T(8,128)(2,1)}, u32[]{:S(2)}, u32[]{:S(2)}) collective-permute-start(bf16[16,192,256]{2,1,0:T(8,128)(2,1)S(1)} %all_to_all.10.mine_ref), channel_id=1, source_target_pairs={{0,1},{1,0},{2,3},{3,2},{4,5},{5,4},{6,7},{7,6},{8,9},{9,8},{10,11... | collective-permute-start | bytes 4718600 | tf_op jit(solution)/shard_map/ppermute | solution.py:54
  91.9 45.0 %copy-start.2 = (bf16[4096,512]{1,0:T(8,128)(2,1)S(1)}, bf16[4096,512]{1,0:T(8,128)(2,1)}, u32[]{:S(2)}) copy-start(bf16[4096,512]{1,0:T(8,128)(2,1)} %refs_10_.5) | copy-start | bytes 12582916
  91.9 45.0 %copy-start.3 = (bf16[4096,512]{1,0:T(8,128)(2,1)S(1)}, bf16[4096,512]{1,0:T(8,128)(2,1)}, u32[]{:S(2)}) copy-start(bf16[4096,512]{1,0:T(8,128)(2,1)} %refs_11_.5) | copy-start | bytes 12582916
  105.0 2.7 %collective-permute-start.21 = (bf16[16,128,256]{2,1,0:T(8,128)(2,1)S(1)}, bf16[16,128,256]{2,1,0:T(8,128)(2,1)S(1)}, u32[]{:S(2)}, u32[]{:S(2)}) collective-permute-start(bf16[16,128,256]{2,1,0:T(8,128)(2,1)S(1)} %get-tuple-element.49), channel_id=1, source_target_pairs={{0,1},{1,0},{2,3},{3,2},{4,5},{5,4},{6,7},{7,6},{8,9},{9,8},{10,11... | collective-permute-start | bytes 3145736 | tf_op jit(solution)/shard_map/ppermute | solution.py:54
  107.8 29.2 %copy-start.1 = (bf16[4096,512]{1,0:T(8,128)(2,1)S(1)}, bf16[4096,512]{1,0:T(8,128)(2,1)}, u32[]{:S(2)}) copy-start(bf16[4096,512]{1,0:T(8,128)(2,1)} %refs_9_.3) | copy-start | bytes 12582916
  108.0 28.9 %copy-start = (bf16[512,4096]{1,0:T(8,128)(2,1)S(1)}, bf16[512,4096]{1,0:T(8,128)(2,1)}, u32[]{:S(2)}) copy-start(bf16[512,4096]{1,0:T(8,128)(2,1)} %refs_12_.5) | copy-start | bytes 12582916
  134.9 2.0 %collective-permute-start.22 = (bf16[4,256,256]{2,1,0:T(8,128)(2,1)S(1)}, bf16[4,256,256]{2,1,0:T(8,128)(2,1)S(1)}, u32[]{:S(2)}, u32[]{:S(2)}) collective-permute-start(bf16[4,256,256]{2,1,0:T(8,128)(2,1)S(1)} %get-tuple-element.52), channel_id=1, source_target_pairs={{0,1},{1,0},{2,3},{3,2},{4,5},{5,4},{6,7},{7,6},{8,9},{9,8},{10,11... | collective-permute-start | bytes 1572872 | tf_op jit(solution)/shard_map/ppermute | solution.py:54
  137.0 2.9 %copy-start.7 = (bf16[256,512]{1,0:T(8,128)(2,1)S(1)}, bf16[256,512]{1,0:T(8,128)(2,1)}, u32[]{:S(2)}) copy-start(bf16[256,512]{1,0:T(8,128)(2,1)} %copy-done.6) | copy-start | bytes 786436
  137.0 2.9 %copy-start.9 = (bf16[256,512]{1,0:T(8,128)(2,1)S(1)}, bf16[256,512]{1,0:T(8,128)(2,1)}, u32[]{:S(2)}) copy-start(bf16[256,512]{1,0:T(8,128)(2,1)} %copy-done.8) | copy-start | bytes 786436
  137.0 2.9 %copy-start.13 = (bf16[256,512]{1,0:T(8,128)(2,1)S(1)}, bf16[256,512]{1,0:T(8,128)(2,1)}, u32[]{:S(2)}) copy-start(bf16[256,512]{1,0:T(8,128)(2,1)} %copy-done.12) | copy-start | bytes 786436
  139.7 4.2 %collective-permute-start.23 = (bf16[4,512,512]{2,1,0:T(8,128)(2,1)S(1)}, bf16[4,512,512]{2,1,0:T(8,128)(2,1)S(1)}, u32[]{:S(2)}, u32[]{:S(2)}) collective-permute-start(bf16[4,512,512]{2,1,0:T(8,128)(2,1)S(1)} %outputs.3), channel_id=1, source_target_pairs={{0,1},{1,0},{2,3},{3,2},{4,5},{5,4},{6,7},{7,6},{8,9},{9,8},{10,11... | collective-permute-start | bytes 6291464 | tf_op jit(solution)/shard_map/ppermute | solution.py:54
  144.4 26.5 %copy-start.19 = (bf16[256,512]{1,0:T(8,128)(2,1)S(1)}, bf16[256,512]{1,0:T(8,128)(2,1)}, u32[]{:S(2)}) copy-start(bf16[256,512]{1,0:T(8,128)(2,1)} %cot_ref.1) | copy-start | bytes 786436
  144.4 10.5 %collective-permute-start.24 = (bf16[512,512]{1,0:T(8,128)(2,1)S(1)}, bf16[512,512]{1,0:T(8,128)(2,1)S(1)}, u32[]{:S(2)}, u32[]{:S(2)}) collective-permute-start(bf16[512,512]{1,0:T(8,128)(2,1)S(1)} %get-tuple-element.58), channel_id=1, source_target_pairs={{0,2},{1,7},{2,4},{3,1},{4,6},{5,3},{6,0},{7,5},{8,10},{9,15},{10,... | collective-permute-start | bytes 1572872 | tf_op jit(solution)/shard_map/ppermute | solution.py:62
  154.9 10.4 %collective-permute-start.26 = (bf16[512,512]{1,0:T(8,128)(2,1)S(1)}, bf16[512,512]{1,0:T(8,128)(2,1)S(1)}, u32[]{:S(2)}, u32[]{:S(2)}) collective-permute-start(bf16[512,512]{1,0:T(8,128)(2,1)S(1)} %get-tuple-element.61), channel_id=1, source_target_pairs={{0,2},{1,7},{2,4},{3,1},{4,6},{5,3},{6,0},{7,5},{8,10},{9,15},{10,... | collective-permute-start | bytes 1572872 | tf_op jit(solution)/shard_map/ppermute | solution.py:62
  155.0 15.9 %collective-permute-start.25 = (bf16[512,512]{1,0:T(8,128)(2,1)S(1)}, bf16[512,512]{1,0:T(8,128)(2,1)S(1)}, u32[]{:S(2)}, u32[]{:S(2)}) collective-permute-start(bf16[512,512]{1,0:T(8,128)(2,1)S(1)} %pass.1), channel_id=1, source_target_pairs={{0,2},{1,7},{2,4},{3,1},{4,6},{5,3},{6,0},{7,5},{8,10},{9,15},{10,... | collective-permute-start | bytes 1572872 | tf_op jit(solution)/shard_map/ppermute | solution.py:62
  165.3 5.6 %collective-permute-start.27 = (bf16[512,512]{1,0:T(8,128)(2,1)S(1)}, bf16[512,512]{1,0:T(8,128)(2,1)S(1)}, u32[]{:S(2)}, u32[]{:S(2)}) collective-permute-start(bf16[512,512]{1,0:T(8,128)(2,1)S(1)} %collective-permute-done.26), channel_id=1, source_target_pairs={{0,1},{1,0},{2,3},{3,2},{4,5},{5,4},{6,7},{7,6},{8,9},{9,8},{10,11... | collective-permute-start | bytes 1572872 | tf_op jit(solution)/shard_map/ppermute | solution.py:54
  (6 other events, 9.0 us)

commit v2 on v1

--- a/solution.py
+++ b/solution.py
@@ -17,6 +17,7 @@
 SCALE = HEAD ** (-0.5)
 LOG2E = 1.4426950408889634
 EXP2_SCALE = SCALE * LOG2E
+DELAY = 8.0
 F32 = jnp.float32
 BF16 = jnp.bfloat16
 NT = (((1,), (1,)), ((), ()))
@@ -128,43 +129,40 @@
     return [2 * x + c, 2 * x + o, back + c, back + o, ahead + o, ahead + c, far + c, far + o]
 
 
+def in_order(refs):
+    own, sibling, piece_a, piece_b, piece_f, theirs = refs
+    a, b, f = (theirs.at[n] for n in range(3))
+    return [own, sibling, piece_a, piece_b, a, b, piece_f, f]
+
+
 def piece_rows(ref, at, size):
     return ref[pl.ds(pl.multiple_of(at * size, size), size), :]
 
 
 def project_kernel(*refs):
-    pieces, (do_ref, gain_ref), weights = refs[:8], refs[8:10], refs[10:13]
-    outs, (held, sems, lats, accs, heads) = refs[13:19], refs[19:24]
+    pieces, (do_ref, gain_ref), weights = in_order(refs[:6]), refs[6:8], refs[8:11]
+    outs, (accs, heads) = refs[11:17], refs[17:19]
     keep_ref, send_ref, qkv_refs, rinv_ref = outs[0], outs[1], outs[2:5], outs[5]
     rows, size = pieces[0].shape
     width = gain_ref.shape[1]
     c = place("c")
-    places = tp_places()
-    copies = []
-    for t in range(8):
-        for kind in range(3):
-            part = weights[kind].at[t * size : (t + 1) * size, :]
-            copies.append(pltpu.make_async_copy(part, held.at[t, kind], sems.at[t, kind]))
-    for copy in copies:
-        copy.start()
-    for piece, at in zip(pieces, places):
-        lats[at] = piece[...]
-    for h in range(4):
-        heads[12 + h] = do_ref[:, h * HEAD : (h + 1) * HEAD]
     square = jnp.zeros((rows, 128), F32)
-    for t in range(8):
-        wide = lats[t].astype(F32)
+    for n, (piece, at) in enumerate(zip(pieces, tp_places())):
+        wide = piece[...].astype(F32)
         squares = wide * wide
         for part in range(0, size, 128):
             square = square + squares[:, part : part + 128]
-        scaled = (wide * gain_ref[:, t * size : (t + 1) * size]).astype(BF16)
+        gain = gain_ref[:, pl.ds(pl.multiple_of(at * size, size), size)]
+        scaled = (wide * gain).astype(BF16)
         for kind in range(3):
-            copies[3 * t + kind].wait()
-            made = jnp.dot(scaled, held[t, kind], preferred_element_type=F32)
-            accs[kind] = made if t == 0 else accs[kind] + made
+            w = piece_rows(weights[kind], at, size)
+            made = jnp.dot(scaled, w, preferred_element_type=F32)
+            accs[kind] = made if n == 0 else accs[kind] + made
     total = jnp.sum(square, axis=1, keepdims=True)
     rinv = lax.rsqrt(total / width + EPS)
     rinv_ref[...] = rinv
+    for h in range(4):
+        heads[12 + h] = do_ref[:, h * HEAD : (h + 1) * HEAD]
     for kind in range(3):
         rounded = (rinv * accs[kind]).astype(BF16)
         qkv_refs[kind][...] = rounded
@@ -187,22 +185,15 @@
         project_kernel,
         (*pieces, d_attn, gain, *weights),
         [both, both] + [shape(rows, size)] * 3 + [shape(rows, 1, dtype=F32)],
-        [
-            pltpu.VMEM((8, 3, size, size), BF16),
-            pltpu.SemaphoreType.DMA((8, 3)),
-            pltpu.VMEM((8, rows, size), BF16),
-            pltpu.VMEM((3, rows, size), F32),
-            pltpu.VMEM((16, rows, HEAD), BF16),
-        ],
+        [pltpu.VMEM((3, rows, size), F32), pltpu.VMEM((16, rows, HEAD), BF16)],
         name="project",
-        megabytes=28,
+        megabytes=24,
         micros=5.0,
-        stay=3,
     )
 
 
 def d_attn_kernel(valid_ref, *refs):
-    grads, w_ref, out_ref, pieces, held, grad_sems, sems = refs[:8], *refs[8:]
+    grads, w_ref, out_ref, pieces, held, grad_sems, sems = in_order(refs[:6]), *refs[6:]
     rows, size = grads[0].shape
     copies = [
         pltpu.make_async_copy(grad, pieces.at[n], grad_sems.at[n]) for n, grad in enumerate(grads)
@@ -241,8 +232,8 @@
         ],
         name="d_attn",
         megabytes=12,
-        micros=2.0,
-        stay=9,
+        micros=DELAY,
+        stay=7,
     )[0]
 
 
@@ -359,8 +350,8 @@
 
 
 def output_kernel(which, keep_ref, got_ref, *refs):
-    qkv, rinv_ref, lats, gain_ref = refs[:3], refs[3], refs[4:8], refs[8]
-    weights, w_out_ref, out_ref, wide = refs[9:12], refs[12], refs[13], refs[14]
+    qkv, rinv_ref, lats, gain_ref = refs[:3], refs[3], in_order(refs[4:10]), refs[10]
+    weights, w_out_ref, out_ref, wide = refs[11:14], refs[14], refs[15], refs[16]
     rows, size = qkv[0].shape
     width = gain_ref.shape[1]
     half = rows // 2
@@ -385,7 +376,7 @@
             for i in range(3)
         )
         columns = pl.ds(pl.multiple_of(at * size, size), size)
-        grad = gain_ref[:, columns] * acc - lats[n][...].astype(F32) * factor
+        grad = gain_ref[:, columns] * acc - lats[kind][...].astype(F32) * factor
         out_ref[n, :rows, :] = grad.astype(BF16)
         mixed = jnp.dot(wide[3], w_out_ref[:, columns], preferred_element_type=F32)
         out_ref[n, rows:, :] = mixed.astype(BF16)
@@ -393,10 +384,9 @@
 
 def outputs_for(which, pieces, keep, got, qkv, rinv, gain, weights, w_out):
     rows, size = pieces[0].shape
-    lats = [pieces[kind] for kind in which]
     return call(
         functools.partial(output_kernel, which),
-        (keep, got, *qkv, rinv, *lats, gain, *weights, w_out),
+        (keep, got, *qkv, rinv, *pieces, gain, *weights, w_out),
         [shape(4, 2 * rows, size)],
         [pltpu.VMEM((4, rows, size), BF16)],
         name="outputs",
@@ -431,10 +421,10 @@
     sibling = other_core(block)
     if beside is not None:
         piece_a, beside = lax.optimization_barrier((piece_a, beside))
+    piece_f = along_x(piece_a)
     piece_b = along_x(sibling)
-    piece_f = along_x(piece_a)
-    pieces = [block, sibling, piece_a, piece_b]
-    pieces += [other_core(piece_a), other_core(piece_b), piece_f, other_core(piece_f)]
+    theirs = other_core(jnp.stack([piece_a, piece_b, piece_f]))
+    pieces = [block, sibling, piece_a, piece_b, piece_f, theirs]
     return pieces if beside is None else (pieces, beside)
 
 
@@ -451,7 +441,7 @@
     row_valid = lax.dynamic_slice_in_dim(is_valid, lax.axis_index(SEQ), 1, 0)
     valid = row_valid.reshape(rows, 1).astype(F32)
 
-    cots = tp_pieces(cotangent)
+    cot_a, cot_sibling = along_x(cotangent), other_core(cotangent)
     sums, lead = call(
         pool_kernel,
         (starts, encoded),
@@ -467,10 +457,14 @@
         name="patch",
         megabytes=4,
     )[0]
+    patches, cot_a, cot_sibling = lax.optimization_barrier((patches, cot_a, cot_sibling))
+    cot_f, cot_b = along_x(cot_a), along_x(cot_sibling)
     shifted = [lax.ppermute(patches, "x", [(i, (i + k) % 4) for i in range(4)]) for k in (1, 2, 3)]
     own_blocks = jnp.stack([patches, *shifted])
+    own_blocks, cot_b, cot_f = lax.optimization_barrier((own_blocks, cot_b, cot_f))
     other_blocks = other_core(own_blocks)
-    other_blocks, cots = lax.optimization_barrier((other_blocks, cots))
+    cot_theirs = other_core(jnp.stack([cot_a, cot_b, cot_f]))
+    cots = [cotangent, cot_sibling, cot_a, cot_b, cot_f, cot_theirs]
     latent = call(
         latent_kernel,
         (own_blocks, other_blocks, w_up),
@@ -478,10 +472,11 @@
         [pltpu.VMEM((8, patch_cap, byte_width), BF16)],
         name="latent",
         megabytes=8,
+        micros=DELAY,
     )[0]
 
     d_attn = d_attn_of(cots, valid, w_out)
-    pieces, d_attn = tp_pieces(latent, d_attn)
+    pieces, (d_attn, bias) = tp_pieces(latent, (d_attn, bias))
     keep, send, *qkv, rinv = project(pieces, d_attn, gain, weights)
     half = rows // 2
     packed = shape(shards // 8, half + half // 2, 2 * HEAD)

time: 172 us -> 167 us (0.971)
  Pallas kernels: 33.8 us -> 29.1 us
  starting transfers between devices: 13.7 us -> 11.6 us
    pallas_call x14, Pallas kernels: 33.8 us -> 29.1 us  [call(): pl.pallas_call(kernel, in_specs=[VMEM] * (len(ins) - stay) + [pl.BlockSpe...]
    ppermute x15 -> x11, starting transfers between devices: 4.01 us -> 1.83 us  [other_core(): return lax.ppermute(block, 'c', [(0, 1), (1, 0)])]
    ppermute x15 -> x11, waiting for transfers between devices: 13.1 us -> 14.1 us  [other_core(): return lax.ppermute(block, 'c', [(0, 1), (1, 0)])]
  transfers between devices with their start and end apart: 28 -> 24, of which waited for: 18 -> 19; matrix products, arithmetic and copies ran while one was open for 1% -> 2% of each run, Pallas kernels for 5% -> 6%
where the time goes in v2:
time: 167 us; the launch traced here: 166 us
  waiting for transfers between devices  62.6 us (37%)
  blocking collectives  57.7 us (35%)
  Pallas kernels  29.1 us (17%)
  starting transfers between devices  11.6 us (7%)
  local copies, waits for them, and re-layouts  3.1 us (2%)
    ppermute x9, waiting for transfers between devices, along_x(): return lax.ppermute(block, XC, route)  40.9 us
    all_to_all x1, blocking collectives, per_device(): mine = lax.all_to_all(sent, SEQ, 0, 0, tiled=True)  31.2 us
    pallas_call x14, Pallas kernels, call(): pl.pallas_call(kernel, in_specs=[VMEM] * (len(ins) - stay) + [pl.BlockSpe...  29.1 us
    all_to_all x1, blocking collectives, per_device(): back = lax.all_to_all(back, SEQ, 0, 0, tiled=True)  26.5 us
    ppermute x11, waiting for transfers between devices, other_core(): return lax.ppermute(block, 'c', [(0, 1), (1, 0)])  14.1 us
    ppermute x3, waiting for transfers between devices, per_device(): lax.ppermute(patches, 'x', [(i, (i + k) % 4) for i in range(4)])  4.98 us
    ppermute x3, starting transfers between devices, per_device(): lax.ppermute(patches, 'x', [(i, (i + k) % 4) for i in range(4)])  4.44 us
    ppermute x9, starting transfers between devices, along_x(): return lax.ppermute(block, XC, route)  4.06 us
  transfers between devices with their start and end apart: 24, of which 19 were waited for; matrix products, arithmetic and copies ran while one was open for 2% of the time, Pallas kernels for 6%

profile of v2, /device:TPU:0, one launch (start us, length us, event | category | flops | bytes accessed | tf_op | source)
XLA Modules:
  0.0 166.3 jit_solution(15220778064026853920)
XLA Ops:
  0.7 1.6 collective-permute-start.1
  2.4 0.8 copy.15.starts_ref
  3.2 1.1 copy-done.7
  4.3 0.4 pool.1
  4.7 1.3 collective-permute-start
  6.0 2.7 %collective-permute-done.next_ref = f32[1,1280]{1,0:T(1,128)S(1)} collective-permute-done((f32[1,1280]{1,0:T(1,128)S(1)}, f32[1,1280]{1,0:T(1,128)S(1)}, u32[]{:S(2)}, u32[]{:S(2)}) %collective-permute-start) | collective-permute-done | bytes 5152 | tf_op jit(solution)/shard_map/ppermute | solution.py:452
  8.7 0.2 patch.1
  8.9 1.7 %collective-permute-start.5 = (bf16[32,1280]{1,0:T(8,128)(2,1)S(1)}, bf16[32,1280]{1,0:T(8,128)(2,1)S(1)}, u32[]{:S(2)}, u32[]{:S(2)}) collective-permute-start(bf16[32,1280]{1,0:T(8,128)(2,1)S(1)} %patch.1), channel_id=1, source_target_pairs={{0,6},{2,0},{4,2},{6,4},{1,7},{3,1},{5,3},{7,5},{8,14},{10,8},{12,... | collective-permute-start | bytes 245768 | tf_op jit(solution)/shard_map/ppermute | solution.py:462
  10.6 2.7 %collective-permute-start.4 = (bf16[32,1280]{1,0:T(8,128)(2,1)S(1)}, bf16[32,1280]{1,0:T(8,128)(2,1)S(1)}, u32[]{:S(2)}, u32[]{:S(2)}) collective-permute-start(bf16[32,1280]{1,0:T(8,128)(2,1)S(1)} %patch.1), channel_id=1, source_target_pairs={{0,4},{2,6},{4,0},{6,2},{1,5},{3,7},{5,1},{7,3},{8,12},{10,14},{12... | collective-permute-start | bytes 245768 | tf_op jit(solution)/shard_map/ppermute | solution.py:462
  13.4 0.8 collective-permute-start.6
  14.1 1.4 collective-permute-start.7
  15.5 1.1 collective-permute-done.4
  16.6 3.9 %collective-permute-done.3 = bf16[32,1280]{1,0:T(8,128)(2,1)S(1)} collective-permute-done((bf16[32,1280]{1,0:T(8,128)(2,1)S(1)}, bf16[32,1280]{1,0:T(8,128)(2,1)S(1)}, u32[]{:S(2)}, u32[]{:S(2)}) %collective-permute-start.3) | collective-permute-done | bytes 81952 | tf_op jit(solution)/shard_map/ppermute | solution.py:462
  20.5 2.8 %collective-permute-done.6.refs_3_ = bf16[256,512]{1,0:T(8,128)(2,1)S(1)} collective-permute-done((bf16[256,512]{1,0:T(8,128)(2,1)S(1)}, bf16[256,512]{1,0:T(8,128)(2,1)S(1)}, u32[]{:S(2)}, u32[]{:S(2)}) %collective-permute-start.6) | collective-permute-done | bytes 262176 | tf_op jit(solution)/shard_map/ppermute | solution.py:63
  23.3 2.8 %collective-permute-done.7.refs_4_ = bf16[256,512]{1,0:T(8,128)(2,1)S(1)} collective-permute-done((bf16[256,512]{1,0:T(8,128)(2,1)S(1)}, bf16[256,512]{1,0:T(8,128)(2,1)S(1)}, u32[]{:S(2)}, u32[]{:S(2)}) %collective-permute-start.7) | collective-permute-done | bytes 262176 | tf_op jit(solution)/shard_map/ppermute | solution.py:63
  26.1 1.0 pad_maximum_fusion
  27.1 0.5 collective-permute-start.11
  27.6 0.1 collective-permute-done.8.other_ref
  27.7 0.5 latent.1.refs_0_.refs_4_.lat_ref
  28.3 0.2 collective-permute-start.9
  29.2 0.7 collective-permute-done.9.refs_1_.refs_5_
  29.9 5.2 %d_attn.1.refs_6_ = bf16[256,512]{1,0:T(8,128)(2,1)S(1)} custom-call(f32[256,1]{1,0:T(8,128)S(1)} %copy.18.valid_ref, bf16[256,512]{1,0:T(8,128)(2,1)} %cot_ref.1, bf16[256,512]{1,0:T(8,128)(2,1)} %copy-done.13, bf16[256,512]{1,0:T(8,128)(2,1)} %copy-done.9, bf16[256,512]{1,0:T(8,128)(2,1)} %copy-done.10, bf16[256,512]{1,0:T(8,128)(2,1)} %copy-done.11, ...), custom_call_target="tpu_custom_call" | custom-call | flops 8000000000 | bytes 24000000 | tf_op jit(solution)/shard_map/d_attn/pallas_call | solution.py:36
  35.2 1.6 collective-permute-done.10.refs_2_.refs_6_
  36.8 0.6 broadcast_in_dim.15.bias_ref
  37.4 2.1 %collective-permute-done.12.refs_3_.refs_7_ = bf16[256,512]{1,0:T(8,128)(2,1)S(1)} collective-permute-done((bf16[256,512]{1,0:T(8,128)(2,1)S(1)}, bf16[256,512]{1,0:T(8,128)(2,1)S(1)}, u32[]{:S(2)}, u32[]{:S(2)}) %collective-permute-start.12) | collective-permute-done | bytes 262176 | tf_op jit(solution)/shard_map/ppermute | solution.py:63
  39.6 5.4 %collective-permute-done.13.refs_4_.refs_8_ = bf16[256,512]{1,0:T(8,128)(2,1)S(1)} collective-permute-done((bf16[256,512]{1,0:T(8,128)(2,1)S(1)}, bf16[256,512]{1,0:T(8,128)(2,1)S(1)}, u32[]{:S(2)}, u32[]{:S(2)}) %collective-permute-start.13) | collective-permute-done | bytes 262176 | tf_op jit(solution)/shard_map/ppermute | solution.py:63
  45.2 2.3 %collective-permute-done.14.refs_5_.refs_9_ = bf16[3,256,512]{2,1,0:T(8,128)(2,1)S(1)} collective-permute-done((bf16[3,256,512]{2,1,0:T(8,128)(2,1)S(1)}, bf16[3,256,512]{2,1,0:T(8,128)(2,1)S(1)}, u32[]{:S(2)}, u32[]{:S(2)}) %collective-permute-start.14) | collective-permute-done | bytes 786464 | tf_op jit(solution)/shard_map/ppermute | solution.py:55
  47.5 3.6 %project.1 = (bf16[4,256,256]{2,1,0:T(8,128)(2,1)S(1)}, bf16[4,256,256]{2,1,0:T(8,128)(2,1)S(1)}, bf16[256,512]{1,0:T(8,128)(2,1)S(1)}, bf16[256,512]{1,0:T(8,12...) custom-call(bf16[256,512]{1,0:T(8,128)(2,1)S(1)} %latent.1.refs_0_.refs_4_.lat_ref, ...), custom_call_target="tpu_custom_call" | custom-call | flops 5000000000 | bytes 15000000 | tf_op jit(solution)/shard_map/project/pallas_call | solution.py:36
  51.1 0.2 collective-permute-start.15
  51.3 1.8 %collective-permute-done.15.got_ref = bf16[4,256,256]{2,1,0:T(8,128)(2,1)S(1)} collective-permute-done((bf16[4,256,256]{2,1,0:T(8,128)(2,1)S(1)}, bf16[4,256,256]{2,1,0:T(8,128)(2,1)S(1)}, u32[]{:S(2)}, u32[]{:S(2)}) %collective-permute-start.15) | collective-permute-done | bytes 524320 | tf_op jit(solution)/shard_map/ppermute | solution.py:55
  53.2 31.2 %all_to_all.10.mine_ref = bf16[16,192,256]{2,1,0:T(8,128)(2,1)S(1)} all-to-all(bf16[16,192,256]{2,1,0:T(8,128)(2,1)S(1)} %pack.1), channel_id=1, replica_groups=mesh['y'=4,'z'=4,'x'=4,'c'=2] {'y','z'}, dimensions={0} | all-to-all | bytes 3145728 | tf_op jit(solution)/shard_map/all_to_all | solution.py:484
  84.4 3.4 %collective-permute-done.16.theirs_ref = bf16[16,192,256]{2,1,0:T(8,128)(2,1)S(1)} collective-permute-done((bf16[16,192,256]{2,1,0:T(8,128)(2,1)S(1)}, bf16[16,192,256]{2,1,0:T(8,128)(2,1)S(1)}, u32[]{:S(2)}, u32[]{:S(2)}) %collective-permute-start.16) | collective-permute-done | bytes 1572896 | tf_op jit(solution)/shard_map/ppermute | solution.py:55
  87.8 11.6 %attention.1 = (bf16[16,128,256]{2,1,0:T(8,128)(2,1)S(1)}, bf16[16,128,256]{2,1,0:T(8,128)(2,1)S(1)}, bf16[16,64,256]{2,1,0:T(8,128)(2,1)S(1)}) custom-call(f32[2,2048,128]{2,1,0:T(8,128)S(1)} %broadcast_in_dim.15.bias_ref, bf16[16,192,256]{2,1,0:T(8,128)(2,1)S(1)} %all_to_all.10.mine_ref, bf16[16,192,256]{2,1,0:T(8,128)(2,1)S(1)} %collective-permute-done.16.theirs_ref), custom_call_target="tpu_custom_call" | custom-call | flops 12000000000 | bytes 36000000 | tf_op jit(solution)/shard_map/attention/pallas_call | solution.py:36
  99.4 0.2 collective-permute-start.17
  99.6 2.5 %collective-permute-done.17.got_ref = bf16[16,128,256]{2,1,0:T(8,128)(2,1)S(1)} collective-permute-done((bf16[16,128,256]{2,1,0:T(8,128)(2,1)S(1)}, bf16[16,128,256]{2,1,0:T(8,128)(2,1)S(1)}, u32[]{:S(2)}, u32[]{:S(2)}) %collective-permute-start.17) | collective-permute-done | bytes 1048608 | tf_op jit(solution)/shard_map/ppermute | solution.py:55
  102.1 0.3 return.1
  102.4 26.5 %all_to_all.11.in_ref = bf16[16,192,256]{2,1,0:T(8,128)(2,1)S(1)} all-to-all(bf16[16,192,256]{2,1,0:T(8,128)(2,1)S(1)} %return.1), channel_id=1, replica_groups=mesh['y'=4,'z'=4,'x'=4,'c'=2] {'y','z'}, dimensions={0} | all-to-all | bytes 3145728 | tf_op jit(solution)/shard_map/all_to_all | solution.py:487
  129.1 0.3 collective-permute-start.18
  129.4 1.9 %collective-permute-done.18.got_ref = bf16[4,256,256]{2,1,0:T(8,128)(2,1)S(1)} collective-permute-done((bf16[4,256,256]{2,1,0:T(8,128)(2,1)S(1)}, bf16[4,256,256]{2,1,0:T(8,128)(2,1)S(1)}, u32[]{:S(2)}, u32[]{:S(2)}) %collective-permute-start.18) | collective-permute-done | bytes 524320 | tf_op jit(solution)/shard_map/ppermute | solution.py:55
  131.3 2.7 %outputs.3 = bf16[4,512,512]{2,1,0:T(8,128)(2,1)S(1)} custom-call(bf16[4,256,256]{2,1,0:T(8,128)(2,1)S(1)} %get-tuple-element.47.keep_ref, bf16[4,256,256]{2,1,0:T(8,128)(2,1)S(1)} %collective-permute-done.18.got_ref, bf16[256,512]{1,0:T(8,128)(2,1)S(1)} %get-tuple-element.49.refs_0_, bf16[256,512]{1,0:T(8,128)(2,1)S(1)} %get-tuple-element.50.refs_1_, ...), custom_call_target="tpu_custom_call" | custom-call | flops 3000000000 | bytes 9000000 | tf_op jit(solution)/shard_map/outputs/pallas_call | solution.py:36
  134.0 0.2 collective-permute-start.19
  134.2 2.7 %outputs.2.own_ref = bf16[4,512,512]{2,1,0:T(8,128)(2,1)S(1)} custom-call(bf16[4,256,256]{2,1,0:T(8,128)(2,1)S(1)} %get-tuple-element.47.keep_ref, bf16[4,256,256]{2,1,0:T(8,128)(2,1)S(1)} %collective-permute-done.18.got_ref, bf16[256,512]{1,0:T(8,128)(2,1)S(1)} %get-tuple-element.49.refs_0_, bf16[256,512]{1,0:T(8,128)(2,1)S(1)} %get-tuple-element.50.refs_1_, ...), custom_call_target="tpu_custom_call" | custom-call | flops 3000000000 | bytes 9000000 | tf_op jit(solution)/shard_map/outputs/pallas_call | solution.py:36
  136.9 1.3 collective-permute-done.19.other_ref
  138.2 0.4 add.9
  138.8 10.4 %collective-permute-done.20.far_ref = bf16[512,512]{1,0:T(8,128)(2,1)S(1)} collective-permute-done((bf16[512,512]{1,0:T(8,128)(2,1)S(1)}, bf16[512,512]{1,0:T(8,128)(2,1)S(1)}, u32[]{:S(2)}, u32[]{:S(2)}) %collective-permute-start.20) | collective-permute-done | bytes 524320 | tf_op jit(solution)/shard_map/ppermute | solution.py:63
  149.3 10.2 %collective-permute-done.22 = bf16[512,512]{1,0:T(8,128)(2,1)S(1)} collective-permute-done((bf16[512,512]{1,0:T(8,128)(2,1)S(1)}, bf16[512,512]{1,0:T(8,128)(2,1)S(1)}, u32[]{:S(2)}, u32[]{:S(2)}) %collective-permute-start.22) | collective-permute-done | bytes 524320 | tf_op jit(solution)/shard_map/ppermute | solution.py:63
  159.6 5.6 %collective-permute-done.21.ahead_ref = bf16[512,512]{1,0:T(8,128)(2,1)S(1)} collective-permute-done((bf16[512,512]{1,0:T(8,128)(2,1)S(1)}, bf16[512,512]{1,0:T(8,128)(2,1)S(1)}, u32[]{:S(2)}, u32[]{:S(2)}) %collective-permute-start.21) | collective-permute-done | bytes 524320 | tf_op jit(solution)/shard_map/ppermute | solution.py:63
  165.2 1.1 final.1
  (56 shorter events, 1.6 us)
Async XLA Ops:
  0.6 8.3 %collective-permute-start.2 = (bf16[256,512]{1,0:T(8,128)(2,1)}, bf16[256,512]{1,0:T(8,128)(2,1)S(1)}, u32[]{:S(2)}, u32[]{:S(2)}) collective-permute-start(bf16[256,512]{1,0:T(8,128)(2,1)} %cot_ref.1), channel_id=1, source_target_pairs={{0,1},{1,0},{2,3},{3,2},{4,5},{5,4},{6,7},{7,6},{8,9},{9,8},{10,11... | collective-permute-start | bytes 786440 | tf_op jit(solution)/shard_map/ppermute | solution.py:55
  0.7 8.2 %collective-permute-start.1 = (bf16[256,512]{1,0:T(8,128)(2,1)}, bf16[256,512]{1,0:T(8,128)(2,1)S(1)}, u32[]{:S(2)}, u32[]{:S(2)}) collective-permute-start(bf16[256,512]{1,0:T(8,128)(2,1)} %cot_ref.1), channel_id=1, source_target_pairs={{0,2},{1,7},{2,4},{3,1},{4,6},{5,3},{6,0},{7,5},{8,10},{9,15},{10,... | collective-permute-start | bytes 786440 | tf_op jit(solution)/shard_map/ppermute | solution.py:63
  3.2 1.1 copy-start.7
  4.7 4.0 %collective-permute-start = (f32[1,1280]{1,0:T(1,128)S(1)}, f32[1,1280]{1,0:T(1,128)S(1)}, u32[]{:S(2)}, u32[]{:S(2)}) collective-permute-start(f32[1,1280]{1,0:T(1,128)S(1)} %get-tuple-element.31), channel_id=1, source_target_pairs={{1,0},{2,1},{3,2},{4,3},{5,4},{6,5},{7,6},{8,7},{9,8},{10,9},{11,1... | collective-permute-start | bytes 15368 | tf_op jit(solution)/shard_map/ppermute | solution.py:452
  8.7 19.0 %copy-start.6 = (bf16[1280,512]{1,0:T(8,128)(2,1)S(1)}, bf16[1280,512]{1,0:T(8,128)(2,1)}, u32[]{:S(2)}) copy-start(bf16[1280,512]{1,0:T(8,128)(2,1)} %w_ref.1) | copy-start | bytes 3932164
  8.9 17.2 %copy-start.13 = (bf16[256,512]{1,0:T(8,128)(2,1)}, bf16[256,512]{1,0:T(8,128)(2,1)S(1)}, u32[]{:S(2)}) copy-start(bf16[256,512]{1,0:T(8,128)(2,1)S(1)} %collective-permute-done.2.refs_1_) | copy-start | bytes 786436
  8.9 19.3 %copy-start.9 = (bf16[256,512]{1,0:T(8,128)(2,1)}, bf16[256,512]{1,0:T(8,128)(2,1)S(1)}, u32[]{:S(2)}) copy-start(bf16[256,512]{1,0:T(8,128)(2,1)S(1)} %collective-permute-done.1.refs_2_) | copy-start | bytes 786436
  8.9 6.6 %collective-permute-start.5 = (bf16[32,1280]{1,0:T(8,128)(2,1)S(1)}, bf16[32,1280]{1,0:T(8,128)(2,1)S(1)}, u32[]{:S(2)}, u32[]{:S(2)}) collective-permute-start(bf16[32,1280]{1,0:T(8,128)(2,1)S(1)} %patch.1), channel_id=1, source_target_pairs={{0,6},{2,0},{4,2},{6,4},{1,7},{3,1},{5,3},{7,5},{8,14},{10,8},{12,... | collective-permute-start | bytes 245768 | tf_op jit(solution)/shard_map/ppermute | solution.py:462
  10.6 5.9 %collective-permute-start.4 = (bf16[32,1280]{1,0:T(8,128)(2,1)S(1)}, bf16[32,1280]{1,0:T(8,128)(2,1)S(1)}, u32[]{:S(2)}, u32[]{:S(2)}) collective-permute-start(bf16[32,1280]{1,0:T(8,128)(2,1)S(1)} %patch.1), channel_id=1, source_target_pairs={{0,4},{2,6},{4,0},{6,2},{1,5},{3,7},{5,1},{7,3},{8,12},{10,14},{12... | collective-permute-start | bytes 245768 | tf_op jit(solution)/shard_map/ppermute | solution.py:462
  13.4 7.1 %collective-permute-start.3 = (bf16[32,1280]{1,0:T(8,128)(2,1)S(1)}, bf16[32,1280]{1,0:T(8,128)(2,1)S(1)}, u32[]{:S(2)}, u32[]{:S(2)}) collective-permute-start(bf16[32,1280]{1,0:T(8,128)(2,1)S(1)} %patch.1), channel_id=1, source_target_pairs={{0,2},{2,4},{4,6},{6,0},{1,3},{3,5},{5,7},{7,1},{8,10},{10,12},{12... | collective-permute-start | bytes 245768 | tf_op jit(solution)/shard_map/ppermute | solution.py:462
  13.4 9.9 %collective-permute-start.6 = (bf16[256,512]{1,0:T(8,128)(2,1)S(1)}, bf16[256,512]{1,0:T(8,128)(2,1)S(1)}, u32[]{:S(2)}, u32[]{:S(2)}) collective-permute-start(bf16[256,512]{1,0:T(8,128)(2,1)S(1)} %collective-permute-done.2.refs_1_), channel_id=1, source_target_pairs={{0,2},{1,7},{2,4},{3,1},{4,6},{5,3},{6,0},{7,5},{8,10},{9,15},{10,... | collective-permute-start | bytes 786440 | tf_op jit(solution)/shard_map/ppermute | solution.py:63
  14.1 12.0 %collective-permute-start.7 = (bf16[256,512]{1,0:T(8,128)(2,1)S(1)}, bf16[256,512]{1,0:T(8,128)(2,1)S(1)}, u32[]{:S(2)}, u32[]{:S(2)}) collective-permute-start(bf16[256,512]{1,0:T(8,128)(2,1)S(1)} %collective-permute-done.1.refs_2_), channel_id=1, source_target_pairs={{0,2},{1,7},{2,4},{3,1},{4,6},{5,3},{6,0},{7,5},{8,10},{9,15},{10,... | collective-permute-start | bytes 786440 | tf_op jit(solution)/shard_map/ppermute | solution.py:63
  23.3 5.0 %copy-start.10 = (bf16[256,512]{1,0:T(8,128)(2,1)}, bf16[256,512]{1,0:T(8,128)(2,1)S(1)}, u32[]{:S(2)}) copy-start(bf16[256,512]{1,0:T(8,128)(2,1)S(1)} %collective-permute-done.6.refs_3_) | copy-start | bytes 786436
  26.1 2.2 %copy-start.11 = (bf16[256,512]{1,0:T(8,128)(2,1)}, bf16[256,512]{1,0:T(8,128)(2,1)S(1)}, u32[]{:S(2)}) copy-start(bf16[256,512]{1,0:T(8,128)(2,1)S(1)} %collective-permute-done.7.refs_4_) | copy-start | bytes 786436
  26.1 1.6 collective-permute-start.8
  27.1 1.4 copy-start.12
  27.1 2.8 %collective-permute-start.11 = (bf16[3,256,512]{2,1,0:T(8,128)(2,1)}, bf16[3,256,512]{2,1,0:T(8,128)(2,1)}, u32[]{:S(2)}, u32[]{:S(2)}) collective-permute-start(bf16[3,256,512]{2,1,0:T(8,128)(2,1)} %pad_maximum_fusion), channel_id=1, source_target_pairs={{0,1},{1,0},{2,3},{3,2},{4,5},{5,4},{6,7},{7,6},{8,9},{9,8},{10,11... | collective-permute-start | bytes 2359304 | tf_op jit(solution)/shard_map/ppermute | solution.py:55
  28.3 1.6 collective-permute-start.9
  29.1 7.7 %collective-permute-start.10 = (bf16[256,512]{1,0:T(8,128)(2,1)S(1)}, bf16[256,512]{1,0:T(8,128)(2,1)S(1)}, u32[]{:S(2)}, u32[]{:S(2)}) collective-permute-start(bf16[256,512]{1,0:T(8,128)(2,1)S(1)} %latent.1.refs_0_.refs_4_.lat_ref), channel_id=1, source_target_pairs={{0,2},{1,7},{2,4},{3,1},{4,6},{5,3},{6,0},{7,5},{8,10},{9,15},{10,... | collective-permute-start | bytes 786440 | tf_op jit(solution)/shard_map/ppermute | solution.py:63
  29.9 9.7 %collective-permute-start.12 = (bf16[256,512]{1,0:T(8,128)(2,1)S(1)}, bf16[256,512]{1,0:T(8,128)(2,1)S(1)}, u32[]{:S(2)}, u32[]{:S(2)}) collective-permute-start(bf16[256,512]{1,0:T(8,128)(2,1)S(1)} %collective-permute-done.9.refs_1_.refs_5_), channel_id=1, source_target_pairs={{0,2},{1,7},{2,4},{3,1},{4,6},{5,3},{6,0},{7,5},{8,10},{9,15},{10,... | collective-permute-start | bytes 786440 | tf_op jit(solution)/shard_map/ppermute | solution.py:63
  29.9 17.6 %copy-start.1 = (bf16[4096,512]{1,0:T(8,128)(2,1)S(1)}, bf16[4096,512]{1,0:T(8,128)(2,1)}, u32[]{:S(2)}) copy-start(bf16[4096,512]{1,0:T(8,128)(2,1)} %refs_11_.3) | copy-start | bytes 12582916
  29.9 17.6 %copy-start.2 = (bf16[4096,512]{1,0:T(8,128)(2,1)S(1)}, bf16[4096,512]{1,0:T(8,128)(2,1)}, u32[]{:S(2)}) copy-start(bf16[4096,512]{1,0:T(8,128)(2,1)} %refs_12_.3) | copy-start | bytes 12582916
  29.9 17.5 %copy-start.3 = (bf16[4096,512]{1,0:T(8,128)(2,1)S(1)}, bf16[4096,512]{1,0:T(8,128)(2,1)}, u32[]{:S(2)}) copy-start(bf16[4096,512]{1,0:T(8,128)(2,1)} %refs_13_.3) | copy-start | bytes 12582916
  35.2 12.3 %copy-start.5 = (f32[4096]{0:T(1024)S(1)}, f32[4096]{0:T(1024)}, u32[]{:S(2)}) copy-start(f32[4096]{0:T(1024)} %param.12) | copy-start | bytes 49156
  37.4 7.7 %collective-permute-start.13 = (bf16[256,512]{1,0:T(8,128)(2,1)S(1)}, bf16[256,512]{1,0:T(8,128)(2,1)S(1)}, u32[]{:S(2)}, u32[]{:S(2)}) collective-permute-start(bf16[256,512]{1,0:T(8,128)(2,1)S(1)} %collective-permute-done.10.refs_2_.refs_6_), channel_id=1, source_target_pairs={{0,2},{1,7},{2,4},{3,1},{4,6},{5,3},{6,0},{7,5},{8,10},{9,15},{10,... | collective-permute-start | bytes 786440 | tf_op jit(solution)/shard_map/ppermute | solution.py:63
  45.1 2.4 %collective-permute-start.14 = (bf16[3,256,512]{2,1,0:T(8,128)(2,1)S(1)}, bf16[3,256,512]{2,1,0:T(8,128)(2,1)S(1)}, u32[]{:S(2)}, u32[]{:S(2)}) collective-permute-start(bf16[3,256,512]{2,1,0:T(8,128)(2,1)S(1)} %pad_maximum_fusion.1), channel_id=1, source_target_pairs={{0,1},{1,0},{2,3},{3,2},{4,5},{5,4},{6,7},{7,6},{8,9},{9,8},{10,11... | collective-permute-start | bytes 2359304 | tf_op jit(solution)/shard_map/ppermute | solution.py:55
  51.1 2.0 %collective-permute-start.15 = (bf16[4,256,256]{2,1,0:T(8,128)(2,1)S(1)}, bf16[4,256,256]{2,1,0:T(8,128)(2,1)S(1)}, u32[]{:S(2)}, u32[]{:S(2)}) collective-permute-start(bf16[4,256,256]{2,1,0:T(8,128)(2,1)S(1)} %get-tuple-element.43), channel_id=1, source_target_pairs={{0,1},{1,0},{2,3},{3,2},{4,5},{5,4},{6,7},{7,6},{8,9},{9,8},{10,11... | collective-permute-start | bytes 1572872 | tf_op jit(solution)/shard_map/ppermute | solution.py:55
  84.4 3.4 %collective-permute-start.16 = (bf16[16,192,256]{2,1,0:T(8,128)(2,1)S(1)}, bf16[16,192,256]{2,1,0:T(8,128)(2,1)S(1)}, u32[]{:S(2)}, u32[]{:S(2)}) collective-permute-start(bf16[16,192,256]{2,1,0:T(8,128)(2,1)S(1)} %all_to_all.10.mine_ref), channel_id=1, source_target_pairs={{0,1},{1,0},{2,3},{3,2},{4,5},{5,4},{6,7},{7,6},{8,9},{9,8},{10,11... | collective-permute-start | bytes 4718600 | tf_op jit(solution)/shard_map/ppermute | solution.py:55
  99.4 2.7 %collective-permute-start.17 = (bf16[16,128,256]{2,1,0:T(8,128)(2,1)S(1)}, bf16[16,128,256]{2,1,0:T(8,128)(2,1)S(1)}, u32[]{:S(2)}, u32[]{:S(2)}) collective-permute-start(bf16[16,128,256]{2,1,0:T(8,128)(2,1)S(1)} %get-tuple-element.45), channel_id=1, source_target_pairs={{0,1},{1,0},{2,3},{3,2},{4,5},{5,4},{6,7},{7,6},{8,9},{9,8},{10,11... | collective-permute-start | bytes 3145736 | tf_op jit(solution)/shard_map/ppermute | solution.py:55
  102.1 29.2 %copy-start.4 = (bf16[4096,512]{1,0:T(8,128)(2,1)S(1)}, bf16[4096,512]{1,0:T(8,128)(2,1)}, u32[]{:S(2)}) copy-start(bf16[4096,512]{1,0:T(8,128)(2,1)} %refs_13_.3) | copy-start | bytes 12582916
  102.4 28.9 %copy-start = (bf16[512,4096]{1,0:T(8,128)(2,1)S(1)}, bf16[512,4096]{1,0:T(8,128)(2,1)}, u32[]{:S(2)}) copy-start(bf16[512,4096]{1,0:T(8,128)(2,1)} %refs_14_.3) | copy-start | bytes 12582916
  129.1 2.2 %collective-permute-start.18 = (bf16[4,256,256]{2,1,0:T(8,128)(2,1)S(1)}, bf16[4,256,256]{2,1,0:T(8,128)(2,1)S(1)}, u32[]{:S(2)}, u32[]{:S(2)}) collective-permute-start(bf16[4,256,256]{2,1,0:T(8,128)(2,1)S(1)} %get-tuple-element.48), channel_id=1, source_target_pairs={{0,1},{1,0},{2,3},{3,2},{4,5},{5,4},{6,7},{7,6},{8,9},{9,8},{10,11... | collective-permute-start | bytes 1572872 | tf_op jit(solution)/shard_map/ppermute | solution.py:55
  134.0 4.2 %collective-permute-start.19 = (bf16[4,512,512]{2,1,0:T(8,128)(2,1)S(1)}, bf16[4,512,512]{2,1,0:T(8,128)(2,1)S(1)}, u32[]{:S(2)}, u32[]{:S(2)}) collective-permute-start(bf16[4,512,512]{2,1,0:T(8,128)(2,1)S(1)} %outputs.3), channel_id=1, source_target_pairs={{0,1},{1,0},{2,3},{3,2},{4,5},{5,4},{6,7},{7,6},{8,9},{9,8},{10,11... | collective-permute-start | bytes 6291464 | tf_op jit(solution)/shard_map/ppermute | solution.py:55
  138.7 26.5 %copy-start.8 = (bf16[256,512]{1,0:T(8,128)(2,1)S(1)}, bf16[256,512]{1,0:T(8,128)(2,1)}, u32[]{:S(2)}) copy-start(bf16[256,512]{1,0:T(8,128)(2,1)} %cot_ref.1) | copy-start | bytes 786436
  138.7 10.5 %collective-permute-start.20 = (bf16[512,512]{1,0:T(8,128)(2,1)S(1)}, bf16[512,512]{1,0:T(8,128)(2,1)S(1)}, u32[]{:S(2)}, u32[]{:S(2)}) collective-permute-start(bf16[512,512]{1,0:T(8,128)(2,1)S(1)} %get-tuple-element.54), channel_id=1, source_target_pairs={{0,2},{1,7},{2,4},{3,1},{4,6},{5,3},{6,0},{7,5},{8,10},{9,15},{10,... | collective-permute-start | bytes 1572872 | tf_op jit(solution)/shard_map/ppermute | solution.py:63
  149.2 10.4 %collective-permute-start.22 = (bf16[512,512]{1,0:T(8,128)(2,1)S(1)}, bf16[512,512]{1,0:T(8,128)(2,1)S(1)}, u32[]{:S(2)}, u32[]{:S(2)}) collective-permute-start(bf16[512,512]{1,0:T(8,128)(2,1)S(1)} %get-tuple-element.57), channel_id=1, source_target_pairs={{0,2},{1,7},{2,4},{3,1},{4,6},{5,3},{6,0},{7,5},{8,10},{9,15},{10,... | collective-permute-start | bytes 1572872 | tf_op jit(solution)/shard_map/ppermute | solution.py:63
  149.3 15.9 %collective-permute-start.21 = (bf16[512,512]{1,0:T(8,128)(2,1)S(1)}, bf16[512,512]{1,0:T(8,128)(2,1)S(1)}, u32[]{:S(2)}, u32[]{:S(2)}) collective-permute-start(bf16[512,512]{1,0:T(8,128)(2,1)S(1)} %pass.1), channel_id=1, source_target_pairs={{0,2},{1,7},{2,4},{3,1},{4,6},{5,3},{6,0},{7,5},{8,10},{9,15},{10,... | collective-permute-start | bytes 1572872 | tf_op jit(solution)/shard_map/ppermute | solution.py:63
  159.6 5.6 %collective-permute-start.23 = (bf16[512,512]{1,0:T(8,128)(2,1)S(1)}, bf16[512,512]{1,0:T(8,128)(2,1)S(1)}, u32[]{:S(2)}, u32[]{:S(2)}) collective-permute-start(bf16[512,512]{1,0:T(8,128)(2,1)S(1)} %collective-permute-done.22), channel_id=1, source_target_pairs={{0,1},{1,0},{2,3},{3,2},{4,5},{5,4},{6,7},{7,6},{8,9},{9,8},{10,11... | collective-permute-start | bytes 1572872 | tf_op jit(solution)/shard_map/ppermute | solution.py:55

commit v3 on v2

--- a/solution.py
+++ b/solution.py
@@ -351,7 +351,7 @@
 
 def output_kernel(which, keep_ref, got_ref, *refs):
     qkv, rinv_ref, lats, gain_ref = refs[:3], refs[3], in_order(refs[4:10]), refs[10]
-    weights, w_out_ref, out_ref, wide = refs[11:14], refs[14], refs[15], refs[16]
+    weights, w_out_ref, outs, wide = refs[11:14], refs[14], refs[15:-1], refs[-1]
     rows, size = qkv[0].shape
     width = gain_ref.shape[1]
     half = rows // 2
@@ -367,7 +367,8 @@
     both = sum(wide[n].astype(F32) * qkv[n][...].astype(F32) for n in range(3))
     factor = jnp.sum(both, axis=1, keepdims=True) * rinv_ref[...] / width
     places = tp_places()
-    for n, kind in enumerate(which):
+    order = [(out, n, kind) for out, kinds in zip(outs, which) for n, kind in enumerate(kinds)]
+    for out_ref, n, kind in order:
         at = places[kind]
         acc = sum(
             lax.dot_general(
@@ -387,16 +388,20 @@
     return call(
         functools.partial(output_kernel, which),
         (keep, got, *qkv, rinv, *pieces, gain, *weights, w_out),
-        [shape(4, 2 * rows, size)],
+        [shape(len(kinds), 2 * rows, size) for kinds in which],
         [pltpu.VMEM((4, rows, size), BF16)],
         name="outputs",
         megabytes=28,
-        micros=3.0,
-    )[0]
-
-
-def add_kernel(own_ref, other_ref, far_ref, side_ref, near_ref, kept_ref):
-    for n, ref in enumerate((far_ref, near_ref, side_ref, kept_ref)):
+        micros=2.0,
+    )
+
+
+def far_kernel(own_ref, other_ref, out_ref):
+    out_ref[...] = (own_ref[0].astype(F32) + other_ref[0].astype(F32)).astype(BF16)
+
+
+def add_kernel(own_ref, other_ref, near_ref, side_ref, kept_ref):
+    for n, ref in enumerate((near_ref, side_ref, kept_ref)):
         total = own_ref[n].astype(F32) + other_ref[n].astype(F32)
         ref[...] = total.astype(ref.dtype)
 
@@ -414,18 +419,6 @@
     grad_ref[...] = grad_out + rinv_ref[...] * total[:rows]
     result = lat_ref[...].astype(F32) + total[rows:]
     out_ref[...] = jnp.where(valid, result, 0.0).astype(BF16)
-
-
-def tp_pieces(block, beside=None):
-    piece_a = along_x(block)
-    sibling = other_core(block)
-    if beside is not None:
-        piece_a, beside = lax.optimization_barrier((piece_a, beside))
-    piece_f = along_x(piece_a)
-    piece_b = along_x(sibling)
-    theirs = other_core(jnp.stack([piece_a, piece_b, piece_f]))
-    pieces = [block, sibling, piece_a, piece_b, piece_f, theirs]
-    return pieces if beside is None else (pieces, beside)
 
 
 def per_device(encoded, starts, w_up, norm_gain, w_query, w_key, w_value, w_out, cotangent):
@@ -461,10 +454,7 @@
     cot_f, cot_b = along_x(cot_a), along_x(cot_sibling)
     shifted = [lax.ppermute(patches, "x", [(i, (i + k) % 4) for i in range(4)]) for k in (1, 2, 3)]
     own_blocks = jnp.stack([patches, *shifted])
-    own_blocks, cot_b, cot_f = lax.optimization_barrier((own_blocks, cot_b, cot_f))
     other_blocks = other_core(own_blocks)
-    cot_theirs = other_core(jnp.stack([cot_a, cot_b, cot_f]))
-    cots = [cotangent, cot_sibling, cot_a, cot_b, cot_f, cot_theirs]
     latent = call(
         latent_kernel,
         (own_blocks, other_blocks, w_up),
@@ -475,27 +465,40 @@
         micros=DELAY,
     )[0]
 
+    latent, cot_b, cot_f = lax.optimization_barrier((latent, cot_b, cot_f))
+    piece_a, sibling = along_x(latent), other_core(latent)
+    cot_theirs = other_core(jnp.stack([cot_a, cot_b, cot_f]))
+    piece_a, cot_theirs = lax.optimization_barrier((piece_a, cot_theirs))
+    piece_f, piece_b = along_x(piece_a), along_x(sibling)
+    cots = [cotangent, cot_sibling, cot_a, cot_b, cot_f, cot_theirs]
     d_attn = d_attn_of(cots, valid, w_out)
-    pieces, (d_attn, bias) = tp_pieces(latent, (d_attn, bias))
+    piece_f, piece_b, d_attn, bias = lax.optimization_barrier((piece_f, piece_b, d_attn, bias))
+    theirs = other_core(jnp.stack([piece_a, piece_b, piece_f]))
+    pieces = [latent, sibling, piece_a, piece_b, piece_f, theirs]
     keep, send, *qkv, rinv = project(pieces, d_attn, gain, weights)
     half = rows // 2
     packed = shape(shards // 8, half + half // 2, 2 * HEAD)
     sent = call(pack_kernel, (keep, other_core(send)), [packed], name="pack")[0]
     mine = lax.all_to_all(sent, SEQ, 0, 0, tiled=True)
-    keep, send, strips = attention(bias, mine, other_core(mine))
+    keep, send, strips = attention(bias, mine, other_core(mine[:, :half]))
     back = call(return_kernel, (keep, other_core(send), strips), [packed], name="return")[0]
     back = lax.all_to_all(back, SEQ, 0, 0, tiled=True)
     both = shape(4, rows, 2 * HEAD)
     keep, send = call(regroup_kernel, (back,), [both, both], name="regroup")
-    rest = (pieces, keep, other_core(send), qkv, rinv, gain, weights, w_out)
-
-    from_other = other_core(outputs_for((7, 3, 2, 1), *rest))
-    for_own = outputs_for((6, 5, 4, 0), *rest)
+    got = other_core(send)
+    rest = (qkv, rinv, gain, weights, w_out)
     block = (2 * rows, columns)
-    far, side, near, kept = call(
+    far_given, far_own, given = outputs_for(((7,), (6,), (3, 2, 1)), pieces, keep, got, *rest)
+    far_other = other_core(far_given)
+    far_other, given = lax.optimization_barrier((far_other, given))
+    from_other = other_core(given)
+    far = call(far_kernel, (far_own, far_other), [shape(*block)], name="far")[0]
+    far, got = lax.optimization_barrier((far, got))
+    (for_own,) = outputs_for(((5, 4, 0),), pieces, keep, got, *rest)
+    near, side, kept = call(
         add_kernel,
         (for_own, from_other),
-        [shape(*block), shape(*block), shape(*block, dtype=F32), shape(*block, dtype=F32)],
+        [shape(*block, dtype=F32), shape(*block), shape(*block, dtype=F32)],
         name="add",
         megabytes=16,
     )

time: 167 us -> 168 us (level)
  waiting for transfers between devices: 62.6 us -> 64.3 us
    ppermute x9, waiting for transfers between devices: 40.9 us -> 38.1 us  [along_x(): return lax.ppermute(block, XC, route)]
    ppermute x11 -> x12, waiting for transfers between devices: 14.1 us -> 16.4 us  [other_core(): return lax.ppermute(block, 'c', [(0, 1), (1, 0)])]
    ppermute x3, waiting for transfers between devices: 4.98 us -> 7.1 us  [per_device(): lax.ppermute(patches, 'x', [(i, (i + k) % 4) for i in range(4)])]
    unnamed x29 -> x31, local copies, waits for them, and re-layouts: 1.96 us -> 3.37 us
    pallas_call x14 -> x15, Pallas kernels: 29.1 us -> 29.1 us  [call(): pl.pallas_call(kernel, in_specs=[VMEM] * (len(ins) - stay) + [pl.BlockSpe...]
  transfers between devices with their start and end apart: 24 -> 25, of which waited for: 19 -> 20; matrix products, arithmetic and copies ran while one was open for 2% -> 1% of each run, Pallas kernels for 6% -> 5%
where the time goes in v3:
time: 168 us
  waiting for transfers between devices  64.3 us (38%)
  blocking collectives  58.4 us (35%)
  Pallas kernels  29.1 us (17%)
  starting transfers between devices  10.5 us (6%)
  local copies, waits for them, and re-layouts  4.58 us (3%)
    ppermute x9, waiting for transfers between devices, along_x(): return lax.ppermute(block, XC, route)  38.1 us
    all_to_all x1, blocking collectives, per_device(): mine = lax.all_to_all(sent, SEQ, 0, 0, tiled=True)  31.8 us
    pallas_call x15, Pallas kernels, call(): pl.pallas_call(kernel, in_specs=[VMEM] * (len(ins) - stay) + [pl.BlockSpe...  29.1 us
    all_to_all x1, blocking collectives, per_device(): back = lax.all_to_all(back, SEQ, 0, 0, tiled=True)  26.5 us
    ppermute x12, waiting for transfers between devices, other_core(): return lax.ppermute(block, 'c', [(0, 1), (1, 0)])  16.4 us
    ppermute x3, waiting for transfers between devices, per_device(): lax.ppermute(patches, 'x', [(i, (i + k) % 4) for i in range(4)])  7.1 us
    ppermute x3, starting transfers between devices, per_device(): lax.ppermute(patches, 'x', [(i, (i + k) % 4) for i in range(4)])  4.44 us
    unnamed x31, local copies, waits for them, and re-layouts  3.37 us
  transfers between devices with their start and end apart: 25, of which 20 were waited for; matrix products, arithmetic and copies ran while one was open for 1% of the time, Pallas kernels for 5%

profile of v3, /device:TPU:0, one launch (start us, length us, event | category | flops | bytes accessed | tf_op | source)
XLA Modules:
  0.0 168.1 jit_solution(11928834608372885798)
XLA Ops:
  0.7 1.6 collective-permute-start.1
  2.4 0.8 copy.15.starts_ref
  3.2 1.1 copy-done.7
  4.3 0.4 pool.1
  4.7 1.3 collective-permute-start
  6.0 2.7 %collective-permute-done.next_ref = f32[1,1280]{1,0:T(1,128)S(1)} collective-permute-done((f32[1,1280]{1,0:T(1,128)S(1)}, f32[1,1280]{1,0:T(1,128)S(1)}, u32[]{:S(2)}, u32[]{:S(2)}) %collective-permute-start) | collective-permute-done | bytes 5152 | tf_op jit(solution)/shard_map/ppermute | solution.py:445
  8.7 0.2 patch.1
  8.9 1.7 %collective-permute-start.5 = (bf16[32,1280]{1,0:T(8,128)(2,1)S(1)}, bf16[32,1280]{1,0:T(8,128)(2,1)S(1)}, u32[]{:S(2)}, u32[]{:S(2)}) collective-permute-start(bf16[32,1280]{1,0:T(8,128)(2,1)S(1)} %patch.1), channel_id=1, source_target_pairs={{0,6},{2,0},{4,2},{6,4},{1,7},{3,1},{5,3},{7,5},{8,14},{10,8},{12,... | collective-permute-start | bytes 245768 | tf_op jit(solution)/shard_map/ppermute | solution.py:455
  10.6 2.7 %collective-permute-start.4 = (bf16[32,1280]{1,0:T(8,128)(2,1)S(1)}, bf16[32,1280]{1,0:T(8,128)(2,1)S(1)}, u32[]{:S(2)}, u32[]{:S(2)}) collective-permute-start(bf16[32,1280]{1,0:T(8,128)(2,1)S(1)} %patch.1), channel_id=1, source_target_pairs={{0,4},{2,6},{4,0},{6,2},{1,5},{3,7},{5,1},{7,3},{8,12},{10,14},{12... | collective-permute-start | bytes 245768 | tf_op jit(solution)/shard_map/ppermute | solution.py:455
  13.4 0.3 collective-permute-done.5
  13.7 2.9 %collective-permute-done.4 = bf16[32,1280]{1,0:T(8,128)(2,1)S(1)} collective-permute-done((bf16[32,1280]{1,0:T(8,128)(2,1)S(1)}, bf16[32,1280]{1,0:T(8,128)(2,1)S(1)}, u32[]{:S(2)}, u32[]{:S(2)}) %collective-permute-start.4) | collective-permute-done | bytes 81952 | tf_op jit(solution)/shard_map/ppermute | solution.py:455
  16.6 3.9 %collective-permute-done.3 = bf16[32,1280]{1,0:T(8,128)(2,1)S(1)} collective-permute-done((bf16[32,1280]{1,0:T(8,128)(2,1)S(1)}, bf16[32,1280]{1,0:T(8,128)(2,1)S(1)}, u32[]{:S(2)}, u32[]{:S(2)}) %collective-permute-start.3) | collective-permute-done | bytes 81952 | tf_op jit(solution)/shard_map/ppermute | solution.py:455
  20.7 0.5 collective-permute-start.8
  21.2 1.1 collective-permute-done.6.other_ref
  22.2 0.5 latent.1.refs_0_.refs_4_.lat_ref
  22.8 5.5 %collective-permute-done.7.refs_3_ = bf16[256,512]{1,0:T(8,128)(2,1)S(1)} collective-permute-done((bf16[256,512]{1,0:T(8,128)(2,1)S(1)}, bf16[256,512]{1,0:T(8,128)(2,1)S(1)}, u32[]{:S(2)}, u32[]{:S(2)}) %collective-permute-start.7) | collective-permute-done | bytes 262176 | tf_op jit(solution)/shard_map/ppermute | solution.py:63
  28.3 2.8 %collective-permute-done.8.refs_4_ = bf16[256,512]{1,0:T(8,128)(2,1)S(1)} collective-permute-done((bf16[256,512]{1,0:T(8,128)(2,1)S(1)}, bf16[256,512]{1,0:T(8,128)(2,1)S(1)}, u32[]{:S(2)}, u32[]{:S(2)}) %collective-permute-start.8) | collective-permute-done | bytes 262176 | tf_op jit(solution)/shard_map/ppermute | solution.py:63
  31.3 0.5 copy-done.11
  32.4 1.5 collective-permute-done.9.refs_1_.refs_5_
  33.9 0.8 collective-permute-start.13
  34.7 4.7 %collective-permute-done.10.refs_2_.refs_6_ = bf16[256,512]{1,0:T(8,128)(2,1)S(1)} collective-permute-done((bf16[256,512]{1,0:T(8,128)(2,1)S(1)}, bf16[256,512]{1,0:T(8,128)(2,1)S(1)}, u32[]{:S(2)}, u32[]{:S(2)}) %collective-permute-start.10) | collective-permute-done | bytes 262176 | tf_op jit(solution)/shard_map/ppermute | solution.py:63
  39.4 0.9 copy-done.13
  40.3 5.2 %d_attn.1.refs_6_ = bf16[256,512]{1,0:T(8,128)(2,1)S(1)} custom-call(f32[256,1]{1,0:T(8,128)S(1)} %copy.18.valid_ref, bf16[256,512]{1,0:T(8,128)(2,1)} %cot_ref.1, bf16[256,512]{1,0:T(8,128)(2,1)} %copy-done.14, bf16[256,512]{1,0:T(8,128)(2,1)} %copy-done.9, bf16[256,512]{1,0:T(8,128)(2,1)} %copy-done.10, bf16[256,512]{1,0:T(8,128)(2,1)} %copy-done.11, ...), custom_call_target="tpu_custom_call" | custom-call | flops 8000000000 | bytes 24000000 | tf_op jit(solution)/shard_map/d_attn/pallas_call | solution.py:36
  45.6 2.3 %collective-permute-done.12.refs_4_.refs_8_ = bf16[256,512]{1,0:T(8,128)(2,1)S(1)} collective-permute-done((bf16[256,512]{1,0:T(8,128)(2,1)S(1)}, bf16[256,512]{1,0:T(8,128)(2,1)S(1)}, u32[]{:S(2)}, u32[]{:S(2)}) %collective-permute-start.12) | collective-permute-done | bytes 262176 | tf_op jit(solution)/shard_map/ppermute | solution.py:63
  47.9 0.6 broadcast_in_dim.15.bias_ref
  48.7 2.3 %collective-permute-done.14.refs_5_.refs_9_ = bf16[3,256,512]{2,1,0:T(8,128)(2,1)S(1)} collective-permute-done((bf16[3,256,512]{2,1,0:T(8,128)(2,1)S(1)}, bf16[3,256,512]{2,1,0:T(8,128)(2,1)S(1)}, u32[]{:S(2)}, u32[]{:S(2)}) %collective-permute-start.14) | collective-permute-done | bytes 786464 | tf_op jit(solution)/shard_map/ppermute | solution.py:55
  50.9 3.6 %project.1 = (bf16[4,256,256]{2,1,0:T(8,128)(2,1)S(1)}, bf16[4,256,256]{2,1,0:T(8,128)(2,1)S(1)}, bf16[256,512]{1,0:T(8,128)(2,1)S(1)}, bf16[256,512]{1,0:T(8,12...) custom-call(bf16[256,512]{1,0:T(8,128)(2,1)S(1)} %latent.1.refs_0_.refs_4_.lat_ref, ...), custom_call_target="tpu_custom_call" | custom-call | flops 5000000000 | bytes 15000000 | tf_op jit(solution)/shard_map/project/pallas_call | solution.py:36
  54.8 1.8 %collective-permute-done.15.got_ref = bf16[4,256,256]{2,1,0:T(8,128)(2,1)S(1)} collective-permute-done((bf16[4,256,256]{2,1,0:T(8,128)(2,1)S(1)}, bf16[4,256,256]{2,1,0:T(8,128)(2,1)S(1)}, u32[]{:S(2)}, u32[]{:S(2)}) %collective-permute-start.15) | collective-permute-done | bytes 524320 | tf_op jit(solution)/shard_map/ppermute | solution.py:55
  56.7 31.8 %all_to_all.10.mine_ref = bf16[16,192,256]{2,1,0:T(8,128)(2,1)S(1)} all-to-all(bf16[16,192,256]{2,1,0:T(8,128)(2,1)S(1)} %pack.1), channel_id=1, replica_groups=mesh['y'=4,'z'=4,'x'=4,'c'=2] {'y','z'}, dimensions={0} | all-to-all | bytes 3145728 | tf_op jit(solution)/shard_map/all_to_all | solution.py:482
  88.6 0.3 collective-permute-start.16
  88.9 2.6 %collective-permute-done.16.theirs_ref = bf16[16,128,256]{2,1,0:T(8,128)(2,1)S(1)} collective-permute-done((bf16[16,128,256]{2,1,0:T(8,128)(2,1)S(1)}, bf16[16,128,256]{2,1,0:T(8,128)(2,1)S(1)}, u32[]{:S(2)}, u32[]{:S(2)}) %collective-permute-start.16) | collective-permute-done | bytes 1048608 | tf_op jit(solution)/shard_map/ppermute | solution.py:55
  91.5 11.6 %attention.1 = (bf16[16,128,256]{2,1,0:T(8,128)(2,1)S(1)}, bf16[16,128,256]{2,1,0:T(8,128)(2,1)S(1)}, bf16[16,64,256]{2,1,0:T(8,128)(2,1)S(1)}) custom-call(f32[2,2048,128]{2,1,0:T(8,128)S(1)} %broadcast_in_dim.15.bias_ref, bf16[16,192,256]{2,1,0:T(8,128)(2,1)S(1)} %all_to_all.10.mine_ref, bf16[16,128,256]{2,1,0:T(8,128)(2,1)S(1)} %collective-permute-done.16.theirs_ref), custom_call_target="tpu_custom_call" | custom-call | flops 12000000000 | bytes 36000000 | tf_op jit(solution)/shard_map/attention/pallas_call | solution.py:36
  103.1 0.2 collective-permute-start.17
  103.3 2.5 %collective-permute-done.17.got_ref = bf16[16,128,256]{2,1,0:T(8,128)(2,1)S(1)} collective-permute-done((bf16[16,128,256]{2,1,0:T(8,128)(2,1)S(1)}, bf16[16,128,256]{2,1,0:T(8,128)(2,1)S(1)}, u32[]{:S(2)}, u32[]{:S(2)}) %collective-permute-start.17) | collective-permute-done | bytes 1048608 | tf_op jit(solution)/shard_map/ppermute | solution.py:55
  105.9 0.3 return.1
  106.1 26.5 %all_to_all.11.in_ref = bf16[16,192,256]{2,1,0:T(8,128)(2,1)S(1)} all-to-all(bf16[16,192,256]{2,1,0:T(8,128)(2,1)S(1)} %return.1), channel_id=1, replica_groups=mesh['y'=4,'z'=4,'x'=4,'c'=2] {'y','z'}, dimensions={0} | all-to-all | bytes 3145728 | tf_op jit(solution)/shard_map/all_to_all | solution.py:485
  132.8 0.3 collective-permute-start.18
  133.1 1.9 %collective-permute-done.18.got_ref = bf16[4,256,256]{2,1,0:T(8,128)(2,1)S(1)} collective-permute-done((bf16[4,256,256]{2,1,0:T(8,128)(2,1)S(1)}, bf16[4,256,256]{2,1,0:T(8,128)(2,1)S(1)}, u32[]{:S(2)}, u32[]{:S(2)}) %collective-permute-start.18) | collective-permute-done | bytes 524320 | tf_op jit(solution)/shard_map/ppermute | solution.py:55
  135.0 3.2 %outputs.2 = (bf16[1,512,512]{2,1,0:T(8,128)(2,1)S(1)}, bf16[1,512,512]{2,1,0:T(8,128)(2,1)S(1)}, bf16[3,512,512]{2,1,0:T(8,128)(2,1)S(1)}) custom-call(bf16[4,256,256]{2,1,0:T(8,128)(2,1)S(1)} %get-tuple-element.59.keep_ref, bf16[4,256,256]{2,1,0:T(8,128)(2,1)S(1)} %collective-permute-done.18.got_ref, bf16[256,512]{1,0:T(8,128)(2,1)S(1)} %get-tuple-element.61.refs_0_, ...), custom_call_target="tpu_custom_call" | custom-call | flops 2000000000 | bytes 6000000 | tf_op jit(solution)/shard_map/outputs/pallas_call | solution.py:36
  138.3 0.2 collective-permute-start.19
  138.5 1.8 %collective-permute-done.19.other_ref = bf16[1,512,512]{2,1,0:T(8,128)(2,1)S(1)} collective-permute-done((bf16[1,512,512]{2,1,0:T(8,128)(2,1)S(1)}, bf16[1,512,512]{2,1,0:T(8,128)(2,1)S(1)}, u32[]{:S(2)}, u32[]{:S(2)}) %collective-permute-start.19) | collective-permute-done | bytes 524320 | tf_op jit(solution)/shard_map/ppermute | solution.py:55
  140.6 2.2 %outputs.3.own_ref = bf16[3,512,512]{2,1,0:T(8,128)(2,1)S(1)} custom-call(bf16[4,256,256]{2,1,0:T(8,128)(2,1)S(1)} %get-tuple-element.59.keep_ref, bf16[4,256,256]{2,1,0:T(8,128)(2,1)S(1)} %collective-permute-done.18.got_ref, bf16[256,512]{1,0:T(8,128)(2,1)S(1)} %get-tuple-element.61.refs_0_, bf16[256,512]{1,0:T(8,128)(2,1)S(1)} %get-tuple-element.62.refs_1_, ...), custom_call_target="tpu_custom_call" | custom-call | flops 2000000000 | bytes 6000000 | tf_op jit(solution)/shard_map/outputs/pallas_call | solution.py:36
  142.8 0.9 collective-permute-done.20.other_ref
  143.7 0.3 add.9
  144.0 7.0 %collective-permute-done.21.far_ref = bf16[512,512]{1,0:T(8,128)(2,1)S(1)} collective-permute-done((bf16[512,512]{1,0:T(8,128)(2,1)S(1)}, bf16[512,512]{1,0:T(8,128)(2,1)S(1)}, u32[]{:S(2)}, u32[]{:S(2)}) %collective-permute-start.21) | collective-permute-done | bytes 524320 | tf_op jit(solution)/shard_map/ppermute | solution.py:63
  151.1 10.2 %collective-permute-done.23 = bf16[512,512]{1,0:T(8,128)(2,1)S(1)} collective-permute-done((bf16[512,512]{1,0:T(8,128)(2,1)S(1)}, bf16[512,512]{1,0:T(8,128)(2,1)S(1)}, u32[]{:S(2)}, u32[]{:S(2)}) %collective-permute-start.23) | collective-permute-done | bytes 524320 | tf_op jit(solution)/shard_map/ppermute | solution.py:63
  161.4 5.6 %collective-permute-done.22.ahead_ref = bf16[512,512]{1,0:T(8,128)(2,1)S(1)} collective-permute-done((bf16[512,512]{1,0:T(8,128)(2,1)S(1)}, bf16[512,512]{1,0:T(8,128)(2,1)S(1)}, u32[]{:S(2)}, u32[]{:S(2)}) %collective-permute-start.22) | collective-permute-done | bytes 524320 | tf_op jit(solution)/shard_map/ppermute | solution.py:63
  167.0 1.1 final.1
  (62 shorter events, 2.3 us)
Async XLA Ops:
  0.6 8.3 %collective-permute-start.2 = (bf16[256,512]{1,0:T(8,128)(2,1)}, bf16[256,512]{1,0:T(8,128)(2,1)S(1)}, u32[]{:S(2)}, u32[]{:S(2)}) collective-permute-start(bf16[256,512]{1,0:T(8,128)(2,1)} %cot_ref.1), channel_id=1, source_target_pairs={{0,1},{1,0},{2,3},{3,2},{4,5},{5,4},{6,7},{7,6},{8,9},{9,8},{10,11... | collective-permute-start | bytes 786440 | tf_op jit(solution)/shard_map/ppermute | solution.py:55
  0.7 8.2 %collective-permute-start.1 = (bf16[256,512]{1,0:T(8,128)(2,1)}, bf16[256,512]{1,0:T(8,128)(2,1)S(1)}, u32[]{:S(2)}, u32[]{:S(2)}) collective-permute-start(bf16[256,512]{1,0:T(8,128)(2,1)} %cot_ref.1), channel_id=1, source_target_pairs={{0,2},{1,7},{2,4},{3,1},{4,6},{5,3},{6,0},{7,5},{8,10},{9,15},{10,... | collective-permute-start | bytes 786440 | tf_op jit(solution)/shard_map/ppermute | solution.py:63
  3.2 1.1 copy-start.7
  4.7 4.0 %collective-permute-start = (f32[1,1280]{1,0:T(1,128)S(1)}, f32[1,1280]{1,0:T(1,128)S(1)}, u32[]{:S(2)}, u32[]{:S(2)}) collective-permute-start(f32[1,1280]{1,0:T(1,128)S(1)} %get-tuple-element.40), channel_id=1, source_target_pairs={{1,0},{2,1},{3,2},{4,3},{5,4},{6,5},{7,6},{8,7},{9,8},{10,9},{11,1... | collective-permute-start | bytes 15368 | tf_op jit(solution)/shard_map/ppermute | solution.py:445
  8.7 13.6 %copy-start.6 = (bf16[1280,512]{1,0:T(8,128)(2,1)S(1)}, bf16[1280,512]{1,0:T(8,128)(2,1)}, u32[]{:S(2)}) copy-start(bf16[1280,512]{1,0:T(8,128)(2,1)} %w_ref.1) | copy-start | bytes 3932164
  8.9 13.9 %copy-start.14 = (bf16[256,512]{1,0:T(8,128)(2,1)}, bf16[256,512]{1,0:T(8,128)(2,1)S(1)}, u32[]{:S(2)}) copy-start(bf16[256,512]{1,0:T(8,128)(2,1)S(1)} %collective-permute-done.2.refs_1_) | copy-start | bytes 786436
  8.9 22.2 %copy-start.9 = (bf16[256,512]{1,0:T(8,128)(2,1)}, bf16[256,512]{1,0:T(8,128)(2,1)S(1)}, u32[]{:S(2)}) copy-start(bf16[256,512]{1,0:T(8,128)(2,1)S(1)} %collective-permute-done.1.refs_2_) | copy-start | bytes 786436
  8.9 4.8 %collective-permute-start.5 = (bf16[32,1280]{1,0:T(8,128)(2,1)S(1)}, bf16[32,1280]{1,0:T(8,128)(2,1)S(1)}, u32[]{:S(2)}, u32[]{:S(2)}) collective-permute-start(bf16[32,1280]{1,0:T(8,128)(2,1)S(1)} %patch.1), channel_id=1, source_target_pairs={{0,6},{2,0},{4,2},{6,4},{1,7},{3,1},{5,3},{7,5},{8,14},{10,8},{12,... | collective-permute-start | bytes 245768 | tf_op jit(solution)/shard_map/ppermute | solution.py:455
  10.6 5.9 %collective-permute-start.4 = (bf16[32,1280]{1,0:T(8,128)(2,1)S(1)}, bf16[32,1280]{1,0:T(8,128)(2,1)S(1)}, u32[]{:S(2)}, u32[]{:S(2)}) collective-permute-start(bf16[32,1280]{1,0:T(8,128)(2,1)S(1)} %patch.1), channel_id=1, source_target_pairs={{0,4},{2,6},{4,0},{6,2},{1,5},{3,7},{5,1},{7,3},{8,12},{10,14},{12... | collective-permute-start | bytes 245768 | tf_op jit(solution)/shard_map/ppermute | solution.py:455
  13.4 7.1 %collective-permute-start.3 = (bf16[32,1280]{1,0:T(8,128)(2,1)S(1)}, bf16[32,1280]{1,0:T(8,128)(2,1)S(1)}, u32[]{:S(2)}, u32[]{:S(2)}) collective-permute-start(bf16[32,1280]{1,0:T(8,128)(2,1)S(1)} %patch.1), channel_id=1, source_target_pairs={{0,2},{2,4},{4,6},{6,0},{1,3},{3,5},{5,7},{7,1},{8,10},{10,12},{12... | collective-permute-start | bytes 245768 | tf_op jit(solution)/shard_map/ppermute | solution.py:455
  20.5 1.7 %collective-permute-start.6 = (bf16[4,32,1280]{2,1,0:T(8,128)(2,1)S(1)}, bf16[4,32,1280]{2,1,0:T(8,128)(2,1)S(1)}, u32[]{:S(2)}, u32[]{:S(2)}) collective-permute-start(bf16[4,32,1280]{2,1,0:T(8,128)(2,1)S(1)} %pad_maximum_fusion.2.own_ref), channel_id=1, source_target_pairs={{0,1},{1,0},{2,3},{3,2},{4,5},{5,4},{6,7},{7,6},{8,9},{9,8},{10,11... | collective-permute-start | bytes 983048 | tf_op jit(solution)/shard_map/ppermute | solution.py:55
  20.6 7.7 %collective-permute-start.7 = (bf16[256,512]{1,0:T(8,128)(2,1)S(1)}, bf16[256,512]{1,0:T(8,128)(2,1)S(1)}, u32[]{:S(2)}, u32[]{:S(2)}) collective-permute-start(bf16[256,512]{1,0:T(8,128)(2,1)S(1)} %collective-permute-done.2.refs_1_), channel_id=1, source_target_pairs={{0,2},{1,7},{2,4},{3,1},{4,6},{5,3},{6,0},{7,5},{8,10},{9,15},{10,... | collective-permute-start | bytes 786440 | tf_op jit(solution)/shard_map/ppermute | solution.py:63
  20.7 10.4 %collective-permute-start.8 = (bf16[256,512]{1,0:T(8,128)(2,1)S(1)}, bf16[256,512]{1,0:T(8,128)(2,1)S(1)}, u32[]{:S(2)}, u32[]{:S(2)}) collective-permute-start(bf16[256,512]{1,0:T(8,128)(2,1)S(1)} %collective-permute-done.1.refs_2_), channel_id=1, source_target_pairs={{0,2},{1,7},{2,4},{3,1},{4,6},{5,3},{6,0},{7,5},{8,10},{9,15},{10,... | collective-permute-start | bytes 786440 | tf_op jit(solution)/shard_map/ppermute | solution.py:63
  22.8 9.0 %copy-start.12 = (s32[128,32]{0,1:T(8,128)S(1)}, s32[128,32]{0,1:T(8,128)}, u32[]{:S(2)}) copy-start(s32[128,32]{0,1:T(8,128)} %param.10) | copy-start | bytes 49156
  28.3 12.0 %copy-start.10 = (bf16[256,512]{1,0:T(8,128)(2,1)}, bf16[256,512]{1,0:T(8,128)(2,1)S(1)}, u32[]{:S(2)}) copy-start(bf16[256,512]{1,0:T(8,128)(2,1)S(1)} %collective-permute-done.7.refs_3_) | copy-start | bytes 786436
  31.1 0.7 copy-start.11
  31.2 8.2 %collective-permute-start.11 = (bf16[3,256,512]{2,1,0:T(8,128)(2,1)S(1)}, bf16[3,256,512]{2,1,0:T(8,128)(2,1)S(1)}, u32[]{:S(2)}, u32[]{:S(2)}) collective-permute-start(bf16[3,256,512]{2,1,0:T(8,128)(2,1)S(1)} %pad_maximum_fusion), channel_id=1, source_target_pairs={{0,1},{1,0},{2,3},{3,2},{4,5},{5,4},{6,7},{7,6},{8,9},{9,8},{10,11... | collective-permute-start | bytes 2359304 | tf_op jit(solution)/shard_map/ppermute | solution.py:55
  31.8 7.6 %collective-permute-start.10 = (bf16[256,512]{1,0:T(8,128)(2,1)S(1)}, bf16[256,512]{1,0:T(8,128)(2,1)S(1)}, u32[]{:S(2)}, u32[]{:S(2)}) collective-permute-start(bf16[256,512]{1,0:T(8,128)(2,1)S(1)} %latent.1.refs_0_.refs_4_.lat_ref), channel_id=1, source_target_pairs={{0,2},{1,7},{2,4},{3,1},{4,6},{5,3},{6,0},{7,5},{8,10},{9,15},{10,... | collective-permute-start | bytes 786440 | tf_op jit(solution)/shard_map/ppermute | solution.py:63
  31.8 2.1 %collective-permute-start.9 = (bf16[256,512]{1,0:T(8,128)(2,1)S(1)}, bf16[256,512]{1,0:T(8,128)(2,1)S(1)}, u32[]{:S(2)}, u32[]{:S(2)}) collective-permute-start(bf16[256,512]{1,0:T(8,128)(2,1)S(1)} %latent.1.refs_0_.refs_4_.lat_ref), channel_id=1, source_target_pairs={{0,1},{1,0},{2,3},{3,2},{4,5},{5,4},{6,7},{7,6},{8,9},{9,8},{10,11... | collective-permute-start | bytes 786440 | tf_op jit(solution)/shard_map/ppermute | solution.py:55
  33.9 11.6 %collective-permute-start.13 = (bf16[256,512]{1,0:T(8,128)(2,1)S(1)}, bf16[256,512]{1,0:T(8,128)(2,1)S(1)}, u32[]{:S(2)}, u32[]{:S(2)}) collective-permute-start(bf16[256,512]{1,0:T(8,128)(2,1)S(1)} %collective-permute-done.9.refs_1_.refs_5_), channel_id=1, source_target_pairs={{0,2},{1,7},{2,4},{3,1},{4,6},{5,3},{6,0},{7,5},{8,10},{9,15},{10,... | collective-permute-start | bytes 786440 | tf_op jit(solution)/shard_map/ppermute | solution.py:63
  39.4 0.9 copy-start.13
  40.3 7.6 %collective-permute-start.12 = (bf16[256,512]{1,0:T(8,128)(2,1)S(1)}, bf16[256,512]{1,0:T(8,128)(2,1)S(1)}, u32[]{:S(2)}, u32[]{:S(2)}) collective-permute-start(bf16[256,512]{1,0:T(8,128)(2,1)S(1)} %collective-permute-done.10.refs_2_.refs_6_), channel_id=1, source_target_pairs={{0,2},{1,7},{2,4},{3,1},{4,6},{5,3},{6,0},{7,5},{8,10},{9,15},{10,... | collective-permute-start | bytes 786440 | tf_op jit(solution)/shard_map/ppermute | solution.py:63
  40.3 10.6 %copy-start.1 = (bf16[4096,512]{1,0:T(8,128)(2,1)S(1)}, bf16[4096,512]{1,0:T(8,128)(2,1)}, u32[]{:S(2)}) copy-start(bf16[4096,512]{1,0:T(8,128)(2,1)} %refs_11_.3) | copy-start | bytes 12582916
  40.3 10.6 %copy-start.2 = (bf16[4096,512]{1,0:T(8,128)(2,1)S(1)}, bf16[4096,512]{1,0:T(8,128)(2,1)}, u32[]{:S(2)}) copy-start(bf16[4096,512]{1,0:T(8,128)(2,1)} %refs_12_.3) | copy-start | bytes 12582916
  40.3 10.6 %copy-start.3 = (bf16[4096,512]{1,0:T(8,128)(2,1)S(1)}, bf16[4096,512]{1,0:T(8,128)(2,1)}, u32[]{:S(2)}) copy-start(bf16[4096,512]{1,0:T(8,128)(2,1)} %refs_13_.3) | copy-start | bytes 12582916
  47.9 3.1 %copy-start.5 = (f32[4096]{0:T(1024)S(1)}, f32[4096]{0:T(1024)}, u32[]{:S(2)}) copy-start(f32[4096]{0:T(1024)} %param.12) | copy-start | bytes 49156
  48.6 2.4 %collective-permute-start.14 = (bf16[3,256,512]{2,1,0:T(8,128)(2,1)S(1)}, bf16[3,256,512]{2,1,0:T(8,128)(2,1)S(1)}, u32[]{:S(2)}, u32[]{:S(2)}) collective-permute-start(bf16[3,256,512]{2,1,0:T(8,128)(2,1)S(1)} %pad_maximum_fusion.1), channel_id=1, source_target_pairs={{0,1},{1,0},{2,3},{3,2},{4,5},{5,4},{6,7},{7,6},{8,9},{9,8},{10,11... | collective-permute-start | bytes 2359304 | tf_op jit(solution)/shard_map/ppermute | solution.py:55
  54.6 2.0 %collective-permute-start.15 = (bf16[4,256,256]{2,1,0:T(8,128)(2,1)S(1)}, bf16[4,256,256]{2,1,0:T(8,128)(2,1)S(1)}, u32[]{:S(2)}, u32[]{:S(2)}) collective-permute-start(bf16[4,256,256]{2,1,0:T(8,128)(2,1)S(1)} %get-tuple-element.55), channel_id=1, source_target_pairs={{0,1},{1,0},{2,3},{3,2},{4,5},{5,4},{6,7},{7,6},{8,9},{9,8},{10,11... | collective-permute-start | bytes 1572872 | tf_op jit(solution)/shard_map/ppermute | solution.py:55
  88.6 2.9 %collective-permute-start.16 = (bf16[16,128,256]{2,1,0:T(8,128)(2,1)S(1)}, bf16[16,128,256]{2,1,0:T(8,128)(2,1)S(1)}, u32[]{:S(2)}, u32[]{:S(2)}) collective-permute-start(bf16[16,128,256]{2,1,0:T(8,128)(2,1)S(1)} %slice.4), channel_id=1, source_target_pairs={{0,1},{1,0},{2,3},{3,2},{4,5},{5,4},{6,7},{7,6},{8,9},{9,8},{10,11... | collective-permute-start | bytes 3145736 | tf_op jit(solution)/shard_map/ppermute | solution.py:55
  103.1 2.7 %collective-permute-start.17 = (bf16[16,128,256]{2,1,0:T(8,128)(2,1)S(1)}, bf16[16,128,256]{2,1,0:T(8,128)(2,1)S(1)}, u32[]{:S(2)}, u32[]{:S(2)}) collective-permute-start(bf16[16,128,256]{2,1,0:T(8,128)(2,1)S(1)} %get-tuple-element.57), channel_id=1, source_target_pairs={{0,1},{1,0},{2,3},{3,2},{4,5},{5,4},{6,7},{7,6},{8,9},{9,8},{10,11... | collective-permute-start | bytes 3145736 | tf_op jit(solution)/shard_map/ppermute | solution.py:55
  105.9 29.1 %copy-start.4 = (bf16[4096,512]{1,0:T(8,128)(2,1)S(1)}, bf16[4096,512]{1,0:T(8,128)(2,1)}, u32[]{:S(2)}) copy-start(bf16[4096,512]{1,0:T(8,128)(2,1)} %refs_13_.3) | copy-start | bytes 12582916
  106.1 28.9 %copy-start = (bf16[512,4096]{1,0:T(8,128)(2,1)S(1)}, bf16[512,4096]{1,0:T(8,128)(2,1)}, u32[]{:S(2)}) copy-start(bf16[512,4096]{1,0:T(8,128)(2,1)} %refs_14_.3) | copy-start | bytes 12582916
  132.8 2.2 %collective-permute-start.18 = (bf16[4,256,256]{2,1,0:T(8,128)(2,1)S(1)}, bf16[4,256,256]{2,1,0:T(8,128)(2,1)S(1)}, u32[]{:S(2)}, u32[]{:S(2)}) collective-permute-start(bf16[4,256,256]{2,1,0:T(8,128)(2,1)S(1)} %get-tuple-element.60), channel_id=1, source_target_pairs={{0,1},{1,0},{2,3},{3,2},{4,5},{5,4},{6,7},{7,6},{8,9},{9,8},{10,11... | collective-permute-start | bytes 1572872 | tf_op jit(solution)/shard_map/ppermute | solution.py:55
  138.3 2.0 %collective-permute-start.19 = (bf16[1,512,512]{2,1,0:T(8,128)(2,1)S(1)}, bf16[1,512,512]{2,1,0:T(8,128)(2,1)S(1)}, u32[]{:S(2)}, u32[]{:S(2)}) collective-permute-start(bf16[1,512,512]{2,1,0:T(8,128)(2,1)S(1)} %get-tuple-element.65), channel_id=1, source_target_pairs={{0,1},{1,0},{2,3},{3,2},{4,5},{5,4},{6,7},{7,6},{8,9},{9,8},{10,11... | collective-permute-start | bytes 1572872 | tf_op jit(solution)/shard_map/ppermute | solution.py:55
  140.2 3.4 %collective-permute-start.20 = (bf16[3,512,512]{2,1,0:T(8,128)(2,1)S(1)}, bf16[3,512,512]{2,1,0:T(8,128)(2,1)S(1)}, u32[]{:S(2)}, u32[]{:S(2)}) collective-permute-start(bf16[3,512,512]{2,1,0:T(8,128)(2,1)S(1)} %get-tuple-element.69), channel_id=1, source_target_pairs={{0,1},{1,0},{2,3},{3,2},{4,5},{5,4},{6,7},{7,6},{8,9},{9,8},{10,11... | collective-permute-start | bytes 4718600 | tf_op jit(solution)/shard_map/ppermute | solution.py:55
  140.5 10.5 %collective-permute-start.21 = (bf16[512,512]{1,0:T(8,128)(2,1)S(1)}, bf16[512,512]{1,0:T(8,128)(2,1)S(1)}, u32[]{:S(2)}, u32[]{:S(2)}) collective-permute-start(bf16[512,512]{1,0:T(8,128)(2,1)S(1)} %far.1), channel_id=1, source_target_pairs={{0,2},{1,7},{2,4},{3,1},{4,6},{5,3},{6,0},{7,5},{8,10},{9,15},{10,... | collective-permute-start | bytes 1572872 | tf_op jit(solution)/shard_map/ppermute | solution.py:63
  151.0 10.4 %collective-permute-start.23 = (bf16[512,512]{1,0:T(8,128)(2,1)S(1)}, bf16[512,512]{1,0:T(8,128)(2,1)S(1)}, u32[]{:S(2)}, u32[]{:S(2)}) collective-permute-start(bf16[512,512]{1,0:T(8,128)(2,1)S(1)} %get-tuple-element.75), channel_id=1, source_target_pairs={{0,2},{1,7},{2,4},{3,1},{4,6},{5,3},{6,0},{7,5},{8,10},{9,15},{10,... | collective-permute-start | bytes 1572872 | tf_op jit(solution)/shard_map/ppermute | solution.py:63
  151.0 16.0 %copy-start.8 = (bf16[256,512]{1,0:T(8,128)(2,1)S(1)}, bf16[256,512]{1,0:T(8,128)(2,1)}, u32[]{:S(2)}) copy-start(bf16[256,512]{1,0:T(8,128)(2,1)} %cot_ref.1) | copy-start | bytes 786436
  151.1 15.9 %collective-permute-start.22 = (bf16[512,512]{1,0:T(8,128)(2,1)S(1)}, bf16[512,512]{1,0:T(8,128)(2,1)S(1)}, u32[]{:S(2)}, u32[]{:S(2)}) collective-permute-start(bf16[512,512]{1,0:T(8,128)(2,1)S(1)} %pass.1), channel_id=1, source_target_pairs={{0,2},{1,7},{2,4},{3,1},{4,6},{5,3},{6,0},{7,5},{8,10},{9,15},{10,... | collective-permute-start | bytes 1572872 | tf_op jit(solution)/shard_map/ppermute | solution.py:63
  161.4 5.6 %collective-permute-start.24 = (bf16[512,512]{1,0:T(8,128)(2,1)S(1)}, bf16[512,512]{1,0:T(8,128)(2,1)S(1)}, u32[]{:S(2)}, u32[]{:S(2)}) collective-permute-start(bf16[512,512]{1,0:T(8,128)(2,1)S(1)} %collective-permute-done.23), channel_id=1, source_target_pairs={{0,1},{1,0},{2,3},{3,2},{4,5},{5,4},{6,7},{7,6},{8,9},{9,8},{10,11... | collective-permute-start | bytes 1572872 | tf_op jit(solution)/shard_map/ppermute | solution.py:55

commit v4 on v3

--- a/solution.py
+++ b/solution.py
@@ -109,7 +109,7 @@
     out_ref[...] = (total / as_column(jnp.maximum(sizes, 1.0), eye)).astype(BF16)
 
 
-def latent_kernel(own_ref, other_ref, w_ref, out_ref, group):
+def latent_kernel(own_ref, other_ref, w_ref, sibling_w_ref, out_ref, group):
     x, c = place("x"), place("c")
     count, rows, width = own_ref.shape
     for k in range(count):
@@ -117,7 +117,8 @@
         group[at + c] = own_ref[k]
         group[at + 1 - c] = other_ref[k]
     whole = group[...].reshape(2 * count * rows, width)
-    out_ref[...] = jnp.dot(whole, w_ref[...], preferred_element_type=F32).astype(BF16)
+    for n, ref in enumerate((w_ref, sibling_w_ref)):
+        out_ref[n] = jnp.dot(whole, ref[...], preferred_element_type=F32).astype(BF16)
 
 
 def tp_places():
@@ -130,9 +131,9 @@
 
 
 def in_order(refs):
-    own, sibling, piece_a, piece_b, piece_f, theirs = refs
+    pair, both, far, theirs = refs
     a, b, f = (theirs.at[n] for n in range(3))
-    return [own, sibling, piece_a, piece_b, a, b, piece_f, f]
+    return [pair.at[0], pair.at[1], both.at[0], both.at[1], a, b, far.at[0], f]
 
 
 def piece_rows(ref, at, size):
@@ -140,8 +141,8 @@
 
 
 def project_kernel(*refs):
-    pieces, (do_ref, gain_ref), weights = in_order(refs[:6]), refs[6:8], refs[8:11]
-    outs, (accs, heads) = refs[11:17], refs[17:19]
+    pieces, (do_ref, gain_ref), weights = in_order(refs[:4]), refs[4:6], refs[6:9]
+    outs, (accs, heads) = refs[9:15], refs[15:17]
     keep_ref, send_ref, qkv_refs, rinv_ref = outs[0], outs[1], outs[2:5], outs[5]
     rows, size = pieces[0].shape
     width = gain_ref.shape[1]
@@ -179,7 +180,7 @@
 
 
 def project(pieces, d_attn, gain, weights):
-    rows, size = pieces[0].shape
+    rows, size = pieces[0].shape[1:]
     both = shape(4, rows, 2 * HEAD)
     return call(
         project_kernel,
@@ -192,48 +193,33 @@
     )
 
 
-def d_attn_kernel(valid_ref, *refs):
-    grads, w_ref, out_ref, pieces, held, grad_sems, sems = in_order(refs[:6]), *refs[6:]
+def d_attn_kernel(valid_ref, w_ref, *refs):
+    grads, (out_ref, pieces, sems) = in_order(refs[:4]), refs[4:]
     rows, size = grads[0].shape
     copies = [
-        pltpu.make_async_copy(grad, pieces.at[n], grad_sems.at[n]) for n, grad in enumerate(grads)
+        pltpu.make_async_copy(grad, pieces.at[n], sems.at[n]) for n, grad in enumerate(grads)
     ]
-    for h in range(4):
-        span = slice(h * HEAD, (h + 1) * HEAD)
-        copies.append(pltpu.make_async_copy(w_ref.at[span, :], held.at[span, :], sems.at[h]))
     for copy in copies:
         copy.start()
-    for copy in copies[:8]:
-        copy.wait()
-    valid = valid_ref[...] > 0.0
-    places = tp_places()
-    for h in range(0, 4, 2):
-        copies[8 + h].wait()
-        copies[9 + h].wait()
-        span = slice(h * HEAD, (h + 2) * HEAD)
-        acc = 0.0
-        for n, at in enumerate(places):
-            w = held[span, pl.ds(pl.multiple_of(at * size, size), size)]
-            acc = acc + lax.dot_general(pieces[n], w, NT, preferred_element_type=F32)
-        out_ref[:, span] = jnp.where(valid, acc, 0.0).astype(BF16)
+    acc = 0.0
+    for n, at in enumerate(tp_places()):
+        copies[n].wait()
+        w = w_ref[:, pl.ds(pl.multiple_of(at * size, size), size)]
+        acc = acc + lax.dot_general(pieces[n], w, NT, preferred_element_type=F32)
+    out_ref[...] = jnp.where(valid_ref[...] > 0.0, acc, 0.0).astype(BF16)
 
 
 def d_attn_of(grads, valid, w_out):
-    rows, size = grads[0].shape
+    rows, size = grads[0].shape[1:]
     return call(
         d_attn_kernel,
-        (valid, *grads, w_out),
+        (valid, w_out, *grads),
         [shape(rows, size)],
-        [
-            pltpu.VMEM((8, rows, size), BF16),
-            pltpu.VMEM(w_out.shape, BF16),
-            pltpu.SemaphoreType.DMA((8,)),
-            pltpu.SemaphoreType.DMA((4,)),
-        ],
+        [pltpu.VMEM((8, rows, size), BF16), pltpu.SemaphoreType.DMA((8,))],
         name="d_attn",
         megabytes=12,
         micros=DELAY,
-        stay=7,
+        stay=4,
     )[0]
 
 
@@ -350,8 +336,8 @@
 
 
 def output_kernel(which, keep_ref, got_ref, *refs):
-    qkv, rinv_ref, lats, gain_ref = refs[:3], refs[3], in_order(refs[4:10]), refs[10]
-    weights, w_out_ref, outs, wide = refs[11:14], refs[14], refs[15:-1], refs[-1]
+    qkv, rinv_ref, lats, gain_ref = refs[:3], refs[3], in_order(refs[4:8]), refs[8]
+    weights, w_out_ref, outs, wide = refs[9:12], refs[12], refs[13:-1], refs[-1]
     rows, size = qkv[0].shape
     width = gain_ref.shape[1]
     half = rows // 2
@@ -384,7 +370,7 @@
 
 
 def outputs_for(which, pieces, keep, got, qkv, rinv, gain, weights, w_out):
-    rows, size = pieces[0].shape
+    rows, size = pieces[0].shape[1:]
     return call(
         functools.partial(output_kernel, which),
         (keep, got, *qkv, rinv, *pieces, gain, *weights, w_out),
@@ -417,7 +403,7 @@
     valid = valid_ref[...] > 0.0
     grad_out = jnp.where(valid, cot_ref[...].astype(F32), 0.0)
     grad_ref[...] = grad_out + rinv_ref[...] * total[:rows]
-    result = lat_ref[...].astype(F32) + total[rows:]
+    result = lat_ref[0].astype(F32) + total[rows:]
     out_ref[...] = jnp.where(valid, result, 0.0).astype(BF16)
 
 
@@ -434,7 +420,8 @@
     row_valid = lax.dynamic_slice_in_dim(is_valid, lax.axis_index(SEQ), 1, 0)
     valid = row_valid.reshape(rows, 1).astype(F32)
 
-    cot_a, cot_sibling = along_x(cotangent), other_core(cotangent)
+    cot_a, cot_sibling, sibling_up = along_x(cotangent), other_core(cotangent), other_core(w_up)
+    sibling_up = pltpu.with_memory_space_constraint(sibling_up, pltpu.HBM)
     sums, lead = call(
         pool_kernel,
         (starts, encoded),
@@ -454,27 +441,26 @@
     cot_f, cot_b = along_x(cot_a), along_x(cot_sibling)
     shifted = [lax.ppermute(patches, "x", [(i, (i + k) % 4) for i in range(4)]) for k in (1, 2, 3)]
     own_blocks = jnp.stack([patches, *shifted])
-    other_blocks = other_core(own_blocks)
-    latent = call(
+    own_blocks, cot_b, cot_f = lax.optimization_barrier((own_blocks, cot_b, cot_f))
+    pair = call(
         latent_kernel,
-        (own_blocks, other_blocks, w_up),
-        [shape(rows, columns)],
+        (own_blocks, other_core(own_blocks), w_up, sibling_up),
+        [shape(2, rows, columns)],
         [pltpu.VMEM((8, patch_cap, byte_width), BF16)],
         name="latent",
         megabytes=8,
         micros=DELAY,
     )[0]
-
-    latent, cot_b, cot_f = lax.optimization_barrier((latent, cot_b, cot_f))
-    piece_a, sibling = along_x(latent), other_core(latent)
-    cot_theirs = other_core(jnp.stack([cot_a, cot_b, cot_f]))
-    piece_a, cot_theirs = lax.optimization_barrier((piece_a, cot_theirs))
-    piece_f, piece_b = along_x(piece_a), along_x(sibling)
-    cots = [cotangent, cot_sibling, cot_a, cot_b, cot_f, cot_theirs]
-    d_attn = d_attn_of(cots, valid, w_out)
-    piece_f, piece_b, d_attn, bias = lax.optimization_barrier((piece_f, piece_b, d_attn, bias))
-    theirs = other_core(jnp.stack([piece_a, piece_b, piece_f]))
-    pieces = [latent, sibling, piece_a, piece_b, piece_f, theirs]
+    lat_both = along_x(pair)
+    cot_both = jnp.stack([cot_a, cot_b])
+    cot_theirs = other_core(jnp.concatenate([cot_both, cot_f[None]]))
+    cot_pair = jnp.stack([cotangent, cot_sibling])
+    lat_both, cot_theirs = lax.optimization_barrier((lat_both, cot_theirs))
+    lat_far = along_x(lat_both[:1])
+    d_attn = d_attn_of([cot_pair, cot_both, cot_f[None], cot_theirs], valid, w_out)
+    lat_far, d_attn, bias = lax.optimization_barrier((lat_far, d_attn, bias))
+    theirs = other_core(jnp.concatenate([lat_both, lat_far]))
+    pieces = [pair, lat_both, lat_far, theirs]
     keep, send, *qkv, rinv = project(pieces, d_attn, gain, weights)
     half = rows // 2
     packed = shape(shards // 8, half + half // 2, 2 * HEAD)
@@ -503,13 +489,12 @@
         megabytes=16,
     )
     far_in = along_x(far)
-    far_in, side = lax.optimization_barrier((far_in, side))
     side_in = other_core(along_x(side))
     ahead = call(pass_kernel, (near, far_in), [shape(*block)], name="pass")[0]
     return tuple(
         call(
             final_kernel,
-            (valid, rinv, cotangent, latent, kept, along_x(ahead), side_in),
+            (valid, rinv, cotangent, pair, kept, along_x(ahead), side_in),
             [shape(rows, columns), shape(rows, columns, dtype=F32)],
             name="final",
         )

time: 168 us -> 163 us (0.970)
  waiting for transfers between devices: 64.3 us -> 54.9 us
  other arithmetic: 0.24 us -> 2.82 us
  starting transfers between devices: 10.5 us -> 12.6 us
    ppermute x9 -> x8, waiting for transfers between devices: 38.1 us -> 33.9 us  [along_x(): return lax.ppermute(block, XC, route)]
    ppermute x12, waiting for transfers between devices: 16.4 us -> 13.9 us  [other_core(): return lax.ppermute(block, 'c', [(0, 1), (1, 0)])]
    ppermute x3, waiting for transfers between devices: 7.1 us -> 4.73 us  [per_device(): lax.ppermute(patches, 'x', [(i, (i + k) % 4) for i in range(4)])]
    ppermute x9 -> x8, starting transfers between devices: 3.09 us -> 4.31 us  [along_x(): return lax.ppermute(block, XC, route)]
    unnamed x31 -> x33, local copies, waits for them, and re-layouts: 3.37 us -> 4.14 us
  transfers between devices with their start and end apart: 25 -> 24, of which waited for: 20 -> 18; matrix products, arithmetic and copies ran while one was open for 1% -> 3% of each run, Pallas kernels for 5% -> 5%
where the time goes in v4:
time: 163 us
  blocking collectives  57.8 us (35%)
  waiting for transfers between devices  54.9 us (34%)
  Pallas kernels  28.5 us (17%)
  starting transfers between devices  12.6 us (8%)
  local copies, waits for them, and re-layouts  5.39 us (3%)
  other arithmetic  2.82 us (2%)
    ppermute x8, waiting for transfers between devices, along_x(): return lax.ppermute(block, XC, route)  33.9 us
    all_to_all x1, blocking collectives, per_device(): mine = lax.all_to_all(sent, SEQ, 0, 0, tiled=True)  31.2 us
    pallas_call x15, Pallas kernels, call(): pl.pallas_call(kernel, in_specs=[VMEM] * (len(ins) - stay) + [pl.BlockSpe...  28.5 us
    all_to_all x1, blocking collectives, per_device(): back = lax.all_to_all(back, SEQ, 0, 0, tiled=True)  26.6 us
    ppermute x12, waiting for transfers between devices, other_core(): return lax.ppermute(block, 'c', [(0, 1), (1, 0)])  13.9 us
    ppermute x3, waiting for transfers between devices, per_device(): lax.ppermute(patches, 'x', [(i, (i + k) % 4) for i in range(4)])  4.73 us
    ppermute x3, starting transfers between devices, per_device(): lax.ppermute(patches, 'x', [(i, (i + k) % 4) for i in range(4)])  4.44 us
    ppermute x8, starting transfers between devices, along_x(): return lax.ppermute(block, XC, route)  4.31 us
  transfers between devices with their start and end apart: 24, of which 18 were waited for; matrix products, arithmetic and copies ran while one was open for 3% of the time, Pallas kernels for 5%

profile of v4, /device:TPU:0, one launch (start us, length us, event | category | flops | bytes accessed | tf_op | source)
XLA Modules:
  0.0 163.0 jit_solution(17793673992221951350)
XLA Ops:
  0.7 0.5 collective-permute-start.2
  1.2 1.6 collective-permute-start.1
  2.8 0.8 copy.15.starts_ref
  3.6 1.1 copy-done.9
  4.7 0.4 pool.1
  5.1 1.3 collective-permute-start
  6.4 2.3 %collective-permute-done.next_ref = f32[1,1280]{1,0:T(1,128)S(1)} collective-permute-done((f32[1,1280]{1,0:T(1,128)S(1)}, f32[1,1280]{1,0:T(1,128)S(1)}, u32[]{:S(2)}, u32[]{:S(2)}) %collective-permute-start) | collective-permute-done | bytes 5152 | tf_op jit(solution)/shard_map/ppermute | solution.py:432
  9.0 1.7 %collective-permute-start.5 = (bf16[32,1280]{1,0:T(8,128)(2,1)S(1)}, bf16[32,1280]{1,0:T(8,128)(2,1)S(1)}, u32[]{:S(2)}, u32[]{:S(2)}) collective-permute-start(bf16[32,1280]{1,0:T(8,128)(2,1)S(1)} %patch.1), channel_id=1, source_target_pairs={{0,6},{2,0},{4,2},{6,4},{1,7},{3,1},{5,3},{7,5},{8,14},{10,8},{12,... | collective-permute-start | bytes 245768 | tf_op jit(solution)/shard_map/ppermute | solution.py:442
  10.7 2.7 %collective-permute-start.4 = (bf16[32,1280]{1,0:T(8,128)(2,1)S(1)}, bf16[32,1280]{1,0:T(8,128)(2,1)S(1)}, u32[]{:S(2)}, u32[]{:S(2)}) collective-permute-start(bf16[32,1280]{1,0:T(8,128)(2,1)S(1)} %patch.1), channel_id=1, source_target_pairs={{0,4},{2,6},{4,0},{6,2},{1,5},{3,7},{5,1},{7,3},{8,12},{10,14},{12... | collective-permute-start | bytes 245768 | tf_op jit(solution)/shard_map/ppermute | solution.py:442
  13.5 0.8 collective-permute-start.6
  14.2 1.6 collective-permute-start.7
  15.8 0.8 collective-permute-done.4
  16.7 3.9 %collective-permute-done.3 = bf16[32,1280]{1,0:T(8,128)(2,1)S(1)} collective-permute-done((bf16[32,1280]{1,0:T(8,128)(2,1)S(1)}, bf16[32,1280]{1,0:T(8,128)(2,1)S(1)}, u32[]{:S(2)}, u32[]{:S(2)}) %collective-permute-start.3) | collective-permute-done | bytes 81952 | tf_op jit(solution)/shard_map/ppermute | solution.py:442
  20.6 2.8 %collective-permute-done.6 = bf16[256,512]{1,0:T(8,128)(2,1)S(1)} collective-permute-done((bf16[256,512]{1,0:T(8,128)(2,1)S(1)}, bf16[256,512]{1,0:T(8,128)(2,1)S(1)}, u32[]{:S(2)}, u32[]{:S(2)}) %collective-permute-start.6) | collective-permute-done | bytes 262176 | tf_op jit(solution)/shard_map/ppermute | solution.py:63
  23.4 2.8 %collective-permute-done.7 = bf16[256,512]{1,0:T(8,128)(2,1)S(1)} collective-permute-done((bf16[256,512]{1,0:T(8,128)(2,1)S(1)}, bf16[256,512]{1,0:T(8,128)(2,1)S(1)}, u32[]{:S(2)}, u32[]{:S(2)}) %collective-permute-start.7) | collective-permute-done | bytes 262176 | tf_op jit(solution)/shard_map/ppermute | solution.py:63
  26.2 1.0 pad_maximum_fusion
  27.2 0.5 collective-permute-start.11
  27.8 2.2 %latent.1.refs_0_.refs_4_.lat_ref = bf16[2,256,512]{2,1,0:T(8,128)(2,1)S(1)} custom-call(bf16[4,32,1280]{2,1,0:T(8,128)(2,1)S(1)} %pad_maximum_fusion.4.own_ref, bf16[4,32,1280]{2,1,0:T(8,128)(2,1)S(1)} %collective-permute-done.8.other_ref, bf16[1280,512]{1,0:T(8,128)(2,1)S(1)} %copy-done.8, bf16[1280,512]{1,0:T(8,128)(2,1)} %collective-permute-done.9.sibling_w_ref), custom_call_target="tpu_custom_call" | custom-call | flops 8000000000 | bytes 24000000 | tf_op jit(solution)/shard_map/latent/pallas_call | solution.py:36
  30.8 0.8 pad_maximum_fusion.2.refs_0_
  31.6 0.9 pad_maximum_fusion.3.refs_1_
  32.5 8.1 %collective-permute-done.10.refs_1_.refs_5_ = bf16[2,256,512]{2,1,0:T(8,128)(2,1)S(1)} collective-permute-done((bf16[2,256,512]{2,1,0:T(8,128)(2,1)S(1)}, bf16[2,256,512]{2,1,0:T(8,128)(2,1)S(1)}, u32[]{:S(2)}, u32[]{:S(2)}) %collective-permute-start.10) | collective-permute-done | bytes 524320 | tf_op jit(solution)/shard_map/ppermute | solution.py:63
  40.6 2.2 %copy-done = bf16[512,4096]{1,0:T(8,128)(2,1)S(1)} copy-done((bf16[512,4096]{1,0:T(8,128)(2,1)S(1)}, bf16[512,4096]{1,0:T(8,128)(2,1)}, u32[]{:S(2)}) %copy-start) | copy-done | bytes 4194328
  42.8 3.0 %d_attn.1.refs_4_ = bf16[256,512]{1,0:T(8,128)(2,1)S(1)} custom-call(f32[256,1]{1,0:T(8,128)S(1)} %copy.18.valid_ref, bf16[512,4096]{1,0:T(8,128)(2,1)S(1)} %copy-done, bf16[2,256,512]{2,1,0:T(8,128)(2,1)} %pad_maximum_fusion.2.refs_0_, bf16[2,256,512]{2,1,0:T(8,128)(2,1)} %pad_maximum_fusion.3.refs_1_, bf16[1,256,512]{2,1,0:T(8,128)(2,1)} %bitcast.26, ...), custom_call_target="tpu_custom_call" | custom-call | flops 8000000000 | bytes 24000000 | tf_op jit(solution)/shard_map/d_attn/pallas_call | solution.py:36
  45.9 2.3 %collective-permute-done.12.refs_2_.refs_6_ = bf16[1,256,512]{2,1,0:T(8,128)(2,1)S(1)} collective-permute-done((bf16[1,256,512]{2,1,0:T(8,128)(2,1)S(1)}, bf16[1,256,512]{2,1,0:T(8,128)(2,1)S(1)}, u32[]{:S(2)}, u32[]{:S(2)}) %collective-permute-start.12) | collective-permute-done | bytes 262176 | tf_op jit(solution)/shard_map/ppermute | solution.py:63
  48.2 0.6 broadcast_in_dim.20.bias_ref
  49.0 2.3 %collective-permute-done.13.refs_3_.refs_7_ = bf16[3,256,512]{2,1,0:T(8,128)(2,1)S(1)} collective-permute-done((bf16[3,256,512]{2,1,0:T(8,128)(2,1)S(1)}, bf16[3,256,512]{2,1,0:T(8,128)(2,1)S(1)}, u32[]{:S(2)}, u32[]{:S(2)}) %collective-permute-start.13) | collective-permute-done | bytes 786464 | tf_op jit(solution)/shard_map/ppermute | solution.py:55
  51.3 3.6 %project.1 = (bf16[4,256,256]{2,1,0:T(8,128)(2,1)S(1)}, bf16[4,256,256]{2,1,0:T(8,128)(2,1)S(1)}, bf16[256,512]{1,0:T(8,128)(2,1)S(1)}, bf16[256,512]{1,0:T(8,12...) custom-call(bf16[2,256,512]{2,1,0:T(8,128)(2,1)S(1)} %latent.1.refs_0_.refs_4_.lat_ref, ...), custom_call_target="tpu_custom_call" | custom-call | flops 5000000000 | bytes 15000000 | tf_op jit(solution)/shard_map/project/pallas_call | solution.py:36
  54.9 0.2 collective-permute-start.14
  55.1 1.8 %collective-permute-done.14.got_ref = bf16[4,256,256]{2,1,0:T(8,128)(2,1)S(1)} collective-permute-done((bf16[4,256,256]{2,1,0:T(8,128)(2,1)S(1)}, bf16[4,256,256]{2,1,0:T(8,128)(2,1)S(1)}, u32[]{:S(2)}, u32[]{:S(2)}) %collective-permute-start.14) | collective-permute-done | bytes 524320 | tf_op jit(solution)/shard_map/ppermute | solution.py:55
  57.0 31.2 %all_to_all.10.mine_ref = bf16[16,192,256]{2,1,0:T(8,128)(2,1)S(1)} all-to-all(bf16[16,192,256]{2,1,0:T(8,128)(2,1)S(1)} %pack.1), channel_id=1, replica_groups=mesh['y'=4,'z'=4,'x'=4,'c'=2] {'y','z'}, dimensions={0} | all-to-all | bytes 3145728 | tf_op jit(solution)/shard_map/all_to_all | solution.py:468
  88.3 0.3 collective-permute-start.15
  88.6 2.6 %collective-permute-done.15.theirs_ref = bf16[16,128,256]{2,1,0:T(8,128)(2,1)S(1)} collective-permute-done((bf16[16,128,256]{2,1,0:T(8,128)(2,1)S(1)}, bf16[16,128,256]{2,1,0:T(8,128)(2,1)S(1)}, u32[]{:S(2)}, u32[]{:S(2)}) %collective-permute-start.15) | collective-permute-done | bytes 1048608 | tf_op jit(solution)/shard_map/ppermute | solution.py:55
  91.2 11.6 %attention.1 = (bf16[16,128,256]{2,1,0:T(8,128)(2,1)S(1)}, bf16[16,128,256]{2,1,0:T(8,128)(2,1)S(1)}, bf16[16,64,256]{2,1,0:T(8,128)(2,1)S(1)}) custom-call(f32[2,2048,128]{2,1,0:T(8,128)S(1)} %broadcast_in_dim.20.bias_ref, bf16[16,192,256]{2,1,0:T(8,128)(2,1)S(1)} %all_to_all.10.mine_ref, bf16[16,128,256]{2,1,0:T(8,128)(2,1)S(1)} %collective-permute-done.15.theirs_ref), custom_call_target="tpu_custom_call" | custom-call | flops 12000000000 | bytes 36000000 | tf_op jit(solution)/shard_map/attention/pallas_call | solution.py:36
  102.8 0.2 collective-permute-start.16
  103.0 2.5 %collective-permute-done.16.got_ref = bf16[16,128,256]{2,1,0:T(8,128)(2,1)S(1)} collective-permute-done((bf16[16,128,256]{2,1,0:T(8,128)(2,1)S(1)}, bf16[16,128,256]{2,1,0:T(8,128)(2,1)S(1)}, u32[]{:S(2)}, u32[]{:S(2)}) %collective-permute-start.16) | collective-permute-done | bytes 1048608 | tf_op jit(solution)/shard_map/ppermute | solution.py:55
  105.5 0.3 return.1
  105.8 26.6 %all_to_all.11.in_ref = bf16[16,192,256]{2,1,0:T(8,128)(2,1)S(1)} all-to-all(bf16[16,192,256]{2,1,0:T(8,128)(2,1)S(1)} %return.1), channel_id=1, replica_groups=mesh['y'=4,'z'=4,'x'=4,'c'=2] {'y','z'}, dimensions={0} | all-to-all | bytes 3145728 | tf_op jit(solution)/shard_map/all_to_all | solution.py:471
  132.5 0.3 collective-permute-start.17
  132.8 1.9 %collective-permute-done.17.got_ref = bf16[4,256,256]{2,1,0:T(8,128)(2,1)S(1)} collective-permute-done((bf16[4,256,256]{2,1,0:T(8,128)(2,1)S(1)}, bf16[4,256,256]{2,1,0:T(8,128)(2,1)S(1)}, u32[]{:S(2)}, u32[]{:S(2)}) %collective-permute-start.17) | collective-permute-done | bytes 524320 | tf_op jit(solution)/shard_map/ppermute | solution.py:55
  134.7 3.2 %outputs.2 = (bf16[1,512,512]{2,1,0:T(8,128)(2,1)S(1)}, bf16[1,512,512]{2,1,0:T(8,128)(2,1)S(1)}, bf16[3,512,512]{2,1,0:T(8,128)(2,1)S(1)}) custom-call(bf16[4,256,256]{2,1,0:T(8,128)(2,1)S(1)} %get-tuple-element.55.keep_ref, bf16[4,256,256]{2,1,0:T(8,128)(2,1)S(1)} %collective-permute-done.17.got_ref, bf16[256,512]{1,0:T(8,128)(2,1)S(1)} %get-tuple-element.57.refs_0_, ...), custom_call_target="tpu_custom_call" | custom-call | flops 2000000000 | bytes 6000000 | tf_op jit(solution)/shard_map/outputs/pallas_call | solution.py:36
  138.1 1.8 %collective-permute-done.18.other_ref = bf16[1,512,512]{2,1,0:T(8,128)(2,1)S(1)} collective-permute-done((bf16[1,512,512]{2,1,0:T(8,128)(2,1)S(1)}, bf16[1,512,512]{2,1,0:T(8,128)(2,1)S(1)}, u32[]{:S(2)}, u32[]{:S(2)}) %collective-permute-start.18) | collective-permute-done | bytes 524320 | tf_op jit(solution)/shard_map/ppermute | solution.py:55
  140.3 2.2 %outputs.3.own_ref = bf16[3,512,512]{2,1,0:T(8,128)(2,1)S(1)} custom-call(bf16[4,256,256]{2,1,0:T(8,128)(2,1)S(1)} %get-tuple-element.55.keep_ref, bf16[4,256,256]{2,1,0:T(8,128)(2,1)S(1)} %collective-permute-done.17.got_ref, bf16[256,512]{1,0:T(8,128)(2,1)S(1)} %get-tuple-element.57.refs_0_, bf16[256,512]{1,0:T(8,128)(2,1)S(1)} %get-tuple-element.58.refs_1_, ...), custom_call_target="tpu_custom_call" | custom-call | flops 2000000000 | bytes 6000000 | tf_op jit(solution)/shard_map/outputs/pallas_call | solution.py:36
  142.4 0.9 collective-permute-done.19.other_ref
  143.3 0.3 add.9
  143.7 6.9 %collective-permute-done.20.far_ref = bf16[512,512]{1,0:T(8,128)(2,1)S(1)} collective-permute-done((bf16[512,512]{1,0:T(8,128)(2,1)S(1)}, bf16[512,512]{1,0:T(8,128)(2,1)S(1)}, u32[]{:S(2)}, u32[]{:S(2)}) %collective-permute-start.20) | collective-permute-done | bytes 524320 | tf_op jit(solution)/shard_map/ppermute | solution.py:63
  150.8 5.4 %collective-permute-done.22 = bf16[512,512]{1,0:T(8,128)(2,1)S(1)} collective-permute-done((bf16[512,512]{1,0:T(8,128)(2,1)S(1)}, bf16[512,512]{1,0:T(8,128)(2,1)S(1)}, u32[]{:S(2)}, u32[]{:S(2)}) %collective-permute-start.22) | collective-permute-done | bytes 524320 | tf_op jit(solution)/shard_map/ppermute | solution.py:63
  156.3 5.6 %collective-permute-done.21.ahead_ref = bf16[512,512]{1,0:T(8,128)(2,1)S(1)} collective-permute-done((bf16[512,512]{1,0:T(8,128)(2,1)S(1)}, bf16[512,512]{1,0:T(8,128)(2,1)S(1)}, u32[]{:S(2)}, u32[]{:S(2)}) %collective-permute-start.21) | collective-permute-done | bytes 524320 | tf_op jit(solution)/shard_map/ppermute | solution.py:63
  161.9 1.1 final.1
  (65 shorter events, 2.6 us)
Async XLA Ops:
  0.6 27.2 %collective-permute-start.9 = (bf16[1280,512]{1,0:T(8,128)(2,1)}, bf16[1280,512]{1,0:T(8,128)(2,1)}, u32[]{:S(2)}, u32[]{:S(2)}) collective-permute-start(bf16[1280,512]{1,0:T(8,128)(2,1)} %w_ref.2), channel_id=1, source_target_pairs={{0,1},{1,0},{2,3},{3,2},{4,5},{5,4},{6,7},{7,6},{8,9},{9,8},{10,11... | collective-permute-start | bytes 3932168 | tf_op jit(solution)/shard_map/ppermute | solution.py:55
  0.7 8.3 %collective-permute-start.2 = (bf16[256,512]{1,0:T(8,128)(2,1)}, bf16[256,512]{1,0:T(8,128)(2,1)S(1)}, u32[]{:S(2)}, u32[]{:S(2)}) collective-permute-start(bf16[256,512]{1,0:T(8,128)(2,1)} %cot_ref.1), channel_id=1, source_target_pairs={{0,1},{1,0},{2,3},{3,2},{4,5},{5,4},{6,7},{7,6},{8,9},{9,8},{10,11... | collective-permute-start | bytes 786440 | tf_op jit(solution)/shard_map/ppermute | solution.py:55
  1.2 7.8 %collective-permute-start.1 = (bf16[256,512]{1,0:T(8,128)(2,1)}, bf16[256,512]{1,0:T(8,128)(2,1)S(1)}, u32[]{:S(2)}, u32[]{:S(2)}) collective-permute-start(bf16[256,512]{1,0:T(8,128)(2,1)} %cot_ref.1), channel_id=1, source_target_pairs={{0,2},{1,7},{2,4},{3,1},{4,6},{5,3},{6,0},{7,5},{8,10},{9,15},{10,... | collective-permute-start | bytes 786440 | tf_op jit(solution)/shard_map/ppermute | solution.py:63
  3.6 1.1 copy-start.9
  5.1 3.6 %collective-permute-start = (f32[1,1280]{1,0:T(1,128)S(1)}, f32[1,1280]{1,0:T(1,128)S(1)}, u32[]{:S(2)}, u32[]{:S(2)}) collective-permute-start(f32[1,1280]{1,0:T(1,128)S(1)} %get-tuple-element.37), channel_id=1, source_target_pairs={{1,0},{2,1},{3,2},{4,3},{5,4},{6,5},{7,6},{8,7},{9,8},{10,9},{11,1... | collective-permute-start | bytes 15368 | tf_op jit(solution)/shard_map/ppermute | solution.py:432
  9.0 18.8 %copy-start.8 = (bf16[1280,512]{1,0:T(8,128)(2,1)S(1)}, bf16[1280,512]{1,0:T(8,128)(2,1)}, u32[]{:S(2)}) copy-start(bf16[1280,512]{1,0:T(8,128)(2,1)} %w_ref.2) | copy-start | bytes 3932164
  9.0 18.8 %copy-start.10 = (bf16[256,512]{1,0:T(8,128)(2,1)}, bf16[256,512]{1,0:T(8,128)(2,1)S(1)}, u32[]{:S(2)}) copy-start(bf16[256,512]{1,0:T(8,128)(2,1)S(1)} %collective-permute-done.1) | copy-start | bytes 786436
  9.0 5.2 %collective-permute-start.5 = (bf16[32,1280]{1,0:T(8,128)(2,1)S(1)}, bf16[32,1280]{1,0:T(8,128)(2,1)S(1)}, u32[]{:S(2)}, u32[]{:S(2)}) collective-permute-start(bf16[32,1280]{1,0:T(8,128)(2,1)S(1)} %patch.1), channel_id=1, source_target_pairs={{0,6},{2,0},{4,2},{6,4},{1,7},{3,1},{5,3},{7,5},{8,14},{10,8},{12,... | collective-permute-start | bytes 245768 | tf_op jit(solution)/shard_map/ppermute | solution.py:442
  10.7 5.9 %collective-permute-start.4 = (bf16[32,1280]{1,0:T(8,128)(2,1)S(1)}, bf16[32,1280]{1,0:T(8,128)(2,1)S(1)}, u32[]{:S(2)}, u32[]{:S(2)}) collective-permute-start(bf16[32,1280]{1,0:T(8,128)(2,1)S(1)} %patch.1), channel_id=1, source_target_pairs={{0,4},{2,6},{4,0},{6,2},{1,5},{3,7},{5,1},{7,3},{8,12},{10,14},{12... | collective-permute-start | bytes 245768 | tf_op jit(solution)/shard_map/ppermute | solution.py:442
  13.5 7.1 %collective-permute-start.3 = (bf16[32,1280]{1,0:T(8,128)(2,1)S(1)}, bf16[32,1280]{1,0:T(8,128)(2,1)S(1)}, u32[]{:S(2)}, u32[]{:S(2)}) collective-permute-start(bf16[32,1280]{1,0:T(8,128)(2,1)S(1)} %patch.1), channel_id=1, source_target_pairs={{0,2},{2,4},{4,6},{6,0},{1,3},{3,5},{5,7},{7,1},{8,10},{10,12},{12... | collective-permute-start | bytes 245768 | tf_op jit(solution)/shard_map/ppermute | solution.py:442
  13.5 9.9 %collective-permute-start.6 = (bf16[256,512]{1,0:T(8,128)(2,1)S(1)}, bf16[256,512]{1,0:T(8,128)(2,1)S(1)}, u32[]{:S(2)}, u32[]{:S(2)}) collective-permute-start(bf16[256,512]{1,0:T(8,128)(2,1)S(1)} %collective-permute-done.2), channel_id=1, source_target_pairs={{0,2},{1,7},{2,4},{3,1},{4,6},{5,3},{6,0},{7,5},{8,10},{9,15},{10,... | collective-permute-start | bytes 786440 | tf_op jit(solution)/shard_map/ppermute | solution.py:63
  14.2 12.0 %collective-permute-start.7 = (bf16[256,512]{1,0:T(8,128)(2,1)S(1)}, bf16[256,512]{1,0:T(8,128)(2,1)S(1)}, u32[]{:S(2)}, u32[]{:S(2)}) collective-permute-start(bf16[256,512]{1,0:T(8,128)(2,1)S(1)} %collective-permute-done.1), channel_id=1, source_target_pairs={{0,2},{1,7},{2,4},{3,1},{4,6},{5,3},{6,0},{7,5},{8,10},{9,15},{10,... | collective-permute-start | bytes 786440 | tf_op jit(solution)/shard_map/ppermute | solution.py:63
  23.4 4.4 %copy-start.12 = (bf16[256,512]{1,0:T(8,128)(2,1)}, bf16[256,512]{1,0:T(8,128)(2,1)S(1)}, u32[]{:S(2)}) copy-start(bf16[256,512]{1,0:T(8,128)(2,1)S(1)} %collective-permute-done.6) | copy-start | bytes 786436
  26.2 3.8 %copy-start.14 = (bf16[256,512]{1,0:T(8,128)(2,1)}, bf16[256,512]{1,0:T(8,128)(2,1)S(1)}, u32[]{:S(2)}) copy-start(bf16[256,512]{1,0:T(8,128)(2,1)S(1)} %collective-permute-done.7) | copy-start | bytes 786436
  26.2 1.6 collective-permute-start.8
  27.2 3.0 %copy-start.15 = (s32[128,32]{0,1:T(8,128)S(1)}, s32[128,32]{0,1:T(8,128)}, u32[]{:S(2)}) copy-start(s32[128,32]{0,1:T(8,128)} %param.10) | copy-start | bytes 49156
  27.2 3.6 %copy-start.6 = (bf16[256,512]{1,0:T(8,128)(2,1)S(1)}, bf16[256,512]{1,0:T(8,128)(2,1)}, u32[]{:S(2)}) copy-start(bf16[256,512]{1,0:T(8,128)(2,1)} %cot_ref.1) | copy-start | bytes 786436
  27.2 5.3 %collective-permute-start.11 = (bf16[3,256,512]{2,1,0:T(8,128)(2,1)}, bf16[3,256,512]{2,1,0:T(8,128)(2,1)}, u32[]{:S(2)}, u32[]{:S(2)}) collective-permute-start(bf16[3,256,512]{2,1,0:T(8,128)(2,1)} %pad_maximum_fusion), channel_id=1, source_target_pairs={{0,1},{1,0},{2,3},{3,2},{4,5},{5,4},{6,7},{7,6},{8,9},{9,8},{10,11... | collective-permute-start | bytes 2359304 | tf_op jit(solution)/shard_map/ppermute | solution.py:55
  30.0 1.6 copy-start.11
  30.1 1.6 copy-start.13
  30.1 10.5 %collective-permute-start.10 = (bf16[2,256,512]{2,1,0:T(8,128)(2,1)S(1)}, bf16[2,256,512]{2,1,0:T(8,128)(2,1)S(1)}, u32[]{:S(2)}, u32[]{:S(2)}) collective-permute-start(bf16[2,256,512]{2,1,0:T(8,128)(2,1)S(1)} %latent.1.refs_0_.refs_4_.lat_ref), channel_id=1, source_target_pairs={{0,2},{1,7},{2,4},{3,1},{4,6},{5,3},{6,0},{7,5},{8,10},{9,15},{10,... | collective-permute-start | bytes 1572872 | tf_op jit(solution)/shard_map/ppermute | solution.py:63
  40.5 7.7 %collective-permute-start.12 = (bf16[1,256,512]{2,1,0:T(8,128)(2,1)S(1)}, bf16[1,256,512]{2,1,0:T(8,128)(2,1)S(1)}, u32[]{:S(2)}, u32[]{:S(2)}) collective-permute-start(bf16[1,256,512]{2,1,0:T(8,128)(2,1)S(1)} %slice.6), channel_id=1, source_target_pairs={{0,2},{1,7},{2,4},{3,1},{4,6},{5,3},{6,0},{7,5},{8,10},{9,15},{10,... | collective-permute-start | bytes 786440 | tf_op jit(solution)/shard_map/ppermute | solution.py:63
  40.6 2.2 %copy-start = (bf16[512,4096]{1,0:T(8,128)(2,1)S(1)}, bf16[512,4096]{1,0:T(8,128)(2,1)}, u32[]{:S(2)}) copy-start(bf16[512,4096]{1,0:T(8,128)(2,1)} %refs_12_.3) | copy-start | bytes 12582916
  42.8 8.4 %copy-start.2 = (bf16[4096,512]{1,0:T(8,128)(2,1)S(1)}, bf16[4096,512]{1,0:T(8,128)(2,1)}, u32[]{:S(2)}) copy-start(bf16[4096,512]{1,0:T(8,128)(2,1)} %refs_9_.3) | copy-start | bytes 12582916
  42.8 8.4 %copy-start.3 = (bf16[4096,512]{1,0:T(8,128)(2,1)S(1)}, bf16[4096,512]{1,0:T(8,128)(2,1)}, u32[]{:S(2)}) copy-start(bf16[4096,512]{1,0:T(8,128)(2,1)} %refs_10_.3) | copy-start | bytes 12582916
  42.8 8.4 %copy-start.4 = (bf16[4096,512]{1,0:T(8,128)(2,1)S(1)}, bf16[4096,512]{1,0:T(8,128)(2,1)}, u32[]{:S(2)}) copy-start(bf16[4096,512]{1,0:T(8,128)(2,1)} %refs_11_.3) | copy-start | bytes 12582916
  48.2 3.1 %copy-start.7 = (f32[4096]{0:T(1024)S(1)}, f32[4096]{0:T(1024)}, u32[]{:S(2)}) copy-start(f32[4096]{0:T(1024)} %param.12) | copy-start | bytes 49156
  48.9 2.4 %collective-permute-start.13 = (bf16[3,256,512]{2,1,0:T(8,128)(2,1)S(1)}, bf16[3,256,512]{2,1,0:T(8,128)(2,1)S(1)}, u32[]{:S(2)}, u32[]{:S(2)}) collective-permute-start(bf16[3,256,512]{2,1,0:T(8,128)(2,1)S(1)} %pad_maximum_fusion.1), channel_id=1, source_target_pairs={{0,1},{1,0},{2,3},{3,2},{4,5},{5,4},{6,7},{7,6},{8,9},{9,8},{10,11... | collective-permute-start | bytes 2359304 | tf_op jit(solution)/shard_map/ppermute | solution.py:55
  54.9 2.0 %collective-permute-start.14 = (bf16[4,256,256]{2,1,0:T(8,128)(2,1)S(1)}, bf16[4,256,256]{2,1,0:T(8,128)(2,1)S(1)}, u32[]{:S(2)}, u32[]{:S(2)}) collective-permute-start(bf16[4,256,256]{2,1,0:T(8,128)(2,1)S(1)} %get-tuple-element.51), channel_id=1, source_target_pairs={{0,1},{1,0},{2,3},{3,2},{4,5},{5,4},{6,7},{7,6},{8,9},{9,8},{10,11... | collective-permute-start | bytes 1572872 | tf_op jit(solution)/shard_map/ppermute | solution.py:55
  88.3 2.9 %collective-permute-start.15 = (bf16[16,128,256]{2,1,0:T(8,128)(2,1)S(1)}, bf16[16,128,256]{2,1,0:T(8,128)(2,1)S(1)}, u32[]{:S(2)}, u32[]{:S(2)}) collective-permute-start(bf16[16,128,256]{2,1,0:T(8,128)(2,1)S(1)} %slice.8), channel_id=1, source_target_pairs={{0,1},{1,0},{2,3},{3,2},{4,5},{5,4},{6,7},{7,6},{8,9},{9,8},{10,11... | collective-permute-start | bytes 3145736 | tf_op jit(solution)/shard_map/ppermute | solution.py:55
  102.8 2.7 %collective-permute-start.16 = (bf16[16,128,256]{2,1,0:T(8,128)(2,1)S(1)}, bf16[16,128,256]{2,1,0:T(8,128)(2,1)S(1)}, u32[]{:S(2)}, u32[]{:S(2)}) collective-permute-start(bf16[16,128,256]{2,1,0:T(8,128)(2,1)S(1)} %get-tuple-element.53), channel_id=1, source_target_pairs={{0,1},{1,0},{2,3},{3,2},{4,5},{5,4},{6,7},{7,6},{8,9},{9,8},{10,11... | collective-permute-start | bytes 3145736 | tf_op jit(solution)/shard_map/ppermute | solution.py:55
  105.5 29.2 %copy-start.5 = (bf16[4096,512]{1,0:T(8,128)(2,1)S(1)}, bf16[4096,512]{1,0:T(8,128)(2,1)}, u32[]{:S(2)}) copy-start(bf16[4096,512]{1,0:T(8,128)(2,1)} %refs_11_.3) | copy-start | bytes 12582916
  105.8 28.9 %copy-start.1 = (bf16[512,4096]{1,0:T(8,128)(2,1)S(1)}, bf16[512,4096]{1,0:T(8,128)(2,1)}, u32[]{:S(2)}) copy-start(bf16[512,4096]{1,0:T(8,128)(2,1)} %refs_12_.3) | copy-start | bytes 12582916
  132.5 2.2 %collective-permute-start.17 = (bf16[4,256,256]{2,1,0:T(8,128)(2,1)S(1)}, bf16[4,256,256]{2,1,0:T(8,128)(2,1)S(1)}, u32[]{:S(2)}, u32[]{:S(2)}) collective-permute-start(bf16[4,256,256]{2,1,0:T(8,128)(2,1)S(1)} %get-tuple-element.56), channel_id=1, source_target_pairs={{0,1},{1,0},{2,3},{3,2},{4,5},{5,4},{6,7},{7,6},{8,9},{9,8},{10,11... | collective-permute-start | bytes 1572872 | tf_op jit(solution)/shard_map/ppermute | solution.py:55
  137.9 2.0 %collective-permute-start.18 = (bf16[1,512,512]{2,1,0:T(8,128)(2,1)S(1)}, bf16[1,512,512]{2,1,0:T(8,128)(2,1)S(1)}, u32[]{:S(2)}, u32[]{:S(2)}) collective-permute-start(bf16[1,512,512]{2,1,0:T(8,128)(2,1)S(1)} %get-tuple-element.61), channel_id=1, source_target_pairs={{0,1},{1,0},{2,3},{3,2},{4,5},{5,4},{6,7},{7,6},{8,9},{9,8},{10,11... | collective-permute-start | bytes 1572872 | tf_op jit(solution)/shard_map/ppermute | solution.py:55
  139.9 3.4 %collective-permute-start.19 = (bf16[3,512,512]{2,1,0:T(8,128)(2,1)S(1)}, bf16[3,512,512]{2,1,0:T(8,128)(2,1)S(1)}, u32[]{:S(2)}, u32[]{:S(2)}) collective-permute-start(bf16[3,512,512]{2,1,0:T(8,128)(2,1)S(1)} %get-tuple-element.65), channel_id=1, source_target_pairs={{0,1},{1,0},{2,3},{3,2},{4,5},{5,4},{6,7},{7,6},{8,9},{9,8},{10,11... | collective-permute-start | bytes 4718600 | tf_op jit(solution)/shard_map/ppermute | solution.py:55
  140.2 10.5 %collective-permute-start.20 = (bf16[512,512]{1,0:T(8,128)(2,1)S(1)}, bf16[512,512]{1,0:T(8,128)(2,1)S(1)}, u32[]{:S(2)}, u32[]{:S(2)}) collective-permute-start(bf16[512,512]{1,0:T(8,128)(2,1)S(1)} %far.1), channel_id=1, source_target_pairs={{0,2},{1,7},{2,4},{3,1},{4,6},{5,3},{6,0},{7,5},{8,10},{9,15},{10,... | collective-permute-start | bytes 1572872 | tf_op jit(solution)/shard_map/ppermute | solution.py:63
  143.7 12.6 %collective-permute-start.22 = (bf16[512,512]{1,0:T(8,128)(2,1)S(1)}, bf16[512,512]{1,0:T(8,128)(2,1)S(1)}, u32[]{:S(2)}, u32[]{:S(2)}) collective-permute-start(bf16[512,512]{1,0:T(8,128)(2,1)S(1)} %get-tuple-element.69), channel_id=1, source_target_pairs={{0,2},{1,7},{2,4},{3,1},{4,6},{5,3},{6,0},{7,5},{8,10},{9,15},{10,... | collective-permute-start | bytes 1572872 | tf_op jit(solution)/shard_map/ppermute | solution.py:63
  150.7 11.1 %collective-permute-start.21 = (bf16[512,512]{1,0:T(8,128)(2,1)S(1)}, bf16[512,512]{1,0:T(8,128)(2,1)S(1)}, u32[]{:S(2)}, u32[]{:S(2)}) collective-permute-start(bf16[512,512]{1,0:T(8,128)(2,1)S(1)} %pass.1), channel_id=1, source_target_pairs={{0,2},{1,7},{2,4},{3,1},{4,6},{5,3},{6,0},{7,5},{8,10},{9,15},{10,... | collective-permute-start | bytes 1572872 | tf_op jit(solution)/shard_map/ppermute | solution.py:63
  156.3 5.6 %collective-permute-start.23 = (bf16[512,512]{1,0:T(8,128)(2,1)S(1)}, bf16[512,512]{1,0:T(8,128)(2,1)S(1)}, u32[]{:S(2)}, u32[]{:S(2)}) collective-permute-start(bf16[512,512]{1,0:T(8,128)(2,1)S(1)} %collective-permute-done.22), channel_id=1, source_target_pairs={{0,1},{1,0},{2,3},{3,2},{4,5},{5,4},{6,7},{7,6},{8,9},{9,8},{10,11... | collective-permute-start | bytes 1572872 | tf_op jit(solution)/shard_map/ppermute | solution.py:55

commit v5 on v4

--- a/solution.py
+++ b/solution.py
@@ -63,50 +63,50 @@
     return lax.ppermute(block, XC, route)
 
 
+def lane_of(table, lane):
+    lanes = lax.broadcasted_iota(jnp.int32, table.shape, 1)
+    return jnp.sum(jnp.where(lanes == lane, table.astype(F32), 0.0), axis=1, keepdims=True)
+
+
 def bounds(starts_ref, shard, byte_rows):
-    row = starts_ref[pl.ds(shard, 1), :]
-    end = jnp.full((1, 1), byte_rows, jnp.int32)
-    return row, jnp.concatenate([row[:, 1:], end], axis=1)
-
-
-def pool_kernel(starts_ref, enc_ref, sums_ref, lead_ref):
+    first = lane_of(starts_ref[...], shard)
+    return first, jnp.concatenate([first[1:], jnp.full((1, 1), byte_rows, F32)], axis=0)
+
+
+def pool_kernel(starts_ref, enc_ref, sums_ref, lead_ref, held, sems):
     byte_rows = enc_ref.shape[0]
-    cap = starts_ref.shape[1]
-    row, following = bounds(starts_ref, place(ALL), byte_rows)
-    places = lax.broadcasted_iota(jnp.int32, (byte_rows, cap), 0)
-    inside = ((places >= row) & (places < following)).astype(F32).astype(BF16)
-    enc = enc_ref[...]
-    sums_ref[...] = lax.dot_general(inside, enc, TN, preferred_element_type=F32)
-    leading = (places < row[:, :1]).astype(F32).astype(BF16)
-    lead = lax.dot_general(leading, enc, TN, preferred_element_type=F32)
-    lead_ref[...] = lead[:1]
-
-
-def as_column(row, eye):
-    return jnp.sum(jnp.where(eye, row, 0.0), axis=1, keepdims=True)
-
-
-def as_row(column, eye):
-    return jnp.sum(jnp.where(eye, column, 0.0), axis=0, keepdims=True)
-
-
-def eye_of(n):
-    return lax.broadcasted_iota(jnp.int32, (n, n), 0) == lax.broadcasted_iota(jnp.int32, (n, n), 1)
+    cap = starts_ref.shape[0]
+    part = byte_rows // 4
+    spans = [slice(n * part, (n + 1) * part) for n in range(4)]
+    copies = [
+        pltpu.make_async_copy(enc_ref.at[span, :], held.at[span, :], sems.at[n])
+        for n, span in enumerate(spans)
+    ]
+    for copy in copies:
+        copy.start()
+    start, following = bounds(starts_ref, place(ALL), byte_rows)
+    places = lax.broadcasted_iota(jnp.int32, (cap, byte_rows), 1).astype(F32)
+    inside = ((places >= start) & (places < following)).astype(F32).astype(BF16)
+    leading = (places[:8] < start[:1]).astype(F32).astype(BF16)
+    for copy in copies:
+        copy.wait()
+    enc = held[...]
+    sums_ref[...] = jnp.dot(inside, enc, preferred_element_type=F32)
+    lead_ref[...] = jnp.dot(leading, enc, preferred_element_type=F32)[:1]
 
 
 def patch_kernel(byte_rows, starts_ref, sums_ref, next_ref, out_ref):
-    shards, cap = starts_ref.shape
+    cap, shards = starts_ref.shape
     shard = place(ALL)
-    row, following = bounds(starts_ref, shard, byte_rows)
-    count = jnp.sum((row < byte_rows).astype(F32), axis=1, keepdims=True)
-    slot = lax.broadcasted_iota(jnp.int32, (1, cap), 1).astype(F32)
+    start, following = bounds(starts_ref, shard, byte_rows)
+    count = jnp.sum((start < byte_rows).astype(F32), axis=0, keepdims=True)
+    slot = lax.broadcasted_iota(jnp.int32, (cap, 1), 0).astype(F32)
     last = (slot == count - 1.0).astype(F32)
-    after = starts_ref[pl.ds(jnp.minimum(shard + 1, shards - 1), 1), :][:, :1].astype(F32)
+    after = lane_of(starts_ref[...], jnp.minimum(shard + 1, shards - 1))[:1]
     after = jnp.where(shard + 1 < shards, after, 0.0)
-    sizes = (following - row).astype(F32) + last * after
-    eye = eye_of(cap)
-    total = sums_ref[...] + as_column(last, eye) * next_ref[...]
-    out_ref[...] = (total / as_column(jnp.maximum(sizes, 1.0), eye)).astype(BF16)
+    sizes = following - start + last * after
+    total = sums_ref[...] + last * next_ref[...]
+    out_ref[...] = (total / jnp.maximum(sizes, 1.0)).astype(BF16)
 
 
 def latent_kernel(own_ref, other_ref, w_ref, sibling_w_ref, out_ref, group):
@@ -194,7 +194,8 @@
 
 
 def d_attn_kernel(valid_ref, w_ref, *refs):
-    grads, (out_ref, pieces, sems) = in_order(refs[:4]), refs[4:]
+    grads, (theirs, out_ref, pieces, sems) = refs[:5], refs[5:]
+    grads = [*grads[:4], theirs.at[0], theirs.at[1], grads[4], theirs.at[2]]
     rows, size = grads[0].shape
     copies = [
         pltpu.make_async_copy(grad, pieces.at[n], sems.at[n]) for n, grad in enumerate(grads)
@@ -210,7 +211,7 @@
 
 
 def d_attn_of(grads, valid, w_out):
-    rows, size = grads[0].shape[1:]
+    rows, size = grads[0].shape
     return call(
         d_attn_kernel,
         (valid, w_out, *grads),
@@ -219,7 +220,7 @@
         name="d_attn",
         megabytes=12,
         micros=DELAY,
-        stay=4,
+        stay=6,
     )[0]
 
 
@@ -412,6 +413,7 @@
     shards, patch_cap = starts.shape
     columns = w_up.shape[1]
     rows = cotangent.shape[0]
+    by_slot = starts.T
     gain = norm_gain.reshape(1, -1)
     weights = (w_query, w_key, w_value)
     is_valid = (starts < byte_rows).reshape(-1, rows)
@@ -424,15 +426,17 @@
     sibling_up = pltpu.with_memory_space_constraint(sibling_up, pltpu.HBM)
     sums, lead = call(
         pool_kernel,
-        (starts, encoded),
+        (by_slot, encoded),
         [shape(patch_cap, byte_width, dtype=F32), shape(1, byte_width, dtype=F32)],
+        [pltpu.VMEM(encoded.shape, BF16), pltpu.SemaphoreType.DMA((4,))],
         name="pool",
         megabytes=4,
+        stay=1,
     )
     next_lead = lax.ppermute(lead, ALL, [(i, i - 1) for i in range(1, shards)])
     patches = call(
         functools.partial(patch_kernel, byte_rows),
-        (starts, sums, next_lead),
+        (by_slot, sums, next_lead),
         [shape(patch_cap, byte_width)],
         name="patch",
         megabytes=4,
@@ -441,10 +445,11 @@
     cot_f, cot_b = along_x(cot_a), along_x(cot_sibling)
     shifted = [lax.ppermute(patches, "x", [(i, (i + k) % 4) for i in range(4)]) for k in (1, 2, 3)]
     own_blocks = jnp.stack([patches, *shifted])
-    own_blocks, cot_b, cot_f = lax.optimization_barrier((own_blocks, cot_b, cot_f))
+    own_blocks, cot_f = lax.optimization_barrier((own_blocks, cot_f))
+    other_blocks = other_core(own_blocks)
     pair = call(
         latent_kernel,
-        (own_blocks, other_core(own_blocks), w_up, sibling_up),
+        (own_blocks, other_blocks, w_up, sibling_up),
         [shape(2, rows, columns)],
         [pltpu.VMEM((8, patch_cap, byte_width), BF16)],
         name="latent",
@@ -452,13 +457,11 @@
         micros=DELAY,
     )[0]
     lat_both = along_x(pair)
-    cot_both = jnp.stack([cot_a, cot_b])
-    cot_theirs = other_core(jnp.concatenate([cot_both, cot_f[None]]))
-    cot_pair = jnp.stack([cotangent, cot_sibling])
-    lat_both, cot_theirs = lax.optimization_barrier((lat_both, cot_theirs))
+    cot_theirs = other_core(jnp.stack([cot_a, cot_b, cot_f]))
+    cots = [cotangent, cot_sibling, cot_a, cot_b, cot_f, cot_theirs]
+    d_attn = d_attn_of(cots, valid, w_out)
+    lat_both, d_attn, bias = lax.optimization_barrier((lat_both, d_attn, bias))
     lat_far = along_x(lat_both[:1])
-    d_attn = d_attn_of([cot_pair, cot_both, cot_f[None], cot_theirs], valid, w_out)
-    lat_far, d_attn, bias = lax.optimization_barrier((lat_far, d_attn, bias))
     theirs = other_core(jnp.concatenate([lat_both, lat_far]))
     pieces = [pair, lat_both, lat_far, theirs]
     keep, send, *qkv, rinv = project(pieces, d_attn, gain, weights)

time: 163 us -> 164 us (level)
  waiting for transfers between devices: 54.9 us -> 59.1 us
  local copies, waits for them, and re-layouts: 5.39 us -> 2.82 us
  other arithmetic: 2.82 us -> 1.17 us
    ppermute x8, waiting for transfers between devices: 33.9 us -> 38.1 us  [along_x(): return lax.ppermute(block, XC, route)]
    unnamed x33 -> x26, local copies, waits for them, and re-layouts: 4.14 us -> 1.57 us
  transfers between devices with their start and end apart: 24 -> 24, of which waited for: 18 -> 18; matrix products, arithmetic and copies ran while one was open for 3% -> 1% of each run, Pallas kernels for 5% -> 6%
where the time goes in v5:
time: 164 us; the launch traced here: 163 us
  waiting for transfers between devices  59.1 us (36%)
  blocking collectives  57.4 us (35%)
  Pallas kernels  29.8 us (18%)
  starting transfers between devices  12 us (7%)
  local copies, waits for them, and re-layouts  2.82 us (2%)
    ppermute x8, waiting for transfers between devices, along_x(): return lax.ppermute(block, XC, route)  38.1 us
    all_to_all x1, blocking collectives, per_device(): mine = lax.all_to_all(sent, SEQ, 0, 0, tiled=True)  31.2 us
    pallas_call x15, Pallas kernels, call(): pl.pallas_call(kernel, in_specs=[VMEM] * (len(ins) - stay) + [pl.BlockSpe...  29.8 us
    all_to_all x1, blocking collectives, per_device(): back = lax.all_to_all(back, SEQ, 0, 0, tiled=True)  26.3 us
    ppermute x12, waiting for transfers between devices, other_core(): return lax.ppermute(block, 'c', [(0, 1), (1, 0)])  13.8 us
    ppermute x3, waiting for transfers between devices, per_device(): lax.ppermute(patches, 'x', [(i, (i + k) % 4) for i in range(4)])  4.73 us
    ppermute x3, starting transfers between devices, per_device(): lax.ppermute(patches, 'x', [(i, (i + k) % 4) for i in range(4)])  4.36 us
    ppermute x8, starting transfers between devices, along_x(): return lax.ppermute(block, XC, route)  4.31 us
  transfers between devices with their start and end apart: 24, of which 18 were waited for; matrix products, arithmetic and copies ran while one was open for 1% of the time, Pallas kernels for 6%

profile of v5, /device:TPU:0, one launch (start us, length us, event | category | flops | bytes accessed | tf_op | source)
XLA Modules:
  0.0 163.3 jit_solution(7513093476788488881)
XLA Ops:
  0.7 0.5 collective-permute-start.2
  1.2 1.6 collective-permute-start.1
  2.8 0.7 copy-done.5
  3.5 1.5 pool.1
  5.0 1.3 collective-permute-start
  6.3 2.3 %collective-permute-done.next_ref = f32[1,1280]{1,0:T(1,128)S(1)} collective-permute-done((f32[1,1280]{1,0:T(1,128)S(1)}, f32[1,1280]{1,0:T(1,128)S(1)}, u32[]{:S(2)}, u32[]{:S(2)}) %collective-permute-start) | collective-permute-done | bytes 5152 | tf_op jit(solution)/shard_map/ppermute | solution.py:436
  8.7 0.2 patch.1
  9.0 1.6 collective-permute-start.5
  10.6 2.7 %collective-permute-start.4 = (bf16[32,1280]{1,0:T(8,128)(2,1)S(1)}, bf16[32,1280]{1,0:T(8,128)(2,1)S(1)}, u32[]{:S(2)}, u32[]{:S(2)}) collective-permute-start(bf16[32,1280]{1,0:T(8,128)(2,1)S(1)} %patch.1), channel_id=1, source_target_pairs={{0,4},{2,6},{4,0},{6,2},{1,5},{3,7},{5,1},{7,3},{8,12},{10,14},{12... | collective-permute-start | bytes 245768 | tf_op jit(solution)/shard_map/ppermute | solution.py:446
  13.4 0.8 collective-permute-start.6
  14.1 1.6 collective-permute-start.10
  15.7 0.8 collective-permute-done.4
  16.6 3.9 %collective-permute-done.3 = bf16[32,1280]{1,0:T(8,128)(2,1)S(1)} collective-permute-done((bf16[32,1280]{1,0:T(8,128)(2,1)S(1)}, bf16[32,1280]{1,0:T(8,128)(2,1)S(1)}, u32[]{:S(2)}, u32[]{:S(2)}) %collective-permute-start.3) | collective-permute-done | bytes 81952 | tf_op jit(solution)/shard_map/ppermute | solution.py:446
  20.5 2.8 %collective-permute-done.6.refs_4_ = bf16[256,512]{1,0:T(8,128)(2,1)S(1)} collective-permute-done((bf16[256,512]{1,0:T(8,128)(2,1)S(1)}, bf16[256,512]{1,0:T(8,128)(2,1)S(1)}, u32[]{:S(2)}, u32[]{:S(2)}) %collective-permute-start.6) | collective-permute-done | bytes 262176 | tf_op jit(solution)/shard_map/ppermute | solution.py:63
  23.5 2.5 %collective-permute-done.10.refs_3_ = bf16[256,512]{1,0:T(8,128)(2,1)S(1)} collective-permute-done((bf16[256,512]{1,0:T(8,128)(2,1)S(1)}, bf16[256,512]{1,0:T(8,128)(2,1)S(1)}, u32[]{:S(2)}, u32[]{:S(2)}) %collective-permute-start.10) | collective-permute-done | bytes 262176 | tf_op jit(solution)/shard_map/ppermute | solution.py:63
  26.1 0.7 copy-done.11
  26.8 1.0 pad_maximum_fusion
  28.2 0.1 copy.14.valid_ref
  28.3 2.3 %latent.1.refs_0_.refs_4_.lat_ref = bf16[2,256,512]{2,1,0:T(8,128)(2,1)S(1)} custom-call(bf16[4,32,1280]{2,1,0:T(8,128)(2,1)S(1)} %pad_maximum_fusion.2.own_ref, bf16[4,32,1280]{2,1,0:T(8,128)(2,1)S(1)} %collective-permute-done.7.other_ref, bf16[1280,512]{1,0:T(8,128)(2,1)S(1)} %copy-done.7, bf16[1280,512]{1,0:T(8,128)(2,1)} %collective-permute-done.8.sibling_w_ref), custom_call_target="tpu_custom_call" | custom-call | flops 8000000000 | bytes 24000000 | tf_op jit(solution)/shard_map/latent/pallas_call | solution.py:36
  30.9 3.1 %d_attn.1.refs_4_ = bf16[256,512]{1,0:T(8,128)(2,1)S(1)} custom-call(f32[256,1]{1,0:T(8,128)S(1)} %copy.14.valid_ref, bf16[512,4096]{1,0:T(8,128)(2,1)S(1)} %copy-done, bf16[256,512]{1,0:T(8,128)(2,1)} %cot_ref.1, bf16[256,512]{1,0:T(8,128)(2,1)} %copy-done.12, bf16[256,512]{1,0:T(8,128)(2,1)} %copy-done.9, bf16[256,512]{1,0:T(8,128)(2,1)} %copy-done.11, ...), custom_call_target="tpu_custom_call" | custom-call | flops 8000000000 | bytes 24000000 | tf_op jit(solution)/shard_map/d_attn/pallas_call | solution.py:36
  34.0 7.2 %collective-permute-done.9.refs_1_.refs_5_ = bf16[2,256,512]{2,1,0:T(8,128)(2,1)S(1)} collective-permute-done((bf16[2,256,512]{2,1,0:T(8,128)(2,1)S(1)}, bf16[2,256,512]{2,1,0:T(8,128)(2,1)S(1)}, u32[]{:S(2)}, u32[]{:S(2)}) %collective-permute-start.9) | collective-permute-done | bytes 524320 | tf_op jit(solution)/shard_map/ppermute | solution.py:63
  41.2 0.6 broadcast_in_dim.15.bias_ref
  41.9 7.6 %collective-permute-done.12.refs_2_.refs_6_ = bf16[1,256,512]{2,1,0:T(8,128)(2,1)S(1)} collective-permute-done((bf16[1,256,512]{2,1,0:T(8,128)(2,1)S(1)}, bf16[1,256,512]{2,1,0:T(8,128)(2,1)S(1)}, u32[]{:S(2)}, u32[]{:S(2)}) %collective-permute-start.12) | collective-permute-done | bytes 262176 | tf_op jit(solution)/shard_map/ppermute | solution.py:63
  49.6 2.3 %collective-permute-done.13.refs_3_.refs_7_ = bf16[3,256,512]{2,1,0:T(8,128)(2,1)S(1)} collective-permute-done((bf16[3,256,512]{2,1,0:T(8,128)(2,1)S(1)}, bf16[3,256,512]{2,1,0:T(8,128)(2,1)S(1)}, u32[]{:S(2)}, u32[]{:S(2)}) %collective-permute-start.13) | collective-permute-done | bytes 786464 | tf_op jit(solution)/shard_map/ppermute | solution.py:55
  51.9 3.6 %project.1 = (bf16[4,256,256]{2,1,0:T(8,128)(2,1)S(1)}, bf16[4,256,256]{2,1,0:T(8,128)(2,1)S(1)}, bf16[256,512]{1,0:T(8,128)(2,1)S(1)}, bf16[256,512]{1,0:T(8,12...) custom-call(bf16[2,256,512]{2,1,0:T(8,128)(2,1)S(1)} %latent.1.refs_0_.refs_4_.lat_ref, ...), custom_call_target="tpu_custom_call" | custom-call | flops 5000000000 | bytes 15000000 | tf_op jit(solution)/shard_map/project/pallas_call | solution.py:36
  55.5 0.2 collective-permute-start.14
  55.8 1.8 %collective-permute-done.14.got_ref = bf16[4,256,256]{2,1,0:T(8,128)(2,1)S(1)} collective-permute-done((bf16[4,256,256]{2,1,0:T(8,128)(2,1)S(1)}, bf16[4,256,256]{2,1,0:T(8,128)(2,1)S(1)}, u32[]{:S(2)}, u32[]{:S(2)}) %collective-permute-start.14) | collective-permute-done | bytes 524320 | tf_op jit(solution)/shard_map/ppermute | solution.py:55
  57.7 31.2 %all_to_all.10.mine_ref = bf16[16,192,256]{2,1,0:T(8,128)(2,1)S(1)} all-to-all(bf16[16,192,256]{2,1,0:T(8,128)(2,1)S(1)} %pack.1), channel_id=1, replica_groups=mesh['y'=4,'z'=4,'x'=4,'c'=2] {'y','z'}, dimensions={0} | all-to-all | bytes 3145728 | tf_op jit(solution)/shard_map/all_to_all | solution.py:471
  88.9 0.3 collective-permute-start.15
  89.2 2.6 %collective-permute-done.15.theirs_ref = bf16[16,128,256]{2,1,0:T(8,128)(2,1)S(1)} collective-permute-done((bf16[16,128,256]{2,1,0:T(8,128)(2,1)S(1)}, bf16[16,128,256]{2,1,0:T(8,128)(2,1)S(1)}, u32[]{:S(2)}, u32[]{:S(2)}) %collective-permute-start.15) | collective-permute-done | bytes 1048608 | tf_op jit(solution)/shard_map/ppermute | solution.py:55
  91.8 11.6 %attention.1 = (bf16[16,128,256]{2,1,0:T(8,128)(2,1)S(1)}, bf16[16,128,256]{2,1,0:T(8,128)(2,1)S(1)}, bf16[16,64,256]{2,1,0:T(8,128)(2,1)S(1)}) custom-call(f32[2,2048,128]{2,1,0:T(8,128)S(1)} %broadcast_in_dim.15.bias_ref, bf16[16,192,256]{2,1,0:T(8,128)(2,1)S(1)} %all_to_all.10.mine_ref, bf16[16,128,256]{2,1,0:T(8,128)(2,1)S(1)} %collective-permute-done.15.theirs_ref), custom_call_target="tpu_custom_call" | custom-call | flops 12000000000 | bytes 36000000 | tf_op jit(solution)/shard_map/attention/pallas_call | solution.py:36
  103.4 0.2 collective-permute-start.16
  103.6 2.5 %collective-permute-done.16.got_ref = bf16[16,128,256]{2,1,0:T(8,128)(2,1)S(1)} collective-permute-done((bf16[16,128,256]{2,1,0:T(8,128)(2,1)S(1)}, bf16[16,128,256]{2,1,0:T(8,128)(2,1)S(1)}, u32[]{:S(2)}, u32[]{:S(2)}) %collective-permute-start.16) | collective-permute-done | bytes 1048608 | tf_op jit(solution)/shard_map/ppermute | solution.py:55
  106.2 0.3 return.1
  106.4 26.3 %all_to_all.11.in_ref = bf16[16,192,256]{2,1,0:T(8,128)(2,1)S(1)} all-to-all(bf16[16,192,256]{2,1,0:T(8,128)(2,1)S(1)} %return.1), channel_id=1, replica_groups=mesh['y'=4,'z'=4,'x'=4,'c'=2] {'y','z'}, dimensions={0} | all-to-all | bytes 3145728 | tf_op jit(solution)/shard_map/all_to_all | solution.py:474
  132.8 0.3 collective-permute-start.17
  133.1 1.9 %collective-permute-done.17.got_ref = bf16[4,256,256]{2,1,0:T(8,128)(2,1)S(1)} collective-permute-done((bf16[4,256,256]{2,1,0:T(8,128)(2,1)S(1)}, bf16[4,256,256]{2,1,0:T(8,128)(2,1)S(1)}, u32[]{:S(2)}, u32[]{:S(2)}) %collective-permute-start.17) | collective-permute-done | bytes 524320 | tf_op jit(solution)/shard_map/ppermute | solution.py:55
  135.0 3.2 %outputs.2 = (bf16[1,512,512]{2,1,0:T(8,128)(2,1)S(1)}, bf16[1,512,512]{2,1,0:T(8,128)(2,1)S(1)}, bf16[3,512,512]{2,1,0:T(8,128)(2,1)S(1)}) custom-call(bf16[4,256,256]{2,1,0:T(8,128)(2,1)S(1)} %get-tuple-element.49.keep_ref, bf16[4,256,256]{2,1,0:T(8,128)(2,1)S(1)} %collective-permute-done.17.got_ref, bf16[256,512]{1,0:T(8,128)(2,1)S(1)} %get-tuple-element.51.refs_0_, ...), custom_call_target="tpu_custom_call" | custom-call | flops 2000000000 | bytes 6000000 | tf_op jit(solution)/shard_map/outputs/pallas_call | solution.py:36
  138.3 0.2 collective-permute-start.18
  138.5 1.8 %collective-permute-done.18.other_ref = bf16[1,512,512]{2,1,0:T(8,128)(2,1)S(1)} collective-permute-done((bf16[1,512,512]{2,1,0:T(8,128)(2,1)S(1)}, bf16[1,512,512]{2,1,0:T(8,128)(2,1)S(1)}, u32[]{:S(2)}, u32[]{:S(2)}) %collective-permute-start.18) | collective-permute-done | bytes 524320 | tf_op jit(solution)/shard_map/ppermute | solution.py:55
  140.3 0.1 collective-permute-start.19
  140.6 2.2 %outputs.3.own_ref = bf16[3,512,512]{2,1,0:T(8,128)(2,1)S(1)} custom-call(bf16[4,256,256]{2,1,0:T(8,128)(2,1)S(1)} %get-tuple-element.49.keep_ref, bf16[4,256,256]{2,1,0:T(8,128)(2,1)S(1)} %collective-permute-done.17.got_ref, bf16[256,512]{1,0:T(8,128)(2,1)S(1)} %get-tuple-element.51.refs_0_, bf16[256,512]{1,0:T(8,128)(2,1)S(1)} %get-tuple-element.52.refs_1_, ...), custom_call_target="tpu_custom_call" | custom-call | flops 2000000000 | bytes 6000000 | tf_op jit(solution)/shard_map/outputs/pallas_call | solution.py:36
  142.8 0.9 collective-permute-done.19.other_ref
  143.7 0.3 add.9
  144.1 6.9 %collective-permute-done.20.far_ref = bf16[512,512]{1,0:T(8,128)(2,1)S(1)} collective-permute-done((bf16[512,512]{1,0:T(8,128)(2,1)S(1)}, bf16[512,512]{1,0:T(8,128)(2,1)S(1)}, u32[]{:S(2)}, u32[]{:S(2)}) %collective-permute-start.20) | collective-permute-done | bytes 524320 | tf_op jit(solution)/shard_map/ppermute | solution.py:63
  151.2 5.4 %collective-permute-done.22 = bf16[512,512]{1,0:T(8,128)(2,1)S(1)} collective-permute-done((bf16[512,512]{1,0:T(8,128)(2,1)S(1)}, bf16[512,512]{1,0:T(8,128)(2,1)S(1)}, u32[]{:S(2)}, u32[]{:S(2)}) %collective-permute-start.22) | collective-permute-done | bytes 524320 | tf_op jit(solution)/shard_map/ppermute | solution.py:63
  156.6 5.6 %collective-permute-done.21.ahead_ref = bf16[512,512]{1,0:T(8,128)(2,1)S(1)} collective-permute-done((bf16[512,512]{1,0:T(8,128)(2,1)S(1)}, bf16[512,512]{1,0:T(8,128)(2,1)S(1)}, u32[]{:S(2)}, u32[]{:S(2)}) %collective-permute-start.21) | collective-permute-done | bytes 524320 | tf_op jit(solution)/shard_map/ppermute | solution.py:63
  162.2 1.1 final.1
  (56 shorter events, 2.0 us)
Async XLA Ops:
  0.6 27.7 %collective-permute-start.8 = (bf16[1280,512]{1,0:T(8,128)(2,1)}, bf16[1280,512]{1,0:T(8,128)(2,1)}, u32[]{:S(2)}, u32[]{:S(2)}) collective-permute-start(bf16[1280,512]{1,0:T(8,128)(2,1)} %w_ref.2), channel_id=1, source_target_pairs={{0,1},{1,0},{2,3},{3,2},{4,5},{5,4},{6,7},{7,6},{8,9},{9,8},{10,11... | collective-permute-start | bytes 3932168 | tf_op jit(solution)/shard_map/ppermute | solution.py:55
  0.7 8.2 %collective-permute-start.2 = (bf16[256,512]{1,0:T(8,128)(2,1)}, bf16[256,512]{1,0:T(8,128)(2,1)S(1)}, u32[]{:S(2)}, u32[]{:S(2)}) collective-permute-start(bf16[256,512]{1,0:T(8,128)(2,1)} %cot_ref.1), channel_id=1, source_target_pairs={{0,1},{1,0},{2,3},{3,2},{4,5},{5,4},{6,7},{7,6},{8,9},{9,8},{10,11... | collective-permute-start | bytes 786440 | tf_op jit(solution)/shard_map/ppermute | solution.py:55
  1.2 7.8 %collective-permute-start.1 = (bf16[256,512]{1,0:T(8,128)(2,1)}, bf16[256,512]{1,0:T(8,128)(2,1)S(1)}, u32[]{:S(2)}, u32[]{:S(2)}) collective-permute-start(bf16[256,512]{1,0:T(8,128)(2,1)} %cot_ref.1), channel_id=1, source_target_pairs={{0,2},{1,7},{2,4},{3,1},{4,6},{5,3},{6,0},{7,5},{8,10},{9,15},{10,... | collective-permute-start | bytes 786440 | tf_op jit(solution)/shard_map/ppermute | solution.py:63
  2.8 0.7 copy-start.5
  5.0 3.6 %collective-permute-start = (f32[1,1280]{1,0:T(1,128)S(1)}, f32[1,1280]{1,0:T(1,128)S(1)}, u32[]{:S(2)}, u32[]{:S(2)}) collective-permute-start(f32[1,1280]{1,0:T(1,128)S(1)} %get-tuple-element.34), channel_id=1, source_target_pairs={{1,0},{2,1},{3,2},{4,3},{5,4},{6,5},{7,6},{8,7},{9,8},{10,9},{11,1... | collective-permute-start | bytes 15368 | tf_op jit(solution)/shard_map/ppermute | solution.py:436
  8.7 14.6 %copy-start.6 = (s32[128,32]{0,1:T(8,128)S(1)}, s32[128,32]{0,1:T(8,128)}, u32[]{:S(2)}) copy-start(s32[128,32]{0,1:T(8,128)} %param.10) | copy-start | bytes 49156
  8.9 19.5 %copy-start.7 = (bf16[1280,512]{1,0:T(8,128)(2,1)S(1)}, bf16[1280,512]{1,0:T(8,128)(2,1)}, u32[]{:S(2)}) copy-start(bf16[1280,512]{1,0:T(8,128)(2,1)} %w_ref.2) | copy-start | bytes 3932164
  8.9 17.2 %copy-start.12 = (bf16[256,512]{1,0:T(8,128)(2,1)}, bf16[256,512]{1,0:T(8,128)(2,1)S(1)}, u32[]{:S(2)}) copy-start(bf16[256,512]{1,0:T(8,128)(2,1)S(1)} %collective-permute-done.2.refs_1_) | copy-start | bytes 786436
  9.0 21.7 %copy-start.9 = (bf16[256,512]{1,0:T(8,128)(2,1)}, bf16[256,512]{1,0:T(8,128)(2,1)S(1)}, u32[]{:S(2)}) copy-start(bf16[256,512]{1,0:T(8,128)(2,1)S(1)} %collective-permute-done.1.refs_2_) | copy-start | bytes 786436
  9.0 5.1 %collective-permute-start.5 = (bf16[32,1280]{1,0:T(8,128)(2,1)S(1)}, bf16[32,1280]{1,0:T(8,128)(2,1)S(1)}, u32[]{:S(2)}, u32[]{:S(2)}) collective-permute-start(bf16[32,1280]{1,0:T(8,128)(2,1)S(1)} %patch.1), channel_id=1, source_target_pairs={{0,6},{2,0},{4,2},{6,4},{1,7},{3,1},{5,3},{7,5},{8,14},{10,8},{12,... | collective-permute-start | bytes 245768 | tf_op jit(solution)/shard_map/ppermute | solution.py:446
  10.6 5.9 %collective-permute-start.4 = (bf16[32,1280]{1,0:T(8,128)(2,1)S(1)}, bf16[32,1280]{1,0:T(8,128)(2,1)S(1)}, u32[]{:S(2)}, u32[]{:S(2)}) collective-permute-start(bf16[32,1280]{1,0:T(8,128)(2,1)S(1)} %patch.1), channel_id=1, source_target_pairs={{0,4},{2,6},{4,0},{6,2},{1,5},{3,7},{5,1},{7,3},{8,12},{10,14},{12... | collective-permute-start | bytes 245768 | tf_op jit(solution)/shard_map/ppermute | solution.py:446
  13.4 7.1 %collective-permute-start.3 = (bf16[32,1280]{1,0:T(8,128)(2,1)S(1)}, bf16[32,1280]{1,0:T(8,128)(2,1)S(1)}, u32[]{:S(2)}, u32[]{:S(2)}) collective-permute-start(bf16[32,1280]{1,0:T(8,128)(2,1)S(1)} %patch.1), channel_id=1, source_target_pairs={{0,2},{2,4},{4,6},{6,0},{1,3},{3,5},{5,7},{7,1},{8,10},{10,12},{12... | collective-permute-start | bytes 245768 | tf_op jit(solution)/shard_map/ppermute | solution.py:446
  13.4 9.9 %collective-permute-start.6 = (bf16[256,512]{1,0:T(8,128)(2,1)S(1)}, bf16[256,512]{1,0:T(8,128)(2,1)S(1)}, u32[]{:S(2)}, u32[]{:S(2)}) collective-permute-start(bf16[256,512]{1,0:T(8,128)(2,1)S(1)} %collective-permute-done.1.refs_2_), channel_id=1, source_target_pairs={{0,2},{1,7},{2,4},{3,1},{4,6},{5,3},{6,0},{7,5},{8,10},{9,15},{10,... | collective-permute-start | bytes 786440 | tf_op jit(solution)/shard_map/ppermute | solution.py:63
  14.1 12.0 %collective-permute-start.10 = (bf16[256,512]{1,0:T(8,128)(2,1)S(1)}, bf16[256,512]{1,0:T(8,128)(2,1)S(1)}, u32[]{:S(2)}, u32[]{:S(2)}) collective-permute-start(bf16[256,512]{1,0:T(8,128)(2,1)S(1)} %collective-permute-done.2.refs_1_), channel_id=1, source_target_pairs={{0,2},{1,7},{2,4},{3,1},{4,6},{5,3},{6,0},{7,5},{8,10},{9,15},{10,... | collective-permute-start | bytes 786440 | tf_op jit(solution)/shard_map/ppermute | solution.py:63
  23.3 4.7 %copy-start.10 = (bf16[256,512]{1,0:T(8,128)(2,1)}, bf16[256,512]{1,0:T(8,128)(2,1)S(1)}, u32[]{:S(2)}) copy-start(bf16[256,512]{1,0:T(8,128)(2,1)S(1)} %collective-permute-done.6.refs_4_) | copy-start | bytes 786436
  23.3 5.0 %collective-permute-start.7 = (bf16[4,32,1280]{2,1,0:T(8,128)(2,1)S(1)}, bf16[4,32,1280]{2,1,0:T(8,128)(2,1)S(1)}, u32[]{:S(2)}, u32[]{:S(2)}) collective-permute-start(bf16[4,32,1280]{2,1,0:T(8,128)(2,1)S(1)} %pad_maximum_fusion.2.own_ref), channel_id=1, source_target_pairs={{0,1},{1,0},{2,3},{3,2},{4,5},{5,4},{6,7},{7,6},{8,9},{9,8},{10,11... | collective-permute-start | bytes 983048 | tf_op jit(solution)/shard_map/ppermute | solution.py:55
  26.1 0.7 copy-start.11
  27.8 2.9 %collective-permute-start.11 = (bf16[3,256,512]{2,1,0:T(8,128)(2,1)S(1)}, bf16[3,256,512]{2,1,0:T(8,128)(2,1)}, u32[]{:S(2)}, u32[]{:S(2)}) collective-permute-start(bf16[3,256,512]{2,1,0:T(8,128)(2,1)S(1)} %pad_maximum_fusion), channel_id=1, source_target_pairs={{0,1},{1,0},{2,3},{3,2},{4,5},{5,4},{6,7},{7,6},{8,9},{9,8},{10,11... | collective-permute-start | bytes 2359304 | tf_op jit(solution)/shard_map/ppermute | solution.py:55
  28.3 2.6 %copy-start = (bf16[512,4096]{1,0:T(8,128)(2,1)S(1)}, bf16[512,4096]{1,0:T(8,128)(2,1)}, u32[]{:S(2)}) copy-start(bf16[512,4096]{1,0:T(8,128)(2,1)} %refs_12_.3) | copy-start | bytes 12582916
  30.7 10.5 %collective-permute-start.9 = (bf16[2,256,512]{2,1,0:T(8,128)(2,1)S(1)}, bf16[2,256,512]{2,1,0:T(8,128)(2,1)S(1)}, u32[]{:S(2)}, u32[]{:S(2)}) collective-permute-start(bf16[2,256,512]{2,1,0:T(8,128)(2,1)S(1)} %latent.1.refs_0_.refs_4_.lat_ref), channel_id=1, source_target_pairs={{0,2},{1,7},{2,4},{3,1},{4,6},{5,3},{6,0},{7,5},{8,10},{9,15},{10,... | collective-permute-start | bytes 1572872 | tf_op jit(solution)/shard_map/ppermute | solution.py:63
  30.9 21.0 %copy-start.2 = (bf16[4096,512]{1,0:T(8,128)(2,1)S(1)}, bf16[4096,512]{1,0:T(8,128)(2,1)}, u32[]{:S(2)}) copy-start(bf16[4096,512]{1,0:T(8,128)(2,1)} %refs_10_.3) | copy-start | bytes 12582916
  30.9 21.0 %copy-start.3 = (bf16[4096,512]{1,0:T(8,128)(2,1)S(1)}, bf16[4096,512]{1,0:T(8,128)(2,1)}, u32[]{:S(2)}) copy-start(bf16[4096,512]{1,0:T(8,128)(2,1)} %refs_11_.3) | copy-start | bytes 12582916
  41.2 10.7 %copy-start.1 = (bf16[4096,512]{1,0:T(8,128)(2,1)S(1)}, bf16[4096,512]{1,0:T(8,128)(2,1)}, u32[]{:S(2)}) copy-start(bf16[4096,512]{1,0:T(8,128)(2,1)} %refs_9_.3) | copy-start | bytes 12582916
  41.8 10.1 %copy-start.4 = (f32[4096]{0:T(1024)S(1)}, f32[4096]{0:T(1024)}, u32[]{:S(2)}) copy-start(f32[4096]{0:T(1024)} %param.12) | copy-start | bytes 49156
  41.8 7.7 %collective-permute-start.12 = (bf16[1,256,512]{2,1,0:T(8,128)(2,1)S(1)}, bf16[1,256,512]{2,1,0:T(8,128)(2,1)S(1)}, u32[]{:S(2)}, u32[]{:S(2)}) collective-permute-start(bf16[1,256,512]{2,1,0:T(8,128)(2,1)S(1)} %slice.6), channel_id=1, source_target_pairs={{0,2},{1,7},{2,4},{3,1},{4,6},{5,3},{6,0},{7,5},{8,10},{9,15},{10,... | collective-permute-start | bytes 786440 | tf_op jit(solution)/shard_map/ppermute | solution.py:63
  49.5 2.4 %collective-permute-start.13 = (bf16[3,256,512]{2,1,0:T(8,128)(2,1)S(1)}, bf16[3,256,512]{2,1,0:T(8,128)(2,1)S(1)}, u32[]{:S(2)}, u32[]{:S(2)}) collective-permute-start(bf16[3,256,512]{2,1,0:T(8,128)(2,1)S(1)} %pad_maximum_fusion.1), channel_id=1, source_target_pairs={{0,1},{1,0},{2,3},{3,2},{4,5},{5,4},{6,7},{7,6},{8,9},{9,8},{10,11... | collective-permute-start | bytes 2359304 | tf_op jit(solution)/shard_map/ppermute | solution.py:55
  55.5 2.0 %collective-permute-start.14 = (bf16[4,256,256]{2,1,0:T(8,128)(2,1)S(1)}, bf16[4,256,256]{2,1,0:T(8,128)(2,1)S(1)}, u32[]{:S(2)}, u32[]{:S(2)}) collective-permute-start(bf16[4,256,256]{2,1,0:T(8,128)(2,1)S(1)} %get-tuple-element.45), channel_id=1, source_target_pairs={{0,1},{1,0},{2,3},{3,2},{4,5},{5,4},{6,7},{7,6},{8,9},{9,8},{10,11... | collective-permute-start | bytes 1572872 | tf_op jit(solution)/shard_map/ppermute | solution.py:55
  88.9 2.9 %collective-permute-start.15 = (bf16[16,128,256]{2,1,0:T(8,128)(2,1)S(1)}, bf16[16,128,256]{2,1,0:T(8,128)(2,1)S(1)}, u32[]{:S(2)}, u32[]{:S(2)}) collective-permute-start(bf16[16,128,256]{2,1,0:T(8,128)(2,1)S(1)} %slice.8), channel_id=1, source_target_pairs={{0,1},{1,0},{2,3},{3,2},{4,5},{5,4},{6,7},{7,6},{8,9},{9,8},{10,11... | collective-permute-start | bytes 3145736 | tf_op jit(solution)/shard_map/ppermute | solution.py:55
  103.4 2.7 %collective-permute-start.16 = (bf16[16,128,256]{2,1,0:T(8,128)(2,1)S(1)}, bf16[16,128,256]{2,1,0:T(8,128)(2,1)S(1)}, u32[]{:S(2)}, u32[]{:S(2)}) collective-permute-start(bf16[16,128,256]{2,1,0:T(8,128)(2,1)S(1)} %get-tuple-element.47), channel_id=1, source_target_pairs={{0,1},{1,0},{2,3},{3,2},{4,5},{5,4},{6,7},{7,6},{8,9},{9,8},{10,11... | collective-permute-start | bytes 3145736 | tf_op jit(solution)/shard_map/ppermute | solution.py:55
  132.8 2.2 %collective-permute-start.17 = (bf16[4,256,256]{2,1,0:T(8,128)(2,1)S(1)}, bf16[4,256,256]{2,1,0:T(8,128)(2,1)S(1)}, u32[]{:S(2)}, u32[]{:S(2)}) collective-permute-start(bf16[4,256,256]{2,1,0:T(8,128)(2,1)S(1)} %get-tuple-element.50), channel_id=1, source_target_pairs={{0,1},{1,0},{2,3},{3,2},{4,5},{5,4},{6,7},{7,6},{8,9},{9,8},{10,11... | collective-permute-start | bytes 1572872 | tf_op jit(solution)/shard_map/ppermute | solution.py:55
  138.3 2.0 %collective-permute-start.18 = (bf16[1,512,512]{2,1,0:T(8,128)(2,1)S(1)}, bf16[1,512,512]{2,1,0:T(8,128)(2,1)S(1)}, u32[]{:S(2)}, u32[]{:S(2)}) collective-permute-start(bf16[1,512,512]{2,1,0:T(8,128)(2,1)S(1)} %get-tuple-element.55), channel_id=1, source_target_pairs={{0,1},{1,0},{2,3},{3,2},{4,5},{5,4},{6,7},{7,6},{8,9},{9,8},{10,11... | collective-permute-start | bytes 1572872 | tf_op jit(solution)/shard_map/ppermute | solution.py:55
  140.3 3.4 %collective-permute-start.19 = (bf16[3,512,512]{2,1,0:T(8,128)(2,1)S(1)}, bf16[3,512,512]{2,1,0:T(8,128)(2,1)S(1)}, u32[]{:S(2)}, u32[]{:S(2)}) collective-permute-start(bf16[3,512,512]{2,1,0:T(8,128)(2,1)S(1)} %get-tuple-element.59), channel_id=1, source_target_pairs={{0,1},{1,0},{2,3},{3,2},{4,5},{5,4},{6,7},{7,6},{8,9},{9,8},{10,11... | collective-permute-start | bytes 4718600 | tf_op jit(solution)/shard_map/ppermute | solution.py:55
  140.5 10.5 %collective-permute-start.20 = (bf16[512,512]{1,0:T(8,128)(2,1)S(1)}, bf16[512,512]{1,0:T(8,128)(2,1)S(1)}, u32[]{:S(2)}, u32[]{:S(2)}) collective-permute-start(bf16[512,512]{1,0:T(8,128)(2,1)S(1)} %far.1), channel_id=1, source_target_pairs={{0,2},{1,7},{2,4},{3,1},{4,6},{5,3},{6,0},{7,5},{8,10},{9,15},{10,... | collective-permute-start | bytes 1572872 | tf_op jit(solution)/shard_map/ppermute | solution.py:63
  144.0 12.6 %collective-permute-start.22 = (bf16[512,512]{1,0:T(8,128)(2,1)S(1)}, bf16[512,512]{1,0:T(8,128)(2,1)S(1)}, u32[]{:S(2)}, u32[]{:S(2)}) collective-permute-start(bf16[512,512]{1,0:T(8,128)(2,1)S(1)} %get-tuple-element.63), channel_id=1, source_target_pairs={{0,2},{1,7},{2,4},{3,1},{4,6},{5,3},{6,0},{7,5},{8,10},{9,15},{10,... | collective-permute-start | bytes 1572872 | tf_op jit(solution)/shard_map/ppermute | solution.py:63
  151.0 11.2 %copy-start.8 = (bf16[256,512]{1,0:T(8,128)(2,1)S(1)}, bf16[256,512]{1,0:T(8,128)(2,1)}, u32[]{:S(2)}) copy-start(bf16[256,512]{1,0:T(8,128)(2,1)} %cot_ref.1) | copy-start | bytes 786436
  151.1 11.1 %collective-permute-start.21 = (bf16[512,512]{1,0:T(8,128)(2,1)S(1)}, bf16[512,512]{1,0:T(8,128)(2,1)S(1)}, u32[]{:S(2)}, u32[]{:S(2)}) collective-permute-start(bf16[512,512]{1,0:T(8,128)(2,1)S(1)} %pass.1), channel_id=1, source_target_pairs={{0,2},{1,7},{2,4},{3,1},{4,6},{5,3},{6,0},{7,5},{8,10},{9,15},{10,... | collective-permute-start | bytes 1572872 | tf_op jit(solution)/shard_map/ppermute | solution.py:63
  156.6 5.6 %collective-permute-start.23 = (bf16[512,512]{1,0:T(8,128)(2,1)S(1)}, bf16[512,512]{1,0:T(8,128)(2,1)S(1)}, u32[]{:S(2)}, u32[]{:S(2)}) collective-permute-start(bf16[512,512]{1,0:T(8,128)(2,1)S(1)} %collective-permute-done.22), channel_id=1, source_target_pairs={{0,1},{1,0},{2,3},{3,2},{4,5},{5,4},{6,7},{7,6},{8,9},{9,8},{10,11... | collective-permute-start | bytes 1572872 | tf_op jit(solution)/shard_map/ppermute | solution.py:55

commit v6 on v5

--- a/solution.py
+++ b/solution.py
@@ -32,7 +32,8 @@
 
 def call(kernel, ins, outs, scratch=(), name=None, megabytes=8, micros=1.0, stay=0):
     here = len(ins) - stay
-    ins = [*ins[:here], *(pltpu.with_memory_space_constraint(a, pltpu.HBM) for a in ins[here:])]
+    if name != "latent":
+        ins = [*ins[:here], *(pltpu.with_memory_space_constraint(a, pltpu.HBM) for a in ins[here:])]
     return pl.pallas_call(
         kernel,
         in_specs=[VMEM] * (len(ins) - stay) + [pl.BlockSpec(memory_space=pltpu.HBM)] * stay,
@@ -109,16 +110,25 @@
     out_ref[...] = (total / jnp.maximum(sizes, 1.0)).astype(BF16)
 
 
-def latent_kernel(own_ref, other_ref, w_ref, sibling_w_ref, out_ref, group):
+def latent_kernel(own_ref, other_ref, w_ref, sibling_w_ref, out_ref, group, held, sems):
     x, c = place("x"), place("c")
     count, rows, width = own_ref.shape
+    spans = [slice(n * width // 4, (n + 1) * width // 4) for n in range(4)]
+    copies = [
+        pltpu.make_async_copy(sibling_w_ref.at[span, :], held.at[span, :], sems.at[n])
+        for n, span in enumerate(spans)
+    ]
+    for copy in copies:
+        copy.start()
     for k in range(count):
         at = lax.rem(x + count - k, count) * 2
         group[at + c] = own_ref[k]
         group[at + 1 - c] = other_ref[k]
     whole = group[...].reshape(2 * count * rows, width)
-    for n, ref in enumerate((w_ref, sibling_w_ref)):
-        out_ref[n] = jnp.dot(whole, ref[...], preferred_element_type=F32).astype(BF16)
+    out_ref[0] = jnp.dot(whole, w_ref[...], preferred_element_type=F32).astype(BF16)
+    for copy in copies:
+        copy.wait()
+    out_ref[1] = jnp.dot(whole, held[...], preferred_element_type=F32).astype(BF16)
 
 
 def tp_places():
@@ -424,6 +434,7 @@
 
     cot_a, cot_sibling, sibling_up = along_x(cotangent), other_core(cotangent), other_core(w_up)
     sibling_up = pltpu.with_memory_space_constraint(sibling_up, pltpu.HBM)
+    cot_b = along_x(cot_sibling)
     sums, lead = call(
         pool_kernel,
         (by_slot, encoded),
@@ -434,6 +445,8 @@
         stay=1,
     )
     next_lead = lax.ppermute(lead, ALL, [(i, i - 1) for i in range(1, shards)])
+    next_lead, cot_a, cot_b = lax.optimization_barrier((next_lead, cot_a, cot_b))
+    cot_f = along_x(cot_a)
     patches = call(
         functools.partial(patch_kernel, byte_rows),
         (by_slot, sums, next_lead),
@@ -441,8 +454,6 @@
         name="patch",
         megabytes=4,
     )[0]
-    patches, cot_a, cot_sibling = lax.optimization_barrier((patches, cot_a, cot_sibling))
-    cot_f, cot_b = along_x(cot_a), along_x(cot_sibling)
     shifted = [lax.ppermute(patches, "x", [(i, (i + k) % 4) for i in range(4)]) for k in (1, 2, 3)]
     own_blocks = jnp.stack([patches, *shifted])
     own_blocks, cot_f = lax.optimization_barrier((own_blocks, cot_f))
@@ -451,17 +462,23 @@
         latent_kernel,
         (own_blocks, other_blocks, w_up, sibling_up),
         [shape(2, rows, columns)],
-        [pltpu.VMEM((8, patch_cap, byte_width), BF16)],
+        [
+            pltpu.VMEM((8, patch_cap, byte_width), BF16),
+            pltpu.VMEM(w_up.shape, BF16),
+            pltpu.SemaphoreType.DMA((4,)),
+        ],
         name="latent",
         megabytes=8,
         micros=DELAY,
+        stay=1,
     )[0]
     lat_both = along_x(pair)
+    ready = (lat_both, cot_a, cot_b, cot_f)
+    lat_both, cot_a, cot_b, cot_f = lax.optimization_barrier(ready)
+    lat_far = along_x(lat_both[:1])
     cot_theirs = other_core(jnp.stack([cot_a, cot_b, cot_f]))
     cots = [cotangent, cot_sibling, cot_a, cot_b, cot_f, cot_theirs]
     d_attn = d_attn_of(cots, valid, w_out)
-    lat_both, d_attn, bias = lax.optimization_barrier((lat_both, d_attn, bias))
-    lat_far = along_x(lat_both[:1])
     theirs = other_core(jnp.concatenate([lat_both, lat_far]))
     pieces = [pair, lat_both, lat_far, theirs]
     keep, send, *qkv, rinv = project(pieces, d_attn, gain, weights)

time: 164 us -> 175 us (1.067)
  local copies, waits for them, and re-layouts: 2.82 us -> 12.1 us
    unnamed x26 -> x52, local copies, waits for them, and re-layouts: 1.57 us -> 6.33 us
    select_n x2, local copies, waits for them, and re-layouts: 0.19 us -> 2.97 us  [per_device(): jnp.where(by_half, 0.0, NEG)]
    ppermute x12, waiting for transfers between devices: 13.8 us -> 11.6 us  [other_core(): return lax.ppermute(block, 'c', [(0, 1), (1, 0)])]
  transfers between devices with their start and end apart: 24 -> 24, of which waited for: 18 -> 17; matrix products, arithmetic and copies ran while one was open for 1% -> 3% of each run, Pallas kernels for 6% -> 4%
where the time goes in v6:
time: 175 us
  blocking collectives  58.4 us (33%)
  waiting for transfers between devices  58.2 us (33%)
  Pallas kernels  31 us (18%)
  starting transfers between devices  12.3 us (7%)
  local copies, waits for them, and re-layouts  12.1 us (7%)
    ppermute x8, waiting for transfers between devices, along_x(): return lax.ppermute(block, XC, route)  37.9 us
    all_to_all x1, blocking collectives, per_device(): mine = lax.all_to_all(sent, SEQ, 0, 0, tiled=True)  31.4 us
    pallas_call x15, Pallas kernels, call(): pl.pallas_call(kernel, in_specs=[VMEM] * (len(ins) - stay) + [pl.BlockSpe...  31 us
    all_to_all x1, blocking collectives, per_device(): back = lax.all_to_all(back, SEQ, 0, 0, tiled=True)  27 us
    ppermute x12, waiting for transfers between devices, other_core(): return lax.ppermute(block, 'c', [(0, 1), (1, 0)])  11.6 us
    unnamed x52, local copies, waits for them, and re-layouts  6.33 us
    ppermute x3, waiting for transfers between devices, per_device(): lax.ppermute(patches, 'x', [(i, (i + k) % 4) for i in range(4)])  6.3 us
    ppermute x3, starting transfers between devices, per_device(): lax.ppermute(patches, 'x', [(i, (i + k) % 4) for i in range(4)])  4.38 us
  transfers between devices with their start and end apart: 24, of which 17 were waited for; matrix products, arithmetic and copies ran while one was open for 3% of the time, Pallas kernels for 4%

profile of v6, /device:TPU:0, one launch (start us, length us, event | category | flops | bytes accessed | tf_op | source)
XLA Modules:
  0.0 174.6 jit_solution(4041676350740855818)
XLA Ops:
  0.7 0.5 collective-permute-start.2
  1.2 1.6 collective-permute-start.1
  2.8 1.5 collective-permute-done.2.refs_1_
  4.3 1.6 collective-permute-start.3
  5.9 0.7 copy-done.17
  6.6 1.5 pool.1
  8.1 1.3 collective-permute-start
  9.4 2.4 %collective-permute-done.next_ref = f32[1,1280]{1,0:T(1,128)S(1)} collective-permute-done((f32[1,1280]{1,0:T(1,128)S(1)}, f32[1,1280]{1,0:T(1,128)S(1)}, u32[]{:S(2)}, u32[]{:S(2)}) %collective-permute-start) | collective-permute-done | bytes 5152 | tf_op jit(solution)/shard_map/ppermute | solution.py:447
  12.1 1.7 collective-permute-start.6
  13.8 2.7 %collective-permute-start.5 = (bf16[32,1280]{1,0:T(8,128)(2,1)S(1)}, bf16[32,1280]{1,0:T(8,128)(2,1)S(1)}, u32[]{:S(2)}, u32[]{:S(2)}) collective-permute-start(bf16[32,1280]{1,0:T(8,128)(2,1)S(1)} %patch.1), channel_id=1, source_target_pairs={{0,4},{2,6},{4,0},{6,2},{1,5},{3,7},{5,1},{7,3},{8,12},{10,14},{12... | collective-permute-start | bytes 245768 | tf_op jit(solution)/shard_map/ppermute | solution.py:457
  16.5 0.8 collective-permute-start.7
  17.3 2.5 %collective-permute-done.5 = bf16[32,1280]{1,0:T(8,128)(2,1)S(1)} collective-permute-done((bf16[32,1280]{1,0:T(8,128)(2,1)S(1)}, bf16[32,1280]{1,0:T(8,128)(2,1)S(1)}, u32[]{:S(2)}, u32[]{:S(2)}) %collective-permute-start.5) | collective-permute-done | bytes 81952 | tf_op jit(solution)/shard_map/ppermute | solution.py:457
  19.8 3.8 %collective-permute-done.4 = bf16[32,1280]{1,0:T(8,128)(2,1)S(1)} collective-permute-done((bf16[32,1280]{1,0:T(8,128)(2,1)S(1)}, bf16[32,1280]{1,0:T(8,128)(2,1)S(1)}, u32[]{:S(2)}, u32[]{:S(2)}) %collective-permute-start.4) | collective-permute-done | bytes 81952 | tf_op jit(solution)/shard_map/ppermute | solution.py:457
  23.7 2.8 %collective-permute-done.7.refs_4_ = bf16[256,512]{1,0:T(8,128)(2,1)S(1)} collective-permute-done((bf16[256,512]{1,0:T(8,128)(2,1)S(1)}, bf16[256,512]{1,0:T(8,128)(2,1)S(1)}, u32[]{:S(2)}, u32[]{:S(2)}) %collective-permute-start.7) | collective-permute-done | bytes 262176 | tf_op jit(solution)/shard_map/ppermute | solution.py:64
  26.4 1.6 collective-permute-done.8.other_ref
  28.1 1.1 copy-done.24
  29.2 2.1 %latent.1.refs_0_.refs_4_.lat_ref = bf16[2,256,512]{2,1,0:T(8,128)(2,1)S(1)} custom-call(bf16[4,32,1280]{2,1,0:T(8,128)(2,1)S(1)} %pad_maximum_fusion.2.own_ref, bf16[4,32,1280]{2,1,0:T(8,128)(2,1)S(1)} %collective-permute-done.8.other_ref, bf16[1280,512]{1,0:T(8,128)(2,1)S(1)} %copy-done.19, bf16[1280,512]{1,0:T(8,128)(2,1)} %copy-done.24), custom_call_target="tpu_custom_call" | custom-call | flops 8000000000 | bytes 24000000 | tf_op jit(solution)/shard_map/latent/pallas_call | solution.py:37
  31.4 10.4 %collective-permute-done.10.refs_1_.refs_5_ = bf16[2,256,512]{2,1,0:T(8,128)(2,1)S(1)} collective-permute-done((bf16[2,256,512]{2,1,0:T(8,128)(2,1)S(1)}, bf16[2,256,512]{2,1,0:T(8,128)(2,1)S(1)}, u32[]{:S(2)}, u32[]{:S(2)}) %collective-permute-start.10) | collective-permute-done | bytes 524320 | tf_op jit(solution)/shard_map/ppermute | solution.py:64
  42.1 0.6 broadcast_select_fusion
  43.0 6.7 %collective-permute-done.11.refs_2_.refs_6_ = bf16[1,256,512]{2,1,0:T(8,128)(2,1)S(1)} collective-permute-done((bf16[1,256,512]{2,1,0:T(8,128)(2,1)S(1)}, bf16[1,256,512]{2,1,0:T(8,128)(2,1)S(1)}, u32[]{:S(2)}, u32[]{:S(2)}) %collective-permute-start.11) | collective-permute-done | bytes 262176 | tf_op jit(solution)/shard_map/ppermute | solution.py:64
  49.7 1.0 pad_maximum_fusion
  50.8 2.2 %copy-done = bf16[512,4096]{1,0:T(8,128)(2,1)S(1)} copy-done((bf16[512,4096]{1,0:T(8,128)(2,1)S(1)}, bf16[512,4096]{1,0:T(8,128)(2,1)}, u32[]{:S(2)}) %copy-start) | copy-done | bytes 4194328
  53.1 3.1 %d_attn.1.refs_4_ = bf16[256,512]{1,0:T(8,128)(2,1)S(1)} custom-call(f32[256,1]{1,0:T(8,128)S(1)} %copy.14.valid_ref, bf16[512,4096]{1,0:T(8,128)(2,1)S(1)} %copy-done, bf16[256,512]{1,0:T(8,128)(2,1)} %cot_ref.1, bf16[256,512]{1,0:T(8,128)(2,1)} %copy-done.25, bf16[256,512]{1,0:T(8,128)(2,1)} %copy-done.21, bf16[256,512]{1,0:T(8,128)(2,1)} %copy-done.22, ...), custom_call_target="tpu_custom_call" | custom-call | flops 8000000000 | bytes 24000000 | tf_op jit(solution)/shard_map/d_attn/pallas_call | solution.py:37
  56.2 1.0 copy-done.4
  57.1 1.2 copy-done.6
  58.3 3.6 %project.1 = (bf16[4,256,256]{2,1,0:T(8,128)(2,1)S(1)}, bf16[4,256,256]{2,1,0:T(8,128)(2,1)S(1)}, bf16[256,512]{1,0:T(8,128)(2,1)S(1)}, bf16[256,512]{1,0:T(8,12...) custom-call(bf16[2,256,512]{2,1,0:T(8,128)(2,1)S(1)} %latent.1.refs_0_.refs_4_.lat_ref, ...), custom_call_target="tpu_custom_call" | custom-call | flops 5000000000 | bytes 15000000 | tf_op jit(solution)/shard_map/project/pallas_call | solution.py:37
  62.0 0.6 collective-permute-start.14
  62.6 1.5 collective-permute-done.14.got_ref
  64.3 31.4 %all_to_all.10.mine_ref = bf16[16,192,256]{2,1,0:T(8,128)(2,1)S(1)} all-to-all(bf16[16,192,256]{2,1,0:T(8,128)(2,1)S(1)} %pack.1), channel_id=1, replica_groups=mesh['y'=4,'z'=4,'x'=4,'c'=2] {'y','z'}, dimensions={0} | all-to-all | bytes 3145728 | tf_op jit(solution)/shard_map/all_to_all | solution.py:488
  95.7 1.1 slice.8
  96.7 1.4 copy.13
  98.2 1.5 select_n.23
  99.7 1.3 broadcast_in_dim.15.bias_ref
  101.1 12.9 %attention.1 = (bf16[16,128,256]{2,1,0:T(8,128)(2,1)S(1)}, bf16[16,128,256]{2,1,0:T(8,128)(2,1)S(1)}, bf16[16,64,256]{2,1,0:T(8,128)(2,1)S(1)}) custom-call(f32[2,2048,128]{2,1,0:T(8,128)S(1)} %broadcast_in_dim.15.bias_ref, bf16[16,192,256]{2,1,0:T(8,128)(2,1)S(1)} %all_to_all.10.mine_ref, bf16[16,128,256]{2,1,0:T(8,128)(2,1)} %collective-permute-done.15.theirs_ref), custom_call_target="tpu_custom_call" | custom-call | flops 12000000000 | bytes 36000000 | tf_op jit(solution)/shard_map/attention/pallas_call | solution.py:37
  114.0 0.6 collective-permute-start.16
  114.6 2.3 %collective-permute-done.16.got_ref = bf16[16,128,256]{2,1,0:T(8,128)(2,1)S(1)} collective-permute-done((bf16[16,128,256]{2,1,0:T(8,128)(2,1)S(1)}, bf16[16,128,256]{2,1,0:T(8,128)(2,1)S(1)}, u32[]{:S(2)}, u32[]{:S(2)}) %collective-permute-start.16) | collective-permute-done | bytes 1048608 | tf_op jit(solution)/shard_map/ppermute | solution.py:56
  116.9 0.3 return.1
  117.2 27.0 %all_to_all.11.in_ref = bf16[16,192,256]{2,1,0:T(8,128)(2,1)S(1)} all-to-all(bf16[16,192,256]{2,1,0:T(8,128)(2,1)S(1)} %return.1), channel_id=1, replica_groups=mesh['y'=4,'z'=4,'x'=4,'c'=2] {'y','z'}, dimensions={0} | all-to-all | bytes 3145728 | tf_op jit(solution)/shard_map/all_to_all | solution.py:491
  144.4 1.9 %collective-permute-done.17.got_ref = bf16[4,256,256]{2,1,0:T(8,128)(2,1)S(1)} collective-permute-done((bf16[4,256,256]{2,1,0:T(8,128)(2,1)S(1)}, bf16[4,256,256]{2,1,0:T(8,128)(2,1)S(1)}, u32[]{:S(2)}, u32[]{:S(2)}) %collective-permute-start.17) | collective-permute-done | bytes 524320 | tf_op jit(solution)/shard_map/ppermute | solution.py:56
  146.3 3.2 %outputs.2 = (bf16[1,512,512]{2,1,0:T(8,128)(2,1)S(1)}, bf16[1,512,512]{2,1,0:T(8,128)(2,1)S(1)}, bf16[3,512,512]{2,1,0:T(8,128)(2,1)S(1)}) custom-call(bf16[4,256,256]{2,1,0:T(8,128)(2,1)S(1)} %get-tuple-element.51.keep_ref, bf16[4,256,256]{2,1,0:T(8,128)(2,1)S(1)} %collective-permute-done.17.got_ref, bf16[256,512]{1,0:T(8,128)(2,1)S(1)} %get-tuple-element.53.refs_0_, ...), custom_call_target="tpu_custom_call" | custom-call | flops 2000000000 | bytes 6000000 | tf_op jit(solution)/shard_map/outputs/pallas_call | solution.py:37
  149.8 1.8 %collective-permute-done.18.other_ref = bf16[1,512,512]{2,1,0:T(8,128)(2,1)S(1)} collective-permute-done((bf16[1,512,512]{2,1,0:T(8,128)(2,1)S(1)}, bf16[1,512,512]{2,1,0:T(8,128)(2,1)S(1)}, u32[]{:S(2)}, u32[]{:S(2)}) %collective-permute-start.18) | collective-permute-done | bytes 524320 | tf_op jit(solution)/shard_map/ppermute | solution.py:56
  151.9 2.2 %outputs.3.own_ref = bf16[3,512,512]{2,1,0:T(8,128)(2,1)S(1)} custom-call(bf16[4,256,256]{2,1,0:T(8,128)(2,1)S(1)} %get-tuple-element.51.keep_ref, bf16[4,256,256]{2,1,0:T(8,128)(2,1)S(1)} %collective-permute-done.17.got_ref, bf16[256,512]{1,0:T(8,128)(2,1)S(1)} %get-tuple-element.53.refs_0_, bf16[256,512]{1,0:T(8,128)(2,1)S(1)} %copy-done.11, ...), custom_call_target="tpu_custom_call" | custom-call | flops 2000000000 | bytes 6000000 | tf_op jit(solution)/shard_map/outputs/pallas_call | solution.py:37
  154.1 0.9 collective-permute-done.19.other_ref
  155.0 0.3 add.9
  155.4 6.9 %collective-permute-done.20.far_ref = bf16[512,512]{1,0:T(8,128)(2,1)S(1)} collective-permute-done((bf16[512,512]{1,0:T(8,128)(2,1)S(1)}, bf16[512,512]{1,0:T(8,128)(2,1)S(1)}, u32[]{:S(2)}, u32[]{:S(2)}) %collective-permute-start.20) | collective-permute-done | bytes 524320 | tf_op jit(solution)/shard_map/ppermute | solution.py:64
  162.5 5.4 %collective-permute-done.22 = bf16[512,512]{1,0:T(8,128)(2,1)S(1)} collective-permute-done((bf16[512,512]{1,0:T(8,128)(2,1)S(1)}, bf16[512,512]{1,0:T(8,128)(2,1)S(1)}, u32[]{:S(2)}, u32[]{:S(2)}) %collective-permute-start.22) | collective-permute-done | bytes 524320 | tf_op jit(solution)/shard_map/ppermute | solution.py:64
  167.9 5.6 %collective-permute-done.21.ahead_ref = bf16[512,512]{1,0:T(8,128)(2,1)S(1)} collective-permute-done((bf16[512,512]{1,0:T(8,128)(2,1)S(1)}, bf16[512,512]{1,0:T(8,128)(2,1)S(1)}, u32[]{:S(2)}, u32[]{:S(2)}) %collective-permute-start.21) | collective-permute-done | bytes 524320 | tf_op jit(solution)/shard_map/ppermute | solution.py:64
  173.5 1.1 final.1
  (82 shorter events, 2.4 us)
Async XLA Ops:
  0.6 27.4 %collective-permute-start.9 = (bf16[1280,512]{1,0:T(8,128)(2,1)}, bf16[1280,512]{1,0:T(8,128)(2,1)S(1)}, u32[]{:S(2)}, u32[]{:S(2)}) collective-permute-start(bf16[1280,512]{1,0:T(8,128)(2,1)} %w_ref.2), channel_id=1, source_target_pairs={{0,1},{1,0},{2,3},{3,2},{4,5},{5,4},{6,7},{7,6},{8,9},{9,8},{10,11... | collective-permute-start | bytes 3932168 | tf_op jit(solution)/shard_map/ppermute | solution.py:56
  0.7 3.6 %collective-permute-start.2 = (bf16[256,512]{1,0:T(8,128)(2,1)}, bf16[256,512]{1,0:T(8,128)(2,1)S(1)}, u32[]{:S(2)}, u32[]{:S(2)}) collective-permute-start(bf16[256,512]{1,0:T(8,128)(2,1)} %cot_ref.1), channel_id=1, source_target_pairs={{0,1},{1,0},{2,3},{3,2},{4,5},{5,4},{6,7},{7,6},{8,9},{9,8},{10,11... | collective-permute-start | bytes 786440 | tf_op jit(solution)/shard_map/ppermute | solution.py:56
  1.2 10.6 %collective-permute-start.1 = (bf16[256,512]{1,0:T(8,128)(2,1)}, bf16[256,512]{1,0:T(8,128)(2,1)S(1)}, u32[]{:S(2)}, u32[]{:S(2)}) collective-permute-start(bf16[256,512]{1,0:T(8,128)(2,1)} %cot_ref.1), channel_id=1, source_target_pairs={{0,2},{1,7},{2,4},{3,1},{4,6},{5,3},{6,0},{7,5},{8,10},{9,15},{10,... | collective-permute-start | bytes 786440 | tf_op jit(solution)/shard_map/ppermute | solution.py:64
  4.3 3.8 %copy-start.25 = (bf16[256,512]{1,0:T(8,128)(2,1)}, bf16[256,512]{1,0:T(8,128)(2,1)S(1)}, u32[]{:S(2)}) copy-start(bf16[256,512]{1,0:T(8,128)(2,1)S(1)} %collective-permute-done.2.refs_1_) | copy-start | bytes 786436
  4.3 7.6 %collective-permute-start.3 = (bf16[256,512]{1,0:T(8,128)(2,1)S(1)}, bf16[256,512]{1,0:T(8,128)(2,1)S(1)}, u32[]{:S(2)}, u32[]{:S(2)}) collective-permute-start(bf16[256,512]{1,0:T(8,128)(2,1)S(1)} %collective-permute-done.2.refs_1_), channel_id=1, source_target_pairs={{0,2},{1,7},{2,4},{3,1},{4,6},{5,3},{6,0},{7,5},{8,10},{9,15},{10,... | collective-permute-start | bytes 786440 | tf_op jit(solution)/shard_map/ppermute | solution.py:64
  8.1 3.7 %collective-permute-start = (f32[1,1280]{1,0:T(1,128)S(1)}, f32[1,1280]{1,0:T(1,128)S(1)}, u32[]{:S(2)}, u32[]{:S(2)}) collective-permute-start(f32[1,1280]{1,0:T(1,128)S(1)} %get-tuple-element.35), channel_id=1, source_target_pairs={{1,0},{2,1},{3,2},{4,3},{5,4},{6,5},{7,6},{8,7},{9,8},{10,9},{11,1... | collective-permute-start | bytes 15368 | tf_op jit(solution)/shard_map/ppermute | solution.py:447
  11.8 30.0 %copy-start.21 = (bf16[256,512]{1,0:T(8,128)(2,1)}, bf16[256,512]{1,0:T(8,128)(2,1)S(1)}, u32[]{:S(2)}) copy-start(bf16[256,512]{1,0:T(8,128)(2,1)S(1)} %collective-permute-done.1.refs_2_) | copy-start | bytes 786436
  11.9 29.9 %copy-start.22 = (bf16[256,512]{1,0:T(8,128)(2,1)}, bf16[256,512]{1,0:T(8,128)(2,1)S(1)}, u32[]{:S(2)}) copy-start(bf16[256,512]{1,0:T(8,128)(2,1)S(1)} %collective-permute-done.3.refs_3_) | copy-start | bytes 786436
  11.9 17.3 %copy-start.19 = (bf16[1280,512]{1,0:T(8,128)(2,1)S(1)}, bf16[1280,512]{1,0:T(8,128)(2,1)}, u32[]{:S(2)}) copy-start(bf16[1280,512]{1,0:T(8,128)(2,1)} %w_ref.2) | copy-start | bytes 3932164
  12.1 5.2 %collective-permute-start.6 = (bf16[32,1280]{1,0:T(8,128)(2,1)S(1)}, bf16[32,1280]{1,0:T(8,128)(2,1)S(1)}, u32[]{:S(2)}, u32[]{:S(2)}) collective-permute-start(bf16[32,1280]{1,0:T(8,128)(2,1)S(1)} %patch.1), channel_id=1, source_target_pairs={{0,6},{2,0},{4,2},{6,4},{1,7},{3,1},{5,3},{7,5},{8,14},{10,8},{12,... | collective-permute-start | bytes 245768 | tf_op jit(solution)/shard_map/ppermute | solution.py:457
  13.8 5.9 %collective-permute-start.5 = (bf16[32,1280]{1,0:T(8,128)(2,1)S(1)}, bf16[32,1280]{1,0:T(8,128)(2,1)S(1)}, u32[]{:S(2)}, u32[]{:S(2)}) collective-permute-start(bf16[32,1280]{1,0:T(8,128)(2,1)S(1)} %patch.1), channel_id=1, source_target_pairs={{0,4},{2,6},{4,0},{6,2},{1,5},{3,7},{5,1},{7,3},{8,12},{10,14},{12... | collective-permute-start | bytes 245768 | tf_op jit(solution)/shard_map/ppermute | solution.py:457
  16.5 7.1 %collective-permute-start.4 = (bf16[32,1280]{1,0:T(8,128)(2,1)S(1)}, bf16[32,1280]{1,0:T(8,128)(2,1)S(1)}, u32[]{:S(2)}, u32[]{:S(2)}) collective-permute-start(bf16[32,1280]{1,0:T(8,128)(2,1)S(1)} %patch.1), channel_id=1, source_target_pairs={{0,2},{2,4},{4,6},{6,0},{1,3},{3,5},{5,7},{7,1},{8,10},{10,12},{12... | collective-permute-start | bytes 245768 | tf_op jit(solution)/shard_map/ppermute | solution.py:457
  16.5 9.9 %collective-permute-start.7 = (bf16[256,512]{1,0:T(8,128)(2,1)S(1)}, bf16[256,512]{1,0:T(8,128)(2,1)S(1)}, u32[]{:S(2)}, u32[]{:S(2)}) collective-permute-start(bf16[256,512]{1,0:T(8,128)(2,1)S(1)} %collective-permute-done.1.refs_2_), channel_id=1, source_target_pairs={{0,2},{1,7},{2,4},{3,1},{4,6},{5,3},{6,0},{7,5},{8,10},{9,15},{10,... | collective-permute-start | bytes 786440 | tf_op jit(solution)/shard_map/ppermute | solution.py:64
  26.4 15.4 %copy-start.23 = (bf16[256,512]{1,0:T(8,128)(2,1)}, bf16[256,512]{1,0:T(8,128)(2,1)S(1)}, u32[]{:S(2)}) copy-start(bf16[256,512]{1,0:T(8,128)(2,1)S(1)} %collective-permute-done.7.refs_4_) | copy-start | bytes 786436
  26.4 1.6 collective-permute-start.8
  31.3 24.8 %copy-start.8 = (bf16[2,256,512]{2,1,0:T(8,128)(2,1)}, bf16[2,256,512]{2,1,0:T(8,128)(2,1)S(1)}, u32[]{:S(2)}) copy-start(bf16[2,256,512]{2,1,0:T(8,128)(2,1)S(1)} %latent.1.refs_0_.refs_4_.lat_ref) | copy-start | bytes 1572868
  31.3 10.8 %copy-start.18 = (s32[128,32]{0,1:T(8,128)S(1)}, s32[128,32]{0,1:T(8,128)}, u32[]{:S(2)}) copy-start(s32[128,32]{0,1:T(8,128)} %param.10) | copy-start | bytes 49156
  31.3 10.5 %collective-permute-start.10 = (bf16[2,256,512]{2,1,0:T(8,128)(2,1)S(1)}, bf16[2,256,512]{2,1,0:T(8,128)(2,1)S(1)}, u32[]{:S(2)}, u32[]{:S(2)}) collective-permute-start(bf16[2,256,512]{2,1,0:T(8,128)(2,1)S(1)} %latent.1.refs_0_.refs_4_.lat_ref), channel_id=1, source_target_pairs={{0,2},{1,7},{2,4},{3,1},{4,6},{5,3},{6,0},{7,5},{8,10},{9,15},{10,... | collective-permute-start | bytes 1572872 | tf_op jit(solution)/shard_map/ppermute | solution.py:64
  41.9 8.9 %collective-permute-start.13 = (bf16[3,256,512]{2,1,0:T(8,128)(2,1)S(1)}, bf16[3,256,512]{2,1,0:T(8,128)(2,1)}, u32[]{:S(2)}, u32[]{:S(2)}) collective-permute-start(bf16[3,256,512]{2,1,0:T(8,128)(2,1)S(1)} %pad_maximum_fusion.1), channel_id=1, source_target_pairs={{0,1},{1,0},{2,3},{3,2},{4,5},{5,4},{6,7},{7,6},{8,9},{9,8},{10,11... | collective-permute-start | bytes 2359304 | tf_op jit(solution)/shard_map/ppermute | solution.py:56
  42.0 7.7 %collective-permute-start.11 = (bf16[1,256,512]{2,1,0:T(8,128)(2,1)S(1)}, bf16[1,256,512]{2,1,0:T(8,128)(2,1)S(1)}, u32[]{:S(2)}, u32[]{:S(2)}) collective-permute-start(bf16[1,256,512]{2,1,0:T(8,128)(2,1)S(1)} %slice.6), channel_id=1, source_target_pairs={{0,2},{1,7},{2,4},{3,1},{4,6},{5,3},{6,0},{7,5},{8,10},{9,15},{10,... | collective-permute-start | bytes 786440 | tf_op jit(solution)/shard_map/ppermute | solution.py:64
  50.6 5.5 %collective-permute-start.12 = (bf16[3,256,512]{2,1,0:T(8,128)(2,1)}, bf16[3,256,512]{2,1,0:T(8,128)(2,1)S(1)}, u32[]{:S(2)}, u32[]{:S(2)}) collective-permute-start(bf16[3,256,512]{2,1,0:T(8,128)(2,1)} %pad_maximum_fusion), channel_id=1, source_target_pairs={{0,1},{1,0},{2,3},{3,2},{4,5},{5,4},{6,7},{7,6},{8,9},{9,8},{10,11... | collective-permute-start | bytes 2359304 | tf_op jit(solution)/shard_map/ppermute | solution.py:56
  50.8 5.3 %copy-start.14 = (f32[256,1]{1,0:T(8,128)}, f32[256,1]{1,0:T(8,128)S(1)}, u32[]{:S(2)}) copy-start(f32[256,1]{1,0:T(8,128)S(1)} %copy.14.valid_ref) | copy-start | bytes 3076
  50.8 2.2 %copy-start = (bf16[512,4096]{1,0:T(8,128)(2,1)S(1)}, bf16[512,4096]{1,0:T(8,128)(2,1)}, u32[]{:S(2)}) copy-start(bf16[512,4096]{1,0:T(8,128)(2,1)} %refs_12_.3) | copy-start | bytes 12582916
  53.0 3.1 %copy-start.2 = (bf16[4096,512]{1,0:T(8,128)(2,1)S(1)}, bf16[4096,512]{1,0:T(8,128)(2,1)}, u32[]{:S(2)}) copy-start(bf16[4096,512]{1,0:T(8,128)(2,1)} %refs_9_.3) | copy-start | bytes 12582916
  53.0 4.1 %copy-start.4 = (bf16[4096,512]{1,0:T(8,128)(2,1)S(1)}, bf16[4096,512]{1,0:T(8,128)(2,1)}, u32[]{:S(2)}) copy-start(bf16[4096,512]{1,0:T(8,128)(2,1)} %refs_10_.3) | copy-start | bytes 12582916
  53.0 5.3 %copy-start.6 = (bf16[4096,512]{1,0:T(8,128)(2,1)S(1)}, bf16[4096,512]{1,0:T(8,128)(2,1)}, u32[]{:S(2)}) copy-start(bf16[4096,512]{1,0:T(8,128)(2,1)} %refs_11_.3) | copy-start | bytes 12582916
  53.0 5.3 %copy-start.16 = (f32[4096]{0:T(1024)S(1)}, f32[4096]{0:T(1024)}, u32[]{:S(2)}) copy-start(f32[4096]{0:T(1024)} %param.12) | copy-start | bytes 49156
  62.0 2.3 %copy-start.10 = (bf16[256,512]{1,0:T(8,128)(2,1)}, bf16[256,512]{1,0:T(8,128)(2,1)S(1)}, u32[]{:S(2)}) copy-start(bf16[256,512]{1,0:T(8,128)(2,1)S(1)} %get-tuple-element.54.refs_1_) | copy-start | bytes 786436
  62.0 2.3 %copy-start.12 = (bf16[256,512]{1,0:T(8,128)(2,1)}, bf16[256,512]{1,0:T(8,128)(2,1)S(1)}, u32[]{:S(2)}) copy-start(bf16[256,512]{1,0:T(8,128)(2,1)S(1)} %get-tuple-element.55.refs_2_) | copy-start | bytes 786436
  62.0 2.1 %collective-permute-start.14 = (bf16[4,256,256]{2,1,0:T(8,128)(2,1)S(1)}, bf16[4,256,256]{2,1,0:T(8,128)(2,1)S(1)}, u32[]{:S(2)}, u32[]{:S(2)}) collective-permute-start(bf16[4,256,256]{2,1,0:T(8,128)(2,1)S(1)} %get-tuple-element.47), channel_id=1, source_target_pairs={{0,1},{1,0},{2,3},{3,2},{4,5},{5,4},{6,7},{7,6},{8,9},{9,8},{10,11... | collective-permute-start | bytes 1572872 | tf_op jit(solution)/shard_map/ppermute | solution.py:56
  96.7 3.0 %collective-permute-start.15 = (bf16[16,128,256]{2,1,0:T(8,128)(2,1)}, bf16[16,128,256]{2,1,0:T(8,128)(2,1)}, u32[]{:S(2)}, u32[]{:S(2)}) collective-permute-start(bf16[16,128,256]{2,1,0:T(8,128)(2,1)} %slice.8), channel_id=1, source_target_pairs={{0,1},{1,0},{2,3},{3,2},{4,5},{5,4},{6,7},{7,6},{8,9},{9,8},{10,11... | collective-permute-start | bytes 3145736 | tf_op jit(solution)/shard_map/ppermute | solution.py:56
  101.1 45.2 %copy-start.5 = (bf16[4096,512]{1,0:T(8,128)(2,1)S(1)}, bf16[4096,512]{1,0:T(8,128)(2,1)}, u32[]{:S(2)}) copy-start(bf16[4096,512]{1,0:T(8,128)(2,1)} %refs_10_.3) | copy-start | bytes 12582916
  101.1 45.2 %copy-start.7 = (bf16[4096,512]{1,0:T(8,128)(2,1)S(1)}, bf16[4096,512]{1,0:T(8,128)(2,1)}, u32[]{:S(2)}) copy-start(bf16[4096,512]{1,0:T(8,128)(2,1)} %refs_11_.3) | copy-start | bytes 12582916
  114.0 2.9 %collective-permute-start.16 = (bf16[16,128,256]{2,1,0:T(8,128)(2,1)S(1)}, bf16[16,128,256]{2,1,0:T(8,128)(2,1)S(1)}, u32[]{:S(2)}, u32[]{:S(2)}) collective-permute-start(bf16[16,128,256]{2,1,0:T(8,128)(2,1)S(1)} %get-tuple-element.49), channel_id=1, source_target_pairs={{0,1},{1,0},{2,3},{3,2},{4,5},{5,4},{6,7},{7,6},{8,9},{9,8},{10,11... | collective-permute-start | bytes 3145736 | tf_op jit(solution)/shard_map/ppermute | solution.py:56
  116.9 29.4 %copy-start.3 = (bf16[4096,512]{1,0:T(8,128)(2,1)S(1)}, bf16[4096,512]{1,0:T(8,128)(2,1)}, u32[]{:S(2)}) copy-start(bf16[4096,512]{1,0:T(8,128)(2,1)} %refs_9_.3) | copy-start | bytes 12582916
  117.1 29.1 %copy-start.1 = (bf16[512,4096]{1,0:T(8,128)(2,1)S(1)}, bf16[512,4096]{1,0:T(8,128)(2,1)}, u32[]{:S(2)}) copy-start(bf16[512,4096]{1,0:T(8,128)(2,1)} %refs_12_.3) | copy-start | bytes 12582916
  144.1 2.1 %copy-start.9 = (bf16[2,256,512]{2,1,0:T(8,128)(2,1)S(1)}, bf16[2,256,512]{2,1,0:T(8,128)(2,1)}, u32[]{:S(2)}) copy-start(bf16[2,256,512]{2,1,0:T(8,128)(2,1)} %copy-done.8) | copy-start | bytes 1572868
  144.1 2.2 %copy-start.11 = (bf16[256,512]{1,0:T(8,128)(2,1)S(1)}, bf16[256,512]{1,0:T(8,128)(2,1)}, u32[]{:S(2)}) copy-start(bf16[256,512]{1,0:T(8,128)(2,1)} %copy-done.10) | copy-start | bytes 786436
  144.1 2.2 %copy-start.13 = (bf16[256,512]{1,0:T(8,128)(2,1)S(1)}, bf16[256,512]{1,0:T(8,128)(2,1)}, u32[]{:S(2)}) copy-start(bf16[256,512]{1,0:T(8,128)(2,1)} %copy-done.12) | copy-start | bytes 786436
  144.3 2.0 %collective-permute-start.17 = (bf16[4,256,256]{2,1,0:T(8,128)(2,1)S(1)}, bf16[4,256,256]{2,1,0:T(8,128)(2,1)S(1)}, u32[]{:S(2)}, u32[]{:S(2)}) collective-permute-start(bf16[4,256,256]{2,1,0:T(8,128)(2,1)S(1)} %get-tuple-element.52), channel_id=1, source_target_pairs={{0,1},{1,0},{2,3},{3,2},{4,5},{5,4},{6,7},{7,6},{8,9},{9,8},{10,11... | collective-permute-start | bytes 1572872 | tf_op jit(solution)/shard_map/ppermute | solution.py:56
  149.6 2.0 %collective-permute-start.18 = (bf16[1,512,512]{2,1,0:T(8,128)(2,1)S(1)}, bf16[1,512,512]{2,1,0:T(8,128)(2,1)S(1)}, u32[]{:S(2)}, u32[]{:S(2)}) collective-permute-start(bf16[1,512,512]{2,1,0:T(8,128)(2,1)S(1)} %get-tuple-element.57), channel_id=1, source_target_pairs={{0,1},{1,0},{2,3},{3,2},{4,5},{5,4},{6,7},{7,6},{8,9},{9,8},{10,11... | collective-permute-start | bytes 1572872 | tf_op jit(solution)/shard_map/ppermute | solution.py:56
  151.6 3.4 %collective-permute-start.19 = (bf16[3,512,512]{2,1,0:T(8,128)(2,1)S(1)}, bf16[3,512,512]{2,1,0:T(8,128)(2,1)S(1)}, u32[]{:S(2)}, u32[]{:S(2)}) collective-permute-start(bf16[3,512,512]{2,1,0:T(8,128)(2,1)S(1)} %get-tuple-element.61), channel_id=1, source_target_pairs={{0,1},{1,0},{2,3},{3,2},{4,5},{5,4},{6,7},{7,6},{8,9},{9,8},{10,11... | collective-permute-start | bytes 4718600 | tf_op jit(solution)/shard_map/ppermute | solution.py:56
  151.8 10.5 %collective-permute-start.20 = (bf16[512,512]{1,0:T(8,128)(2,1)S(1)}, bf16[512,512]{1,0:T(8,128)(2,1)S(1)}, u32[]{:S(2)}, u32[]{:S(2)}) collective-permute-start(bf16[512,512]{1,0:T(8,128)(2,1)S(1)} %far.1), channel_id=1, source_target_pairs={{0,2},{1,7},{2,4},{3,1},{4,6},{5,3},{6,0},{7,5},{8,10},{9,15},{10,... | collective-permute-start | bytes 1572872 | tf_op jit(solution)/shard_map/ppermute | solution.py:64
  155.3 12.6 %collective-permute-start.22 = (bf16[512,512]{1,0:T(8,128)(2,1)S(1)}, bf16[512,512]{1,0:T(8,128)(2,1)S(1)}, u32[]{:S(2)}, u32[]{:S(2)}) collective-permute-start(bf16[512,512]{1,0:T(8,128)(2,1)S(1)} %get-tuple-element.65), channel_id=1, source_target_pairs={{0,2},{1,7},{2,4},{3,1},{4,6},{5,3},{6,0},{7,5},{8,10},{9,15},{10,... | collective-permute-start | bytes 1572872 | tf_op jit(solution)/shard_map/ppermute | solution.py:64
  162.3 11.2 %copy-start.15 = (f32[256,1]{1,0:T(8,128)S(1)}, f32[256,1]{1,0:T(8,128)}, u32[]{:S(2)}) copy-start(f32[256,1]{1,0:T(8,128)} %copy-done.14) | copy-start | bytes 3076
  162.3 11.2 %copy-start.20 = (bf16[256,512]{1,0:T(8,128)(2,1)S(1)}, bf16[256,512]{1,0:T(8,128)(2,1)}, u32[]{:S(2)}) copy-start(bf16[256,512]{1,0:T(8,128)(2,1)} %cot_ref.1) | copy-start | bytes 786436
  162.4 11.1 %collective-permute-start.21 = (bf16[512,512]{1,0:T(8,128)(2,1)S(1)}, bf16[512,512]{1,0:T(8,128)(2,1)S(1)}, u32[]{:S(2)}, u32[]{:S(2)}) collective-permute-start(bf16[512,512]{1,0:T(8,128)(2,1)S(1)} %pass.1), channel_id=1, source_target_pairs={{0,2},{1,7},{2,4},{3,1},{4,6},{5,3},{6,0},{7,5},{8,10},{9,15},{10,... | collective-permute-start | bytes 1572872 | tf_op jit(solution)/shard_map/ppermute | solution.py:64
  167.9 5.6 %collective-permute-start.23 = (bf16[512,512]{1,0:T(8,128)(2,1)S(1)}, bf16[512,512]{1,0:T(8,128)(2,1)S(1)}, u32[]{:S(2)}, u32[]{:S(2)}) collective-permute-start(bf16[512,512]{1,0:T(8,128)(2,1)S(1)} %collective-permute-done.22), channel_id=1, source_target_pairs={{0,1},{1,0},{2,3},{3,2},{4,5},{5,4},{6,7},{7,6},{8,9},{9,8},{10,11... | collective-permute-start | bytes 1572872 | tf_op jit(solution)/shard_map/ppermute | solution.py:56
  (2 other events, 1.8 us)

commit v7 on v5

--- a/solution.py
+++ b/solution.py
@@ -131,24 +131,18 @@
 
 
 def in_order(refs):
-    pair, both, far, theirs = refs
-    a, b, f = (theirs.at[n] for n in range(3))
-    return [pair.at[0], pair.at[1], both.at[0], both.at[1], a, b, far.at[0], f]
+    pair, both, far, their_both, their_far = refs
+    theirs = [their_both.at[0], their_both.at[1]]
+    return [pair.at[0], pair.at[1], both.at[0], both.at[1], *theirs, far.at[0], their_far.at[0]]
 
 
 def piece_rows(ref, at, size):
     return ref[pl.ds(pl.multiple_of(at * size, size), size), :]
 
 
-def project_kernel(*refs):
-    pieces, (do_ref, gain_ref), weights = in_order(refs[:4]), refs[4:6], refs[6:9]
-    outs, (accs, heads) = refs[9:15], refs[15:17]
-    keep_ref, send_ref, qkv_refs, rinv_ref = outs[0], outs[1], outs[2:5], outs[5]
-    rows, size = pieces[0].shape
-    width = gain_ref.shape[1]
-    c = place("c")
-    square = jnp.zeros((rows, 128), F32)
-    for n, (piece, at) in enumerate(zip(pieces, tp_places())):
+def add_products(pieces, places, gain_ref, weights, accs, square, first):
+    size = pieces[0].shape[1]
+    for n, (piece, at) in enumerate(zip(pieces, places)):
         wide = piece[...].astype(F32)
         squares = wide * wide
         for part in range(0, size, 128):
@@ -158,7 +152,39 @@
         for kind in range(3):
             w = piece_rows(weights[kind], at, size)
             made = jnp.dot(scaled, w, preferred_element_type=F32)
-            accs[kind] = made if n == 0 else accs[kind] + made
+            accs[kind] = made if first and n == 0 else accs[kind] + made
+    return square
+
+
+def near_kernel(pair_ref, both_ref, gain_ref, wq_ref, wk_ref, wv_ref, accs, square_ref):
+    pieces = [pair_ref.at[0], pair_ref.at[1], both_ref.at[0], both_ref.at[1]]
+    square = jnp.zeros(square_ref.shape, F32)
+    weights = (wq_ref, wk_ref, wv_ref)
+    square_ref[...] = add_products(pieces, tp_places()[:4], gain_ref, weights, accs, square, True)
+
+
+def near_part(pair, both, gain, weights):
+    rows, size = pair.shape[1:]
+    return call(
+        near_kernel,
+        (pair, both, gain, *weights),
+        [shape(3, rows, size, dtype=F32), shape(rows, 128, dtype=F32)],
+        name="project_near",
+        megabytes=20,
+        micros=2.0,
+    )
+
+
+def project_kernel(far_ref, their_both, their_far, given, square_ref, do_ref, gain_ref, *refs):
+    weights, outs, (accs, heads) = refs[:3], refs[3:9], refs[9:11]
+    keep_ref, send_ref, qkv_refs, rinv_ref = outs[0], outs[1], outs[2:5], outs[5]
+    rows, size = do_ref.shape
+    width = gain_ref.shape[1]
+    c = place("c")
+    pieces = [their_both.at[0], their_both.at[1], far_ref.at[0], their_far.at[0]]
+    accs[...] = given[...]
+    square = square_ref[...]
+    square = add_products(pieces, tp_places()[4:], gain_ref, weights, accs, square, False)
     total = jnp.sum(square, axis=1, keepdims=True)
     rinv = lax.rsqrt(total / width + EPS)
     rinv_ref[...] = rinv
@@ -179,17 +205,17 @@
             out[h, half:, HEAD:] = heads[12 + h, span, :]
 
 
-def project(pieces, d_attn, gain, weights):
-    rows, size = pieces[0].shape[1:]
+def project(far, theirs, near, d_attn, gain, weights):
+    rows, size = d_attn.shape
     both = shape(4, rows, 2 * HEAD)
     return call(
         project_kernel,
-        (*pieces, d_attn, gain, *weights),
+        (far, *theirs, *near, d_attn, gain, *weights),
         [both, both] + [shape(rows, size)] * 3 + [shape(rows, 1, dtype=F32)],
         [pltpu.VMEM((3, rows, size), F32), pltpu.VMEM((16, rows, HEAD), BF16)],
         name="project",
         megabytes=24,
-        micros=5.0,
+        micros=3.0,
     )
 
 
@@ -337,8 +363,8 @@
 
 
 def output_kernel(which, keep_ref, got_ref, *refs):
-    qkv, rinv_ref, lats, gain_ref = refs[:3], refs[3], in_order(refs[4:8]), refs[8]
-    weights, w_out_ref, outs, wide = refs[9:12], refs[12], refs[13:-1], refs[-1]
+    qkv, rinv_ref, lats, gain_ref = refs[:3], refs[3], in_order(refs[4:9]), refs[9]
+    weights, w_out_ref, outs, wide = refs[10:13], refs[13], refs[14:-1], refs[-1]
     rows, size = qkv[0].shape
     width = gain_ref.shape[1]
     half = rows // 2
@@ -462,9 +488,12 @@
     d_attn = d_attn_of(cots, valid, w_out)
     lat_both, d_attn, bias = lax.optimization_barrier((lat_both, d_attn, bias))
     lat_far = along_x(lat_both[:1])
-    theirs = other_core(jnp.concatenate([lat_both, lat_far]))
-    pieces = [pair, lat_both, lat_far, theirs]
-    keep, send, *qkv, rinv = project(pieces, d_attn, gain, weights)
+    their_both = other_core(lat_both)
+    near = near_part(pair, lat_both, gain, weights)
+    lat_far, near, their_both = lax.optimization_barrier((lat_far, near, their_both))
+    theirs = (their_both, other_core(lat_far))
+    pieces = [pair, lat_both, lat_far, *theirs]
+    keep, send, *qkv, rinv = project(lat_far, theirs, near, d_attn, gain, weights)
     half = rows // 2
     packed = shape(shards // 8, half + half // 2, 2 * HEAD)
     sent = call(pack_kernel, (keep, other_core(send)), [packed], name="pack")[0]

time: 164 us -> 161 us (0.982)
  waiting for transfers between devices: 59.1 us -> 56.4 us
    ppermute x8, waiting for transfers between devices: 38.1 us -> 36.3 us  [along_x(): return lax.ppermute(block, XC, route)]
    ppermute x12 -> x13, waiting for transfers between devices: 13.8 us -> 13 us  [other_core(): return lax.ppermute(block, 'c', [(0, 1), (1, 0)])]
    pallas_call x15 -> x16, Pallas kernels: 29.8 us -> 30 us  [call(): pl.pallas_call(kernel, in_specs=[VMEM] * (len(ins) - stay) + [pl.BlockSpe...]
  transfers between devices with their start and end apart: 24 -> 25, of which waited for: 18 -> 18; matrix products, arithmetic and copies ran while one was open for 1% -> 1% of each run, Pallas kernels for 6% -> 7%
where the time goes in v7:
time: 161 us
  blocking collectives  57.7 us (36%)
  waiting for transfers between devices  56.4 us (35%)
  Pallas kernels  30 us (19%)
  starting transfers between devices  12.1 us (8%)
  local copies, waits for them, and re-layouts  2.83 us (2%)
    ppermute x8, waiting for transfers between devices, along_x(): return lax.ppermute(block, XC, route)  36.3 us
    all_to_all x1, blocking collectives, per_device(): mine = lax.all_to_all(sent, SEQ, 0, 0, tiled=True)  31.2 us
    pallas_call x16, Pallas kernels, call(): pl.pallas_call(kernel, in_specs=[VMEM] * (len(ins) - stay) + [pl.BlockSpe...  30 us
    all_to_all x1, blocking collectives, per_device(): back = lax.all_to_all(back, SEQ, 0, 0, tiled=True)  26.6 us
    ppermute x13, waiting for transfers between devices, other_core(): return lax.ppermute(block, 'c', [(0, 1), (1, 0)])  13 us
    ppermute x3, waiting for transfers between devices, per_device(): lax.ppermute(patches, 'x', [(i, (i + k) % 4) for i in range(4)])  4.73 us
    ppermute x3, starting transfers between devices, per_device(): lax.ppermute(patches, 'x', [(i, (i + k) % 4) for i in range(4)])  4.36 us
    ppermute x8, starting transfers between devices, along_x(): return lax.ppermute(block, XC, route)  4.31 us
  transfers between devices with their start and end apart: 25, of which 18 were waited for; matrix products, arithmetic and copies ran while one was open for 1% of the time, Pallas kernels for 7%

profile of v7, /device:TPU:0, one launch (start us, length us, event | category | flops | bytes accessed | tf_op | source)
XLA Modules:
  0.0 161.2 jit_solution(9538800083881755204)
XLA Ops:
  0.7 0.5 collective-permute-start.2
  1.2 1.6 collective-permute-start.1
  2.8 0.7 copy-done.6
  3.5 1.5 pool.1
  5.0 1.3 collective-permute-start
  6.3 2.3 %collective-permute-done.next_ref = f32[1,1280]{1,0:T(1,128)S(1)} collective-permute-done((f32[1,1280]{1,0:T(1,128)S(1)}, f32[1,1280]{1,0:T(1,128)S(1)}, u32[]{:S(2)}, u32[]{:S(2)}) %collective-permute-start) | collective-permute-done | bytes 5152 | tf_op jit(solution)/shard_map/ppermute | solution.py:462
  8.7 0.2 patch.1
  9.0 1.6 %collective-permute-start.5 = (bf16[32,1280]{1,0:T(8,128)(2,1)S(1)}, bf16[32,1280]{1,0:T(8,128)(2,1)S(1)}, u32[]{:S(2)}, u32[]{:S(2)}) collective-permute-start(bf16[32,1280]{1,0:T(8,128)(2,1)S(1)} %patch.1), channel_id=1, source_target_pairs={{0,6},{2,0},{4,2},{6,4},{1,7},{3,1},{5,3},{7,5},{8,14},{10,8},{12,... | collective-permute-start | bytes 245768 | tf_op jit(solution)/shard_map/ppermute | solution.py:472
  10.6 2.7 %collective-permute-start.4 = (bf16[32,1280]{1,0:T(8,128)(2,1)S(1)}, bf16[32,1280]{1,0:T(8,128)(2,1)S(1)}, u32[]{:S(2)}, u32[]{:S(2)}) collective-permute-start(bf16[32,1280]{1,0:T(8,128)(2,1)S(1)} %patch.1), channel_id=1, source_target_pairs={{0,4},{2,6},{4,0},{6,2},{1,5},{3,7},{5,1},{7,3},{8,12},{10,14},{12... | collective-permute-start | bytes 245768 | tf_op jit(solution)/shard_map/ppermute | solution.py:472
  13.4 0.8 collective-permute-start.6
  14.1 1.6 collective-permute-start.10
  15.7 0.8 collective-permute-done.4
  16.6 3.9 %collective-permute-done.3 = bf16[32,1280]{1,0:T(8,128)(2,1)S(1)} collective-permute-done((bf16[32,1280]{1,0:T(8,128)(2,1)S(1)}, bf16[32,1280]{1,0:T(8,128)(2,1)S(1)}, u32[]{:S(2)}, u32[]{:S(2)}) %collective-permute-start.3) | collective-permute-done | bytes 81952 | tf_op jit(solution)/shard_map/ppermute | solution.py:472
  20.5 2.8 %collective-permute-done.6.refs_4_ = bf16[256,512]{1,0:T(8,128)(2,1)S(1)} collective-permute-done((bf16[256,512]{1,0:T(8,128)(2,1)S(1)}, bf16[256,512]{1,0:T(8,128)(2,1)S(1)}, u32[]{:S(2)}, u32[]{:S(2)}) %collective-permute-start.6) | collective-permute-done | bytes 262176 | tf_op jit(solution)/shard_map/ppermute | solution.py:63
  23.5 2.5 %collective-permute-done.10.refs_3_ = bf16[256,512]{1,0:T(8,128)(2,1)S(1)} collective-permute-done((bf16[256,512]{1,0:T(8,128)(2,1)S(1)}, bf16[256,512]{1,0:T(8,128)(2,1)S(1)}, u32[]{:S(2)}, u32[]{:S(2)}) %collective-permute-start.10) | collective-permute-done | bytes 262176 | tf_op jit(solution)/shard_map/ppermute | solution.py:63
  26.1 0.7 copy-done.12
  26.8 1.0 pad_maximum_fusion
  28.3 2.3 %latent.1.pair_ref.refs_4_.lat_ref = bf16[2,256,512]{2,1,0:T(8,128)(2,1)S(1)} custom-call(bf16[4,32,1280]{2,1,0:T(8,128)(2,1)S(1)} %pad_maximum_fusion.1.own_ref, bf16[4,32,1280]{2,1,0:T(8,128)(2,1)S(1)} %collective-permute-done.7.other_ref, bf16[1280,512]{1,0:T(8,128)(2,1)S(1)} %copy-done.8, bf16[1280,512]{1,0:T(8,128)(2,1)} %collective-permute-done.8.sibling_w_ref), custom_call_target="tpu_custom_call" | custom-call | flops 8000000000 | bytes 24000000 | tf_op jit(solution)/shard_map/latent/pallas_call | solution.py:36
  30.9 3.1 %d_attn.1.do_ref = bf16[256,512]{1,0:T(8,128)(2,1)S(1)} custom-call(f32[256,1]{1,0:T(8,128)S(1)} %copy.14.valid_ref, bf16[512,4096]{1,0:T(8,128)(2,1)S(1)} %copy-done.3, bf16[256,512]{1,0:T(8,128)(2,1)} %cot_ref.1, bf16[256,512]{1,0:T(8,128)(2,1)} %copy-done.13, bf16[256,512]{1,0:T(8,128)(2,1)} %copy-done.10, bf16[256,512]{1,0:T(8,128)(2,1)} %copy-done.12, ...), custom_call_target="tpu_custom_call" | custom-call | flops 8000000000 | bytes 24000000 | tf_op jit(solution)/shard_map/d_attn/pallas_call | solution.py:36
  34.0 7.2 %collective-permute-done.9.both_ref.refs_5_ = bf16[2,256,512]{2,1,0:T(8,128)(2,1)S(1)} collective-permute-done((bf16[2,256,512]{2,1,0:T(8,128)(2,1)S(1)}, bf16[2,256,512]{2,1,0:T(8,128)(2,1)S(1)}, u32[]{:S(2)}, u32[]{:S(2)}) %collective-permute-start.9) | collective-permute-done | bytes 524320 | tf_op jit(solution)/shard_map/ppermute | solution.py:63
  41.2 0.6 broadcast_in_dim.15.bias_ref
  42.0 1.8 %project_near.1 = (f32[3,256,512]{2,1,0:T(8,128)S(1)}, f32[256,128]{1,0:T(8,128)S(1)}) custom-call(bf16[2,256,512]{2,1,0:T(8,128)(2,1)S(1)} %latent.1.pair_ref.refs_4_.lat_ref, bf16[2,256,512]{2,1,0:T(8,128)(2,1)S(1)} %collective-permute-done.9.both_ref.refs_5_, f32[1,4096]{1,0:T(1,128)S(1)} %bitcast.14, bf16[4096,512]{1,0:T(8,128)(2,1)S(1)} %copy-done, ...), custom_call_target="tpu_custom_call" | custom-call | flops 2000000000 | bytes 6000000 | tf_op jit(solution)/shard_map/project_near/pallas_call | solution.py:36
  43.8 5.7 %collective-permute-done.12.far_ref.refs_6_ = bf16[1,256,512]{2,1,0:T(8,128)(2,1)S(1)} collective-permute-done((bf16[1,256,512]{2,1,0:T(8,128)(2,1)S(1)}, bf16[1,256,512]{2,1,0:T(8,128)(2,1)S(1)}, u32[]{:S(2)}, u32[]{:S(2)}) %collective-permute-start.12) | collective-permute-done | bytes 262176 | tf_op jit(solution)/shard_map/ppermute | solution.py:63
  49.5 1.5 collective-permute-done.14.their_far.refs_8_
  51.1 2.1 %project.1 = (bf16[4,256,256]{2,1,0:T(8,128)(2,1)S(1)}, bf16[4,256,256]{2,1,0:T(8,128)(2,1)S(1)}, bf16[256,512]{1,0:T(8,128)(2,1)S(1)}, bf16[256,512]{1,0:T(8,12...) custom-call(bf16[1,256,512]{2,1,0:T(8,128)(2,1)S(1)} %collective-permute-done.12.far_ref.refs_6_, ...), custom_call_target="tpu_custom_call" | custom-call | flops 3000000000 | bytes 9000000 | tf_op jit(solution)/shard_map/project/pallas_call | solution.py:36
  53.1 0.2 collective-permute-start.15
  53.4 1.8 %collective-permute-done.15.got_ref = bf16[4,256,256]{2,1,0:T(8,128)(2,1)S(1)} collective-permute-done((bf16[4,256,256]{2,1,0:T(8,128)(2,1)S(1)}, bf16[4,256,256]{2,1,0:T(8,128)(2,1)S(1)}, u32[]{:S(2)}, u32[]{:S(2)}) %collective-permute-start.15) | collective-permute-done | bytes 524320 | tf_op jit(solution)/shard_map/ppermute | solution.py:55
  55.2 31.2 %all_to_all.10.mine_ref = bf16[16,192,256]{2,1,0:T(8,128)(2,1)S(1)} all-to-all(bf16[16,192,256]{2,1,0:T(8,128)(2,1)S(1)} %pack.1), channel_id=1, replica_groups=mesh['y'=4,'z'=4,'x'=4,'c'=2] {'y','z'}, dimensions={0} | all-to-all | bytes 3145728 | tf_op jit(solution)/shard_map/all_to_all | solution.py:500
  86.5 0.3 collective-permute-start.16
  86.8 2.6 %collective-permute-done.16.theirs_ref = bf16[16,128,256]{2,1,0:T(8,128)(2,1)S(1)} collective-permute-done((bf16[16,128,256]{2,1,0:T(8,128)(2,1)S(1)}, bf16[16,128,256]{2,1,0:T(8,128)(2,1)S(1)}, u32[]{:S(2)}, u32[]{:S(2)}) %collective-permute-start.16) | collective-permute-done | bytes 1048608 | tf_op jit(solution)/shard_map/ppermute | solution.py:55
  89.4 11.6 %attention.1 = (bf16[16,128,256]{2,1,0:T(8,128)(2,1)S(1)}, bf16[16,128,256]{2,1,0:T(8,128)(2,1)S(1)}, bf16[16,64,256]{2,1,0:T(8,128)(2,1)S(1)}) custom-call(f32[2,2048,128]{2,1,0:T(8,128)S(1)} %broadcast_in_dim.15.bias_ref, bf16[16,192,256]{2,1,0:T(8,128)(2,1)S(1)} %all_to_all.10.mine_ref, bf16[16,128,256]{2,1,0:T(8,128)(2,1)S(1)} %collective-permute-done.16.theirs_ref), custom_call_target="tpu_custom_call" | custom-call | flops 12000000000 | bytes 36000000 | tf_op jit(solution)/shard_map/attention/pallas_call | solution.py:36
  101.0 0.2 collective-permute-start.17
  101.2 2.5 %collective-permute-done.17.got_ref = bf16[16,128,256]{2,1,0:T(8,128)(2,1)S(1)} collective-permute-done((bf16[16,128,256]{2,1,0:T(8,128)(2,1)S(1)}, bf16[16,128,256]{2,1,0:T(8,128)(2,1)S(1)}, u32[]{:S(2)}, u32[]{:S(2)}) %collective-permute-start.17) | collective-permute-done | bytes 1048608 | tf_op jit(solution)/shard_map/ppermute | solution.py:55
  103.7 0.3 return.1
  104.0 26.6 %all_to_all.11.in_ref = bf16[16,192,256]{2,1,0:T(8,128)(2,1)S(1)} all-to-all(bf16[16,192,256]{2,1,0:T(8,128)(2,1)S(1)} %return.1), channel_id=1, replica_groups=mesh['y'=4,'z'=4,'x'=4,'c'=2] {'y','z'}, dimensions={0} | all-to-all | bytes 3145728 | tf_op jit(solution)/shard_map/all_to_all | solution.py:503
  130.7 0.3 collective-permute-start.18
  131.0 1.9 %collective-permute-done.18.got_ref = bf16[4,256,256]{2,1,0:T(8,128)(2,1)S(1)} collective-permute-done((bf16[4,256,256]{2,1,0:T(8,128)(2,1)S(1)}, bf16[4,256,256]{2,1,0:T(8,128)(2,1)S(1)}, u32[]{:S(2)}, u32[]{:S(2)}) %collective-permute-start.18) | collective-permute-done | bytes 524320 | tf_op jit(solution)/shard_map/ppermute | solution.py:55
  132.9 3.2 %outputs.2 = (bf16[1,512,512]{2,1,0:T(8,128)(2,1)S(1)}, bf16[1,512,512]{2,1,0:T(8,128)(2,1)S(1)}, bf16[3,512,512]{2,1,0:T(8,128)(2,1)S(1)}) custom-call(bf16[4,256,256]{2,1,0:T(8,128)(2,1)S(1)} %get-tuple-element.61.keep_ref, bf16[4,256,256]{2,1,0:T(8,128)(2,1)S(1)} %collective-permute-done.18.got_ref, bf16[256,512]{1,0:T(8,128)(2,1)S(1)} %get-tuple-element.63.refs_0_, ...), custom_call_target="tpu_custom_call" | custom-call | flops 2000000000 | bytes 6000000 | tf_op jit(solution)/shard_map/outputs/pallas_call | solution.py:36
  136.2 0.2 collective-permute-start.19
  136.4 1.8 %collective-permute-done.19.other_ref = bf16[1,512,512]{2,1,0:T(8,128)(2,1)S(1)} collective-permute-done((bf16[1,512,512]{2,1,0:T(8,128)(2,1)S(1)}, bf16[1,512,512]{2,1,0:T(8,128)(2,1)S(1)}, u32[]{:S(2)}, u32[]{:S(2)}) %collective-permute-start.19) | collective-permute-done | bytes 524320 | tf_op jit(solution)/shard_map/ppermute | solution.py:55
  138.1 0.1 collective-permute-start.20
  138.5 2.2 %outputs.3.own_ref = bf16[3,512,512]{2,1,0:T(8,128)(2,1)S(1)} custom-call(bf16[4,256,256]{2,1,0:T(8,128)(2,1)S(1)} %get-tuple-element.61.keep_ref, bf16[4,256,256]{2,1,0:T(8,128)(2,1)S(1)} %collective-permute-done.18.got_ref, bf16[256,512]{1,0:T(8,128)(2,1)S(1)} %get-tuple-element.63.refs_0_, bf16[256,512]{1,0:T(8,128)(2,1)S(1)} %get-tuple-element.64.refs_1_, ...), custom_call_target="tpu_custom_call" | custom-call | flops 2000000000 | bytes 6000000 | tf_op jit(solution)/shard_map/outputs/pallas_call | solution.py:36
  140.7 0.9 collective-permute-done.20.other_ref
  141.6 0.3 add.9
  142.0 6.9 %collective-permute-done.21.far_ref = bf16[512,512]{1,0:T(8,128)(2,1)S(1)} collective-permute-done((bf16[512,512]{1,0:T(8,128)(2,1)S(1)}, bf16[512,512]{1,0:T(8,128)(2,1)S(1)}, u32[]{:S(2)}, u32[]{:S(2)}) %collective-permute-start.21) | collective-permute-done | bytes 524320 | tf_op jit(solution)/shard_map/ppermute | solution.py:63
  149.0 5.4 %collective-permute-done.23 = bf16[512,512]{1,0:T(8,128)(2,1)S(1)} collective-permute-done((bf16[512,512]{1,0:T(8,128)(2,1)S(1)}, bf16[512,512]{1,0:T(8,128)(2,1)S(1)}, u32[]{:S(2)}, u32[]{:S(2)}) %collective-permute-start.23) | collective-permute-done | bytes 524320 | tf_op jit(solution)/shard_map/ppermute | solution.py:63
  154.5 5.6 %collective-permute-done.22.ahead_ref = bf16[512,512]{1,0:T(8,128)(2,1)S(1)} collective-permute-done((bf16[512,512]{1,0:T(8,128)(2,1)S(1)}, bf16[512,512]{1,0:T(8,128)(2,1)S(1)}, u32[]{:S(2)}, u32[]{:S(2)}) %collective-permute-start.22) | collective-permute-done | bytes 524320 | tf_op jit(solution)/shard_map/ppermute | solution.py:63
  160.1 1.1 final.1
  (60 shorter events, 2.1 us)
Async XLA Ops:
  0.6 27.7 %collective-permute-start.8 = (bf16[1280,512]{1,0:T(8,128)(2,1)}, bf16[1280,512]{1,0:T(8,128)(2,1)}, u32[]{:S(2)}, u32[]{:S(2)}) collective-permute-start(bf16[1280,512]{1,0:T(8,128)(2,1)} %w_ref.2), channel_id=1, source_target_pairs={{0,1},{1,0},{2,3},{3,2},{4,5},{5,4},{6,7},{7,6},{8,9},{9,8},{10,11... | collective-permute-start | bytes 3932168 | tf_op jit(solution)/shard_map/ppermute | solution.py:55
  0.7 8.2 %collective-permute-start.2 = (bf16[256,512]{1,0:T(8,128)(2,1)}, bf16[256,512]{1,0:T(8,128)(2,1)S(1)}, u32[]{:S(2)}, u32[]{:S(2)}) collective-permute-start(bf16[256,512]{1,0:T(8,128)(2,1)} %cot_ref.1), channel_id=1, source_target_pairs={{0,1},{1,0},{2,3},{3,2},{4,5},{5,4},{6,7},{7,6},{8,9},{9,8},{10,11... | collective-permute-start | bytes 786440 | tf_op jit(solution)/shard_map/ppermute | solution.py:55
  1.2 7.8 %collective-permute-start.1 = (bf16[256,512]{1,0:T(8,128)(2,1)}, bf16[256,512]{1,0:T(8,128)(2,1)S(1)}, u32[]{:S(2)}, u32[]{:S(2)}) collective-permute-start(bf16[256,512]{1,0:T(8,128)(2,1)} %cot_ref.1), channel_id=1, source_target_pairs={{0,2},{1,7},{2,4},{3,1},{4,6},{5,3},{6,0},{7,5},{8,10},{9,15},{10,... | collective-permute-start | bytes 786440 | tf_op jit(solution)/shard_map/ppermute | solution.py:63
  2.8 0.7 copy-start.6
  5.0 3.6 %collective-permute-start = (f32[1,1280]{1,0:T(1,128)S(1)}, f32[1,1280]{1,0:T(1,128)S(1)}, u32[]{:S(2)}, u32[]{:S(2)}) collective-permute-start(f32[1,1280]{1,0:T(1,128)S(1)} %get-tuple-element.40), channel_id=1, source_target_pairs={{1,0},{2,1},{3,2},{4,3},{5,4},{6,5},{7,6},{8,7},{9,8},{10,9},{11,1... | collective-permute-start | bytes 15368 | tf_op jit(solution)/shard_map/ppermute | solution.py:462
  8.7 14.6 %copy-start.7 = (s32[128,32]{0,1:T(8,128)S(1)}, s32[128,32]{0,1:T(8,128)}, u32[]{:S(2)}) copy-start(s32[128,32]{0,1:T(8,128)} %param.10) | copy-start | bytes 49156
  8.9 19.5 %copy-start.8 = (bf16[1280,512]{1,0:T(8,128)(2,1)S(1)}, bf16[1280,512]{1,0:T(8,128)(2,1)}, u32[]{:S(2)}) copy-start(bf16[1280,512]{1,0:T(8,128)(2,1)} %w_ref.2) | copy-start | bytes 3932164
  8.9 17.2 %copy-start.13 = (bf16[256,512]{1,0:T(8,128)(2,1)}, bf16[256,512]{1,0:T(8,128)(2,1)S(1)}, u32[]{:S(2)}) copy-start(bf16[256,512]{1,0:T(8,128)(2,1)S(1)} %collective-permute-done.2.refs_1_) | copy-start | bytes 786436
  9.0 21.7 %copy-start.10 = (bf16[256,512]{1,0:T(8,128)(2,1)}, bf16[256,512]{1,0:T(8,128)(2,1)S(1)}, u32[]{:S(2)}) copy-start(bf16[256,512]{1,0:T(8,128)(2,1)S(1)} %collective-permute-done.1.refs_2_) | copy-start | bytes 786436
  9.0 5.1 %collective-permute-start.5 = (bf16[32,1280]{1,0:T(8,128)(2,1)S(1)}, bf16[32,1280]{1,0:T(8,128)(2,1)S(1)}, u32[]{:S(2)}, u32[]{:S(2)}) collective-permute-start(bf16[32,1280]{1,0:T(8,128)(2,1)S(1)} %patch.1), channel_id=1, source_target_pairs={{0,6},{2,0},{4,2},{6,4},{1,7},{3,1},{5,3},{7,5},{8,14},{10,8},{12,... | collective-permute-start | bytes 245768 | tf_op jit(solution)/shard_map/ppermute | solution.py:472
  10.6 5.9 %collective-permute-start.4 = (bf16[32,1280]{1,0:T(8,128)(2,1)S(1)}, bf16[32,1280]{1,0:T(8,128)(2,1)S(1)}, u32[]{:S(2)}, u32[]{:S(2)}) collective-permute-start(bf16[32,1280]{1,0:T(8,128)(2,1)S(1)} %patch.1), channel_id=1, source_target_pairs={{0,4},{2,6},{4,0},{6,2},{1,5},{3,7},{5,1},{7,3},{8,12},{10,14},{12... | collective-permute-start | bytes 245768 | tf_op jit(solution)/shard_map/ppermute | solution.py:472
  13.4 7.1 %collective-permute-start.3 = (bf16[32,1280]{1,0:T(8,128)(2,1)S(1)}, bf16[32,1280]{1,0:T(8,128)(2,1)S(1)}, u32[]{:S(2)}, u32[]{:S(2)}) collective-permute-start(bf16[32,1280]{1,0:T(8,128)(2,1)S(1)} %patch.1), channel_id=1, source_target_pairs={{0,2},{2,4},{4,6},{6,0},{1,3},{3,5},{5,7},{7,1},{8,10},{10,12},{12... | collective-permute-start | bytes 245768 | tf_op jit(solution)/shard_map/ppermute | solution.py:472
  13.4 9.9 %collective-permute-start.6 = (bf16[256,512]{1,0:T(8,128)(2,1)S(1)}, bf16[256,512]{1,0:T(8,128)(2,1)S(1)}, u32[]{:S(2)}, u32[]{:S(2)}) collective-permute-start(bf16[256,512]{1,0:T(8,128)(2,1)S(1)} %collective-permute-done.1.refs_2_), channel_id=1, source_target_pairs={{0,2},{1,7},{2,4},{3,1},{4,6},{5,3},{6,0},{7,5},{8,10},{9,15},{10,... | collective-permute-start | bytes 786440 | tf_op jit(solution)/shard_map/ppermute | solution.py:63
  14.1 12.0 %collective-permute-start.10 = (bf16[256,512]{1,0:T(8,128)(2,1)S(1)}, bf16[256,512]{1,0:T(8,128)(2,1)S(1)}, u32[]{:S(2)}, u32[]{:S(2)}) collective-permute-start(bf16[256,512]{1,0:T(8,128)(2,1)S(1)} %collective-permute-done.2.refs_1_), channel_id=1, source_target_pairs={{0,2},{1,7},{2,4},{3,1},{4,6},{5,3},{6,0},{7,5},{8,10},{9,15},{10,... | collective-permute-start | bytes 786440 | tf_op jit(solution)/shard_map/ppermute | solution.py:63
  23.3 4.7 %copy-start.11 = (bf16[256,512]{1,0:T(8,128)(2,1)}, bf16[256,512]{1,0:T(8,128)(2,1)S(1)}, u32[]{:S(2)}) copy-start(bf16[256,512]{1,0:T(8,128)(2,1)S(1)} %collective-permute-done.6.refs_4_) | copy-start | bytes 786436
  23.3 5.0 %collective-permute-start.7 = (bf16[4,32,1280]{2,1,0:T(8,128)(2,1)S(1)}, bf16[4,32,1280]{2,1,0:T(8,128)(2,1)S(1)}, u32[]{:S(2)}, u32[]{:S(2)}) collective-permute-start(bf16[4,32,1280]{2,1,0:T(8,128)(2,1)S(1)} %pad_maximum_fusion.1.own_ref), channel_id=1, source_target_pairs={{0,1},{1,0},{2,3},{3,2},{4,5},{5,4},{6,7},{7,6},{8,9},{9,8},{10,11... | collective-permute-start | bytes 983048 | tf_op jit(solution)/shard_map/ppermute | solution.py:55
  26.1 0.7 copy-start.12
  27.8 2.9 %collective-permute-start.11 = (bf16[3,256,512]{2,1,0:T(8,128)(2,1)S(1)}, bf16[3,256,512]{2,1,0:T(8,128)(2,1)}, u32[]{:S(2)}, u32[]{:S(2)}) collective-permute-start(bf16[3,256,512]{2,1,0:T(8,128)(2,1)S(1)} %pad_maximum_fusion), channel_id=1, source_target_pairs={{0,1},{1,0},{2,3},{3,2},{4,5},{5,4},{6,7},{7,6},{8,9},{9,8},{10,11... | collective-permute-start | bytes 2359304 | tf_op jit(solution)/shard_map/ppermute | solution.py:55
  28.3 2.6 %copy-start.3 = (bf16[512,4096]{1,0:T(8,128)(2,1)S(1)}, bf16[512,4096]{1,0:T(8,128)(2,1)}, u32[]{:S(2)}) copy-start(bf16[512,4096]{1,0:T(8,128)(2,1)} %refs_13_.3) | copy-start | bytes 12582916
  30.7 10.5 %collective-permute-start.9 = (bf16[2,256,512]{2,1,0:T(8,128)(2,1)S(1)}, bf16[2,256,512]{2,1,0:T(8,128)(2,1)S(1)}, u32[]{:S(2)}, u32[]{:S(2)}) collective-permute-start(bf16[2,256,512]{2,1,0:T(8,128)(2,1)S(1)} %latent.1.pair_ref.refs_4_.lat_ref), channel_id=1, source_target_pairs={{0,2},{1,7},{2,4},{3,1},{4,6},{5,3},{6,0},{7,5},{8,10},{9,15},{10,... | collective-permute-start | bytes 1572872 | tf_op jit(solution)/shard_map/ppermute | solution.py:63
  30.9 11.1 %copy-start = (bf16[4096,512]{1,0:T(8,128)(2,1)S(1)}, bf16[4096,512]{1,0:T(8,128)(2,1)}, u32[]{:S(2)}) copy-start(bf16[4096,512]{1,0:T(8,128)(2,1)} %refs_10_.3) | copy-start | bytes 12582916
  30.9 11.1 %copy-start.1 = (bf16[4096,512]{1,0:T(8,128)(2,1)S(1)}, bf16[4096,512]{1,0:T(8,128)(2,1)}, u32[]{:S(2)}) copy-start(bf16[4096,512]{1,0:T(8,128)(2,1)} %refs_11_.3) | copy-start | bytes 12582916
  30.9 11.1 %copy-start.2 = (bf16[4096,512]{1,0:T(8,128)(2,1)S(1)}, bf16[4096,512]{1,0:T(8,128)(2,1)}, u32[]{:S(2)}) copy-start(bf16[4096,512]{1,0:T(8,128)(2,1)} %refs_12_.3) | copy-start | bytes 12582916
  34.0 8.0 %copy-start.5 = (f32[4096]{0:T(1024)S(1)}, f32[4096]{0:T(1024)}, u32[]{:S(2)}) copy-start(f32[4096]{0:T(1024)} %param.12) | copy-start | bytes 49156
  41.8 7.8 %collective-permute-start.13 = (bf16[2,256,512]{2,1,0:T(8,128)(2,1)S(1)}, bf16[2,256,512]{2,1,0:T(8,128)(2,1)S(1)}, u32[]{:S(2)}, u32[]{:S(2)}) collective-permute-start(bf16[2,256,512]{2,1,0:T(8,128)(2,1)S(1)} %collective-permute-done.9.both_ref.refs_5_), channel_id=1, source_target_pairs={{0,1},{1,0},{2,3},{3,2},{4,5},{5,4},{6,7},{7,6},{8,9},{9,8},{10,11... | collective-permute-start | bytes 1572872 | tf_op jit(solution)/shard_map/ppermute | solution.py:55
  41.9 7.7 %collective-permute-start.12 = (bf16[1,256,512]{2,1,0:T(8,128)(2,1)S(1)}, bf16[1,256,512]{2,1,0:T(8,128)(2,1)S(1)}, u32[]{:S(2)}, u32[]{:S(2)}) collective-permute-start(bf16[1,256,512]{2,1,0:T(8,128)(2,1)S(1)} %slice.6), channel_id=1, source_target_pairs={{0,2},{1,7},{2,4},{3,1},{4,6},{5,3},{6,0},{7,5},{8,10},{9,15},{10,... | collective-permute-start | bytes 786440 | tf_op jit(solution)/shard_map/ppermute | solution.py:63
  49.5 1.5 collective-permute-start.14
  53.1 2.0 %collective-permute-start.15 = (bf16[4,256,256]{2,1,0:T(8,128)(2,1)S(1)}, bf16[4,256,256]{2,1,0:T(8,128)(2,1)S(1)}, u32[]{:S(2)}, u32[]{:S(2)}) collective-permute-start(bf16[4,256,256]{2,1,0:T(8,128)(2,1)S(1)} %get-tuple-element.57), channel_id=1, source_target_pairs={{0,1},{1,0},{2,3},{3,2},{4,5},{5,4},{6,7},{7,6},{8,9},{9,8},{10,11... | collective-permute-start | bytes 1572872 | tf_op jit(solution)/shard_map/ppermute | solution.py:55
  86.5 2.9 %collective-permute-start.16 = (bf16[16,128,256]{2,1,0:T(8,128)(2,1)S(1)}, bf16[16,128,256]{2,1,0:T(8,128)(2,1)S(1)}, u32[]{:S(2)}, u32[]{:S(2)}) collective-permute-start(bf16[16,128,256]{2,1,0:T(8,128)(2,1)S(1)} %slice.8), channel_id=1, source_target_pairs={{0,1},{1,0},{2,3},{3,2},{4,5},{5,4},{6,7},{7,6},{8,9},{9,8},{10,11... | collective-permute-start | bytes 3145736 | tf_op jit(solution)/shard_map/ppermute | solution.py:55
  101.0 2.7 %collective-permute-start.17 = (bf16[16,128,256]{2,1,0:T(8,128)(2,1)S(1)}, bf16[16,128,256]{2,1,0:T(8,128)(2,1)S(1)}, u32[]{:S(2)}, u32[]{:S(2)}) collective-permute-start(bf16[16,128,256]{2,1,0:T(8,128)(2,1)S(1)} %get-tuple-element.59), channel_id=1, source_target_pairs={{0,1},{1,0},{2,3},{3,2},{4,5},{5,4},{6,7},{7,6},{8,9},{9,8},{10,11... | collective-permute-start | bytes 3145736 | tf_op jit(solution)/shard_map/ppermute | solution.py:55
  104.0 28.9 %copy-start.4 = (bf16[512,4096]{1,0:T(8,128)(2,1)S(1)}, bf16[512,4096]{1,0:T(8,128)(2,1)}, u32[]{:S(2)}) copy-start(bf16[512,4096]{1,0:T(8,128)(2,1)} %refs_13_.3) | copy-start | bytes 12582916
  130.7 2.2 %collective-permute-start.18 = (bf16[4,256,256]{2,1,0:T(8,128)(2,1)S(1)}, bf16[4,256,256]{2,1,0:T(8,128)(2,1)S(1)}, u32[]{:S(2)}, u32[]{:S(2)}) collective-permute-start(bf16[4,256,256]{2,1,0:T(8,128)(2,1)S(1)} %get-tuple-element.62), channel_id=1, source_target_pairs={{0,1},{1,0},{2,3},{3,2},{4,5},{5,4},{6,7},{7,6},{8,9},{9,8},{10,11... | collective-permute-start | bytes 1572872 | tf_op jit(solution)/shard_map/ppermute | solution.py:55
  136.2 2.0 %collective-permute-start.19 = (bf16[1,512,512]{2,1,0:T(8,128)(2,1)S(1)}, bf16[1,512,512]{2,1,0:T(8,128)(2,1)S(1)}, u32[]{:S(2)}, u32[]{:S(2)}) collective-permute-start(bf16[1,512,512]{2,1,0:T(8,128)(2,1)S(1)} %get-tuple-element.67), channel_id=1, source_target_pairs={{0,1},{1,0},{2,3},{3,2},{4,5},{5,4},{6,7},{7,6},{8,9},{9,8},{10,11... | collective-permute-start | bytes 1572872 | tf_op jit(solution)/shard_map/ppermute | solution.py:55
  138.1 3.4 %collective-permute-start.20 = (bf16[3,512,512]{2,1,0:T(8,128)(2,1)S(1)}, bf16[3,512,512]{2,1,0:T(8,128)(2,1)S(1)}, u32[]{:S(2)}, u32[]{:S(2)}) collective-permute-start(bf16[3,512,512]{2,1,0:T(8,128)(2,1)S(1)} %get-tuple-element.71), channel_id=1, source_target_pairs={{0,1},{1,0},{2,3},{3,2},{4,5},{5,4},{6,7},{7,6},{8,9},{9,8},{10,11... | collective-permute-start | bytes 4718600 | tf_op jit(solution)/shard_map/ppermute | solution.py:55
  138.4 10.5 %collective-permute-start.21 = (bf16[512,512]{1,0:T(8,128)(2,1)S(1)}, bf16[512,512]{1,0:T(8,128)(2,1)S(1)}, u32[]{:S(2)}, u32[]{:S(2)}) collective-permute-start(bf16[512,512]{1,0:T(8,128)(2,1)S(1)} %far.1), channel_id=1, source_target_pairs={{0,2},{1,7},{2,4},{3,1},{4,6},{5,3},{6,0},{7,5},{8,10},{9,15},{10,... | collective-permute-start | bytes 1572872 | tf_op jit(solution)/shard_map/ppermute | solution.py:63
  141.9 12.6 %collective-permute-start.23 = (bf16[512,512]{1,0:T(8,128)(2,1)S(1)}, bf16[512,512]{1,0:T(8,128)(2,1)S(1)}, u32[]{:S(2)}, u32[]{:S(2)}) collective-permute-start(bf16[512,512]{1,0:T(8,128)(2,1)S(1)} %get-tuple-element.75), channel_id=1, source_target_pairs={{0,2},{1,7},{2,4},{3,1},{4,6},{5,3},{6,0},{7,5},{8,10},{9,15},{10,... | collective-permute-start | bytes 1572872 | tf_op jit(solution)/shard_map/ppermute | solution.py:63
  148.9 11.2 %copy-start.9 = (bf16[256,512]{1,0:T(8,128)(2,1)S(1)}, bf16[256,512]{1,0:T(8,128)(2,1)}, u32[]{:S(2)}) copy-start(bf16[256,512]{1,0:T(8,128)(2,1)} %cot_ref.1) | copy-start | bytes 786436
  149.0 11.1 %collective-permute-start.22 = (bf16[512,512]{1,0:T(8,128)(2,1)S(1)}, bf16[512,512]{1,0:T(8,128)(2,1)S(1)}, u32[]{:S(2)}, u32[]{:S(2)}) collective-permute-start(bf16[512,512]{1,0:T(8,128)(2,1)S(1)} %pass.1), channel_id=1, source_target_pairs={{0,2},{1,7},{2,4},{3,1},{4,6},{5,3},{6,0},{7,5},{8,10},{9,15},{10,... | collective-permute-start | bytes 1572872 | tf_op jit(solution)/shard_map/ppermute | solution.py:63
  154.5 5.6 %collective-permute-start.24 = (bf16[512,512]{1,0:T(8,128)(2,1)S(1)}, bf16[512,512]{1,0:T(8,128)(2,1)S(1)}, u32[]{:S(2)}, u32[]{:S(2)}) collective-permute-start(bf16[512,512]{1,0:T(8,128)(2,1)S(1)} %collective-permute-done.23), channel_id=1, source_target_pairs={{0,1},{1,0},{2,3},{3,2},{4,5},{5,4},{6,7},{7,6},{8,9},{9,8},{10,11... | collective-permute-start | bytes 1572872 | tf_op jit(solution)/shard_map/ppermute | solution.py:55

commit v8 on v7

--- a/solution.py
+++ b/solution.py
@@ -275,8 +275,6 @@
         return keys, ref[4 * u : 4 * u + 4, :half, HEAD:].reshape(span, HEAD)
 
     biases[0], biases[1] = bias_ref[c], bias_ref[1 - c]
-    dks[...] = jnp.zeros_like(dks)
-    dvs[...] = jnp.zeros_like(dvs)
     lane = lax.broadcasted_iota(jnp.int32, (1, rows), 1)
     place_q = (lane // strip) * 256 + lax.rem(lane, strip) + c * half + e * strip
     line = lax.broadcasted_iota(jnp.int32, (span, 1), 0)
@@ -319,8 +317,10 @@
                 dp = lax.dot_general(values, do, NT, preferred_element_type=F32)
                 ds = (p * (dp - delta)).astype(BF16)
                 at = slice(u * span, (u + 1) * span)
-                dvs[side, at, :] += jnp.dot(p.astype(BF16), do, preferred_element_type=F32)
-                dks[side, at, :] += jnp.dot(ds, q, preferred_element_type=F32)
+                dv = jnp.dot(p.astype(BF16), do, preferred_element_type=F32)
+                dk = jnp.dot(ds, q, preferred_element_type=F32)
+                dvs[side, at, :] = dv if u == t else dvs[side, at, :] + dv
+                dks[side, at, :] = dk if u == t else dks[side, at, :] + dk
                 dq = dq + lax.dot_general(keys, ds, TN, preferred_element_type=F32)
         dq = jnp.transpose(dq * SCALE).astype(BF16)
         strip_ref[4 * t : 4 * t + 4, :, :HEAD] = dq.reshape(4, strip, HEAD)

time: 161 us -> 161 us (level)
  no operation moved by 1% of the time
where the time goes in v8:
time: 161 us
  blocking collectives  57.7 us (36%)
  waiting for transfers between devices  56.4 us (35%)
  Pallas kernels  30 us (19%)
  starting transfers between devices  12.1 us (8%)
  local copies, waits for them, and re-layouts  2.83 us (2%)
    ppermute x8, waiting for transfers between devices, along_x(): return lax.ppermute(block, XC, route)  36.3 us
    all_to_all x1, blocking collectives, per_device(): mine = lax.all_to_all(sent, SEQ, 0, 0, tiled=True)  31.2 us
    pallas_call x16, Pallas kernels, call(): pl.pallas_call(kernel, in_specs=[VMEM] * (len(ins) - stay) + [pl.BlockSpe...  30 us
    all_to_all x1, blocking collectives, per_device(): back = lax.all_to_all(back, SEQ, 0, 0, tiled=True)  26.6 us
    ppermute x13, waiting for transfers between devices, other_core(): return lax.ppermute(block, 'c', [(0, 1), (1, 0)])  13 us
    ppermute x3, waiting for transfers between devices, per_device(): lax.ppermute(patches, 'x', [(i, (i + k) % 4) for i in range(4)])  4.73 us
    ppermute x3, starting transfers between devices, per_device(): lax.ppermute(patches, 'x', [(i, (i + k) % 4) for i in range(4)])  4.36 us
    ppermute x8, starting transfers between devices, along_x(): return lax.ppermute(block, XC, route)  4.31 us
  transfers between devices with their start and end apart: 25, of which 18 were waited for; matrix products, arithmetic and copies ran while one was open for 1% of the time, Pallas kernels for 7%

profile of v8, /device:TPU:0, one launch (start us, length us, event | category | flops | bytes accessed | tf_op | source)
XLA Modules:
  0.0 161.2 jit_solution(9538800083881755204)
XLA Ops:
  0.7 0.5 collective-permute-start.2
  1.2 1.6 collective-permute-start.1
  2.8 0.7 copy-done.6
  3.5 1.5 pool.1
  5.0 1.3 collective-permute-start
  6.3 2.3 %collective-permute-done.next_ref = f32[1,1280]{1,0:T(1,128)S(1)} collective-permute-done((f32[1,1280]{1,0:T(1,128)S(1)}, f32[1,1280]{1,0:T(1,128)S(1)}, u32[]{:S(2)}, u32[]{:S(2)}) %collective-permute-start) | collective-permute-done | bytes 5152 | tf_op jit(solution)/shard_map/ppermute | solution.py:462
  8.7 0.2 patch.1
  9.0 1.6 %collective-permute-start.5 = (bf16[32,1280]{1,0:T(8,128)(2,1)S(1)}, bf16[32,1280]{1,0:T(8,128)(2,1)S(1)}, u32[]{:S(2)}, u32[]{:S(2)}) collective-permute-start(bf16[32,1280]{1,0:T(8,128)(2,1)S(1)} %patch.1), channel_id=1, source_target_pairs={{0,6},{2,0},{4,2},{6,4},{1,7},{3,1},{5,3},{7,5},{8,14},{10,8},{12,... | collective-permute-start | bytes 245768 | tf_op jit(solution)/shard_map/ppermute | solution.py:472
  10.6 2.7 %collective-permute-start.4 = (bf16[32,1280]{1,0:T(8,128)(2,1)S(1)}, bf16[32,1280]{1,0:T(8,128)(2,1)S(1)}, u32[]{:S(2)}, u32[]{:S(2)}) collective-permute-start(bf16[32,1280]{1,0:T(8,128)(2,1)S(1)} %patch.1), channel_id=1, source_target_pairs={{0,4},{2,6},{4,0},{6,2},{1,5},{3,7},{5,1},{7,3},{8,12},{10,14},{12... | collective-permute-start | bytes 245768 | tf_op jit(solution)/shard_map/ppermute | solution.py:472
  13.4 0.8 collective-permute-start.6
  14.1 1.6 collective-permute-start.10
  15.7 0.8 collective-permute-done.4
  16.6 3.9 %collective-permute-done.3 = bf16[32,1280]{1,0:T(8,128)(2,1)S(1)} collective-permute-done((bf16[32,1280]{1,0:T(8,128)(2,1)S(1)}, bf16[32,1280]{1,0:T(8,128)(2,1)S(1)}, u32[]{:S(2)}, u32[]{:S(2)}) %collective-permute-start.3) | collective-permute-done | bytes 81952 | tf_op jit(solution)/shard_map/ppermute | solution.py:472
  20.5 2.8 %collective-permute-done.6.refs_4_ = bf16[256,512]{1,0:T(8,128)(2,1)S(1)} collective-permute-done((bf16[256,512]{1,0:T(8,128)(2,1)S(1)}, bf16[256,512]{1,0:T(8,128)(2,1)S(1)}, u32[]{:S(2)}, u32[]{:S(2)}) %collective-permute-start.6) | collective-permute-done | bytes 262176 | tf_op jit(solution)/shard_map/ppermute | solution.py:63
  23.5 2.5 %collective-permute-done.10.refs_3_ = bf16[256,512]{1,0:T(8,128)(2,1)S(1)} collective-permute-done((bf16[256,512]{1,0:T(8,128)(2,1)S(1)}, bf16[256,512]{1,0:T(8,128)(2,1)S(1)}, u32[]{:S(2)}, u32[]{:S(2)}) %collective-permute-start.10) | collective-permute-done | bytes 262176 | tf_op jit(solution)/shard_map/ppermute | solution.py:63
  26.1 0.7 copy-done.12
  26.8 1.0 pad_maximum_fusion
  28.3 2.3 %latent.1.pair_ref.refs_4_.lat_ref = bf16[2,256,512]{2,1,0:T(8,128)(2,1)S(1)} custom-call(bf16[4,32,1280]{2,1,0:T(8,128)(2,1)S(1)} %pad_maximum_fusion.1.own_ref, bf16[4,32,1280]{2,1,0:T(8,128)(2,1)S(1)} %collective-permute-done.7.other_ref, bf16[1280,512]{1,0:T(8,128)(2,1)S(1)} %copy-done.8, bf16[1280,512]{1,0:T(8,128)(2,1)} %collective-permute-done.8.sibling_w_ref), custom_call_target="tpu_custom_call" | custom-call | flops 8000000000 | bytes 24000000 | tf_op jit(solution)/shard_map/latent/pallas_call | solution.py:36
  30.9 3.1 %d_attn.1.do_ref = bf16[256,512]{1,0:T(8,128)(2,1)S(1)} custom-call(f32[256,1]{1,0:T(8,128)S(1)} %copy.14.valid_ref, bf16[512,4096]{1,0:T(8,128)(2,1)S(1)} %copy-done.3, bf16[256,512]{1,0:T(8,128)(2,1)} %cot_ref.1, bf16[256,512]{1,0:T(8,128)(2,1)} %copy-done.13, bf16[256,512]{1,0:T(8,128)(2,1)} %copy-done.10, bf16[256,512]{1,0:T(8,128)(2,1)} %copy-done.12, ...), custom_call_target="tpu_custom_call" | custom-call | flops 8000000000 | bytes 24000000 | tf_op jit(solution)/shard_map/d_attn/pallas_call | solution.py:36
  34.0 7.2 %collective-permute-done.9.both_ref.refs_5_ = bf16[2,256,512]{2,1,0:T(8,128)(2,1)S(1)} collective-permute-done((bf16[2,256,512]{2,1,0:T(8,128)(2,1)S(1)}, bf16[2,256,512]{2,1,0:T(8,128)(2,1)S(1)}, u32[]{:S(2)}, u32[]{:S(2)}) %collective-permute-start.9) | collective-permute-done | bytes 524320 | tf_op jit(solution)/shard_map/ppermute | solution.py:63
  41.2 0.6 broadcast_in_dim.15.bias_ref
  42.0 1.8 %project_near.1 = (f32[3,256,512]{2,1,0:T(8,128)S(1)}, f32[256,128]{1,0:T(8,128)S(1)}) custom-call(bf16[2,256,512]{2,1,0:T(8,128)(2,1)S(1)} %latent.1.pair_ref.refs_4_.lat_ref, bf16[2,256,512]{2,1,0:T(8,128)(2,1)S(1)} %collective-permute-done.9.both_ref.refs_5_, f32[1,4096]{1,0:T(1,128)S(1)} %bitcast.14, bf16[4096,512]{1,0:T(8,128)(2,1)S(1)} %copy-done, ...), custom_call_target="tpu_custom_call" | custom-call | flops 2000000000 | bytes 6000000 | tf_op jit(solution)/shard_map/project_near/pallas_call | solution.py:36
  43.8 5.7 %collective-permute-done.12.far_ref.refs_6_ = bf16[1,256,512]{2,1,0:T(8,128)(2,1)S(1)} collective-permute-done((bf16[1,256,512]{2,1,0:T(8,128)(2,1)S(1)}, bf16[1,256,512]{2,1,0:T(8,128)(2,1)S(1)}, u32[]{:S(2)}, u32[]{:S(2)}) %collective-permute-start.12) | collective-permute-done | bytes 262176 | tf_op jit(solution)/shard_map/ppermute | solution.py:63
  49.5 1.5 collective-permute-done.14.their_far.refs_8_
  51.1 2.1 %project.1 = (bf16[4,256,256]{2,1,0:T(8,128)(2,1)S(1)}, bf16[4,256,256]{2,1,0:T(8,128)(2,1)S(1)}, bf16[256,512]{1,0:T(8,128)(2,1)S(1)}, bf16[256,512]{1,0:T(8,12...) custom-call(bf16[1,256,512]{2,1,0:T(8,128)(2,1)S(1)} %collective-permute-done.12.far_ref.refs_6_, ...), custom_call_target="tpu_custom_call" | custom-call | flops 3000000000 | bytes 9000000 | tf_op jit(solution)/shard_map/project/pallas_call | solution.py:36
  53.1 0.2 collective-permute-start.15
  53.4 1.8 %collective-permute-done.15.got_ref = bf16[4,256,256]{2,1,0:T(8,128)(2,1)S(1)} collective-permute-done((bf16[4,256,256]{2,1,0:T(8,128)(2,1)S(1)}, bf16[4,256,256]{2,1,0:T(8,128)(2,1)S(1)}, u32[]{:S(2)}, u32[]{:S(2)}) %collective-permute-start.15) | collective-permute-done | bytes 524320 | tf_op jit(solution)/shard_map/ppermute | solution.py:55
  55.2 31.2 %all_to_all.10.mine_ref = bf16[16,192,256]{2,1,0:T(8,128)(2,1)S(1)} all-to-all(bf16[16,192,256]{2,1,0:T(8,128)(2,1)S(1)} %pack.1), channel_id=1, replica_groups=mesh['y'=4,'z'=4,'x'=4,'c'=2] {'y','z'}, dimensions={0} | all-to-all | bytes 3145728 | tf_op jit(solution)/shard_map/all_to_all | solution.py:500
  86.5 0.3 collective-permute-start.16
  86.8 2.6 %collective-permute-done.16.theirs_ref = bf16[16,128,256]{2,1,0:T(8,128)(2,1)S(1)} collective-permute-done((bf16[16,128,256]{2,1,0:T(8,128)(2,1)S(1)}, bf16[16,128,256]{2,1,0:T(8,128)(2,1)S(1)}, u32[]{:S(2)}, u32[]{:S(2)}) %collective-permute-start.16) | collective-permute-done | bytes 1048608 | tf_op jit(solution)/shard_map/ppermute | solution.py:55
  89.4 11.6 %attention.1 = (bf16[16,128,256]{2,1,0:T(8,128)(2,1)S(1)}, bf16[16,128,256]{2,1,0:T(8,128)(2,1)S(1)}, bf16[16,64,256]{2,1,0:T(8,128)(2,1)S(1)}) custom-call(f32[2,2048,128]{2,1,0:T(8,128)S(1)} %broadcast_in_dim.15.bias_ref, bf16[16,192,256]{2,1,0:T(8,128)(2,1)S(1)} %all_to_all.10.mine_ref, bf16[16,128,256]{2,1,0:T(8,128)(2,1)S(1)} %collective-permute-done.16.theirs_ref), custom_call_target="tpu_custom_call" | custom-call | flops 12000000000 | bytes 36000000 | tf_op jit(solution)/shard_map/attention/pallas_call | solution.py:36
  101.0 0.2 collective-permute-start.17
  101.2 2.5 %collective-permute-done.17.got_ref = bf16[16,128,256]{2,1,0:T(8,128)(2,1)S(1)} collective-permute-done((bf16[16,128,256]{2,1,0:T(8,128)(2,1)S(1)}, bf16[16,128,256]{2,1,0:T(8,128)(2,1)S(1)}, u32[]{:S(2)}, u32[]{:S(2)}) %collective-permute-start.17) | collective-permute-done | bytes 1048608 | tf_op jit(solution)/shard_map/ppermute | solution.py:55
  103.7 0.3 return.1
  104.0 26.6 %all_to_all.11.in_ref = bf16[16,192,256]{2,1,0:T(8,128)(2,1)S(1)} all-to-all(bf16[16,192,256]{2,1,0:T(8,128)(2,1)S(1)} %return.1), channel_id=1, replica_groups=mesh['y'=4,'z'=4,'x'=4,'c'=2] {'y','z'}, dimensions={0} | all-to-all | bytes 3145728 | tf_op jit(solution)/shard_map/all_to_all | solution.py:503
  130.7 0.3 collective-permute-start.18
  131.0 1.9 %collective-permute-done.18.got_ref = bf16[4,256,256]{2,1,0:T(8,128)(2,1)S(1)} collective-permute-done((bf16[4,256,256]{2,1,0:T(8,128)(2,1)S(1)}, bf16[4,256,256]{2,1,0:T(8,128)(2,1)S(1)}, u32[]{:S(2)}, u32[]{:S(2)}) %collective-permute-start.18) | collective-permute-done | bytes 524320 | tf_op jit(solution)/shard_map/ppermute | solution.py:55
  132.9 3.2 %outputs.2 = (bf16[1,512,512]{2,1,0:T(8,128)(2,1)S(1)}, bf16[1,512,512]{2,1,0:T(8,128)(2,1)S(1)}, bf16[3,512,512]{2,1,0:T(8,128)(2,1)S(1)}) custom-call(bf16[4,256,256]{2,1,0:T(8,128)(2,1)S(1)} %get-tuple-element.61.keep_ref, bf16[4,256,256]{2,1,0:T(8,128)(2,1)S(1)} %collective-permute-done.18.got_ref, bf16[256,512]{1,0:T(8,128)(2,1)S(1)} %get-tuple-element.63.refs_0_, ...), custom_call_target="tpu_custom_call" | custom-call | flops 2000000000 | bytes 6000000 | tf_op jit(solution)/shard_map/outputs/pallas_call | solution.py:36
  136.2 0.2 collective-permute-start.19
  136.4 1.8 %collective-permute-done.19.other_ref = bf16[1,512,512]{2,1,0:T(8,128)(2,1)S(1)} collective-permute-done((bf16[1,512,512]{2,1,0:T(8,128)(2,1)S(1)}, bf16[1,512,512]{2,1,0:T(8,128)(2,1)S(1)}, u32[]{:S(2)}, u32[]{:S(2)}) %collective-permute-start.19) | collective-permute-done | bytes 524320 | tf_op jit(solution)/shard_map/ppermute | solution.py:55
  138.1 0.1 collective-permute-start.20
  138.5 2.2 %outputs.3.own_ref = bf16[3,512,512]{2,1,0:T(8,128)(2,1)S(1)} custom-call(bf16[4,256,256]{2,1,0:T(8,128)(2,1)S(1)} %get-tuple-element.61.keep_ref, bf16[4,256,256]{2,1,0:T(8,128)(2,1)S(1)} %collective-permute-done.18.got_ref, bf16[256,512]{1,0:T(8,128)(2,1)S(1)} %get-tuple-element.63.refs_0_, bf16[256,512]{1,0:T(8,128)(2,1)S(1)} %get-tuple-element.64.refs_1_, ...), custom_call_target="tpu_custom_call" | custom-call | flops 2000000000 | bytes 6000000 | tf_op jit(solution)/shard_map/outputs/pallas_call | solution.py:36
  140.7 0.9 collective-permute-done.20.other_ref
  141.6 0.3 add.9
  142.0 6.9 %collective-permute-done.21.far_ref = bf16[512,512]{1,0:T(8,128)(2,1)S(1)} collective-permute-done((bf16[512,512]{1,0:T(8,128)(2,1)S(1)}, bf16[512,512]{1,0:T(8,128)(2,1)S(1)}, u32[]{:S(2)}, u32[]{:S(2)}) %collective-permute-start.21) | collective-permute-done | bytes 524320 | tf_op jit(solution)/shard_map/ppermute | solution.py:63
  149.0 5.4 %collective-permute-done.23 = bf16[512,512]{1,0:T(8,128)(2,1)S(1)} collective-permute-done((bf16[512,512]{1,0:T(8,128)(2,1)S(1)}, bf16[512,512]{1,0:T(8,128)(2,1)S(1)}, u32[]{:S(2)}, u32[]{:S(2)}) %collective-permute-start.23) | collective-permute-done | bytes 524320 | tf_op jit(solution)/shard_map/ppermute | solution.py:63
  154.5 5.6 %collective-permute-done.22.ahead_ref = bf16[512,512]{1,0:T(8,128)(2,1)S(1)} collective-permute-done((bf16[512,512]{1,0:T(8,128)(2,1)S(1)}, bf16[512,512]{1,0:T(8,128)(2,1)S(1)}, u32[]{:S(2)}, u32[]{:S(2)}) %collective-permute-start.22) | collective-permute-done | bytes 524320 | tf_op jit(solution)/shard_map/ppermute | solution.py:63
  160.1 1.1 final.1
  (60 shorter events, 2.1 us)
Async XLA Ops:
  0.6 27.7 %collective-permute-start.8 = (bf16[1280,512]{1,0:T(8,128)(2,1)}, bf16[1280,512]{1,0:T(8,128)(2,1)}, u32[]{:S(2)}, u32[]{:S(2)}) collective-permute-start(bf16[1280,512]{1,0:T(8,128)(2,1)} %w_ref.2), channel_id=1, source_target_pairs={{0,1},{1,0},{2,3},{3,2},{4,5},{5,4},{6,7},{7,6},{8,9},{9,8},{10,11... | collective-permute-start | bytes 3932168 | tf_op jit(solution)/shard_map/ppermute | solution.py:55
  0.7 8.2 %collective-permute-start.2 = (bf16[256,512]{1,0:T(8,128)(2,1)}, bf16[256,512]{1,0:T(8,128)(2,1)S(1)}, u32[]{:S(2)}, u32[]{:S(2)}) collective-permute-start(bf16[256,512]{1,0:T(8,128)(2,1)} %cot_ref.1), channel_id=1, source_target_pairs={{0,1},{1,0},{2,3},{3,2},{4,5},{5,4},{6,7},{7,6},{8,9},{9,8},{10,11... | collective-permute-start | bytes 786440 | tf_op jit(solution)/shard_map/ppermute | solution.py:55
  1.2 7.8 %collective-permute-start.1 = (bf16[256,512]{1,0:T(8,128)(2,1)}, bf16[256,512]{1,0:T(8,128)(2,1)S(1)}, u32[]{:S(2)}, u32[]{:S(2)}) collective-permute-start(bf16[256,512]{1,0:T(8,128)(2,1)} %cot_ref.1), channel_id=1, source_target_pairs={{0,2},{1,7},{2,4},{3,1},{4,6},{5,3},{6,0},{7,5},{8,10},{9,15},{10,... | collective-permute-start | bytes 786440 | tf_op jit(solution)/shard_map/ppermute | solution.py:63
  2.8 0.7 copy-start.6
  5.0 3.6 %collective-permute-start = (f32[1,1280]{1,0:T(1,128)S(1)}, f32[1,1280]{1,0:T(1,128)S(1)}, u32[]{:S(2)}, u32[]{:S(2)}) collective-permute-start(f32[1,1280]{1,0:T(1,128)S(1)} %get-tuple-element.40), channel_id=1, source_target_pairs={{1,0},{2,1},{3,2},{4,3},{5,4},{6,5},{7,6},{8,7},{9,8},{10,9},{11,1... | collective-permute-start | bytes 15368 | tf_op jit(solution)/shard_map/ppermute | solution.py:462
  8.7 14.6 %copy-start.7 = (s32[128,32]{0,1:T(8,128)S(1)}, s32[128,32]{0,1:T(8,128)}, u32[]{:S(2)}) copy-start(s32[128,32]{0,1:T(8,128)} %param.10) | copy-start | bytes 49156
  8.9 19.5 %copy-start.8 = (bf16[1280,512]{1,0:T(8,128)(2,1)S(1)}, bf16[1280,512]{1,0:T(8,128)(2,1)}, u32[]{:S(2)}) copy-start(bf16[1280,512]{1,0:T(8,128)(2,1)} %w_ref.2) | copy-start | bytes 3932164
  8.9 17.2 %copy-start.13 = (bf16[256,512]{1,0:T(8,128)(2,1)}, bf16[256,512]{1,0:T(8,128)(2,1)S(1)}, u32[]{:S(2)}) copy-start(bf16[256,512]{1,0:T(8,128)(2,1)S(1)} %collective-permute-done.2.refs_1_) | copy-start | bytes 786436
  9.0 21.7 %copy-start.10 = (bf16[256,512]{1,0:T(8,128)(2,1)}, bf16[256,512]{1,0:T(8,128)(2,1)S(1)}, u32[]{:S(2)}) copy-start(bf16[256,512]{1,0:T(8,128)(2,1)S(1)} %collective-permute-done.1.refs_2_) | copy-start | bytes 786436
  9.0 5.1 %collective-permute-start.5 = (bf16[32,1280]{1,0:T(8,128)(2,1)S(1)}, bf16[32,1280]{1,0:T(8,128)(2,1)S(1)}, u32[]{:S(2)}, u32[]{:S(2)}) collective-permute-start(bf16[32,1280]{1,0:T(8,128)(2,1)S(1)} %patch.1), channel_id=1, source_target_pairs={{0,6},{2,0},{4,2},{6,4},{1,7},{3,1},{5,3},{7,5},{8,14},{10,8},{12,... | collective-permute-start | bytes 245768 | tf_op jit(solution)/shard_map/ppermute | solution.py:472
  10.6 5.9 %collective-permute-start.4 = (bf16[32,1280]{1,0:T(8,128)(2,1)S(1)}, bf16[32,1280]{1,0:T(8,128)(2,1)S(1)}, u32[]{:S(2)}, u32[]{:S(2)}) collective-permute-start(bf16[32,1280]{1,0:T(8,128)(2,1)S(1)} %patch.1), channel_id=1, source_target_pairs={{0,4},{2,6},{4,0},{6,2},{1,5},{3,7},{5,1},{7,3},{8,12},{10,14},{12... | collective-permute-start | bytes 245768 | tf_op jit(solution)/shard_map/ppermute | solution.py:472
  13.4 7.1 %collective-permute-start.3 = (bf16[32,1280]{1,0:T(8,128)(2,1)S(1)}, bf16[32,1280]{1,0:T(8,128)(2,1)S(1)}, u32[]{:S(2)}, u32[]{:S(2)}) collective-permute-start(bf16[32,1280]{1,0:T(8,128)(2,1)S(1)} %patch.1), channel_id=1, source_target_pairs={{0,2},{2,4},{4,6},{6,0},{1,3},{3,5},{5,7},{7,1},{8,10},{10,12},{12... | collective-permute-start | bytes 245768 | tf_op jit(solution)/shard_map/ppermute | solution.py:472
  13.4 9.9 %collective-permute-start.6 = (bf16[256,512]{1,0:T(8,128)(2,1)S(1)}, bf16[256,512]{1,0:T(8,128)(2,1)S(1)}, u32[]{:S(2)}, u32[]{:S(2)}) collective-permute-start(bf16[256,512]{1,0:T(8,128)(2,1)S(1)} %collective-permute-done.1.refs_2_), channel_id=1, source_target_pairs={{0,2},{1,7},{2,4},{3,1},{4,6},{5,3},{6,0},{7,5},{8,10},{9,15},{10,... | collective-permute-start | bytes 786440 | tf_op jit(solution)/shard_map/ppermute | solution.py:63
  14.1 12.0 %collective-permute-start.10 = (bf16[256,512]{1,0:T(8,128)(2,1)S(1)}, bf16[256,512]{1,0:T(8,128)(2,1)S(1)}, u32[]{:S(2)}, u32[]{:S(2)}) collective-permute-start(bf16[256,512]{1,0:T(8,128)(2,1)S(1)} %collective-permute-done.2.refs_1_), channel_id=1, source_target_pairs={{0,2},{1,7},{2,4},{3,1},{4,6},{5,3},{6,0},{7,5},{8,10},{9,15},{10,... | collective-permute-start | bytes 786440 | tf_op jit(solution)/shard_map/ppermute | solution.py:63
  23.3 4.7 %copy-start.11 = (bf16[256,512]{1,0:T(8,128)(2,1)}, bf16[256,512]{1,0:T(8,128)(2,1)S(1)}, u32[]{:S(2)}) copy-start(bf16[256,512]{1,0:T(8,128)(2,1)S(1)} %collective-permute-done.6.refs_4_) | copy-start | bytes 786436
  23.3 5.0 %collective-permute-start.7 = (bf16[4,32,1280]{2,1,0:T(8,128)(2,1)S(1)}, bf16[4,32,1280]{2,1,0:T(8,128)(2,1)S(1)}, u32[]{:S(2)}, u32[]{:S(2)}) collective-permute-start(bf16[4,32,1280]{2,1,0:T(8,128)(2,1)S(1)} %pad_maximum_fusion.1.own_ref), channel_id=1, source_target_pairs={{0,1},{1,0},{2,3},{3,2},{4,5},{5,4},{6,7},{7,6},{8,9},{9,8},{10,11... | collective-permute-start | bytes 983048 | tf_op jit(solution)/shard_map/ppermute | solution.py:55
  26.1 0.7 copy-start.12
  27.8 2.9 %collective-permute-start.11 = (bf16[3,256,512]{2,1,0:T(8,128)(2,1)S(1)}, bf16[3,256,512]{2,1,0:T(8,128)(2,1)}, u32[]{:S(2)}, u32[]{:S(2)}) collective-permute-start(bf16[3,256,512]{2,1,0:T(8,128)(2,1)S(1)} %pad_maximum_fusion), channel_id=1, source_target_pairs={{0,1},{1,0},{2,3},{3,2},{4,5},{5,4},{6,7},{7,6},{8,9},{9,8},{10,11... | collective-permute-start | bytes 2359304 | tf_op jit(solution)/shard_map/ppermute | solution.py:55
  28.3 2.6 %copy-start.3 = (bf16[512,4096]{1,0:T(8,128)(2,1)S(1)}, bf16[512,4096]{1,0:T(8,128)(2,1)}, u32[]{:S(2)}) copy-start(bf16[512,4096]{1,0:T(8,128)(2,1)} %refs_13_.3) | copy-start | bytes 12582916
  30.7 10.5 %collective-permute-start.9 = (bf16[2,256,512]{2,1,0:T(8,128)(2,1)S(1)}, bf16[2,256,512]{2,1,0:T(8,128)(2,1)S(1)}, u32[]{:S(2)}, u32[]{:S(2)}) collective-permute-start(bf16[2,256,512]{2,1,0:T(8,128)(2,1)S(1)} %latent.1.pair_ref.refs_4_.lat_ref), channel_id=1, source_target_pairs={{0,2},{1,7},{2,4},{3,1},{4,6},{5,3},{6,0},{7,5},{8,10},{9,15},{10,... | collective-permute-start | bytes 1572872 | tf_op jit(solution)/shard_map/ppermute | solution.py:63
  30.9 11.1 %copy-start = (bf16[4096,512]{1,0:T(8,128)(2,1)S(1)}, bf16[4096,512]{1,0:T(8,128)(2,1)}, u32[]{:S(2)}) copy-start(bf16[4096,512]{1,0:T(8,128)(2,1)} %refs_10_.3) | copy-start | bytes 12582916
  30.9 11.1 %copy-start.1 = (bf16[4096,512]{1,0:T(8,128)(2,1)S(1)}, bf16[4096,512]{1,0:T(8,128)(2,1)}, u32[]{:S(2)}) copy-start(bf16[4096,512]{1,0:T(8,128)(2,1)} %refs_11_.3) | copy-start | bytes 12582916
  30.9 11.1 %copy-start.2 = (bf16[4096,512]{1,0:T(8,128)(2,1)S(1)}, bf16[4096,512]{1,0:T(8,128)(2,1)}, u32[]{:S(2)}) copy-start(bf16[4096,512]{1,0:T(8,128)(2,1)} %refs_12_.3) | copy-start | bytes 12582916
  34.0 8.0 %copy-start.5 = (f32[4096]{0:T(1024)S(1)}, f32[4096]{0:T(1024)}, u32[]{:S(2)}) copy-start(f32[4096]{0:T(1024)} %param.12) | copy-start | bytes 49156
  41.8 7.8 %collective-permute-start.13 = (bf16[2,256,512]{2,1,0:T(8,128)(2,1)S(1)}, bf16[2,256,512]{2,1,0:T(8,128)(2,1)S(1)}, u32[]{:S(2)}, u32[]{:S(2)}) collective-permute-start(bf16[2,256,512]{2,1,0:T(8,128)(2,1)S(1)} %collective-permute-done.9.both_ref.refs_5_), channel_id=1, source_target_pairs={{0,1},{1,0},{2,3},{3,2},{4,5},{5,4},{6,7},{7,6},{8,9},{9,8},{10,11... | collective-permute-start | bytes 1572872 | tf_op jit(solution)/shard_map/ppermute | solution.py:55
  41.9 7.7 %collective-permute-start.12 = (bf16[1,256,512]{2,1,0:T(8,128)(2,1)S(1)}, bf16[1,256,512]{2,1,0:T(8,128)(2,1)S(1)}, u32[]{:S(2)}, u32[]{:S(2)}) collective-permute-start(bf16[1,256,512]{2,1,0:T(8,128)(2,1)S(1)} %slice.6), channel_id=1, source_target_pairs={{0,2},{1,7},{2,4},{3,1},{4,6},{5,3},{6,0},{7,5},{8,10},{9,15},{10,... | collective-permute-start | bytes 786440 | tf_op jit(solution)/shard_map/ppermute | solution.py:63
  49.5 1.5 collective-permute-start.14
  53.1 2.0 %collective-permute-start.15 = (bf16[4,256,256]{2,1,0:T(8,128)(2,1)S(1)}, bf16[4,256,256]{2,1,0:T(8,128)(2,1)S(1)}, u32[]{:S(2)}, u32[]{:S(2)}) collective-permute-start(bf16[4,256,256]{2,1,0:T(8,128)(2,1)S(1)} %get-tuple-element.57), channel_id=1, source_target_pairs={{0,1},{1,0},{2,3},{3,2},{4,5},{5,4},{6,7},{7,6},{8,9},{9,8},{10,11... | collective-permute-start | bytes 1572872 | tf_op jit(solution)/shard_map/ppermute | solution.py:55
  86.5 2.9 %collective-permute-start.16 = (bf16[16,128,256]{2,1,0:T(8,128)(2,1)S(1)}, bf16[16,128,256]{2,1,0:T(8,128)(2,1)S(1)}, u32[]{:S(2)}, u32[]{:S(2)}) collective-permute-start(bf16[16,128,256]{2,1,0:T(8,128)(2,1)S(1)} %slice.8), channel_id=1, source_target_pairs={{0,1},{1,0},{2,3},{3,2},{4,5},{5,4},{6,7},{7,6},{8,9},{9,8},{10,11... | collective-permute-start | bytes 3145736 | tf_op jit(solution)/shard_map/ppermute | solution.py:55
  101.0 2.7 %collective-permute-start.17 = (bf16[16,128,256]{2,1,0:T(8,128)(2,1)S(1)}, bf16[16,128,256]{2,1,0:T(8,128)(2,1)S(1)}, u32[]{:S(2)}, u32[]{:S(2)}) collective-permute-start(bf16[16,128,256]{2,1,0:T(8,128)(2,1)S(1)} %get-tuple-element.59), channel_id=1, source_target_pairs={{0,1},{1,0},{2,3},{3,2},{4,5},{5,4},{6,7},{7,6},{8,9},{9,8},{10,11... | collective-permute-start | bytes 3145736 | tf_op jit(solution)/shard_map/ppermute | solution.py:55
  104.0 28.9 %copy-start.4 = (bf16[512,4096]{1,0:T(8,128)(2,1)S(1)}, bf16[512,4096]{1,0:T(8,128)(2,1)}, u32[]{:S(2)}) copy-start(bf16[512,4096]{1,0:T(8,128)(2,1)} %refs_13_.3) | copy-start | bytes 12582916
  130.7 2.2 %collective-permute-start.18 = (bf16[4,256,256]{2,1,0:T(8,128)(2,1)S(1)}, bf16[4,256,256]{2,1,0:T(8,128)(2,1)S(1)}, u32[]{:S(2)}, u32[]{:S(2)}) collective-permute-start(bf16[4,256,256]{2,1,0:T(8,128)(2,1)S(1)} %get-tuple-element.62), channel_id=1, source_target_pairs={{0,1},{1,0},{2,3},{3,2},{4,5},{5,4},{6,7},{7,6},{8,9},{9,8},{10,11... | collective-permute-start | bytes 1572872 | tf_op jit(solution)/shard_map/ppermute | solution.py:55
  136.2 2.0 %collective-permute-start.19 = (bf16[1,512,512]{2,1,0:T(8,128)(2,1)S(1)}, bf16[1,512,512]{2,1,0:T(8,128)(2,1)S(1)}, u32[]{:S(2)}, u32[]{:S(2)}) collective-permute-start(bf16[1,512,512]{2,1,0:T(8,128)(2,1)S(1)} %get-tuple-element.67), channel_id=1, source_target_pairs={{0,1},{1,0},{2,3},{3,2},{4,5},{5,4},{6,7},{7,6},{8,9},{9,8},{10,11... | collective-permute-start | bytes 1572872 | tf_op jit(solution)/shard_map/ppermute | solution.py:55
  138.1 3.4 %collective-permute-start.20 = (bf16[3,512,512]{2,1,0:T(8,128)(2,1)S(1)}, bf16[3,512,512]{2,1,0:T(8,128)(2,1)S(1)}, u32[]{:S(2)}, u32[]{:S(2)}) collective-permute-start(bf16[3,512,512]{2,1,0:T(8,128)(2,1)S(1)} %get-tuple-element.71), channel_id=1, source_target_pairs={{0,1},{1,0},{2,3},{3,2},{4,5},{5,4},{6,7},{7,6},{8,9},{9,8},{10,11... | collective-permute-start | bytes 4718600 | tf_op jit(solution)/shard_map/ppermute | solution.py:55
  138.4 10.5 %collective-permute-start.21 = (bf16[512,512]{1,0:T(8,128)(2,1)S(1)}, bf16[512,512]{1,0:T(8,128)(2,1)S(1)}, u32[]{:S(2)}, u32[]{:S(2)}) collective-permute-start(bf16[512,512]{1,0:T(8,128)(2,1)S(1)} %far.1), channel_id=1, source_target_pairs={{0,2},{1,7},{2,4},{3,1},{4,6},{5,3},{6,0},{7,5},{8,10},{9,15},{10,... | collective-permute-start | bytes 1572872 | tf_op jit(solution)/shard_map/ppermute | solution.py:63
  141.9 12.6 %collective-permute-start.23 = (bf16[512,512]{1,0:T(8,128)(2,1)S(1)}, bf16[512,512]{1,0:T(8,128)(2,1)S(1)}, u32[]{:S(2)}, u32[]{:S(2)}) collective-permute-start(bf16[512,512]{1,0:T(8,128)(2,1)S(1)} %get-tuple-element.75), channel_id=1, source_target_pairs={{0,2},{1,7},{2,4},{3,1},{4,6},{5,3},{6,0},{7,5},{8,10},{9,15},{10,... | collective-permute-start | bytes 1572872 | tf_op jit(solution)/shard_map/ppermute | solution.py:63
  148.9 11.2 %copy-start.9 = (bf16[256,512]{1,0:T(8,128)(2,1)S(1)}, bf16[256,512]{1,0:T(8,128)(2,1)}, u32[]{:S(2)}) copy-start(bf16[256,512]{1,0:T(8,128)(2,1)} %cot_ref.1) | copy-start | bytes 786436
  149.0 11.1 %collective-permute-start.22 = (bf16[512,512]{1,0:T(8,128)(2,1)S(1)}, bf16[512,512]{1,0:T(8,128)(2,1)S(1)}, u32[]{:S(2)}, u32[]{:S(2)}) collective-permute-start(bf16[512,512]{1,0:T(8,128)(2,1)S(1)} %pass.1), channel_id=1, source_target_pairs={{0,2},{1,7},{2,4},{3,1},{4,6},{5,3},{6,0},{7,5},{8,10},{9,15},{10,... | collective-permute-start | bytes 1572872 | tf_op jit(solution)/shard_map/ppermute | solution.py:63
  154.5 5.6 %collective-permute-start.24 = (bf16[512,512]{1,0:T(8,128)(2,1)S(1)}, bf16[512,512]{1,0:T(8,128)(2,1)S(1)}, u32[]{:S(2)}, u32[]{:S(2)}) collective-permute-start(bf16[512,512]{1,0:T(8,128)(2,1)S(1)} %collective-permute-done.23), channel_id=1, source_target_pairs={{0,1},{1,0},{2,3},{3,2},{4,5},{5,4},{6,7},{7,6},{8,9},{9,8},{10,11... | collective-permute-start | bytes 1572872 | tf_op jit(solution)/shard_map/ppermute | solution.py:55
